TPU v7x, 32 devices: a whole 2x2x4 slice. The times are simulated.
32 devices in a mesh: slides: 1, row: 2 (over core), col: 16 (over z, y, x).
Axes of the slice: x: 2, y: 2, z: 4, core: 2. Of those that a mesh axis runs over, the one named last changes fastest.
Arguments:
- slide: bfloat16 [56, 112, 1024], P(('slides', 'row'), 'col'), may hold values from -6 to 6
- tissue: int32 [56, 112], P(('slides', 'row'), 'col'), may hold values from 0 to 1, as said below
- w_in: bfloat16 [1024, 2048], replicated, may hold values from -0.1875 to 0.1875
- w_bcd: bfloat16 [1024, 48], replicated, may hold values from -0.1875 to 0.1875
- dt_bias: float32 [16], replicated, may hold values from -2 to 1
- rate_x: float32 [16], replicated, as said below
- rate_y: float32 [16], replicated, as said below
- d_skip: float32 [16], replicated, may hold values from 0.5 to 2
- norm_gain: float32 [1024], replicated, may hold values from 0.1 to 1.9
- w_out: bfloat16 [1024, 1024], replicated, may hold values from -0.1875 to 0.1875
Outputs:
- mixed: bfloat16 [56, 112, 1024], P(('slides', 'row'), 'col')
Inputs may be any that keep to these rules, and one draw needn't show every extreme that they name: 1 marks a tissue patch, 0 background. `rate_x`: positive decay rates per head. `rate_y`: positive decay rates per head.
All inputs are finite; a program needn't handle non-finite values.
Results may differ from a plain program's by a relative error of at most 0.013.
Values may be sent and summed in bfloat16 or wider, within the bound.
No kernel may reach another device: no remote copies, remote signals or barrier semaphores. Data moves between devices by JAX's collectives and lax.ppermute only.
A program may use at most 320 MiB of HBM per device.

v0:
```python
import jax
import jax.numpy as jnp
from jax import lax
from jax.sharding import PartitionSpec as P

norm_eps = 1e-05


def carried_in_2(value, axis, join, neutral):
    count, mine = (lax.axis_size(axis), lax.axis_index(axis))
    pieces = jax.tree.map(lambda part: lax.all_gather(part, axis), value)
    so_far = jax.tree.map(
        lambda part, zero: jnp.full_like(part, 0) + jnp.asarray(zero, part.dtype), value, neutral
    )

    def hop(position, so_far):
        longer = join(so_far, jax.tree.map(lambda part: part[position], pieces))
        return jax.tree.map(lambda new, old: jnp.where(position < mine, new, old), longer, so_far)

    return lax.fori_loop(0, count - 1, hop, so_far)


def chain_join(earlier, later):
    return (earlier[0] + later[0], jnp.exp(later[0]) * earlier[1] + later[1])


def per_device(slide, tissue, w_in, w_bcd, dt_bias, rate_x, rate_y, d_skip, norm_gain, w_out):
    tile_rows, tile_cols, model_width = slide.shape
    inner_width = w_out.shape[0]
    head_count = dt_bias.shape[0]
    head_width = inner_width // head_count
    state_size = (w_bcd.shape[1] - head_count) // 2
    cell_mask = tissue.astype(jnp.float32).reshape(tile_rows * tile_cols, 1)
    flat_cells = slide.reshape(tile_rows * tile_cols, model_width)
    has_tissue = jnp.any(tissue > 0)

    def project_cells():
        projected = jnp.dot(flat_cells, w_in, preferred_element_type=jnp.float32)
        values = projected[:, :inner_width].astype(jnp.bfloat16) * cell_mask.astype(jnp.bfloat16)
        gate_part = projected[:, inner_width:].astype(jnp.bfloat16)
        terms = jnp.dot(flat_cells, w_bcd, preferred_element_type=jnp.float32)
        step_part = (cell_mask * jax.nn.softplus(terms[:, 2 * state_size :] + dt_bias)).astype(
            jnp.bfloat16
        )
        packed = jnp.concatenate(
            [terms[:, : 2 * state_size].astype(jnp.bfloat16), step_part], axis=1
        )
        return (values, gate_part, packed)

    def empty_terms():
        return (
            jnp.zeros((tile_rows * tile_cols, inner_width), jnp.bfloat16),
            jnp.zeros((tile_rows * tile_cols, inner_width), jnp.bfloat16),
            jnp.zeros((tile_rows * tile_cols, 2 * state_size + head_count), jnp.bfloat16),
        )

    values, gate_z, packed = lax.cond(has_tissue, project_cells, empty_terms)
    step_cells = (
        packed[:, 2 * state_size :].astype(jnp.float32).reshape(tile_rows, tile_cols, head_count)
    )
    b_cells = packed[:, :state_size].astype(jnp.float32).reshape(tile_rows, tile_cols, state_size)
    c_cells = (
        packed[:, state_size : 2 * state_size]
        .astype(jnp.float32)
        .reshape(tile_rows, tile_cols, state_size)
    )
    vals_cells = values.astype(jnp.float32).reshape(tile_rows, tile_cols, inner_width)
    step_chan = jnp.repeat(step_cells, head_width, axis=2)
    source_cells = step_chan * vals_cells
    log_x = -step_chan * jnp.repeat(rate_x, head_width)
    decay_x = jnp.exp(log_x)
    log_y = -step_chan * jnp.repeat(rate_y, head_width)
    decay_y = jnp.exp(log_y)
    edge = jnp.zeros((tile_rows, state_size, inner_width), jnp.float32)
    for column in range(tile_cols):
        edge = (
            decay_x[:, column, None, :] * edge
            + b_cells[:, column, :, None] * source_cells[:, column, None, :]
        )
    log_edge = jnp.sum(log_x, axis=1)[:, None, :]
    from_left = carried_in_2(
        (log_edge, edge), "col", chain_join, (jnp.zeros_like(log_edge), jnp.zeros_like(edge))
    )
    entry_left = from_left[1]

    def cell_row(carry, row_data):
        vertical, cum = carry
        a_row, ay_row, ly_row, u_row, b_row, c_row, left = row_data
        running = left
        pieces = []
        for column in range(tile_cols):
            running = (
                a_row[column][None, :] * running + b_row[column][:, None] * u_row[column][None, :]
            )
            pieces.append(running)
        vertical = ay_row[:, None, :] * vertical + jnp.stack(pieces)
        cum = cum + ly_row[:, None, :]
        out_row = jnp.einsum("jn,jnc->jc", c_row, vertical, precision=lax.Precision.HIGHEST)
        return ((vertical, cum), (out_row, cum[:, 0, :]))

    start = (
        jnp.zeros((tile_cols, state_size, inner_width), jnp.float32),
        jnp.zeros((tile_cols, 1, inner_width), jnp.float32),
    )
    (bottom_state, bottom_log), (local_out, cum_rows) = lax.scan(
        cell_row, start, (decay_x, decay_y, log_y, source_cells, b_cells, c_cells, entry_left)
    )
    top_zero = (jnp.zeros_like(bottom_log), jnp.zeros_like(bottom_state))
    from_above = carried_in_2((bottom_log, bottom_state), "row", chain_join, top_zero)
    entry_down = from_above[1]
    carried_in = jnp.einsum("ijn,jnc->ijc", c_cells, entry_down, precision=lax.Precision.HIGHEST)
    cell_out = (
        local_out + jnp.exp(cum_rows) * carried_in + jnp.repeat(d_skip, head_width) * vals_cells
    )
    y_cells = cell_out.astype(jnp.bfloat16).reshape(tile_rows * tile_cols, inner_width)

    def finish_cells():
        gated = y_cells.astype(jnp.float32) * jax.nn.silu(gate_z.astype(jnp.float32))
        scaled = (
            gated
            * lax.rsqrt(jnp.mean(gated * gated, axis=-1, keepdims=True) + norm_eps)
            * norm_gain
        )
        result = (
            jnp.dot(scaled.astype(jnp.bfloat16), w_out, preferred_element_type=jnp.float32)
            * cell_mask
        )
        return result.astype(jnp.bfloat16)

    def empty_output():
        return jnp.zeros((tile_rows * tile_cols, model_width), jnp.bfloat16)

    final_cells = lax.cond(has_tissue, finish_cells, empty_output)
    return final_cells.reshape(tile_rows, tile_cols, model_width)


def solution(mesh):
    placed = (
        P(("slides", "row"), "col", None),
        P(("slides", "row"), "col"),
        P(),
        P(),
        P(),
        P(),
        P(),
        P(),
        P(),
        P(),
    )
    return jax.shard_map(
        per_device,
        mesh=mesh,
        in_specs=placed,
        out_specs=P(("slides", "row"), "col", None),
        check_vma=False,
    )
```

profile of v0, /device:TPU:0, one launch (start us, length us, event | category | flops | bytes accessed | tf_op | source)
XLA Modules:
  0.0 686.1 jit_solution(13298296646756493034)
XLA Ops:
  13.0 2.1 fusion.36
  16.7 2.8 multiply_add_fusion.6
  20.4 58.8 %all-gather.5.cloned.1.call-done = f32[16,28,1,1024]{3,2,1,0:T(1,128)} async-done(((f32[1,28,1,1024]{3,2,1,0:T(1,128)}), f32[16,28,1,1024]{3,2,1,0:T(1,128)}) %all-gather.5.cloned.1.call-update) | async-done | bytes 1835024 | tf_op jit(solution)/shard_map/all_gather | solution.py:11
  79.1 311.5 %all-gather.7.cloned.1.call-done = f32[16,28,16,1024]{3,2,1,0:T(8,128)} async-done(((f32[1,28,16,1024]{3,2,1,0:T(8,128)}), f32[16,28,16,1024]{3,2,1,0:T(8,128)}) %all-gather.7.cloned.1.call-update) | async-done | bytes 29360144 | tf_op jit(solution)/shard_map/all_gather | solution.py:11
  390.7 60.2 %while.36 = (s32[]{:T(128)}, f32[28,16,1024]{2,1,0:T(8,128)S(1)}, s32[]{:T(128)}, f32[16,28,1,1024]{3,2,1,0:T(1,128)}, f32[16,28,16,1024]{3,2,1,0:T(8,128)}, /*index=5*/s32[]{:T(128)}, s32[]{:T(128)}) while((s32[]{:T(128)}, f32[28,16,1024]{2,1,0:T(8,128)S(1)}, s32[]{:T(128)}, f32[16,28,1,1024]{3,2,1,0:T(1,128)}, ...), condition=%wide.region_5.6_spmd.clone, body=%wide.region_4.5_spmd.clone.sunk | while | flops 1835012 | bytes 6078569 | solution.py:20
  391.6 3.0 fusion.58
  395.7 3.0 fusion.58
  399.7 3.0 fusion.58
  403.7 3.0 fusion.58
  407.7 3.0 fusion.58
  411.7 3.0 fusion.58
  415.7 3.0 fusion.58
  419.7 3.0 fusion.58
  423.7 3.0 fusion.58
  427.8 3.0 fusion.58
  431.8 3.0 fusion.58
  435.8 3.0 fusion.58
  439.8 3.0 fusion.58
  443.8 3.0 fusion.58
  447.8 3.0 fusion.58
  450.9 220.8 %while.37 = (s32[]{:T(128)}, f32[7,16,1024]{2,1,0:T(8,128)S(1)}, f32[7,1,1024]{2,1,0:T(1,128)S(1)}, f32[28,7,1024]{2,0,1:T(8,128)}, f32[28,7,1024]{2,0,1:T(8,128...) while((s32[]{:T(128)}, f32[7,16,1024]{2,1,0:T(8,128)S(1)}, ...), condition=%wide.region_7.8_spmd.clone, body=%wide.region_6.7_spmd.clone.sunk | while | flops 3110920 | bytes 3601364 | solution.py:105
  454.3 1.8 dynamic_update_slice.11
  462.2 1.8 dynamic_update_slice.11
  464.9 1.7 dynamic_update_slice.12
  470.1 1.8 dynamic_update_slice.11
  472.8 1.7 dynamic_update_slice.12
  478.0 1.8 dynamic_update_slice.11
  485.9 1.8 dynamic_update_slice.11
  488.6 1.7 dynamic_update_slice.12
  493.8 1.8 dynamic_update_slice.11
  496.5 1.7 dynamic_update_slice.12
  501.6 1.8 dynamic_update_slice.11
  509.5 1.8 dynamic_update_slice.11
  517.4 1.8 dynamic_update_slice.11
  520.2 1.7 dynamic_update_slice.12
  525.3 1.8 dynamic_update_slice.11
  528.1 1.7 dynamic_update_slice.12
  533.2 1.8 dynamic_update_slice.11
  536.0 1.7 dynamic_update_slice.12
  541.1 1.8 dynamic_update_slice.11
  543.9 1.7 dynamic_update_slice.12
  549.0 1.8 dynamic_update_slice.11
  551.7 1.7 dynamic_update_slice.12
  556.9 1.8 dynamic_update_slice.11
  559.6 1.7 dynamic_update_slice.12
  564.8 1.8 dynamic_update_slice.11
  567.5 1.7 dynamic_update_slice.12
  572.7 1.8 dynamic_update_slice.11
  575.4 1.7 dynamic_update_slice.12
  580.6 1.8 dynamic_update_slice.11
  588.5 1.8 dynamic_update_slice.11
  596.3 1.8 dynamic_update_slice.11
  604.2 1.8 dynamic_update_slice.11
  612.1 1.8 dynamic_update_slice.11
  620.0 1.8 dynamic_update_slice.11
  627.8 1.8 dynamic_update_slice.11
  635.7 1.8 dynamic_update_slice.11
  646.3 1.8 dynamic_update_slice.12
  654.2 1.8 dynamic_update_slice.12
  662.1 1.8 dynamic_update_slice.12
  670.0 1.8 dynamic_update_slice.12
  671.7 2.6 all-gather.1
  674.3 1.8 all-gather
  676.2 2.2 fusion.25
  (587 shorter events, 171.4 us)
Async XLA Ops:
  6.5 72.6 %all-gather.5.cloned.1.call-start = ((), (), s32[]{:S(2)}) async-start(), calls=%async_computation | async-start | bytes 1949696 | tf_op jit(solution)/shard_map/all_gather | solution.py:11
  9.4 0.7 copy-start.5
  9.6 1.8 copy-start.2
  9.6 3.4 copy-start
  11.4 379.3 %all-gather.7.cloned.1.call-start = ((), (), s32[]{:S(2)}) async-start(), calls=%async_computation.1 | async-start | bytes 31195136 | tf_op jit(solution)/shard_map/all_gather | solution.py:11
  11.5 1.0 copy-start.6
  19.6 0.7 copy-start.7
  671.7 4.5 copy-start.1
  676.2 2.2 copy-start.3
  676.2 2.2 copy-start.8
  678.5 0.8 copy-start.4
Sparse Core Ops, SparseCore 0:
  11.5 67.5 all-gather.4
  81.8 308.8 all-gather.6
where the time goes:
time: 696 us; the launch traced here: 686 us
  waiting for transfers between devices  370 us (53%)
  local copies, waits for them, and re-layouts  174 us (25%)
  other arithmetic  108 us (16%)
  between operations  14.4 us (2%)
  matrix products  11.9 us (2%)
    all_gather x2, waiting for transfers between devices, carried_in_2(): pieces = jax.tree.map(lambda part: lax.all_gather(part, axis), value)  370 us
    dynamic_update_slice x84, local copies, waits for them, and re-layouts, per_device(): lax.scan(cell_row, start, (decay_x, decay_y, log_y, source_cells, b_cells...  98.8 us
    select_n x15, other arithmetic, hop(): jnp.where(position < mine, new, old)  45.6 us
    slice x28, local copies, waits for them, and re-layouts, cell_row(): u_row[column][None, :]  28.3 us
    dynamic_slice x84, local copies, waits for them, and re-layouts, per_device(): lax.scan(cell_row, start, (decay_x, decay_y, log_y, source_cells, b_cells...  27.7 us
    add x28, other arithmetic, cell_row(): cum = cum + ly_row[:, None, :]  27.5 us
    while x168, other arithmetic  16.3 us
  transfers between devices with their start and end apart: 2, of which 2 were waited for; matrix products, arithmetic and copies ran while one was open for 1% of the time, Pallas kernels for 0%

commit v1 on v0

v1 whole, which is shorter than its diff:
```python
import functools

import jax
import jax.numpy as jnp
import numpy as np
from jax import lax
from jax.experimental import pallas as pl
from jax.experimental.pallas import tpu as pltpu
from jax.sharding import PartitionSpec as P

norm_eps = 1e-05
LANES = 128
F32 = jnp.float32
BF16 = jnp.bfloat16


def round_up(value, step):
    return -(-value // step) * step


def mm(a, b):
    return jnp.dot(a, b, preferred_element_type=F32)


def nt_dot(a, b):
    return lax.dot_general(a, b, (((1,), (1,)), ((), ())), preferred_element_type=F32)


class Plan:
    def __init__(self, rows, cols, states, heads, width, devices):
        self.rows, self.cols, self.states, self.heads = rows, cols, states, heads
        self.cells = rows * cols
        self.padded = round_up(self.cells, 8)
        self.group = width // devices
        self.devices = devices
        self.head_width = width // heads
        self.width = width
        assert self.head_width % self.group == 0
        assert self.group + 2 * states + heads <= LANES and LANES % self.group == 0
        self.row_pad = LANES // (LANES // round_up(rows, 8))
        while LANES % self.row_pad:
            self.row_pad += 8
        self.copies = LANES // self.row_pad
        assert states % self.copies == 0
        self.col_pad = round_up(cols, 8)
        self.edge = states * self.row_pad
        self.top = states * self.col_pad
        self.blocks = LANES // self.group
        self.block = round_up(-(-self.cells // self.blocks), 8)

    def constants(self):
        rows, cols, cells, padded = self.rows, self.cols, self.cells, self.padded
        i = np.arange(padded) // cols
        j = np.arange(padded) % cols
        real = np.arange(padded) < cells
        io = np.concatenate([i, np.full(self.col_pad, rows - 1)])
        jo = np.concatenate([j, np.arange(self.col_pad)])
        ro = np.concatenate([real, np.arange(self.col_pad) < cols])
        le = np.arange(self.row_pad)
        both = real[:, None] & real[None, :]
        out = {}
        a1 = (j[None] <= jo[:, None]) & ro[:, None] & real[None]
        a2 = (j[None] == jo[:, None]) & (i[None] <= io[:, None]) & ro[:, None] & real[None]
        out["a1"], out["a2"] = a1, a2
        out["b1"] = (i[:, None] == i[None]) & (j[:, None] > j[None]) & both
        out["b2"] = (i[:, None] > i[None]) & both
        edge = np.tile(le, self.copies)
        out["e1"] = (i[:, None] == edge[None]) & real[:, None]
        out["e2"] = (i[:, None] > edge[None]) & real[:, None]
        out["mask"] = (io[:, None] >= i[None]) & (jo[:, None] >= j[None]) & ro[:, None] & real[None]
        out["emask"] = (io[:, None] >= edge[None]) & (edge < rows)[None] & ro[:, None]
        out["rowsel"] = (le[:, None] == i[None]) & real[None]
        n = np.arange(self.states)
        out["rep"] = n[:, None] == np.repeat(n, self.row_pad)[None]
        out["rep8"] = n[:, None] == np.repeat(n, self.col_pad)[None]
        out["diag"] = np.repeat(n, self.col_pad)[:, None] == np.repeat(n, self.row_pad)[None]
        out["colsel"] = (
            np.tile(np.arange(self.col_pad), self.states)[None] == j[:, None]
        ) & real[:, None]
        return {k: jnp.asarray(x.astype(np.float32), BF16) for k, x in out.items()}


def full(shape):
    return pl.BlockSpec(shape, lambda *_: (0,) * len(shape))


def project_kernel(plan, tile, x_ref, w_ref, wt_ref, mask_ref, bias_ref, v_ref, pay_ref, terms):
    step = pl.program_id(0)
    group, states, cells = plan.group, plan.states, plan.cells
    x = x_ref[...]
    m = mask_ref[...]
    lane = lax.broadcasted_iota(jnp.int32, (cells, LANES), 1)

    @pl.when(step == 0)
    def _():
        t = mm(x, wt_ref[...])
        z = t + bias_ref[...]
        soft = jnp.maximum(z, 0.0) + jnp.log1p(jnp.exp(-jnp.abs(z)))
        t = jnp.where(lane < group + 2 * states, t, m * soft)
        terms[...] = jnp.where(lane < group + 2 * states + plan.heads, t, 0.0)

    v = mm(x, w_ref[...]).astype(BF16).astype(F32) * m
    v_ref[...] = v.astype(BF16)
    rest = terms[...]
    for k in range(tile // group):
        lo = k * group
        base = lo // LANES * LANES
        part = v[:, base : base + LANES]
        if lo % LANES:
            part = pltpu.roll(part, LANES - lo % LANES, 1)
        pay_ref[k, 0:cells, :] = jnp.where(lane < group, part, rest).astype(BF16)
        if plan.padded > cells:
            pay_ref[k, cells : plan.padded, :] = jnp.zeros((plan.padded - cells, LANES), BF16)


def project(plan, x, w_in, w_bcd, cell_mask, dt_bias):
    group, states, heads = plan.group, plan.states, plan.heads
    tile = max(2 * LANES, group)
    before = group
    after = LANES - group - 2 * states - heads
    wt = jnp.pad(w_bcd, ((0, 0), (before, after)))
    bias = jnp.pad(dt_bias, (group + 2 * states, after)).reshape(1, LANES)
    depth = x.shape[1]
    return pl.pallas_call(
        functools.partial(project_kernel, plan, tile),
        grid=(plan.width // tile,),
        in_specs=[
            full(x.shape),
            pl.BlockSpec((depth, tile), lambda s: (0, s)),
            full(wt.shape),
            full(cell_mask.shape),
            full(bias.shape),
        ],
        out_specs=[
            pl.BlockSpec((plan.cells, tile), lambda s: (0, s)),
            pl.BlockSpec((tile // group, plan.padded, LANES), lambda s: (s, 0, 0)),
        ],
        out_shape=[
            jax.ShapeDtypeStruct((plan.cells, plan.width), BF16),
            jax.ShapeDtypeStruct((plan.devices, plan.padded, LANES), BF16),
        ],
        scratch_shapes=[pltpu.VMEM((plan.cells, LANES), F32)],
        name="project",
    )(x, w_in, wt, cell_mask, bias)


def my_head(plan, axis):
    return lax.axis_index(axis) * plan.group // plan.head_width


def rows_of(plan, head, pay):
    shape = (plan.states + 16, LANES)
    at = lax.broadcasted_iota(jnp.int32, shape, 0)
    lane = lax.broadcasted_iota(jnp.int32, shape, 1)
    first = plan.group + 2 * plan.states
    wanted = jnp.where(at < plan.states, plan.group + at, first + head)
    select = (lane == wanted).astype(F32).astype(BF16)
    return nt_dot(select, pay)


def edges_kernel(
    plan, axis, rates, pay_ref, a1_ref, a2_ref, b1_ref, b2_ref, e1_ref, e2_ref, mask_ref, emask_ref,
    rowsel_ref, diag_ref, edge_ref, top_ref, carry,
):
    states, group, padded = plan.states, plan.group, plan.padded
    head = my_head(plan, axis)
    rate_x, rate_y = rates[0, head], rates[1, head]

    @pl.when(pl.program_id(0) == 0)
    def _():
        carry[...] = jnp.zeros_like(carry)

    pay = pay_ref[0]
    v = pay[:, :group]
    table = rows_of(plan, head, pay)
    dt_row = table[states : states + 1]
    dt_low = table[states : states + 16].astype(BF16)
    bdt = table[:states] * dt_row
    before = carry[...]
    before_low = before.astype(BF16)
    edge_ref[0] = before_low

    right = jnp.exp(-rate_x * mm(dt_low, b1_ref[...])[0:1])
    bd = (bdt * right).astype(BF16)
    rowsel = rowsel_ref[...]
    left_map = jnp.concatenate(
        [rowsel * jnp.broadcast_to(bd[n : n + 1], rowsel.shape) for n in range(states)], axis=0
    )
    total = jnp.sum(rowsel.astype(F32) * dt_row, axis=1, keepdims=True)
    decay = jnp.broadcast_to(jnp.exp(-rate_x * total), (plan.row_pad, group))
    decay = jnp.concatenate([decay] * states, axis=0)
    carry[...] = decay * before + mm(left_map, v)

    dt_cells = dt_low[0:1]
    a1 = a1_ref[...] * dt_cells
    a2 = a2_ref[...] * dt_cells
    down = jnp.exp(-(rate_x * mm(a1, b1_ref[...]) + rate_y * mm(a2, b2_ref[...])))
    down = down * mask_ref[...].astype(F32)
    side = jnp.exp(-(rate_x * mm(a1, e1_ref[...]) + rate_y * mm(a2, e2_ref[...])))
    side = side * emask_ref[...].astype(F32)
    top_map = jnp.concatenate(
        [down * jnp.broadcast_to(bdt[n : n + 1], down.shape) for n in range(states)], axis=0
    ).astype(BF16)
    side = jnp.concatenate([side] * (states // plan.copies), axis=1)
    side_map = jnp.concatenate([side] * states, axis=0).astype(BF16) * diag_ref[...]
    top_ref[0] = (mm(top_map, v) + mm(side_map, before_low)).astype(BF16)


def cells_kernel(
    plan, axis, rates, pay_ref, edge_ref, top_ref, a1_ref, a2_ref, b1_ref, b2_ref, e1_ref, e2_ref,
    mask_ref, emask_ref, rep_ref, rep8_ref, colsel_ref, out_ref,
):
    states, group, padded = plan.states, plan.group, plan.padded
    head = my_head(plan, axis)
    rate_x, rate_y = rates[0, head], rates[1, head]
    pay = pay_ref[0]
    v = pay[:, :group]
    table = rows_of(plan, head, pay)
    dt_row = table[states : states + 1]
    dt_cells = dt_row.astype(BF16)
    bdt = (table[:states] * dt_row).astype(BF16)
    c = pay[:, group + states : group + 2 * states]

    a1 = a1_ref[...] * dt_cells
    a2 = a2_ref[...] * dt_cells
    inner = jnp.exp(-(rate_x * mm(a1, b1_ref[...]) + rate_y * mm(a2, b2_ref[...])))
    scores = mm(c, bdt) * inner * mask_ref[...].astype(F32)
    y = mm(scores.astype(BF16), v)

    side = jnp.exp(-(rate_x * mm(a1, e1_ref[...]) + rate_y * mm(a2, e2_ref[...])))
    side = side * emask_ref[...].astype(F32)
    side = jnp.concatenate([side] * (states // plan.copies), axis=1)
    y = y + mm((mm(c, rep_ref[...]) * side).astype(BF16), edge_ref[0])

    above = jnp.exp(-rate_y * jnp.sum(a2.astype(F32), axis=1, keepdims=True))
    down = mm(c, rep8_ref[...]) * colsel_ref[...].astype(F32) * above
    y = y + mm(down.astype(BF16), top_ref[0])

    y = y.astype(BF16).astype(F32)
    for k in range(plan.blocks):
        lo, hi = k * plan.block, min((k + 1) * plan.block, padded)
        if lo < hi:
            out_ref[0, 0 : hi - lo, k * group : (k + 1) * group] = y[lo:hi].astype(BF16)


def scan_calls(plan, row_axis, col_axis, pay, rates):
    consts = plan.constants()
    tiles = plan.devices
    cut = plan.padded
    tile_spec = pl.BlockSpec((1, plan.padded, LANES), lambda t: (t, 0, 0))
    edge_spec = pl.BlockSpec((1, plan.edge, plan.group), lambda t: (t, 0, 0))
    top_spec = pl.BlockSpec((1, plan.top, plan.group), lambda t: (t, 0, 0))
    smem = pl.BlockSpec(memory_space=pltpu.SMEM)
    shared = [consts[k] for k in ("b1", "b2", "e1", "e2")]
    low = [consts[k][cut:] for k in ("a1", "a2")]
    low += shared + [consts["mask"][cut:], consts["emask"][cut:], consts["rowsel"], consts["diag"]]
    edges, tops = pl.pallas_call(
        functools.partial(edges_kernel, plan, col_axis),
        grid=(tiles,),
        in_specs=[smem, tile_spec] + [full(x.shape) for x in low],
        out_specs=[edge_spec, top_spec],
        out_shape=[
            jax.ShapeDtypeStruct((tiles, plan.edge, plan.group), BF16),
            jax.ShapeDtypeStruct((tiles, plan.top, plan.group), BF16),
        ],
        scratch_shapes=[pltpu.VMEM((plan.edge, plan.group), F32)],
        name="edges",
    )(rates, pay, *low)

    count = lax.axis_size(row_axis)
    down = [(r, r + 1) for r in range(count - 1)]
    entry = lax.ppermute(tops, row_axis, down)
    if count > 2:
        head = my_head(plan, col_axis)
        at = plan.group + 2 * plan.states + head
        dt = lax.dynamic_slice_in_dim(pay[:, : plan.cells].astype(F32), at, 1, 2)
        total = jnp.sum(dt.reshape(tiles, plan.rows, plan.cols), axis=1)
        total = jnp.pad(total, ((0, 0), (0, plan.col_pad - plan.cols)))
        keep = jnp.tile(jnp.exp(-rates[1, head] * total), (1, plan.states))[..., None]
        for _ in range(count - 2):
            entry = lax.ppermute(
                (tops.astype(F32) + keep * entry.astype(F32)).astype(BF16), row_axis, down
            )

    high = [consts[k][:cut] for k in ("a1", "a2")]
    high += shared + [consts["mask"][:cut], consts["emask"][:cut]]
    high += [consts[k] for k in ("rep", "rep8", "colsel")]
    return pl.pallas_call(
        functools.partial(cells_kernel, plan, col_axis),
        grid=(tiles,),
        in_specs=[smem, tile_spec, edge_spec, top_spec] + [full(x.shape) for x in high],
        out_specs=pl.BlockSpec((1, plan.block, LANES), lambda t: (t, 0, 0)),
        out_shape=jax.ShapeDtypeStruct((tiles, plan.block, LANES), BF16),
        name="cells",
    )(rates, pay, edges, entry, *high)


def finish_kernel(plan, y_ref, v_ref, z_ref, skip_ref, gain_ref, mask_ref, w_ref, out_ref, full_ref):
    group, blocks, block, cells = plan.group, plan.blocks, plan.block, plan.cells
    lane = lax.broadcasted_iota(jnp.int32, (block, LANES), 1)
    for tile in range(plan.width // LANES):
        for k in range(blocks):
            lo, hi = k * block, min((k + 1) * block, cells)
            if lo >= hi:
                continue
            joined = None
            for d in range(blocks):
                part = y_ref[tile * blocks + d].astype(F32)
                shift = (d - k) * group % LANES
                if shift:
                    part = pltpu.roll(part, shift, 1)
                joined = part if joined is None else jnp.where(lane < d * group, joined, part)
            full_ref[lo:hi, tile * LANES : (tile + 1) * LANES] = joined[: hi - lo]
    y = full_ref[...] + skip_ref[...] * v_ref[...].astype(F32)
    y = y.astype(BF16).astype(F32)
    z = z_ref[...].astype(F32)
    gated = y * (z * (1.0 / (1.0 + jnp.exp(-z))))
    scale = lax.rsqrt(jnp.mean(gated * gated, axis=-1, keepdims=True) + norm_eps)
    normed = (gated * scale * gain_ref[...]).astype(BF16)
    out_ref[...] = (mm(normed, w_ref[...]) * mask_ref[...]).astype(BF16)


def finish(plan, y, v, z, skip, gain, cell_mask, w_out):
    args = (y, v, z, skip, gain, cell_mask, w_out)
    return pl.pallas_call(
        functools.partial(finish_kernel, plan),
        in_specs=[full(a.shape) for a in args],
        out_specs=full((plan.cells, w_out.shape[1])),
        out_shape=jax.ShapeDtypeStruct((plan.cells, w_out.shape[1]), BF16),
        scratch_shapes=[pltpu.VMEM((plan.cells, plan.width), F32)],
        grid=(1,),
        name="finish",
    )(*args)


def per_device(slide, tissue, w_in, w_bcd, dt_bias, rate_x, rate_y, d_skip, norm_gain, w_out):
    rows, cols, model_width = slide.shape
    width = w_out.shape[0]
    heads = dt_bias.shape[0]
    states = (w_bcd.shape[1] - heads) // 2
    plan = Plan(rows, cols, states, heads, width, lax.axis_size("col"))
    cell_mask = tissue.astype(F32).reshape(plan.cells, 1)
    x = slide.reshape(plan.cells, model_width)
    v, pay = project(plan, x, w_in, w_bcd, cell_mask, dt_bias)
    pay = lax.all_to_all(pay, "col", 0, 0, tiled=True)
    z = jnp.dot(x, w_in[:, width:], preferred_element_type=F32).astype(BF16)
    rates = jnp.stack([rate_x, rate_y])
    y = scan_calls(plan, "row", "col", pay, rates)
    y = lax.all_to_all(y, "col", 0, 0, tiled=True)
    skip = jnp.repeat(d_skip, width // heads).reshape(1, width)
    out = finish(plan, y, v, z, skip, norm_gain.reshape(1, width), cell_mask, w_out)
    return out.reshape(rows, cols, model_width)


def solution(mesh):
    placed = (
        P(("slides", "row"), "col", None),
        P(("slides", "row"), "col"),
        P(),
        P(),
        P(),
        P(),
        P(),
        P(),
        P(),
        P(),
    )
    return jax.shard_map(
        per_device,
        mesh=mesh,
        in_specs=placed,
        out_specs=P(("slides", "row"), "col", None),
        check_vma=False,
    )
```

time: 696 us -> 103 us (0.15); the launches traced: 686 us -> 101 us
  waiting for transfers between devices: 370 us -> 31.4 us
  local copies, waits for them, and re-layouts: 174 us -> 11.1 us
  other arithmetic: 108 us -> 1.28 us
  Pallas kernels: 0 us -> 39.8 us
  starting transfers between devices: 0.04 us -> 14.7 us
  between operations: 14.4 us -> 0.07 us
  matrix products: 11.9 us -> 2.94 us
    all_gather x2 -> x0, waiting for transfers between devices: 370 us -> none  [carried_in_2(): pieces = jax.tree.map(lambda part: lax.all_gather(part, axis), value)]
    dynamic_update_slice x84 -> x0, local copies, waits for them, and re-layouts: 98.8 us -> none  [per_device(): lax.scan(cell_row, start, (decay_x, decay_y, log_y, source_cells, b_cells...]
    select_n x15 -> x0, other arithmetic: 45.6 us -> none  [hop(): jnp.where(position < mine, new, old)]
    dynamic_slice x99 -> x0, local copies, waits for them, and re-layouts: 41.3 us -> none  [the longest x84 27.7 us: per_device(): lax.scan(cell_row, start, (decay_x, decay_y, log_y, source_cells, b_cells...]
    pallas_call x0 -> x4, Pallas kernels: none -> 39.8 us  [the longest x1 17.6 us: scan_calls(): pl.pallas_call(functools.partial(cells_kernel, plan, col_axis), grid=(til...]
    add x57 -> x0, other arithmetic: 36.6 us -> none  [the longest x28 27.5 us: cell_row(): cum = cum + ly_row[:, None, :]]
    all_to_all x0 -> x2, waiting for transfers between devices: none -> 29.7 us  [the longest x1 19.7 us: per_device(): pay = lax.all_to_all(pay, 'col', 0, 0, tiled=True)]
    slice x30 -> x0, local copies, waits for them, and re-layouts: 28.5 us -> none  [the longest x28 28.3 us: cell_row(): u_row[column][None, :]]
  transfers between devices with their start and end apart: 2 -> 3, of which waited for: 2 -> 3; matrix products, arithmetic and copies ran while one was open for 1% -> 4% of each run, Pallas kernels for 0% -> 0%
where the time goes in v1:
time: 103 us; the launch traced here: 101 us
  Pallas kernels  39.8 us (39%)
  waiting for transfers between devices  31.4 us (30%)
  starting transfers between devices  14.7 us (14%)
  local copies, waits for them, and re-layouts  11.1 us (11%)
  matrix products  2.94 us (3%)
  other arithmetic  1.28 us (1%)
    all_to_all x1, waiting for transfers between devices, per_device(): pay = lax.all_to_all(pay, 'col', 0, 0, tiled=True)  19.7 us
    pallas_call x1, Pallas kernels, scan_calls(): pl.pallas_call(functools.partial(cells_kernel, plan, col_axis), grid=(til...  17.6 us
    pallas_call x1, Pallas kernels, scan_calls(): pl.pallas_call(functools.partial(edges_kernel, plan, col_axis), grid=(til...  13.3 us
    all_to_all x1, waiting for transfers between devices, per_device(): y = lax.all_to_all(y, 'col', 0, 0, tiled=True)  10.1 us
    all_to_all x1, starting transfers between devices, per_device(): pay = lax.all_to_all(pay, 'col', 0, 0, tiled=True)  8.33 us
    all_to_all x1, starting transfers between devices, per_device(): y = lax.all_to_all(y, 'col', 0, 0, tiled=True)  5.08 us
    pallas_call x1, Pallas kernels, project(): pl.pallas_call(functools.partial(project_kernel, plan, tile), grid=(plan....  4.86 us
    pallas_call x1, Pallas kernels, finish(): pl.pallas_call(functools.partial(finish_kernel, plan), in_specs=[full(a.s...  4.01 us
  transfers between devices with their start and end apart: 3, of which 3 were waited for; matrix products, arithmetic and copies ran while one was open for 4% of the time, Pallas kernels for 0%

profile of v1, /device:TPU:0, one launch (start us, length us, event | category | flops | bytes accessed | tf_op | source)
XLA Modules:
  0.0 101.3 jit_solution(3147837783618165917)
XLA Ops:
  0.0 1.9 %reshape.15.x_ref = bf16[196,1024]{1,0:T(8,128)(2,1)} reshape(bf16[28,7,1024]{2,1,0:T(8,128)(2,1)} %param.23) | data formatting | bytes 802816 | tf_op jit(solution)/shard_map/reshape | solution.py:343
  1.9 1.1 %copy.26 = bf16[1024,48]{1,0:T(8,128)(2,1)S(1)} copy(bf16[1024,48]{0,1:T(8,128)(2,1)} %param.26) | data formatting | bytes 196608 | tf_op args[3]
  3.0 0.7 convert_element_type.10
  3.7 0.1 copy.27
  3.8 0.7 reshape.20.mask_ref
  4.5 1.3 %pad_bitcast_fusion.bias_ref = f32[1,128]{1,0:T(1,128)} fusion(f32[16]{0:T(128)} %param.27), kind=kLoop, calls=%fused_computation.4 | loop fusion | bytes 576 | tf_op jit(solution)/shard_map/reshape | solution.py:122
  5.8 0.8 pad.8.wt_ref
  6.7 0.0 copy-start.5
  6.7 0.0 copy-start.6
  6.7 4.9 %project.1 = (bf16[196,1024]{1,0:T(8,128)(2,1)}, bf16[16,200,128]{2,1,0:T(8,128)(2,1)}) custom-call(bf16[196,1024]{1,0:T(8,128)(2,1)} %reshape.15.x_ref, bf16[1024,2048]{1,0:T(8,128)(2,1)} %w_ref.2, bf16[1024,128]{1,0:T(8,128)(2,1)} %pad.8.wt_ref, f32[196,1]{1,0:T(8,128)} %reshape.20.mask_ref, f32[1,128]{1,0:T(1,128)} %pad_bitcast_fusion.bias_ref), custom_call_target="tpu_custom_call" | custom-call | tf_op jit(solution)/shard_map/project/pallas_call | solution.py:124
  11.5 8.3 %all-to-all-start = ((bf16[16,200,128]{2,1,0:T(8,128)(2,1)}), bf16[16,200,128]{2,1,0:T(8,128)(2,1)S(1)}, u32[]{:S(2)}, u32[]{:S(2)}) async-start(bf16[16,200,128]{2,1,0:T(8,128)(2,1)} %get-tuple-element.9), calls=%async_computation | async-start | bytes 1638400 | tf_op jit(solution)/shard_map/all_to_all | solution.py:345
  19.9 0.0 copy-done.5
  19.9 0.0 copy-done.6
  19.9 0.6 pad_maximum_fusion.rates
  20.5 19.7 %all-to-all-done.pay_ref = bf16[16,200,128]{2,1,0:T(8,128)(2,1)S(1)} async-done(((bf16[16,200,128]{2,1,0:T(8,128)(2,1)}), bf16[16,200,128]{2,1,0:T(8,128)(2,1)S(1)}, u32[]{:S(2)}, u32[]{:S(2)}) %all-to-all-start) | async-done | bytes 819232 | tf_op jit(solution)/shard_map/all_to_all | solution.py:345
  40.1 0.0 copy-start
  40.1 0.9 copy-done
  41.0 13.3 %edges.1 = (bf16[16,512,64]{2,1,0:T(8,128)(2,1)}, bf16[16,128,64]{2,1,0:T(8,128)(2,1)}) custom-call(f32[2,16]{1,0:T(2,128)} %pad_maximum_fusion.rates, bf16[16,200,128]{2,1,0:T(8,128)(2,1)} %copy-done, bf16[8,200]{1,0:T(8,128)(2,1)} %constant.50.a1_ref.mask_ref, bf16[8,200]{1,0:T(8,128)(2,1)} %constant.51.a2_ref, bf16[200,200]{1,0:T(8,128)(2,1)} %constant.33.clone.b1_ref, ...), custom_call_target="tpu_custom_call" | custom-call | tf_op jit(solution)/shard_map/edges/pallas_call | solution.py:257
  54.4 1.3 %collective-permute-start = (bf16[16,128,64]{2,1,0:T(8,128)(2,1)}, bf16[16,128,64]{2,1,0:T(8,128)(2,1)S(1)}, u32[]{:S(2)}, u32[]{:S(2)}) collective-permute-start(bf16[16,128,64]{2,1,0:T(8,128)(2,1)} %get-tuple-element.11), channel_id=1, source_target_pairs={{0,16},{1,17},{2,18},{3,19},{4,20},{5,21},{6,22},{7,23},{8,24},{9,... | collective-permute-start | bytes 786440 | tf_op jit(solution)/shard_map/ppermute | solution.py:272
  55.7 1.7 %collective-permute-done.top_ref = bf16[16,128,64]{2,1,0:T(8,128)(2,1)S(1)} collective-permute-done((bf16[16,128,64]{2,1,0:T(8,128)(2,1)}, bf16[16,128,64]{2,1,0:T(8,128)(2,1)S(1)}, u32[]{:S(2)}, u32[]{:S(2)}) %collective-permute-start) | collective-permute-done | bytes 262176 | tf_op jit(solution)/shard_map/ppermute | solution.py:272
  57.4 0.0 copy-start.3
  57.4 0.8 copy-done.3
  58.2 0.0 copy-start.4
  58.2 0.0 copy-start.2
  58.2 17.6 %cells.1 = bf16[16,104,128]{2,1,0:T(8,128)(2,1)} custom-call(f32[2,16]{1,0:T(2,128)} %pad_maximum_fusion.rates, bf16[16,200,128]{2,1,0:T(8,128)(2,1)} %copy-done, bf16[16,512,64]{2,1,0:T(8,128)(2,1)} %get-tuple-element.10.edge_ref, bf16[16,128,64]{2,1,0:T(8,128)(2,1)} %copy-done.3, bf16[200,200]{1,0:T(8,128)(2,1)} %constant.54.a1_ref, ...), custom_call_target="tpu_custom_call" | custom-call | tf_op jit(solution)/shard_map/cells/pallas_call | solution.py:288
  75.8 5.1 %all-to-all-start.1 = ((bf16[16,104,128]{2,1,0:T(8,128)(2,1)}), bf16[16,104,128]{2,1,0:T(8,128)(2,1)S(1)}, u32[]{:S(2)}, u32[]{:S(2)}) async-start(bf16[16,104,128]{2,1,0:T(8,128)(2,1)} %cells.1), calls=%async_computation.1 | async-start | bytes 851968 | tf_op jit(solution)/shard_map/all_to_all | solution.py:349
  80.9 0.0 copy-done.4
  80.9 0.1 broadcast_in_dim.3
  80.9 0.7 reshape_reshape.3.skip_ref
  81.6 0.0 copy-done.2
  81.6 2.9 %fusion.2.z_ref = bf16[196,1024]{1,0:T(8,128)(2,1)} fusion(bf16[196,1024]{1,0:T(8,128)(2,1)S(1)} %copy-done.2, bf16[1024,2048]{1,0:T(8,128)(2,1)} %w_ref.2), kind=kOutput, calls=%fused_computation.2 | convolution fusion | flops 411242496 | bytes 2899968 | tf_op jit(solution)/shard_map/dot_general | solution.py:346
  84.6 10.1 %all-to-all-done.1.y_ref = bf16[16,104,128]{2,1,0:T(8,128)(2,1)S(1)} async-done(((bf16[16,104,128]{2,1,0:T(8,128)(2,1)}), bf16[16,104,128]{2,1,0:T(8,128)(2,1)S(1)}, u32[]{:S(2)}, u32[]{:S(2)}) %all-to-all-start.1) | async-done | bytes 426016 | tf_op jit(solution)/shard_map/all_to_all | solution.py:349
  94.6 0.0 copy-start.1
  94.6 0.8 copy-done.1
  95.4 4.0 %finish.1 = bf16[196,1024]{1,0:T(8,128)(2,1)} custom-call(bf16[16,104,128]{2,1,0:T(8,128)(2,1)} %copy-done.1, bf16[196,1024]{1,0:T(8,128)(2,1)} %get-tuple-element.12.v_ref, bf16[196,1024]{1,0:T(8,128)(2,1)} %fusion.2.z_ref, f32[1,1024]{1,0:T(1,128)} %reshape_reshape.3.skip_ref, f32[1,1024]{1,0:T(1,128)} %bitcast.6, f32[196,1]{1,0:T(8,128)} %reshape.20.mask_ref, ...), custom_call_target="tpu_custom_call" | custom-call | tf_op jit(solution)/shard_map/finish/pallas_call | solution.py:325
  99.4 1.9 %reshape.19 = bf16[28,7,1024]{2,1,0:T(8,128)(2,1)} reshape(bf16[196,1024]{1,0:T(8,128)(2,1)} %finish.1) | data formatting | bytes 802816 | tf_op jit(solution)/shard_map/reshape | solution.py:352
Async XLA Ops:
  6.7 13.2 %copy-start.5 = (f32[16]{0:T(128)S(1)}, f32[16]{0:T(128)}, u32[]{:S(2)}) copy-start(f32[16]{0:T(128)} %param.29) | copy-start | bytes 196
  6.7 13.2 %copy-start.6 = (f32[16]{0:T(128)S(1)}, f32[16]{0:T(128)}, u32[]{:S(2)}) copy-start(f32[16]{0:T(128)} %param.28) | copy-start | bytes 196
  11.5 28.6 %all-to-all-start = ((bf16[16,200,128]{2,1,0:T(8,128)(2,1)}), bf16[16,200,128]{2,1,0:T(8,128)(2,1)S(1)}, u32[]{:S(2)}, u32[]{:S(2)}) async-start(bf16[16,200,128]{2,1,0:T(8,128)(2,1)} %get-tuple-element.9), calls=%async_computation | async-start | bytes 1638400 | tf_op jit(solution)/shard_map/all_to_all | solution.py:345
  40.1 0.9 copy-start
  54.4 3.0 %collective-permute-start = (bf16[16,128,64]{2,1,0:T(8,128)(2,1)}, bf16[16,128,64]{2,1,0:T(8,128)(2,1)S(1)}, u32[]{:S(2)}, u32[]{:S(2)}) collective-permute-start(bf16[16,128,64]{2,1,0:T(8,128)(2,1)} %get-tuple-element.11), channel_id=1, source_target_pairs={{0,16},{1,17},{2,18},{3,19},{4,20},{5,21},{6,22},{7,23},{8,24},{9,... | collective-permute-start | bytes 786440 | tf_op jit(solution)/shard_map/ppermute | solution.py:272
  57.4 0.8 copy-start.3
  58.2 22.7 %copy-start.4 = (f32[16]{0:T(128)S(1)}, f32[16]{0:T(128)}, u32[]{:S(2)}) copy-start(f32[16]{0:T(128)} %param.30) | copy-start | bytes 196
  58.2 23.4 %copy-start.2 = (bf16[196,1024]{1,0:T(8,128)(2,1)S(1)}, bf16[196,1024]{1,0:T(8,128)(2,1)}, u32[]{:S(2)}) copy-start(bf16[196,1024]{1,0:T(8,128)(2,1)} %reshape.15.x_ref) | copy-start | bytes 1204228
  75.8 18.9 %all-to-all-start.1 = ((bf16[16,104,128]{2,1,0:T(8,128)(2,1)}), bf16[16,104,128]{2,1,0:T(8,128)(2,1)S(1)}, u32[]{:S(2)}, u32[]{:S(2)}) async-start(bf16[16,104,128]{2,1,0:T(8,128)(2,1)} %cells.1), calls=%async_computation.1 | async-start | bytes 851968 | tf_op jit(solution)/shard_map/all_to_all | solution.py:349
  94.6 0.8 copy-start.1

commit v2 on v0

v2 whole, which is shorter than its diff:
```python
import functools

import jax
import jax.numpy as jnp
import numpy as np
from jax import lax
from jax.experimental import pallas as pl
from jax.experimental.pallas import tpu as pltpu
from jax.sharding import PartitionSpec as P

norm_eps = 1e-05
LANES = 128
HALF = LANES // 2
F32 = jnp.float32
BF16 = jnp.bfloat16


def round_up(value, step):
    return -(-value // step) * step


def mm(a, b):
    return jnp.dot(a, b, preferred_element_type=F32)


def nt_dot(a, b):
    return lax.dot_general(a, b, (((1,), (1,)), ((), ())), preferred_element_type=F32)


def tn_dot(a, b):
    return lax.dot_general(a, b, (((0,), (0,)), ((), ())), preferred_element_type=F32)


class Plan:
    def __init__(self, rows, cols, states, heads, width, devices):
        self.rows, self.cols, self.states, self.heads = rows, cols, states, heads
        self.width, self.devices = width, devices
        self.group = width // devices
        self.head_width = width // heads
        self.col_pad = round_up(cols, 8)
        self.upper = -(-rows // 2)
        self.half = round_up(self.upper * self.col_pad, 8)
        self.cells = rows * self.col_pad
        self.row_pad = 32
        self.edge = states * self.row_pad
        self.top = states * self.col_pad
        self.bc = 2 * states
        self.at_bc = self.half
        self.at_dt = self.at_bc + 2 * self.bc
        self.message = round_up(self.at_dt + 2, 8)
        assert self.head_width % self.group == 0 and self.group <= HALF
        assert LANES % self.head_width == 0 and self.half <= LANES
        assert rows <= self.row_pad and self.cells - self.half <= self.half
        assert states % 16 == 0 and self.edge % LANES == 0 and heads % 8 == 0

    def lanes(self):
        at = np.arange(2 * LANES)
        cell = np.where(at < LANES, at, at - LANES + self.half)
        live = np.where(at < LANES, at < self.half, cell < self.cells)
        i, j = cell // self.col_pad, cell % self.col_pad
        return i, j, live & (j < self.cols)

    def constants(self):
        i, j, real = self.lanes()
        both = real[:, None] & real[None]
        cell = np.arange(self.cells)
        ci, cj = cell // self.col_pad, cell % self.col_pad
        creal = cj < self.cols
        le = np.arange(self.row_pad)
        lj = np.arange(self.col_pad)
        n = np.arange(self.states)
        edge = np.tile(le, LANES // self.row_pad)
        out = {}
        out["to1"] = (j[:, None] <= j[None]) & both
        out["to2"] = (j[:, None] == j[None]) & (i[:, None] <= i[None]) & both
        out["from1"] = (i[:, None] == i[None]) & (j[:, None] > j[None]) & both
        out["from2"] = (i[:, None] > i[None]) & both
        out["side1"] = (i[None] == le[:, None]) & real[None]
        out["side2"] = (i[None] > le[:, None]) & real[None]
        out["sidemask"] = (i[None] >= le[:, None]) & (le < self.rows)[:, None] & real[None]
        out["down1"] = (j[None] <= lj[:, None]) & real[None]
        out["down2"] = (j[None] == lj[:, None]) & real[None]
        out["downmask"] = (j[None] <= lj[:, None]) & (lj < self.cols)[:, None] & real[None]
        out["keep"] = (i[:, None] == edge[None]) & real[:, None]
        out["pick"] = (
            (i == self.rows - 1)[:, None] & real[:, None] & (j[:, None] == np.tile(lj, self.states)[None])
        )
        out["diag"] = np.repeat(n, self.row_pad)[:, None] == np.repeat(n, self.col_pad)[None]
        cboth = creal[:, None] & real[None]
        out["own1"] = (j[None] <= cj[:, None]) & cboth
        out["own2"] = (j[None] == cj[:, None]) & (i[None] <= ci[:, None]) & cboth
        out["ownmask"] = (i[None] <= ci[:, None]) & (j[None] <= cj[:, None]) & cboth
        out["rowj"] = cj[:, None] == np.arange(self.cols)[None]
        out["rowi"] = ci[:, None] == np.arange(self.rows)[None]
        out["lanei"] = (np.arange(self.rows)[:, None] == i[None]) & real[None]
        out["lanej"] = (np.arange(self.cols)[:, None] == j[None]) & real[None]
        return {k: jnp.asarray(x.astype(np.float32), BF16) for k, x in out.items()}


def full(shape):
    return pl.BlockSpec(shape, lambda *_: (0,) * len(shape))


SMEM = pl.BlockSpec(memory_space=pltpu.SMEM)


def cell_mask_of(t_ref, rowj_ref, rowi_ref):
    t = t_ref[...].astype(F32).astype(BF16)
    return jnp.sum(mm(rowj_ref[...], t) * rowi_ref[...].astype(F32), axis=1, keepdims=True)


def project_kernel(
    plan, tile, bias_ref, x_ref, w_ref, wt_ref, t_ref, rowj_ref, rowi_ref, lanei_ref, lanej_ref,
    v_ref, pay_ref, rows_ref, flat_ref, wide, keep,
):
    step = pl.program_id(0)
    group, states, cells, heads = plan.group, plan.states, plan.cells, plan.heads
    half, rest = plan.half, plan.cells - plan.half

    @pl.when(step == 0)
    def _():
        wide[...] = jnp.zeros_like(wide)
        for i in range(plan.rows):
            wide[i * plan.col_pad : i * plan.col_pad + plan.cols, :] = x_ref[i].astype(F32)
        flat_ref[...] = wide[...].astype(BF16)
        keep[...] = jnp.broadcast_to(cell_mask_of(t_ref, rowj_ref, rowi_ref), keep.shape)
        t = t_ref[...].astype(F32).astype(BF16)
        m = jnp.sum(mm(t, lanei_ref[...]) * lanej_ref[...].astype(F32), axis=0, keepdims=True)
        x = flat_ref[...]
        table = nt_dot(wt_ref[...], x)
        ext = jnp.concatenate([table, jnp.zeros((table.shape[0], 2 * LANES - cells), F32)], axis=1)
        lane = lax.broadcasted_iota(jnp.int32, (table.shape[0], LANES), 1)
        lo, hi = ext[:, :LANES], ext[:, LANES:]
        shift = half % LANES
        if shift:
            moved = jnp.where(
                lane < LANES - shift, pltpu.roll(lo, LANES - shift, 1), pltpu.roll(hi, LANES - shift, 1)
            )
        else:
            moved = hi
        table = jnp.concatenate([jnp.where(lane < half, lo, 0.0), jnp.where(lane < rest, moved, 0.0)], axis=1)
        z = table[2 * states :]
        at = lax.broadcasted_iota(jnp.int32, z.shape, 0)
        for h in range(heads):
            z = jnp.where(at == h, z + bias_ref[h], z)
        soft = m * (jnp.maximum(z, 0.0) + jnp.log1p(jnp.exp(-jnp.abs(z))))
        rows_ref[...] = jnp.concatenate([table[: 2 * states], soft], axis=0).astype(BF16).astype(F32)
        v_ref[...] = jnp.zeros_like(v_ref)

    v = mm(flat_ref[...], w_ref[...]).astype(BF16).astype(F32) * keep[:, :1]
    low = v.astype(BF16)
    v_ref[0:half, :] = low[:half]
    v_ref[LANES : LANES + rest, :] = low[half:]
    lane = lax.broadcasted_iota(jnp.int32, (half, LANES), 1)
    for k in range(tile // group):
        base = k * group // LANES * LANES
        at = k * group % LANES
        first = v[:half, base : base + LANES]
        last = v[half:, base : base + LANES]
        if rest < half:
            last = jnp.concatenate([last, jnp.zeros((half - rest, LANES), F32)], axis=0)
        if at:
            first = pltpu.roll(first, LANES - at, 1)
        if at != HALF:
            last = pltpu.roll(last, (HALF - at) % LANES, 1)
        both = jnp.where(lane < HALF, first, last)
        if group < HALF:
            both = jnp.where(lane % HALF < group, both, 0.0)
        pay_ref[k, 0:half, :] = both.astype(BF16)
        bc = rows_ref[0 : 2 * states, :].astype(BF16)
        pay_ref[k, plan.at_bc : plan.at_bc + plan.bc, :] = bc[:, :LANES]
        pay_ref[k, plan.at_bc + plan.bc : plan.at_dt, :] = bc[:, LANES:]
        head = (step * tile + k * group) // plan.head_width
        dt = rows_ref[pl.ds(2 * states + head, 1), :]
        dt = jnp.concatenate(
            [dt[:, :LANES], dt[:, LANES:], jnp.zeros((plan.message - plan.at_dt - 2, LANES), F32)], axis=0
        )
        pay_ref[k, plan.at_dt : plan.message, :] = dt.astype(BF16)


def project(plan, consts, slide, w_in, w_bcd, tissue, dt_bias):
    tile = plan.width // 2
    picks = [consts[k] for k in ("rowj", "rowi", "lanei", "lanej")]
    wt, t = w_bcd.T, tissue.T
    depth = slide.shape[2]
    count = 2 * plan.states + plan.heads
    return pl.pallas_call(
        functools.partial(project_kernel, plan, tile),
        grid=(plan.width // tile,),
        in_specs=[
            SMEM,
            full(slide.shape),
            pl.BlockSpec((depth, tile), lambda s: (0, s)),
            full(wt.shape),
            full(t.shape),
        ]
        + [full(x.shape) for x in picks],
        out_specs=[
            pl.BlockSpec((2 * LANES, tile), lambda s: (0, s)),
            pl.BlockSpec((tile // plan.group, plan.message, LANES), lambda s: (s, 0, 0)),
            full((count, 2 * LANES)),
            full((plan.cells, depth)),
        ],
        out_shape=[
            jax.ShapeDtypeStruct((2 * LANES, plan.width), BF16),
            jax.ShapeDtypeStruct((plan.devices, plan.message, LANES), BF16),
            jax.ShapeDtypeStruct((count, 2 * LANES), F32),
            jax.ShapeDtypeStruct((plan.cells, depth), BF16),
        ],
        scratch_shapes=[pltpu.VMEM((plan.cells, depth), F32), pltpu.VMEM((plan.cells, LANES), F32)],
        name="project",
    )(dt_bias, slide, w_in, wt, t, *picks)


def own_kernel(
    plan, rx_ref, ry_ref, skip_ref, v_ref, rows_ref, own1_ref, own2_ref, from1_ref, from2_ref,
    mask_ref, out_ref, pair,
):
    states, cells, half = plan.states, plan.cells, plan.half
    b = rows_ref[0:states, :].astype(BF16)
    c = rows_ref[states : 2 * states, :].astype(BF16)
    pairs = tn_dot(c, b)
    pairs = jnp.concatenate([pairs[:half], pairs[LANES : LANES + cells - half]], axis=0)
    pair[...] = pairs * mask_ref[...].astype(F32)
    lane = lax.broadcasted_iota(jnp.int32, (cells, LANES), 1)
    per = LANES // plan.head_width
    for block in range(plan.width // LANES):
        v = v_ref[:, block * LANES : (block + 1) * LANES]
        vc = jnp.concatenate([v[:half], v[LANES : LANES + cells - half]], axis=0).astype(F32)
        total = None
        for k in range(per):
            h = block * per + k
            dt = rows_ref[2 * states + h : 2 * states + h + 1, :]
            low = dt.astype(BF16)
            x = mm(own1_ref[...] * low, from1_ref[...])
            y = mm(own2_ref[...] * low, from2_ref[...])
            weight = jnp.exp(-(rx_ref[h] * x + ry_ref[h] * y)) * pair[...] * dt
            part = mm(weight.astype(BF16), v) + skip_ref[h] * vc
            total = part if total is None else jnp.where(lane < k * plan.head_width, total, part)
        out_ref[:, block * LANES : (block + 1) * LANES] = total.astype(BF16)


def own_tile(plan, consts, v, rows, rate_x, rate_y, d_skip):
    maps = [consts[k] for k in ("own1", "own2", "from1", "from2", "ownmask")]
    args = [v, rows] + maps
    return pl.pallas_call(
        functools.partial(own_kernel, plan),
        grid=(1,),
        in_specs=[SMEM, SMEM, SMEM] + [full(x.shape) for x in args],
        out_specs=full((plan.cells, plan.width)),
        out_shape=jax.ShapeDtypeStruct((plan.cells, plan.width), BF16),
        scratch_shapes=[pltpu.VMEM((plan.cells, 2 * LANES), F32)],
        name="own",
    )(rate_x, rate_y, d_skip, *args)


def my_head(plan, axis):
    return lax.axis_index(axis) * plan.group // plan.head_width


def wide_rows(pay_ref, t, at, count, gap):
    return jnp.concatenate([pay_ref[t, at : at + count, :], pay_ref[t, at + gap : at + gap + count, :]], axis=1)


def unroll_of(plan):
    return plan.devices if plan.devices <= 16 else 1


def edges_kernel(
    plan, axis, rx_ref, ry_ref, pay_ref, to1_ref, to2_ref, from1_ref, from2_ref, side1_ref, side2_ref,
    sidemask_ref, down1_ref, down2_ref, downmask_ref, keep_ref, pick_ref, diag_ref,
    edge_ref, top_ref, side_ref, above_ref, dts, inner, kept, s1, s2, d1, d2, down, bottom, carry,
):
    states, tiles, rp, cp = plan.states, plan.devices, plan.row_pad, plan.col_pad
    head = my_head(plan, axis)
    rate_x, rate_y = rx_ref[head], ry_ref[head]
    for t in range(tiles):
        both = pay_ref[t, plan.at_dt : plan.message, :].astype(F32)
        dts[t : t + 1, :LANES] = both[0:1]
        dts[t : t + 1, LANES:] = both[1:2]
    dt = dts[...]
    low = dt.astype(BF16)
    inner[...] = jnp.exp(-rate_x * mm(low, from1_ref[...])) * dt
    kept[...] = jnp.exp(-rate_x * mm(low, keep_ref[...]))
    above_ref[...] = jnp.exp(-rate_y * mm(low, to2_ref[...]))
    for t in range(tiles):
        row = low[t : t + 1]
        s1[t * rp : (t + 1) * rp, :] = side1_ref[...] * row
        s2[t * rp : (t + 1) * rp, :] = side2_ref[...] * row
        rf = dts[t : t + 1, :]
        d1[t * cp : (t + 1) * cp, :] = down1_ref[...].astype(F32) * rf
        d2[t * cp : (t + 1) * cp, :] = down2_ref[...].astype(F32) * rf
    sides = jnp.exp(-(rate_x * mm(s1[...], to1_ref[...]) + rate_y * mm(s2[...], to2_ref[...])))
    mask = sidemask_ref[...].astype(F32)
    for t in range(tiles):
        side_ref[t] = (sides[t * rp : (t + 1) * rp] * mask).astype(BF16)
    falls = jnp.exp(
        -(rate_x * mm(d1[...].astype(BF16), from1_ref[...]) + rate_y * mm(d2[...].astype(BF16), from2_ref[...]))
    )
    mask = downmask_ref[...].astype(F32)
    for t in range(tiles):
        down[t * cp : (t + 1) * cp, :] = falls[t * cp : (t + 1) * cp] * mask
        bottom[t] = mm(side_ref[t], pick_ref[...]).astype(BF16)
    carry[...] = jnp.zeros_like(carry)

    def tile(t, _):
        rowsel = side1_ref[...]
        b = wide_rows(pay_ref, t, plan.at_bc, states, plan.bc).astype(F32)
        bd = (b * inner[pl.ds(t, 1), :]).astype(BF16)
        bdt = b * dts[pl.ds(t, 1), :]
        left = jnp.concatenate([rowsel * bd[n : n + 1] for n in range(states)], axis=0)
        v = pay_ref[t, 0 : plan.half, :].astype(F32)
        if plan.half < LANES:
            v = jnp.concatenate([v, jnp.zeros((LANES - plan.half, LANES), F32)], axis=0)
        v = v.T
        v = jnp.concatenate([v[:HALF], v[HALF:]], axis=1).astype(BF16)
        fall = down[pl.ds(t * cp, cp), :]
        falls = jnp.concatenate([fall * bdt[n : n + 1] for n in range(states)], axis=0).astype(BF16)
        before = carry[...]
        before_low = before.astype(BF16)
        edge_ref[t] = before_low
        passed = jnp.concatenate([bottom[t]] * states, axis=0) * diag_ref[...]
        top_ref[t] = (nt_dot(v, falls) + mm(before_low, passed)).astype(BF16)
        kept_row = kept[pl.ds(t, 1), :]
        kept_row = jnp.concatenate([kept_row] * (plan.edge // LANES), axis=1)
        carry[...] = before * kept_row + nt_dot(v, left)
        return 0

    lax.fori_loop(0, tiles, tile, 0, unroll=unroll_of(plan))


def cells_kernel(plan, pay_ref, edge_ref, top_ref, side_ref, above_ref, colsel_ref, out_ref):
    states = plan.states

    def tile(t, _):
        c = wide_rows(pay_ref, t, plan.at_bc + states, states, plan.bc)
        side = side_ref[t]
        left = jnp.concatenate([side * c[n : n + 1] for n in range(states)], axis=0)
        ca = c.astype(F32) * above_ref[pl.ds(t, 1), :]
        colsel = colsel_ref[...].astype(F32)
        down = jnp.concatenate([colsel * ca[n : n + 1] for n in range(states)], axis=0).astype(BF16)
        y = mm(edge_ref[t], left) + mm(top_ref[t], down)
        y = jnp.concatenate([y[:, :LANES], y[:, LANES:]], axis=0).T
        out_ref[t] = y[: plan.half].astype(BF16)
        return 0

    lax.fori_loop(0, plan.devices, tile, 0, unroll=unroll_of(plan))


def scan_calls(plan, consts, row_axis, col_axis, pay, rate_x, rate_y):
    tiles, rp, cp = plan.devices, plan.row_pad, plan.col_pad
    names = ("to1", "to2", "from1", "from2", "side1", "side2", "sidemask", "down1", "down2")
    maps = [consts[k] for k in names + ("downmask", "keep", "pick", "diag")]
    shapes = [
        ((tiles, HALF, plan.edge), BF16),
        ((tiles, HALF, plan.top), BF16),
        ((tiles, rp, 2 * LANES), BF16),
        ((tiles, 2 * LANES), F32),
    ]
    edges, tops, side, above = pl.pallas_call(
        functools.partial(edges_kernel, plan, col_axis),
        grid=(1,),
        in_specs=[SMEM, SMEM, full(pay.shape)] + [full(x.shape) for x in maps],
        out_specs=[full(s) for s, _ in shapes],
        out_shape=[jax.ShapeDtypeStruct(s, d) for s, d in shapes],
        scratch_shapes=[
            pltpu.VMEM((tiles, 2 * LANES), F32),
            pltpu.VMEM((tiles, 2 * LANES), F32),
            pltpu.VMEM((tiles, LANES), F32),
            pltpu.VMEM((tiles * rp, 2 * LANES), BF16),
            pltpu.VMEM((tiles * rp, 2 * LANES), BF16),
            pltpu.VMEM((tiles * cp, 2 * LANES), F32),
            pltpu.VMEM((tiles * cp, 2 * LANES), F32),
            pltpu.VMEM((tiles * cp, 2 * LANES), F32),
            pltpu.VMEM((tiles, rp, LANES), BF16),
            pltpu.VMEM((HALF, plan.edge), F32),
        ],
        name="edges",
    )(rate_x, rate_y, pay, *maps)

    count = lax.axis_size(row_axis)
    chain = [(r, r + 1) for r in range(count - 1)]
    entry = lax.ppermute(tops, row_axis, chain)
    if count > 2:
        keep = jnp.dot(above.astype(BF16), consts["pick"], preferred_element_type=F32)[:, None, :]
        for _ in range(count - 2):
            entry = lax.ppermute(
                (tops.astype(F32) + keep * entry.astype(F32)).astype(BF16), row_axis, chain
            )

    args = (pay, edges, entry, side, above, consts["down2"])
    shape = (tiles, plan.half, LANES)
    return pl.pallas_call(
        functools.partial(cells_kernel, plan),
        grid=(1,),
        in_specs=[full(x.shape) for x in args],
        out_specs=full(shape),
        out_shape=jax.ShapeDtypeStruct(shape, BF16),
        name="cells",
    )(*args)


def finish_kernel(plan, y_ref, own_ref, z_ref, gain_ref, t_ref, rowj_ref, rowi_ref, w_ref, out_ref, full_ref):
    group, half, cells = plan.group, plan.half, plan.cells
    per = LANES // group
    lane = lax.broadcasted_iota(jnp.int32, (half, LANES), 1)
    for block in range(plan.width // LANES):
        for k, (lo, hi) in enumerate(((0, half), (half, cells))):
            joined = None
            for d in range(per):
                part = y_ref[block * per + d].astype(F32)
                shift = (d * group - k * HALF) % LANES
                if shift:
                    part = pltpu.roll(part, shift, 1)
                joined = part if joined is None else jnp.where(lane < d * group, joined, part)
            full_ref[lo:hi, block * LANES : (block + 1) * LANES] = joined[: hi - lo]
    y = full_ref[...] + own_ref[...].astype(F32)
    y = y.astype(BF16).astype(F32)
    z = z_ref[...].astype(F32)
    gated = y * (z * (1.0 / (1.0 + jnp.exp(-z))))
    scale = lax.rsqrt(jnp.mean(gated * gated, axis=-1, keepdims=True) + norm_eps)
    normed = (gated * scale * gain_ref[...]).astype(BF16)
    full_ref[...] = mm(normed, w_ref[...]) * cell_mask_of(t_ref, rowj_ref, rowi_ref)
    for i in range(plan.rows):
        out_ref[i] = full_ref[i * plan.col_pad : i * plan.col_pad + plan.cols, :].astype(BF16)


def finish(plan, consts, y, own, z, gain, tissue, w_out):
    args = (y, own, z, gain, tissue.T, consts["rowj"], consts["rowi"], w_out)
    shape = (plan.rows, plan.cols, w_out.shape[1])
    assert w_out.shape[1] == plan.width
    return pl.pallas_call(
        functools.partial(finish_kernel, plan),
        grid=(1,),
        in_specs=[full(a.shape) for a in args],
        out_specs=full(shape),
        out_shape=jax.ShapeDtypeStruct(shape, BF16),
        scratch_shapes=[pltpu.VMEM((plan.cells, plan.width), F32)],
        name="finish",
    )(*args)


def per_device(slide, tissue, w_in, w_bcd, dt_bias, rate_x, rate_y, d_skip, norm_gain, w_out):
    rows, cols, model_width = slide.shape
    width = w_out.shape[0]
    heads = dt_bias.shape[0]
    states = (w_bcd.shape[1] - heads) // 2
    plan = Plan(rows, cols, states, heads, width, lax.axis_size("col"))
    consts = plan.constants()
    v, pay, table, x = project(plan, consts, slide, w_in, w_bcd, tissue, dt_bias)
    pay = lax.all_to_all(pay, "col", 0, 0, tiled=True)
    own = own_tile(plan, consts, v, table, rate_x, rate_y, d_skip)
    z = jnp.dot(x, w_in[:, width:], preferred_element_type=F32).astype(BF16)
    y = scan_calls(plan, consts, "row", "col", pay, rate_x, rate_y)
    y = lax.all_to_all(y, "col", 0, 0, tiled=True)
    return finish(plan, consts, y, own, z, norm_gain.reshape(1, width), tissue, w_out)


def solution(mesh):
    placed = (
        P(("slides", "row"), "col", None),
        P(("slides", "row"), "col"),
        P(),
        P(),
        P(),
        P(),
        P(),
        P(),
        P(),
        P(),
    )
    return jax.shard_map(
        per_device,
        mesh=mesh,
        in_specs=placed,
        out_specs=P(("slides", "row"), "col", None),
        check_vma=False,
    )
```

time: 696 us -> 69.8 us (0.10); the launches traced: 686 us -> 69.3 us
  waiting for transfers between devices: 370 us -> 7.11 us
  local copies, waits for them, and re-layouts: 174 us -> 1.48 us
  other arithmetic: 108 us -> 0 us
  blocking collectives: 4.42 us -> 29.3 us
  Pallas kernels: 0 us -> 23.6 us
  between operations: 14.4 us -> 0.03 us
  matrix products: 11.9 us -> 3.01 us
    all_gather x2 -> x0, waiting for transfers between devices: 370 us -> none  [carried_in_2(): pieces = jax.tree.map(lambda part: lax.all_gather(part, axis), value)]
    dynamic_update_slice x84 -> x0, local copies, waits for them, and re-layouts: 98.8 us -> none  [per_device(): lax.scan(cell_row, start, (decay_x, decay_y, log_y, source_cells, b_cells...]
    select_n x15 -> x0, other arithmetic: 45.6 us -> none  [hop(): jnp.where(position < mine, new, old)]
    dynamic_slice x99 -> x0, local copies, waits for them, and re-layouts: 41.3 us -> none  [the longest x84 27.7 us: per_device(): lax.scan(cell_row, start, (decay_x, decay_y, log_y, source_cells, b_cells...]
    add x57 -> x0, other arithmetic: 36.6 us -> none  [the longest x28 27.5 us: cell_row(): cum = cum + ly_row[:, None, :]]
    all_to_all x0 -> x1, blocking collectives: none -> 29.3 us  [per_device(): pay = lax.all_to_all(pay, 'col', 0, 0, tiled=True)]
    slice x30 -> x0, local copies, waits for them, and re-layouts: 28.5 us -> none  [the longest x28 28.3 us: cell_row(): u_row[column][None, :]]
    pallas_call x0 -> x5, Pallas kernels: none -> 23.6 us  [the longest x1 6.28 us: scan_calls(): pl.pallas_call(functools.partial(edges_kernel, plan, col_axis), grid=(1,)...]
  transfers between devices with their start and end apart: 2 -> 2, of which waited for: 2 -> 2; matrix products, arithmetic and copies ran while one was open for 1% -> 4% of each run, Pallas kernels for 0% -> 8%
where the time goes in v2:
time: 69.8 us; the launch traced here: 69.3 us
  blocking collectives  29.3 us (42%)
  Pallas kernels  23.6 us (34%)
  waiting for transfers between devices  7.11 us (10%)
  starting transfers between devices  4.86 us (7%)
  matrix products  3.01 us (4%)
  local copies, waits for them, and re-layouts  1.48 us (2%)
    all_to_all x1, blocking collectives, per_device(): pay = lax.all_to_all(pay, 'col', 0, 0, tiled=True)  29.3 us
    pallas_call x1, Pallas kernels, scan_calls(): pl.pallas_call(functools.partial(edges_kernel, plan, col_axis), grid=(1,)...  6.28 us
    all_to_all x1, waiting for transfers between devices, per_device(): y = lax.all_to_all(y, 'col', 0, 0, tiled=True)  5.77 us
    pallas_call x1, Pallas kernels, own_tile(): pl.pallas_call(functools.partial(own_kernel, plan), grid=(1,), in_specs=[...  5.52 us
    pallas_call x1, Pallas kernels, finish(): pl.pallas_call(functools.partial(finish_kernel, plan), grid=(1,), in_spec...  4.38 us
    pallas_call x1, Pallas kernels, project(): pl.pallas_call(functools.partial(project_kernel, plan, tile), grid=(plan....  3.91 us
    all_to_all x1, starting transfers between devices, per_device(): y = lax.all_to_all(y, 'col', 0, 0, tiled=True)  3.56 us
    pallas_call x1, Pallas kernels, scan_calls(): pl.pallas_call(functools.partial(cells_kernel, plan), grid=(1,), in_specs...  3.49 us
  transfers between devices with their start and end apart: 2, of which 2 were waited for; matrix products, arithmetic and copies ran while one was open for 4% of the time, Pallas kernels for 8%

profile of v2, /device:TPU:0, one launch (start us, length us, event | category | flops | bytes accessed | tf_op | source)
XLA Modules:
  0.0 69.3 jit_solution(12910712122842420925)
XLA Ops:
  0.0 3.9 %project.1 = (bf16[256,1024]{1,0:T(8,128)(2,1)}, bf16[16,184,128]{2,1,0:T(8,128)(2,1)}, f32[48,256]{1,0:T(8,128)}, bf16[224,1024]{1,0:T(8,128)(2,1)}) custom-call(f32[16]{0:T(128)} %bias_ref.1, bf16[28,7,1024]{2,1,0:T(8,128)(2,1)} %x_ref.1, bf16[1024,2048]{1,0:T(8,128)(2,1)} %w_ref.2, bf16[48,1024]{1,0:T(8,128)(2,1)} %bitcast.4, s32[7,28]{1,0:T(8,128)} %bitcast.5, ...), custom_call_target="tpu_custom_call" | custom-call | tf_op jit(solution)/shard_map/project/pallas_call | solution.py:187
  3.9 0.0 copy-start.2
  3.9 29.3 %all_to_all.10.pay_ref = bf16[16,184,128]{2,1,0:T(8,128)(2,1)} all-to-all(bf16[16,184,128]{2,1,0:T(8,128)(2,1)} %get-tuple-element.13), channel_id=1, replica_groups=mesh['slides'=1,'row'=2,'col'=16] {'col'}, dimensions={0} | all-to-all | bytes 1507328 | tf_op jit(solution)/shard_map/all_to_all | solution.py:451
  33.2 6.3 %edges.1 = (bf16[16,64,512]{2,1,0:T(8,128)(2,1)}, bf16[16,64,128]{2,1,0:T(8,128)(2,1)}, bf16[16,32,256]{2,1,0:T(8,128)(2,1)}, f32[16,256]{1,0:T(8,128)}) custom-call(f32[16]{0:T(128)} %rx_ref.3, f32[16]{0:T(128)} %ry_ref.3, bf16[16,184,128]{2,1,0:T(8,128)(2,1)} %all_to_all.10.pay_ref, bf16[256,256]{1,0:T(8,128)(2,1)} %constant.40.clone.to1_ref, ...), custom_call_target="tpu_custom_call" | custom-call | tf_op jit(solution)/shard_map/edges/pallas_call | solution.py:360
  39.5 1.3 %collective-permute-start = (bf16[16,64,128]{2,1,0:T(8,128)(2,1)}, bf16[16,64,128]{2,1,0:T(8,128)(2,1)S(1)}, u32[]{:S(2)}, u32[]{:S(2)}) collective-permute-start(bf16[16,64,128]{2,1,0:T(8,128)(2,1)} %get-tuple-element.15), channel_id=1, source_target_pairs={{0,16},{1,17},{2,18},{3,19},{4,20},{5,21},{6,22},{7,23},{8,24},{9,... | collective-permute-start | bytes 786440 | tf_op jit(solution)/shard_map/ppermute | solution.py:383
  40.8 1.3 %collective-permute-done.top_ref = bf16[16,64,128]{2,1,0:T(8,128)(2,1)S(1)} collective-permute-done((bf16[16,64,128]{2,1,0:T(8,128)(2,1)}, bf16[16,64,128]{2,1,0:T(8,128)(2,1)S(1)}, u32[]{:S(2)}, u32[]{:S(2)}) %collective-permute-start) | collective-permute-done | bytes 262176 | tf_op jit(solution)/shard_map/ppermute | solution.py:383
  42.1 0.0 copy-start.1
  42.1 0.7 %copy-done.1 = bf16[16,64,128]{2,1,0:T(8,128)(2,1)} copy-done((bf16[16,64,128]{2,1,0:T(8,128)(2,1)}, bf16[16,64,128]{2,1,0:T(8,128)(2,1)S(1)}, u32[]{:S(2)}) %copy-start.1) | copy-done | bytes 262168
  42.8 3.5 %cells.1 = bf16[16,112,128]{2,1,0:T(8,128)(2,1)} custom-call(bf16[16,184,128]{2,1,0:T(8,128)(2,1)} %all_to_all.10.pay_ref, bf16[16,64,512]{2,1,0:T(8,128)(2,1)} %get-tuple-element.14.edge_ref, bf16[16,64,128]{2,1,0:T(8,128)(2,1)} %copy-done.1, bf16[16,32,256]{2,1,0:T(8,128)(2,1)} %get-tuple-element.16.side_ref, f32[16,256]{1,0:T(8,128)} %get-tuple-element.17.above_ref, ...), custom_call_target="tpu_custom_call" | custom-call | tf_op jit(solution)/shard_map/cells/pallas_call | solution.py:393
  46.3 3.6 %all-to-all-start.1 = ((bf16[16,112,128]{2,1,0:T(8,128)(2,1)}), bf16[16,112,128]{2,1,0:T(8,128)(2,1)S(1)}, u32[]{:S(2)}, u32[]{:S(2)}) async-start(bf16[16,112,128]{2,1,0:T(8,128)(2,1)} %cells.1), calls=%async_computation.1 | async-start | bytes 917504 | tf_op jit(solution)/shard_map/all_to_all | solution.py:455
  49.9 5.5 %own.1.own_ref = bf16[224,1024]{1,0:T(8,128)(2,1)} custom-call(f32[16]{0:T(128)} %rx_ref.3, f32[16]{0:T(128)} %ry_ref.3, f32[16]{0:T(128)} %skip_ref.1, bf16[256,1024]{1,0:T(8,128)(2,1)} %get-tuple-element.18.v_ref, f32[48,256]{1,0:T(8,128)} %get-tuple-element.19.rows_ref, bf16[224,256]{1,0:T(8,128)(2,1)} %constant.53.clone.own1_ref, ...), custom_call_target="tpu_custom_call" | custom-call | tf_op jit(solution)/shard_map/own/pallas_call | solution.py:246
  55.4 0.0 copy-done.2
  55.4 3.0 %fusion.2.z_ref = bf16[224,1024]{1,0:T(8,128)(2,1)} fusion(bf16[224,1024]{1,0:T(8,128)(2,1)S(1)} %copy-done.2, bf16[1024,2048]{1,0:T(8,128)(2,1)} %w_ref.2), kind=kOutput, calls=%fused_computation.2 | convolution fusion | flops 469991424 | bytes 3014656 | tf_op jit(solution)/shard_map/dot_general | solution.py:453
  58.4 5.8 %all-to-all-done.1.y_ref = bf16[16,112,128]{2,1,0:T(8,128)(2,1)S(1)} async-done(((bf16[16,112,128]{2,1,0:T(8,128)(2,1)}), bf16[16,112,128]{2,1,0:T(8,128)(2,1)S(1)}, u32[]{:S(2)}, u32[]{:S(2)}) %all-to-all-start.1) | async-done | bytes 458784 | tf_op jit(solution)/shard_map/all_to_all | solution.py:455
  64.2 0.0 copy-start
  64.2 0.8 %copy-done = bf16[16,112,128]{2,1,0:T(8,128)(2,1)} copy-done((bf16[16,112,128]{2,1,0:T(8,128)(2,1)}, bf16[16,112,128]{2,1,0:T(8,128)(2,1)S(1)}, u32[]{:S(2)}) %copy-start) | copy-done | bytes 458776
  64.9 4.4 %finish.1 = bf16[28,7,1024]{2,1,0:T(8,128)(2,1)} custom-call(bf16[16,112,128]{2,1,0:T(8,128)(2,1)} %copy-done, bf16[224,1024]{1,0:T(8,128)(2,1)} %own.1.own_ref, bf16[224,1024]{1,0:T(8,128)(2,1)} %fusion.2.z_ref, f32[1,1024]{1,0:T(1,128)} %bitcast.7, s32[7,28]{1,0:T(8,128)} %bitcast.6, bf16[224,7]{1,0:T(8,128)(2,1)} %constant.56.clone.rowj_ref, ...), custom_call_target="tpu_custom_call" | custom-call | tf_op jit(solution)/shard_map/finish/pallas_call | solution.py:432
Async XLA Ops:
  3.9 51.5 %copy-start.2 = (bf16[224,1024]{1,0:T(8,128)(2,1)S(1)}, bf16[224,1024]{1,0:T(8,128)(2,1)}, u32[]{:S(2)}) copy-start(bf16[224,1024]{1,0:T(8,128)(2,1)} %get-tuple-element.20) | copy-start | bytes 1376260
  39.5 2.6 %collective-permute-start = (bf16[16,64,128]{2,1,0:T(8,128)(2,1)}, bf16[16,64,128]{2,1,0:T(8,128)(2,1)S(1)}, u32[]{:S(2)}, u32[]{:S(2)}) collective-permute-start(bf16[16,64,128]{2,1,0:T(8,128)(2,1)} %get-tuple-element.15), channel_id=1, source_target_pairs={{0,16},{1,17},{2,18},{3,19},{4,20},{5,21},{6,22},{7,23},{8,24},{9,... | collective-permute-start | bytes 786440 | tf_op jit(solution)/shard_map/ppermute | solution.py:383
  42.1 0.7 %copy-start.1 = (bf16[16,64,128]{2,1,0:T(8,128)(2,1)}, bf16[16,64,128]{2,1,0:T(8,128)(2,1)S(1)}, u32[]{:S(2)}) copy-start(bf16[16,64,128]{2,1,0:T(8,128)(2,1)S(1)} %collective-permute-done.top_ref) | copy-start | bytes 786436
  46.3 17.9 %all-to-all-start.1 = ((bf16[16,112,128]{2,1,0:T(8,128)(2,1)}), bf16[16,112,128]{2,1,0:T(8,128)(2,1)S(1)}, u32[]{:S(2)}, u32[]{:S(2)}) async-start(bf16[16,112,128]{2,1,0:T(8,128)(2,1)} %cells.1), calls=%async_computation.1 | async-start | bytes 917504 | tf_op jit(solution)/shard_map/all_to_all | solution.py:455
  64.2 0.8 %copy-start = (bf16[16,112,128]{2,1,0:T(8,128)(2,1)}, bf16[16,112,128]{2,1,0:T(8,128)(2,1)S(1)}, u32[]{:S(2)}) copy-start(bf16[16,112,128]{2,1,0:T(8,128)(2,1)S(1)} %all-to-all-done.1.y_ref) | copy-start | bytes 1376260

commit v3 on v2

v3 whole, which is shorter than its diff:
```python
import functools

import jax
import jax.numpy as jnp
import numpy as np
from jax import lax
from jax.experimental import pallas as pl
from jax.experimental.pallas import tpu as pltpu
from jax.sharding import PartitionSpec as P

norm_eps = 1e-05
LANES = 128
HALF = LANES // 2
F32 = jnp.float32
BF16 = jnp.bfloat16


def round_up(value, step):
    return -(-value // step) * step


def mm(a, b):
    return jnp.dot(a, b, preferred_element_type=F32)


def nt_dot(a, b):
    return lax.dot_general(a, b, (((1,), (1,)), ((), ())), preferred_element_type=F32)


def tn_dot(a, b):
    return lax.dot_general(a, b, (((0,), (0,)), ((), ())), preferred_element_type=F32)


class Plan:
    def __init__(self, rows, cols, states, heads, width, devices):
        self.rows, self.cols, self.states, self.heads = rows, cols, states, heads
        self.width = width
        self.parts = 2 if devices % 2 == 0 and devices > 2 else 1
        self.devices = devices // self.parts
        self.group = width // self.devices
        self.slot = min(self.group, HALF)
        self.slots = self.group // self.slot
        self.work = self.slots * self.devices
        self.head_width = width // heads
        self.col_pad = round_up(cols, 8)
        self.upper = -(-rows // 2)
        self.half = round_up(self.upper * self.col_pad, 8)
        self.cells = rows * self.col_pad
        self.row_pad = 32
        self.edge = states * self.row_pad
        self.top = states * self.col_pad
        self.bc = 2 * states
        self.at_bc = self.slots * self.half
        self.at_dt = self.at_bc + 2 * self.bc
        self.message = round_up(self.at_dt + 2 * self.slots, 8)
        assert self.head_width % self.slot == 0 and self.group % self.slot == 0
        assert LANES % self.head_width == 0 and self.half <= LANES
        assert rows <= self.row_pad and self.cells - self.half <= self.half
        assert states % 16 == 0 and self.edge % LANES == 0 and heads % 8 == 0

    def segments(self):
        return [list(range(p * self.devices, (p + 1) * self.devices)) for p in range(self.parts)]

    def lanes(self):
        at = np.arange(2 * LANES)
        cell = np.where(at < LANES, at, at - LANES + self.half)
        live = np.where(at < LANES, at < self.half, cell < self.cells)
        i, j = cell // self.col_pad, cell % self.col_pad
        return i, j, live & (j < self.cols)

    def constants(self):
        i, j, real = self.lanes()
        both = real[:, None] & real[None]
        cell = np.arange(self.cells)
        ci, cj = cell // self.col_pad, cell % self.col_pad
        creal = cj < self.cols
        le = np.arange(self.row_pad)
        lj = np.arange(self.col_pad)
        n = np.arange(self.states)
        edge = np.tile(le, LANES // self.row_pad)
        out = {}
        out["to1"] = (j[:, None] <= j[None]) & both
        out["to2"] = (j[:, None] == j[None]) & (i[:, None] <= i[None]) & both
        out["from1"] = (i[:, None] == i[None]) & (j[:, None] > j[None]) & both
        out["from2"] = (i[:, None] > i[None]) & both
        out["side1"] = (i[None] == le[:, None]) & real[None]
        out["side2"] = (i[None] > le[:, None]) & real[None]
        out["sidemask"] = (i[None] >= le[:, None]) & (le < self.rows)[:, None] & real[None]
        out["down1"] = (j[None] <= lj[:, None]) & real[None]
        out["down2"] = (j[None] == lj[:, None]) & real[None]
        out["downmask"] = (j[None] <= lj[:, None]) & (lj < self.cols)[:, None] & real[None]
        out["keep"] = (i[:, None] == edge[None]) & real[:, None]
        out["pick"] = (
            (i == self.rows - 1)[:, None] & real[:, None] & (j[:, None] == np.tile(lj, self.states)[None])
        )
        out["diag"] = np.repeat(n, self.row_pad)[:, None] == np.repeat(n, self.col_pad)[None]
        cboth = creal[:, None] & real[None]
        out["own1"] = (j[None] <= cj[:, None]) & cboth
        out["own2"] = (j[None] == cj[:, None]) & (i[None] <= ci[:, None]) & cboth
        out["ownmask"] = (i[None] <= ci[:, None]) & (j[None] <= cj[:, None]) & cboth
        out["lanei"] = (np.arange(self.rows)[:, None] == i[None]) & real[None]
        out["lanej"] = (np.arange(self.cols)[:, None] == j[None]) & real[None]
        return {k: jnp.asarray(x.astype(np.float32), BF16) for k, x in out.items()}


def full(shape):
    return pl.BlockSpec(shape, lambda *_: (0,) * len(shape))


SMEM = pl.BlockSpec(memory_space=pltpu.SMEM)


def cell_mask_of(plan, t_ref):
    t = t_ref[...].astype(F32).astype(BF16)
    cell = lax.broadcasted_iota(jnp.int32, (plan.cells, plan.cols), 0)
    col = lax.broadcasted_iota(jnp.int32, (plan.cells, plan.cols), 1)
    pick = (lax.rem(cell, plan.col_pad) == col).astype(F32).astype(BF16)
    cell = lax.broadcasted_iota(jnp.int32, (plan.cells, plan.rows), 0)
    row = lax.broadcasted_iota(jnp.int32, (plan.cells, plan.rows), 1)
    return jnp.sum(jnp.where(lax.div(cell, plan.col_pad) == row, mm(pick, t), 0.0), axis=1, keepdims=True)


def project_kernel(
    plan, tile, bias_ref, x_ref, w_ref, wt_ref, t_ref, lanei_ref, lanej_ref,
    v_ref, pay_ref, rows_ref, flat_ref, wide, keep,
):
    step = pl.program_id(0)
    group, states, cells, heads = plan.group, plan.states, plan.cells, plan.heads
    half, rest = plan.half, plan.cells - plan.half

    @pl.when(step == 0)
    def _():
        wide[...] = jnp.zeros_like(wide)
        for i in range(plan.rows):
            wide[i * plan.col_pad : i * plan.col_pad + plan.cols, :] = x_ref[i].astype(F32)
        flat_ref[...] = wide[...].astype(BF16)
        keep[...] = jnp.broadcast_to(cell_mask_of(plan, t_ref), keep.shape)
        t = t_ref[...].astype(F32).astype(BF16)
        m = jnp.sum(mm(t, lanei_ref[...]) * lanej_ref[...].astype(F32), axis=0, keepdims=True)
        x = flat_ref[...]
        table = nt_dot(wt_ref[...], x)
        ext = jnp.concatenate([table, jnp.zeros((table.shape[0], 2 * LANES - cells), F32)], axis=1)
        lane = lax.broadcasted_iota(jnp.int32, (table.shape[0], LANES), 1)
        lo, hi = ext[:, :LANES], ext[:, LANES:]
        shift = half % LANES
        if shift:
            moved = jnp.where(
                lane < LANES - shift, pltpu.roll(lo, LANES - shift, 1), pltpu.roll(hi, LANES - shift, 1)
            )
        else:
            moved = hi
        table = jnp.concatenate([jnp.where(lane < half, lo, 0.0), jnp.where(lane < rest, moved, 0.0)], axis=1)
        z = table[2 * states :]
        at = lax.broadcasted_iota(jnp.int32, z.shape, 0)
        for h in range(heads):
            z = jnp.where(at == h, z + bias_ref[h], z)
        soft = m * (jnp.maximum(z, 0.0) + jnp.log1p(jnp.exp(-jnp.abs(z))))
        rows_ref[...] = jnp.concatenate([table[: 2 * states], soft], axis=0).astype(BF16).astype(F32)
        v_ref[...] = jnp.zeros_like(v_ref)

    v = mm(flat_ref[...], w_ref[...]).astype(BF16).astype(F32) * keep[:, :1]
    low = v.astype(BF16)
    v_ref[0:half, :] = low[:half]
    v_ref[LANES : LANES + rest, :] = low[half:]
    lane = lax.broadcasted_iota(jnp.int32, (half, LANES), 1)
    bc = rows_ref[0 : 2 * states, :].astype(BF16)
    for k in range(tile // group):
        dts = []
        for s in range(plan.slots):
            offset = k * group + s * plan.slot
            base = offset // LANES * LANES
            at = offset % LANES
            first = v[:half, base : base + LANES]
            last = v[half:, base : base + LANES]
            if rest < half:
                last = jnp.concatenate([last, jnp.zeros((half - rest, LANES), F32)], axis=0)
            if at:
                first = pltpu.roll(first, LANES - at, 1)
            if at != HALF:
                last = pltpu.roll(last, (HALF - at) % LANES, 1)
            both = jnp.where(lane < HALF, first, last)
            if plan.slot < HALF:
                both = jnp.where(lane % HALF < plan.slot, both, 0.0)
            pay_ref[k, s * half : (s + 1) * half, :] = both.astype(BF16)
            head = (step * tile + offset) // plan.head_width
            dt = rows_ref[pl.ds(2 * states + head, 1), :]
            dts += [dt[:, :LANES], dt[:, LANES:]]
        pay_ref[k, plan.at_bc : plan.at_bc + plan.bc, :] = bc[:, :LANES]
        pay_ref[k, plan.at_bc + plan.bc : plan.at_dt, :] = bc[:, LANES:]
        spare = plan.message - plan.at_dt - len(dts)
        dts += [jnp.zeros((spare, LANES), F32)] if spare else []
        pay_ref[k, plan.at_dt : plan.message, :] = jnp.concatenate(dts, axis=0).astype(BF16)


def project(plan, consts, slide, w_in, w_bcd, tissue, dt_bias):
    tile = plan.width // 2
    picks = [consts[k] for k in ("lanei", "lanej")]
    wt, t = w_bcd.T, tissue.T
    depth = slide.shape[2]
    count = 2 * plan.states + plan.heads
    return pl.pallas_call(
        functools.partial(project_kernel, plan, tile),
        grid=(plan.width // tile,),
        in_specs=[
            SMEM,
            full(slide.shape),
            pl.BlockSpec((depth, tile), lambda s: (0, s)),
            full(wt.shape),
            full(t.shape),
        ]
        + [full(x.shape) for x in picks],
        out_specs=[
            pl.BlockSpec((2 * LANES, tile), lambda s: (0, s)),
            pl.BlockSpec((tile // plan.group, plan.message, LANES), lambda s: (s, 0, 0)),
            full((count, 2 * LANES)),
            full((plan.cells, depth)),
        ],
        out_shape=[
            jax.ShapeDtypeStruct((2 * LANES, plan.width), BF16),
            jax.ShapeDtypeStruct((plan.devices, plan.message, LANES), BF16),
            jax.ShapeDtypeStruct((count, 2 * LANES), F32),
            jax.ShapeDtypeStruct((plan.cells, depth), BF16),
        ],
        scratch_shapes=[pltpu.VMEM((plan.cells, depth), F32), pltpu.VMEM((plan.cells, LANES), F32)],
        name="project",
    )(dt_bias, slide, w_in, wt, t, *picks)


def own_kernel(
    plan, rx_ref, ry_ref, skip_ref, v_ref, rows_ref, own1_ref, own2_ref, from1_ref, from2_ref,
    mask_ref, out_ref, pair,
):
    states, cells, half = plan.states, plan.cells, plan.half
    b = rows_ref[0:states, :].astype(BF16)
    c = rows_ref[states : 2 * states, :].astype(BF16)
    pairs = tn_dot(c, b)
    pairs = jnp.concatenate([pairs[:half], pairs[LANES : LANES + cells - half]], axis=0)
    pair[...] = pairs * mask_ref[...].astype(F32)
    lane = lax.broadcasted_iota(jnp.int32, (cells, LANES), 1)
    per = LANES // plan.head_width
    for block in range(plan.width // LANES):
        v = v_ref[:, block * LANES : (block + 1) * LANES]
        vc = jnp.concatenate([v[:half], v[LANES : LANES + cells - half]], axis=0).astype(F32)
        total = None
        for k in range(per):
            h = block * per + k
            dt = rows_ref[2 * states + h : 2 * states + h + 1, :]
            low = dt.astype(BF16)
            x = mm(own1_ref[...] * low, from1_ref[...])
            y = mm(own2_ref[...] * low, from2_ref[...])
            weight = jnp.exp(-(rx_ref[h] * x + ry_ref[h] * y)) * pair[...] * dt
            part = mm(weight.astype(BF16), v) + skip_ref[h] * vc
            total = part if total is None else jnp.where(lane < k * plan.head_width, total, part)
        out_ref[:, block * LANES : (block + 1) * LANES] = total.astype(BF16)


def own_tile(plan, consts, v, rows, rate_x, rate_y, d_skip):
    maps = [consts[k] for k in ("own1", "own2", "from1", "from2", "ownmask")]
    args = [v, rows] + maps
    return pl.pallas_call(
        functools.partial(own_kernel, plan),
        grid=(1,),
        in_specs=[SMEM, SMEM, SMEM] + [full(x.shape) for x in args],
        out_specs=full((plan.cells, plan.width)),
        out_shape=jax.ShapeDtypeStruct((plan.cells, plan.width), BF16),
        scratch_shapes=[pltpu.VMEM((plan.cells, 2 * LANES), F32)],
        compiler_params=pltpu.CompilerParams(vmem_limit_bytes=24 * 2**20),
        name="own",
    )(rate_x, rate_y, d_skip, *args)


def my_head(plan, axis, slot):
    place = lax.rem(lax.axis_index(axis), plan.devices)
    return (place * plan.group + slot * plan.slot) // plan.head_width


def wide_rows(pay_ref, t, at, count, gap):
    return jnp.concatenate([pay_ref[t, at : at + count, :], pay_ref[t, at + gap : at + gap + count, :]], axis=1)


def turned(plan, pay_ref, t, s):
    v = pay_ref[t, s * plan.half : (s + 1) * plan.half, :].astype(F32)
    if plan.half < LANES:
        v = jnp.concatenate([v, jnp.zeros((LANES - plan.half, LANES), F32)], axis=0)
    v = v.T
    return jnp.concatenate([v[:HALF], v[HALF:]], axis=1).astype(BF16)


def repeat_lanes(row, count):
    return jnp.concatenate([row] * count, axis=1)


def load_steps(plan, pay_ref, dts):
    for t in range(plan.devices):
        rows = pay_ref[t, plan.at_dt : plan.message, :].astype(F32)
        for s in range(plan.slots):
            w = s * plan.devices + t
            dts[w : w + 1, :LANES] = rows[2 * s : 2 * s + 1]
            dts[w : w + 1, LANES:] = rows[2 * s + 1 : 2 * s + 2]


def slot_rates(plan, axis, ref, shape):
    rate = jnp.full(shape, ref[my_head(plan, axis, 0)], F32)
    at = lax.broadcasted_iota(jnp.int32, shape, 0)
    for s in range(1, plan.slots):
        rate = jnp.where(at >= s * (shape[0] // plan.slots), ref[my_head(plan, axis, s)], rate)
    return rate


def edges_kernel(
    plan, axis, rx_ref, pay_ref, from1_ref, side1_ref, keep_ref, edge_ref, upto_ref, last_ref,
    dts, inner, kept,
):
    states, tiles = plan.states, plan.devices
    load_steps(plan, pay_ref, dts)
    dt = dts[...]
    low = dt.astype(BF16)
    rate = slot_rates(plan, axis, rx_ref, (plan.work, 2 * LANES))
    inner[...] = jnp.exp(-rate * mm(low, from1_ref[...])) * dt
    kept[...] = jnp.exp(-rate[:, :LANES] * mm(low, keep_ref[...]))
    rowsel = side1_ref[...]
    width = plan.edge // LANES
    for s in range(plan.slots):
        held = jnp.zeros((HALF, plan.edge), F32)
        product = jnp.ones((1, LANES), F32)
        for t in range(tiles):
            w = s * tiles + t
            b = wide_rows(pay_ref, t, plan.at_bc, states, plan.bc).astype(F32)
            bd = (b * inner[w : w + 1, :]).astype(BF16)
            left = jnp.concatenate([rowsel * bd[n : n + 1] for n in range(states)], axis=0)
            edge_ref[w] = held.astype(BF16)
            upto_ref[w : w + 1, :] = product
            now = kept[w : w + 1, :]
            held = held * repeat_lanes(now, width) + nt_dot(turned(plan, pay_ref, t, s), left)
            product = product * now
        last_ref[s] = held.astype(BF16)


def maps_kernel(
    plan, axis, rx_ref, ry_ref, pay_ref, to1_ref, to2_ref, from1_ref, from2_ref, side1_ref, side2_ref,
    sidemask_ref, down1_ref, down2_ref, downmask_ref, pick_ref,
    side_ref, above_ref, bottom_ref, top_ref, dts, s1, s2, d1, d2, down,
):
    states, tiles, rp, cp, work = plan.states, plan.devices, plan.row_pad, plan.col_pad, plan.work
    load_steps(plan, pay_ref, dts)
    low = dts[...].astype(BF16)
    rate_y = slot_rates(plan, axis, ry_ref, (work, 2 * LANES))
    above_ref[...] = jnp.exp(-rate_y * mm(low, to2_ref[...]))
    for w in range(work):
        row = low[w : w + 1]
        s1[w * rp : (w + 1) * rp, :] = side1_ref[...] * row
        s2[w * rp : (w + 1) * rp, :] = side2_ref[...] * row
        rf = dts[w : w + 1, :]
        d1[w * cp : (w + 1) * cp, :] = down1_ref[...].astype(F32) * rf
        d2[w * cp : (w + 1) * cp, :] = down2_ref[...].astype(F32) * rf
    mask = sidemask_ref[...].astype(F32)
    x, y = mm(s1[...], to1_ref[...]), mm(s2[...], to2_ref[...])
    for w in range(work):
        head = my_head(plan, axis, w // tiles)
        at = slice(w * rp, (w + 1) * rp)
        side_ref[w] = (jnp.exp(-(rx_ref[head] * x[at] + ry_ref[head] * y[at])) * mask).astype(BF16)
        bottom_ref[w] = mm(side_ref[w], pick_ref[...]).astype(BF16)
    x, y = mm(d1[...].astype(BF16), from1_ref[...]), mm(d2[...].astype(BF16), from2_ref[...])
    mask = downmask_ref[...].astype(F32)
    for w in range(work):
        head = my_head(plan, axis, w // tiles)
        at = slice(w * cp, (w + 1) * cp)
        fall = jnp.exp(-(rx_ref[head] * x[at] + ry_ref[head] * y[at])) * mask * dts[w : w + 1, :]
        b = wide_rows(pay_ref, w % tiles, plan.at_bc, states, plan.bc).astype(F32)
        falls = jnp.concatenate([fall * b[n : n + 1] for n in range(states)], axis=0).astype(BF16)
        top_ref[w] = nt_dot(turned(plan, pay_ref, w % tiles, w // tiles), falls)


def join_kernel(plan, edge_ref, upto_ref, entry_ref, bottom_ref, top_ref, diag_ref, whole_ref, out_ref):
    width = plan.edge // LANES
    for w in range(plan.work):
        entry = entry_ref[w // plan.devices].astype(F32)
        whole = edge_ref[w].astype(F32) + entry * repeat_lanes(upto_ref[w : w + 1, :], width)
        whole = whole.astype(BF16)
        whole_ref[w] = whole
        passed = jnp.concatenate([bottom_ref[w]] * plan.states, axis=0) * diag_ref[...]
        out_ref[w] = (top_ref[w] + mm(whole, passed)).astype(BF16)


def cells_kernel(plan, pay_ref, edge_ref, top_ref, side_ref, above_ref, colsel_ref, out_ref):
    states, tiles = plan.states, plan.devices
    colsel = colsel_ref[...].astype(F32)
    for w in range(plan.work):
        t, s = w % tiles, w // tiles
        c = wide_rows(pay_ref, t, plan.at_bc + states, states, plan.bc)
        side = side_ref[w]
        left = jnp.concatenate([side * c[n : n + 1] for n in range(states)], axis=0)
        ca = c.astype(F32) * above_ref[w : w + 1, :]
        down = jnp.concatenate([colsel * ca[n : n + 1] for n in range(states)], axis=0).astype(BF16)
        y = mm(edge_ref[w], left) + mm(top_ref[w], down)
        y = jnp.concatenate([y[:, :LANES], y[:, LANES:]], axis=0).T
        out_ref[t, s * plan.half : (s + 1) * plan.half, :] = y[: plan.half].astype(BF16)


def call(kernel, name, smem, args, outs, scratch=(), mib=24):
    return pl.pallas_call(
        kernel,
        grid=(1,),
        in_specs=[SMEM] * len(smem) + [full(x.shape) for x in args],
        out_specs=[full(s) for s, _ in outs],
        out_shape=[jax.ShapeDtypeStruct(s, d) for s, d in outs],
        scratch_shapes=[pltpu.VMEM(s, d) for s, d in scratch],
        compiler_params=pltpu.CompilerParams(vmem_limit_bytes=mib * 2**20),
        name=name,
    )(*smem, *args)


def scan_calls(plan, consts, row_axis, col_axis, pay, rate_x, rate_y):
    work, rp, cp, wide = plan.work, plan.row_pad, plan.col_pad, 2 * LANES
    names = ("from1", "side1", "keep")
    edges, upto, last = call(
        functools.partial(edges_kernel, plan, col_axis),
        "edges",
        [rate_x],
        [pay] + [consts[k] for k in names],
        [((work, HALF, plan.edge), BF16), ((work, LANES), F32), ((plan.slots, HALF, plan.edge), BF16)],
        [((work, wide), F32), ((work, wide), F32), ((work, LANES), F32)],
    )
    if plan.parts > 1:
        hops = [(k, k + plan.devices) for k in range(plan.devices)]
        entry = lax.ppermute(last, col_axis, hops)
    else:
        entry = jnp.zeros_like(last)
    names = ("to1", "to2", "from1", "from2", "side1", "side2", "sidemask", "down1", "down2", "downmask", "pick")
    side, above, bottom, tops = call(
        functools.partial(maps_kernel, plan, col_axis),
        "maps",
        [rate_x, rate_y],
        [pay] + [consts[k] for k in names],
        [
            ((work, rp, wide), BF16),
            ((work, wide), F32),
            ((work, rp, LANES), BF16),
            ((work, HALF, plan.top), F32),
        ],
        [
            ((work, wide), F32),
            ((work * rp, wide), BF16),
            ((work * rp, wide), BF16),
            ((work * cp, wide), F32),
            ((work * cp, wide), F32),
            ((work * cp, wide), F32),
        ],
    )
    edges, tops = call(
        functools.partial(join_kernel, plan),
        "join",
        [],
        [edges, upto, entry, bottom, tops, consts["diag"]],
        [((work, HALF, plan.edge), BF16), ((work, HALF, plan.top), BF16)],
    )
    count = lax.axis_size(row_axis)
    chain = [(r, r + 1) for r in range(count - 1)]
    entry = lax.ppermute(tops, row_axis, chain)
    if count > 2:
        keep = jnp.dot(above.astype(BF16), consts["pick"], preferred_element_type=F32)[:, None, :]
        for _ in range(count - 2):
            entry = lax.ppermute(
                (tops.astype(F32) + keep * entry.astype(F32)).astype(BF16), row_axis, chain
            )
    return call(
        functools.partial(cells_kernel, plan),
        "cells",
        [],
        [pay, edges, entry, side, above, consts["down2"]],
        [((plan.devices, plan.slots * plan.half, LANES), BF16)],
    )[0]


def finish_kernel(plan, y_ref, own_ref, z_ref, gain_ref, t_ref, w_ref, out_ref, full_ref):
    half, cells = plan.half, plan.cells
    slot, slots = plan.slot, plan.slots
    per = LANES // slot
    lane = lax.broadcasted_iota(jnp.int32, (half, LANES), 1)
    for block in range(plan.width // LANES):
        for k, (lo, hi) in enumerate(((0, half), (half, cells))):
            joined = None
            for d in range(per):
                at = block * per + d
                part = y_ref[at // slots, at % slots * half : (at % slots + 1) * half, :].astype(F32)
                shift = (d * slot - k * HALF) % LANES
                if shift:
                    part = pltpu.roll(part, shift, 1)
                joined = part if joined is None else jnp.where(lane < d * slot, joined, part)
            full_ref[lo:hi, block * LANES : (block + 1) * LANES] = joined[: hi - lo]
    y = full_ref[...] + own_ref[...].astype(F32)
    y = y.astype(BF16).astype(F32)
    z = z_ref[...].astype(F32)
    gated = y * (z * (1.0 / (1.0 + jnp.exp(-z))))
    scale = lax.rsqrt(jnp.mean(gated * gated, axis=-1, keepdims=True) + norm_eps)
    normed = (gated * scale * gain_ref[...]).astype(BF16)
    full_ref[...] = mm(normed, w_ref[...]) * cell_mask_of(plan, t_ref)
    for i in range(plan.rows):
        out_ref[i] = full_ref[i * plan.col_pad : i * plan.col_pad + plan.cols, :].astype(BF16)


def finish(plan, consts, y, own, z, gain, tissue, w_out):
    args = (y, own, z, gain, tissue.T, w_out)
    shape = (plan.rows, plan.cols, w_out.shape[1])
    assert w_out.shape[1] == plan.width
    return pl.pallas_call(
        functools.partial(finish_kernel, plan),
        grid=(1,),
        in_specs=[full(a.shape) for a in args],
        out_specs=full(shape),
        out_shape=jax.ShapeDtypeStruct(shape, BF16),
        scratch_shapes=[pltpu.VMEM((plan.cells, plan.width), F32)],
        compiler_params=pltpu.CompilerParams(vmem_limit_bytes=24 * 2**20),
        name="finish",
    )(*args)


def per_device(slide, tissue, w_in, w_bcd, dt_bias, rate_x, rate_y, d_skip, norm_gain, w_out):
    rows, cols, model_width = slide.shape
    width = w_out.shape[0]
    heads = dt_bias.shape[0]
    states = (w_bcd.shape[1] - heads) // 2
    plan = Plan(rows, cols, states, heads, width, lax.axis_size("col"))
    consts = plan.constants()
    v, pay, table, x = project(plan, consts, slide, w_in, w_bcd, tissue, dt_bias)
    groups = plan.segments()
    pay = lax.all_to_all(pay, "col", 0, 0, tiled=True, axis_index_groups=groups)
    own = own_tile(plan, consts, v, table, rate_x, rate_y, d_skip)
    z = jnp.dot(x, w_in[:, width:], preferred_element_type=F32).astype(BF16)
    y = scan_calls(plan, consts, "row", "col", pay, rate_x, rate_y)
    y = lax.all_to_all(y, "col", 0, 0, tiled=True, axis_index_groups=groups)
    return finish(plan, consts, y, own, z, norm_gain.reshape(1, width), tissue, w_out)


def solution(mesh):
    placed = (
        P(("slides", "row"), "col", None),
        P(("slides", "row"), "col"),
        P(),
        P(),
        P(),
        P(),
        P(),
        P(),
        P(),
        P(),
    )
    return jax.shard_map(
        per_device,
        mesh=mesh,
        in_specs=placed,
        out_specs=P(("slides", "row"), "col", None),
        check_vma=False,
    )
```

time: 69.8 us -> 54.5 us (0.78)
  blocking collectives: 29.3 us -> 16.9 us
  Pallas kernels: 23.6 us -> 16.6 us
  starting transfers between devices: 4.86 us -> 10.4 us
  waiting for transfers between devices: 7.11 us -> 1.99 us
  local copies, waits for them, and re-layouts: 1.48 us -> 5.37 us
    all_to_all x1, blocking collectives: 29.3 us -> 16.9 us  [per_device(): pay = lax.all_to_all(pay, 'col', 0, 0, tiled=True, axis_index_groups=groups)]
    all_to_all x1, waiting for transfers between devices: 5.77 us -> 0.01 us  [per_device(): y = lax.all_to_all(y, 'col', 0, 0, tiled=True, axis_index_groups=groups)]
    ppermute x0 -> x1, starting transfers between devices: none -> 4.5 us  [scan_calls(): entry = lax.ppermute(last, col_axis, hops)]
    unnamed x6 -> x52, local copies, waits for them, and re-layouts: 1.48 us -> 5.37 us
    pallas_call x2 -> x4, Pallas kernels: 9.77 us -> 6.23 us  [call(): pl.pallas_call(kernel, grid=(1,), in_specs=[SMEM] * len(smem) + [full(x.s...]
    pallas_call x1, Pallas kernels: 4.38 us -> 2.26 us  [finish(): pl.pallas_call(functools.partial(finish_kernel, plan), grid=(1,), in_spec...]
    pallas_call x1, Pallas kernels: 5.52 us -> 4.02 us  [own_tile(): pl.pallas_call(functools.partial(own_kernel, plan), grid=(1,), in_specs=[...]
    all_to_all x1, starting transfers between devices: 3.56 us -> 4.63 us  [per_device(): y = lax.all_to_all(y, 'col', 0, 0, tiled=True, axis_index_groups=groups)]
  transfers between devices with their start and end apart: 2 -> 3, of which waited for: 2 -> 2; matrix products, arithmetic and copies ran while one was open for 4% -> 4% of each run, Pallas kernels for 8% -> 10%
where the time goes in v3:
time: 54.5 us; the launch traced here: 54 us
  blocking collectives  16.9 us (31%)
  Pallas kernels  16.6 us (30%)
  starting transfers between devices  10.4 us (19%)
  local copies, waits for them, and re-layouts  5.37 us (10%)
  matrix products  2.39 us (4%)
  waiting for transfers between devices  1.99 us (4%)
    all_to_all x1, blocking collectives, per_device(): pay = lax.all_to_all(pay, 'col', 0, 0, tiled=True, axis_index_groups=groups)  16.9 us
    pallas_call x4, Pallas kernels, call(): pl.pallas_call(kernel, grid=(1,), in_specs=[SMEM] * len(smem) + [full(x.s...  6.23 us
    unnamed x52, local copies, waits for them, and re-layouts  5.37 us
    all_to_all x1, starting transfers between devices, per_device(): y = lax.all_to_all(y, 'col', 0, 0, tiled=True, axis_index_groups=groups)  4.63 us
    ppermute x1, starting transfers between devices, scan_calls(): entry = lax.ppermute(last, col_axis, hops)  4.5 us
    pallas_call x1, Pallas kernels, project(): pl.pallas_call(functools.partial(project_kernel, plan, tile), grid=(plan....  4.08 us
    pallas_call x1, Pallas kernels, own_tile(): pl.pallas_call(functools.partial(own_kernel, plan), grid=(1,), in_specs=[...  4.02 us
    dot_general x1, matrix products, per_device(): z = jnp.dot(x, w_in[:, width:], preferred_element_type=F32).astype(BF16)  2.39 us
  transfers between devices with their start and end apart: 3, of which 2 were waited for; matrix products, arithmetic and copies ran while one was open for 4% of the time, Pallas kernels for 10%

profile of v3, /device:TPU:0, one launch (start us, length us, event | category | flops | bytes accessed | tf_op | source)
XLA Modules:
  0.0 54.0 jit_solution(14054368550828770353)
XLA Ops:
  0.0 0.0 copy-start.1
  0.0 0.0 copy-start.10
  0.0 0.0 copy-start.3
  0.0 0.0 copy-start.16
  0.0 0.0 copy-start.11
  0.0 0.0 copy-start.20
  0.0 0.0 copy-start.21
  0.1 0.0 copy-start.14
  0.1 0.0 copy-start.15
  0.1 0.0 copy-start.4
  0.1 0.0 copy-start.5
  0.1 0.0 copy-start.6
  0.1 0.0 copy-start.18
  0.1 0.0 copy-start.23
  0.1 4.1 %project.1 = (bf16[256,1024]{1,0:T(8,128)(2,1)}, bf16[8,296,128]{2,1,0:T(8,128)(2,1)}, f32[48,256]{1,0:T(8,128)}, bf16[224,1024]{1,0:T(8,128)(2,1)}) custom-call(f32[16]{0:T(128)} %bias_ref.1, bf16[28,7,1024]{2,1,0:T(8,128)(2,1)} %x_ref.1, bf16[1024,2048]{1,0:T(8,128)(2,1)} %w_ref.2, bf16[48,1024]{1,0:T(8,128)(2,1)} %bitcast.7, s32[7,28]{1,0:T(8,128)} %bitcast.4, ...), custom_call_target="tpu_custom_call" | custom-call | tf_op jit(solution)/shard_map/project/pallas_call | solution.py:201
  4.2 0.0 copy-start.7
  4.2 0.0 copy-start.8
  4.2 0.0 copy-start.13
  4.2 16.9 %all_to_all.10.pay_ref = bf16[8,296,128]{2,1,0:T(8,128)(2,1)S(1)} all-to-all(bf16[8,296,128]{2,1,0:T(8,128)(2,1)} %get-tuple-element.18), channel_id=1, replica_groups={{0,1,2,3,4,5,6,7},{8,9,10,11,12,13,14,15},{16,17,18,19,20,21,22,23},{24..., dimensions={0} | all-to-all | bytes 1212416 | tf_op jit(solution)/shard_map/all_to_all | solution.py:527
  21.1 0.0 copy-done.1
  21.2 0.0 copy-done.10
  21.2 0.0 copy-done.12
  21.2 0.0 copy-done.18
  21.2 2.1 %edges.1 = (bf16[16,64,512]{2,1,0:T(8,128)(2,1)S(1)}, f32[16,128]{1,0:T(8,128)S(1)}, bf16[2,64,512]{2,1,0:T(8,128)(2,1)S(1)}) custom-call(f32[16]{0:T(128)S(1)} %copy-done.18, bf16[8,296,128]{2,1,0:T(8,128)(2,1)S(1)} %all_to_all.10.pay_ref, bf16[256,256]{1,0:T(8,128)(2,1)S(1)} %copy-done.1, bf16[32,256]{1,0:T(8,128)(2,1)S(1)} %copy-done.10, ...), custom_call_target="tpu_custom_call" | custom-call | tf_op jit(solution)/shard_map/edges/pallas_call | solution.py:401
  23.3 4.5 %collective-permute-start = (bf16[2,64,512]{2,1,0:T(8,128)(2,1)S(1)}, bf16[2,64,512]{2,1,0:T(8,128)(2,1)S(1)}, u32[]{:S(2)}, u32[]{:S(2)}) collective-permute-start(bf16[2,64,512]{2,1,0:T(8,128)(2,1)S(1)} %get-tuple-element.21), channel_id=1, source_target_pairs={{0,8},{1,9},{2,10},{3,11},{4,12},{5,13},{6,14},{7,15},{16,24},{17,... | collective-permute-start | bytes 393224 | tf_op jit(solution)/shard_map/ppermute | solution.py:426
  27.8 0.0 copy-done.3
  27.8 0.0 copy-done.16
  27.8 0.0 copy-done.11
  27.8 0.0 copy-done.20
  27.8 0.0 copy-done.21
  27.8 0.0 copy-done.14
  27.9 0.0 copy-done.15
  27.9 0.0 copy-done.4
  27.9 0.0 copy-done.5
  27.9 0.0 copy-done.23
  27.9 1.5 %maps.1 = (bf16[16,32,256]{2,1,0:T(8,128)(2,1)S(1)}, f32[16,256]{1,0:T(8,128)S(1)}, bf16[16,32,128]{2,1,0:T(8,128)(2,1)S(1)}, f32[16,64,128]{2,1,0:T(8,128)S(1)}) custom-call(f32[16]{0:T(128)S(1)} %copy-done.18, f32[16]{0:T(128)S(1)} %copy-done.23, bf16[8,296,128]{2,1,0:T(8,128)(2,1)S(1)} %all_to_all.10.pay_ref, bf16[256,256]{1,0:T(8,128)(2,1)S(1)} %copy-done.5, ...), custom_call_target="tpu_custom_call" | custom-call | tf_op jit(solution)/shard_map/maps/pallas_call | solution.py:401
  29.4 0.9 %collective-permute-done.entry_ref = bf16[2,64,512]{2,1,0:T(8,128)(2,1)S(1)} collective-permute-done((bf16[2,64,512]{2,1,0:T(8,128)(2,1)S(1)}, bf16[2,64,512]{2,1,0:T(8,128)(2,1)S(1)}, u32[]{:S(2)}, u32[]{:S(2)}) %collective-permute-start) | collective-permute-done | bytes 131104 | tf_op jit(solution)/shard_map/ppermute | solution.py:426
  30.3 0.0 copy-done.6
  30.3 0.7 %join.1 = (bf16[16,64,512]{2,1,0:T(8,128)(2,1)S(1)}, bf16[16,64,128]{2,1,0:T(8,128)(2,1)S(1)}) custom-call(bf16[16,64,512]{2,1,0:T(8,128)(2,1)S(1)} %get-tuple-element.19.edge_ref, f32[16,128]{1,0:T(8,128)S(1)} %get-tuple-element.20.upto_ref, bf16[2,64,512]{2,1,0:T(8,128)(2,1)S(1)} %collective-permute-done.entry_ref, ...), custom_call_target="tpu_custom_call" | custom-call | tf_op jit(solution)/shard_map/join/pallas_call | solution.py:401
  31.0 1.3 %collective-permute-start.1 = (bf16[16,64,128]{2,1,0:T(8,128)(2,1)S(1)}, bf16[16,64,128]{2,1,0:T(8,128)(2,1)S(1)}, u32[]{:S(2)}, u32[]{:S(2)}) collective-permute-start(bf16[16,64,128]{2,1,0:T(8,128)(2,1)S(1)} %get-tuple-element.25), channel_id=1, source_target_pairs={{0,16},{1,17},{2,18},{3,19},{4,20},{5,21},{6,22},{7,23},{8,24},{9,... | collective-permute-start | bytes 786440 | tf_op jit(solution)/shard_map/ppermute | solution.py:459
  32.3 1.1 %collective-permute-done.1.top_ref = bf16[16,64,128]{2,1,0:T(8,128)(2,1)S(1)} collective-permute-done((bf16[16,64,128]{2,1,0:T(8,128)(2,1)S(1)}, bf16[16,64,128]{2,1,0:T(8,128)(2,1)S(1)}, u32[]{:S(2)}, u32[]{:S(2)}) %collective-permute-start.1) | collective-permute-done | bytes 262176 | tf_op jit(solution)/shard_map/ppermute | solution.py:459
  33.4 0.0 copy-start
  33.4 1.9 %cells.1 = bf16[8,224,128]{2,1,0:T(8,128)(2,1)} custom-call(bf16[8,296,128]{2,1,0:T(8,128)(2,1)S(1)} %all_to_all.10.pay_ref, bf16[16,64,512]{2,1,0:T(8,128)(2,1)S(1)} %get-tuple-element.24.edge_ref, bf16[16,64,128]{2,1,0:T(8,128)(2,1)S(1)} %collective-permute-done.1.top_ref, bf16[16,32,256]{2,1,0:T(8,128)(2,1)S(1)} %get-tuple-element.26.side_ref, ...), custom_call_target="tpu_custom_call" | custom-call | tf_op jit(solution)/shard_map/cells/pallas_call | solution.py:401
  35.3 4.6 %all-to-all-start.1 = ((bf16[8,224,128]{2,1,0:T(8,128)(2,1)}), bf16[8,224,128]{2,1,0:T(8,128)(2,1)S(1)}, u32[]{:S(2)}, u32[]{:S(2)}) async-start(bf16[8,224,128]{2,1,0:T(8,128)(2,1)} %cells.1), calls=%async_computation.1 | async-start | bytes 917504 | tf_op jit(solution)/shard_map/all_to_all | solution.py:531
  40.0 0.0 copy-done.7
  40.0 0.0 copy-done.8
  40.0 0.0 copy-done.13
  40.0 0.0 copy-start.2
  40.0 1.0 %copy-done.2 = bf16[256,1024]{1,0:T(8,128)(2,1)S(1)} copy-done((bf16[256,1024]{1,0:T(8,128)(2,1)S(1)}, bf16[256,1024]{1,0:T(8,128)(2,1)}, u32[]{:S(2)}) %copy-start.2) | copy-done | bytes 524312
  41.0 0.0 copy-start.9
  41.0 0.9 %copy-done.9 = bf16[224,256]{1,0:T(8,128)(2,1)S(1)} copy-done((bf16[224,256]{1,0:T(8,128)(2,1)S(1)}, bf16[224,256]{1,0:T(8,128)(2,1)}, u32[]{:S(2)}) %copy-start.9) | copy-done | bytes 114712
  41.9 0.0 copy-start.19
  41.9 0.7 %copy-done.19 = f32[16]{0:T(128)S(1)} copy-done((f32[16]{0:T(128)S(1)}, f32[16]{0:T(128)}, u32[]{:S(2)}) %copy-start.19) | copy-done | bytes 88
  42.6 0.0 copy-start.24
  42.6 0.7 %copy-done.24 = f32[16]{0:T(128)S(1)} copy-done((f32[16]{0:T(128)S(1)}, f32[16]{0:T(128)}, u32[]{:S(2)}) %copy-start.24) | copy-done | bytes 88
  43.2 0.7 %copy-done.25 = f32[16]{0:T(128)S(1)} copy-done((f32[16]{0:T(128)S(1)}, f32[16]{0:T(128)}, u32[]{:S(2)}) %copy-start.25) | copy-done | bytes 88
  43.9 4.0 %own.1.own_ref = bf16[224,1024]{1,0:T(8,128)(2,1)S(1)} custom-call(f32[16]{0:T(128)S(1)} %copy-done.19, f32[16]{0:T(128)S(1)} %copy-done.24, f32[16]{0:T(128)S(1)} %copy-done.25, bf16[256,1024]{1,0:T(8,128)(2,1)S(1)} %copy-done.2, f32[48,256]{1,0:T(8,128)S(1)} %copy-done.13, bf16[224,256]{1,0:T(8,128)(2,1)S(1)} %copy-done.9, bf16[224,256]{1,0:T(8,128)(2,1)S(1)} %copy-done.8, ...), custom_call_target="tpu_custom_call" | custom-call | tf_op jit(solution)/shard_map/own/pallas_call | solution.py:260
  47.9 2.4 %fusion.2.z_ref = bf16[224,1024]{1,0:T(8,128)(2,1)S(1)} fusion(bf16[224,1024]{1,0:T(8,128)(2,1)} %get-tuple-element.30, bf16[1024,2048]{1,0:T(8,128)(2,1)} %w_ref.2), kind=kOutput, calls=%fused_computation.2 | convolution fusion | flops 469991424 | bytes 3014656 | tf_op jit(solution)/shard_map/dot_general | solution.py:529
  50.3 0.0 all-to-all-done.1.y_ref
  50.3 0.0 copy-done
  50.3 0.0 copy-start.17
  50.4 0.7 %copy-done.17 = s32[28,7]{0,1:T(8,128)S(1)} copy-done((s32[28,7]{0,1:T(8,128)S(1)}, s32[28,7]{0,1:T(8,128)}, u32[]{:S(2)}) %copy-start.17) | copy-done | bytes 808
  51.0 0.7 %copy-done.22 = f32[1024]{0:T(1024)S(1)} copy-done((f32[1024]{0:T(1024)S(1)}, f32[1024]{0:T(1024)}, u32[]{:S(2)}) %copy-start.22) | copy-done | bytes 4120
  51.7 2.3 %finish.1 = bf16[28,7,1024]{2,1,0:T(8,128)(2,1)} custom-call(bf16[8,224,128]{2,1,0:T(8,128)(2,1)S(1)} %all-to-all-done.1.y_ref, bf16[224,1024]{1,0:T(8,128)(2,1)S(1)} %own.1.own_ref, bf16[224,1024]{1,0:T(8,128)(2,1)S(1)} %fusion.2.z_ref, f32[1,1024]{1,0:T(1,128)S(1)} %bitcast.6, s32[7,28]{1,0:T(8,128)S(1)} %bitcast.5, bf16[1024,1024]{1,0:T(8,128)(2,1)S(1)} %copy-done), custom_call_target="tpu_custom_call" | custom-call | tf_op jit(solution)/shard_map/finish/pallas_call | solution.py:506
  (3 shorter events, 0.0 us)
Async XLA Ops:
  0.0 21.2 %copy-start.1 = (bf16[256,256]{1,0:T(8,128)(2,1)S(1)}, bf16[256,256]{1,0:T(8,128)(2,1)}, u32[]{:S(2)}) copy-start(bf16[256,256]{1,0:T(8,128)(2,1)} %constant.38.clone.from1_ref) | copy-start | bytes 393220
  0.0 21.2 %copy-start.10 = (bf16[32,256]{1,0:T(8,128)(2,1)S(1)}, bf16[32,256]{1,0:T(8,128)(2,1)}, u32[]{:S(2)}) copy-start(bf16[32,256]{1,0:T(8,128)(2,1)} %constant.40.clone.side1_ref) | copy-start | bytes 49156
  0.0 21.2 %copy-start.12 = (bf16[256,128]{1,0:T(8,128)(2,1)S(1)}, bf16[256,128]{1,0:T(8,128)(2,1)}, u32[]{:S(2)}) copy-start(bf16[256,128]{1,0:T(8,128)(2,1)} %constant.46.clone.keep_ref) | copy-start | bytes 196612
  0.0 27.8 %copy-start.3 = (bf16[256,256]{1,0:T(8,128)(2,1)S(1)}, bf16[256,256]{1,0:T(8,128)(2,1)}, u32[]{:S(2)}) copy-start(bf16[256,256]{1,0:T(8,128)(2,1)} %constant.39.clone.from2_ref) | copy-start | bytes 393220
  0.0 27.8 %copy-start.16 = (bf16[8,256]{1,0:T(8,128)(2,1)S(1)}, bf16[8,256]{1,0:T(8,128)(2,1)}, u32[]{:S(2)}) copy-start(bf16[8,256]{1,0:T(8,128)(2,1)} %constant.44.clone.down2_ref.colsel_ref) | copy-start | bytes 12292
  0.0 27.8 %copy-start.11 = (bf16[256,128]{1,0:T(8,128)(2,1)S(1)}, bf16[256,128]{1,0:T(8,128)(2,1)}, u32[]{:S(2)}) copy-start(bf16[256,128]{1,0:T(8,128)(2,1)} %constant.47.clone.pick_ref) | copy-start | bytes 196612
  0.0 27.8 %copy-start.20 = (bf16[8,256]{1,0:T(8,128)(2,1)S(1)}, bf16[8,256]{1,0:T(8,128)(2,1)}, u32[]{:S(2)}) copy-start(bf16[8,256]{1,0:T(8,128)(2,1)} %constant.45.clone.downmask_ref) | copy-start | bytes 12292
  0.0 27.8 %copy-start.21 = (bf16[8,256]{1,0:T(8,128)(2,1)S(1)}, bf16[8,256]{1,0:T(8,128)(2,1)}, u32[]{:S(2)}) copy-start(bf16[8,256]{1,0:T(8,128)(2,1)} %constant.43.clone.down1_ref) | copy-start | bytes 12292
  0.1 27.8 %copy-start.14 = (bf16[32,256]{1,0:T(8,128)(2,1)S(1)}, bf16[32,256]{1,0:T(8,128)(2,1)}, u32[]{:S(2)}) copy-start(bf16[32,256]{1,0:T(8,128)(2,1)} %constant.42.clone.sidemask_ref) | copy-start | bytes 49156
  0.1 27.8 %copy-start.15 = (bf16[32,256]{1,0:T(8,128)(2,1)S(1)}, bf16[32,256]{1,0:T(8,128)(2,1)}, u32[]{:S(2)}) copy-start(bf16[32,256]{1,0:T(8,128)(2,1)} %constant.41.clone.side2_ref) | copy-start | bytes 49156
  0.1 27.8 %copy-start.4 = (bf16[256,256]{1,0:T(8,128)(2,1)S(1)}, bf16[256,256]{1,0:T(8,128)(2,1)}, u32[]{:S(2)}) copy-start(bf16[256,256]{1,0:T(8,128)(2,1)} %constant.37.clone.to2_ref) | copy-start | bytes 393220
  0.1 27.8 %copy-start.5 = (bf16[256,256]{1,0:T(8,128)(2,1)S(1)}, bf16[256,256]{1,0:T(8,128)(2,1)}, u32[]{:S(2)}) copy-start(bf16[256,256]{1,0:T(8,128)(2,1)} %constant.36.clone.to1_ref) | copy-start | bytes 393220
  0.1 30.2 %copy-start.6 = (bf16[512,128]{1,0:T(8,128)(2,1)S(1)}, bf16[512,128]{1,0:T(8,128)(2,1)}, u32[]{:S(2)}) copy-start(bf16[512,128]{1,0:T(8,128)(2,1)} %constant.48.clone.diag_ref) | copy-start | bytes 393220
  0.1 21.0 %copy-start.18 = (f32[16]{0:T(128)S(1)}, f32[16]{0:T(128)}, u32[]{:S(2)}) copy-start(f32[16]{0:T(128)} %rx_ref.5) | copy-start | bytes 196
  0.1 27.8 %copy-start.23 = (f32[16]{0:T(128)S(1)}, f32[16]{0:T(128)}, u32[]{:S(2)}) copy-start(f32[16]{0:T(128)} %ry_ref.3) | copy-start | bytes 196
  4.2 35.7 %copy-start.7 = (bf16[224,256]{1,0:T(8,128)(2,1)S(1)}, bf16[224,256]{1,0:T(8,128)(2,1)}, u32[]{:S(2)}) copy-start(bf16[224,256]{1,0:T(8,128)(2,1)} %constant.51.clone.mask_ref) | copy-start | bytes 344068
  4.2 35.7 %copy-start.8 = (bf16[224,256]{1,0:T(8,128)(2,1)S(1)}, bf16[224,256]{1,0:T(8,128)(2,1)}, u32[]{:S(2)}) copy-start(bf16[224,256]{1,0:T(8,128)(2,1)} %constant.50.clone.own2_ref) | copy-start | bytes 344068
  4.2 35.7 %copy-start.13 = (f32[48,256]{1,0:T(8,128)S(1)}, f32[48,256]{1,0:T(8,128)}, u32[]{:S(2)}) copy-start(f32[48,256]{1,0:T(8,128)} %get-tuple-element.29.rows_ref) | copy-start | bytes 147460
  23.3 7.0 %collective-permute-start = (bf16[2,64,512]{2,1,0:T(8,128)(2,1)S(1)}, bf16[2,64,512]{2,1,0:T(8,128)(2,1)S(1)}, u32[]{:S(2)}, u32[]{:S(2)}) collective-permute-start(bf16[2,64,512]{2,1,0:T(8,128)(2,1)S(1)} %get-tuple-element.21), channel_id=1, source_target_pairs={{0,8},{1,9},{2,10},{3,11},{4,12},{5,13},{6,14},{7,15},{16,24},{17,... | collective-permute-start | bytes 393224 | tf_op jit(solution)/shard_map/ppermute | solution.py:426
  31.0 2.4 %collective-permute-start.1 = (bf16[16,64,128]{2,1,0:T(8,128)(2,1)S(1)}, bf16[16,64,128]{2,1,0:T(8,128)(2,1)S(1)}, u32[]{:S(2)}, u32[]{:S(2)}) collective-permute-start(bf16[16,64,128]{2,1,0:T(8,128)(2,1)S(1)} %get-tuple-element.25), channel_id=1, source_target_pairs={{0,16},{1,17},{2,18},{3,19},{4,20},{5,21},{6,22},{7,23},{8,24},{9,... | collective-permute-start | bytes 786440 | tf_op jit(solution)/shard_map/ppermute | solution.py:459
  33.4 16.9 %copy-start = (bf16[1024,1024]{1,0:T(8,128)(2,1)S(1)}, bf16[1024,1024]{1,0:T(8,128)(2,1)}, u32[]{:S(2)}) copy-start(bf16[1024,1024]{1,0:T(8,128)(2,1)} %w_ref.3) | copy-start | bytes 6291460
  35.3 15.0 %all-to-all-start.1 = ((bf16[8,224,128]{2,1,0:T(8,128)(2,1)}), bf16[8,224,128]{2,1,0:T(8,128)(2,1)S(1)}, u32[]{:S(2)}, u32[]{:S(2)}) async-start(bf16[8,224,128]{2,1,0:T(8,128)(2,1)} %cells.1), calls=%async_computation.1 | async-start | bytes 917504 | tf_op jit(solution)/shard_map/all_to_all | solution.py:531
  40.0 1.0 %copy-start.2 = (bf16[256,1024]{1,0:T(8,128)(2,1)S(1)}, bf16[256,1024]{1,0:T(8,128)(2,1)}, u32[]{:S(2)}) copy-start(bf16[256,1024]{1,0:T(8,128)(2,1)} %get-tuple-element.28.v_ref) | copy-start | bytes 1572868
  41.0 0.9 %copy-start.9 = (bf16[224,256]{1,0:T(8,128)(2,1)S(1)}, bf16[224,256]{1,0:T(8,128)(2,1)}, u32[]{:S(2)}) copy-start(bf16[224,256]{1,0:T(8,128)(2,1)} %constant.49.clone.own1_ref) | copy-start | bytes 344068
  41.9 0.7 %copy-start.19 = (f32[16]{0:T(128)S(1)}, f32[16]{0:T(128)}, u32[]{:S(2)}) copy-start(f32[16]{0:T(128)} %rx_ref.5) | copy-start | bytes 196
  42.6 0.7 %copy-start.24 = (f32[16]{0:T(128)S(1)}, f32[16]{0:T(128)}, u32[]{:S(2)}) copy-start(f32[16]{0:T(128)} %ry_ref.3) | copy-start | bytes 196
  43.2 0.7 %copy-start.25 = (f32[16]{0:T(128)S(1)}, f32[16]{0:T(128)}, u32[]{:S(2)}) copy-start(f32[16]{0:T(128)} %skip_ref.1) | copy-start | bytes 196
  50.3 0.7 %copy-start.17 = (s32[28,7]{0,1:T(8,128)S(1)}, s32[28,7]{0,1:T(8,128)}, u32[]{:S(2)}) copy-start(s32[28,7]{0,1:T(8,128)} %param.29) | copy-start | bytes 2356
  51.0 0.7 %copy-start.22 = (f32[1024]{0:T(1024)S(1)}, f32[1024]{0:T(1024)}, u32[]{:S(2)}) copy-start(f32[1024]{0:T(1024)} %param.36) | copy-start | bytes 12292

commit v4 on v3

--- a/solution.py
+++ b/solution.py
@@ -17,6 +17,10 @@
 
 def round_up(value, step):
     return -(-value // step) * step
+
+
+def in_hbm(x):
+    return pltpu.with_memory_space_constraint(x, pltpu.HBM)
 
 
 def mm(a, b):
@@ -100,13 +104,14 @@
         out["ownmask"] = (i[None] <= ci[:, None]) & (j[None] <= cj[:, None]) & cboth
         out["lanei"] = (np.arange(self.rows)[:, None] == i[None]) & real[None]
         out["lanej"] = (np.arange(self.cols)[:, None] == j[None]) & real[None]
-        return {k: jnp.asarray(x.astype(np.float32), BF16) for k, x in out.items()}
+        return {k: in_hbm(jnp.asarray(x.astype(np.float32), BF16)) for k, x in out.items()}
 
 
 def full(shape):
     return pl.BlockSpec(shape, lambda *_: (0,) * len(shape))
 
 
+HBM = pl.BlockSpec(memory_space=pltpu.HBM)
 SMEM = pl.BlockSpec(memory_space=pltpu.SMEM)
 
 
@@ -121,116 +126,128 @@
 
 
 def project_kernel(
-    plan, tile, bias_ref, x_ref, w_ref, wt_ref, t_ref, lanei_ref, lanej_ref,
-    v_ref, pay_ref, rows_ref, flat_ref, wide, keep,
+    plan, chunks, bias_ref, x_hbm, w_hbm, wt_ref, t_ref, lanei_ref, lanej_ref,
+    v_ref, pay_ref, rows_ref, flat_ref, x_ref, w_ref, wide, x_sem, w_sems,
 ):
-    step = pl.program_id(0)
     group, states, cells, heads = plan.group, plan.states, plan.cells, plan.heads
     half, rest = plan.half, plan.cells - plan.half
-
-    @pl.when(step == 0)
-    def _():
-        wide[...] = jnp.zeros_like(wide)
-        for i in range(plan.rows):
-            wide[i * plan.col_pad : i * plan.col_pad + plan.cols, :] = x_ref[i].astype(F32)
-        flat_ref[...] = wide[...].astype(BF16)
-        keep[...] = jnp.broadcast_to(cell_mask_of(plan, t_ref), keep.shape)
-        t = t_ref[...].astype(F32).astype(BF16)
-        m = jnp.sum(mm(t, lanei_ref[...]) * lanej_ref[...].astype(F32), axis=0, keepdims=True)
-        x = flat_ref[...]
-        table = nt_dot(wt_ref[...], x)
-        ext = jnp.concatenate([table, jnp.zeros((table.shape[0], 2 * LANES - cells), F32)], axis=1)
-        lane = lax.broadcasted_iota(jnp.int32, (table.shape[0], LANES), 1)
-        lo, hi = ext[:, :LANES], ext[:, LANES:]
-        shift = half % LANES
-        if shift:
-            moved = jnp.where(
-                lane < LANES - shift, pltpu.roll(lo, LANES - shift, 1), pltpu.roll(hi, LANES - shift, 1)
-            )
-        else:
-            moved = hi
-        table = jnp.concatenate([jnp.where(lane < half, lo, 0.0), jnp.where(lane < rest, moved, 0.0)], axis=1)
-        z = table[2 * states :]
-        at = lax.broadcasted_iota(jnp.int32, z.shape, 0)
-        for h in range(heads):
-            z = jnp.where(at == h, z + bias_ref[h], z)
-        soft = m * (jnp.maximum(z, 0.0) + jnp.log1p(jnp.exp(-jnp.abs(z))))
-        rows_ref[...] = jnp.concatenate([table[: 2 * states], soft], axis=0).astype(BF16).astype(F32)
-        v_ref[...] = jnp.zeros_like(v_ref)
-
-    v = mm(flat_ref[...], w_ref[...]).astype(BF16).astype(F32) * keep[:, :1]
-    low = v.astype(BF16)
-    v_ref[0:half, :] = low[:half]
-    v_ref[LANES : LANES + rest, :] = low[half:]
+    tile = plan.width // chunks
+    x_copy = pltpu.make_async_copy(x_hbm, x_ref, x_sem)
+    x_copy.start()
+    copies = [
+        pltpu.make_async_copy(w_hbm.at[:, k * tile : (k + 1) * tile], w_ref.at[k], w_sems.at[k])
+        for k in range(chunks)
+    ]
+    for copy in copies:
+        copy.start()
+    keep = cell_mask_of(plan, t_ref)
+    t = t_ref[...].astype(F32).astype(BF16)
+    m = jnp.sum(mm(t, lanei_ref[...]) * lanej_ref[...].astype(F32), axis=0, keepdims=True)
+    wide[...] = jnp.zeros_like(wide)
+    v_ref[half:LANES, :] = jnp.zeros((LANES - half, plan.width), BF16)
+    v_ref[LANES + rest :, :] = jnp.zeros((LANES - rest, plan.width), BF16)
+
+    x_copy.wait()
+    for i in range(plan.rows):
+        wide[i * plan.col_pad : i * plan.col_pad + plan.cols, :] = x_ref[i].astype(F32)
+    x = wide[...].astype(BF16)
+    flat_ref[...] = x
+    table = nt_dot(wt_ref[...], x)
+    ext = jnp.concatenate([table, jnp.zeros((table.shape[0], 2 * LANES - cells), F32)], axis=1)
+    lane = lax.broadcasted_iota(jnp.int32, (table.shape[0], LANES), 1)
+    lo, hi = ext[:, :LANES], ext[:, LANES:]
+    shift = half % LANES
+    if shift:
+        moved = jnp.where(
+            lane < LANES - shift, pltpu.roll(lo, LANES - shift, 1), pltpu.roll(hi, LANES - shift, 1)
+        )
+    else:
+        moved = hi
+    table = jnp.concatenate([jnp.where(lane < half, lo, 0.0), jnp.where(lane < rest, moved, 0.0)], axis=1)
+    z = table[2 * states :]
+    at = lax.broadcasted_iota(jnp.int32, z.shape, 0)
+    for h in range(heads):
+        z = jnp.where(at == h, z + bias_ref[h], z)
+    soft = m * (jnp.maximum(z, 0.0) + jnp.log1p(jnp.exp(-jnp.abs(z))))
+    table = jnp.concatenate([table[: 2 * states], soft], axis=0).astype(BF16)
+    rows_ref[...] = table.astype(F32)
+    bc = table[: 2 * states]
+    steps = rows_ref[2 * states :, :]
+
     lane = lax.broadcasted_iota(jnp.int32, (half, LANES), 1)
-    bc = rows_ref[0 : 2 * states, :].astype(BF16)
-    for k in range(tile // group):
-        dts = []
-        for s in range(plan.slots):
-            offset = k * group + s * plan.slot
-            base = offset // LANES * LANES
-            at = offset % LANES
-            first = v[:half, base : base + LANES]
-            last = v[half:, base : base + LANES]
-            if rest < half:
-                last = jnp.concatenate([last, jnp.zeros((half - rest, LANES), F32)], axis=0)
-            if at:
-                first = pltpu.roll(first, LANES - at, 1)
-            if at != HALF:
-                last = pltpu.roll(last, (HALF - at) % LANES, 1)
-            both = jnp.where(lane < HALF, first, last)
-            if plan.slot < HALF:
-                both = jnp.where(lane % HALF < plan.slot, both, 0.0)
-            pay_ref[k, s * half : (s + 1) * half, :] = both.astype(BF16)
-            head = (step * tile + offset) // plan.head_width
-            dt = rows_ref[pl.ds(2 * states + head, 1), :]
-            dts += [dt[:, :LANES], dt[:, LANES:]]
-        pay_ref[k, plan.at_bc : plan.at_bc + plan.bc, :] = bc[:, :LANES]
-        pay_ref[k, plan.at_bc + plan.bc : plan.at_dt, :] = bc[:, LANES:]
-        spare = plan.message - plan.at_dt - len(dts)
-        dts += [jnp.zeros((spare, LANES), F32)] if spare else []
-        pay_ref[k, plan.at_dt : plan.message, :] = jnp.concatenate(dts, axis=0).astype(BF16)
+    for chunk in range(chunks):
+        copies[chunk].wait()
+        v = mm(flat_ref[...], w_ref[chunk]).astype(BF16).astype(F32) * keep
+        low = v.astype(BF16)
+        v_ref[0:half, chunk * tile : (chunk + 1) * tile] = low[:half]
+        v_ref[LANES : LANES + rest, chunk * tile : (chunk + 1) * tile] = low[half:]
+        for k in range(tile // group):
+            dest = chunk * (tile // group) + k
+            dts = []
+            for s in range(plan.slots):
+                offset = k * group + s * plan.slot
+                base = offset // LANES * LANES
+                at = offset % LANES
+                first = v[:half, base : base + LANES]
+                last = v[half:, base : base + LANES]
+                if rest < half:
+                    last = jnp.concatenate([last, jnp.zeros((half - rest, LANES), F32)], axis=0)
+                if at:
+                    first = pltpu.roll(first, LANES - at, 1)
+                if at != HALF:
+                    last = pltpu.roll(last, (HALF - at) % LANES, 1)
+                both = jnp.where(lane < HALF, first, last)
+                if plan.slot < HALF:
+                    both = jnp.where(lane % HALF < plan.slot, both, 0.0)
+                pay_ref[dest, s * half : (s + 1) * half, :] = both.astype(BF16)
+                head = (chunk * tile + offset) // plan.head_width
+                dts += [steps[head : head + 1, :LANES], steps[head : head + 1, LANES:]]
+            pay_ref[dest, plan.at_bc : plan.at_bc + plan.bc, :] = bc[:, :LANES]
+            pay_ref[dest, plan.at_bc + plan.bc : plan.at_dt, :] = bc[:, LANES:]
+            spare = plan.message - plan.at_dt - len(dts)
+            dts += [jnp.zeros((spare, LANES), F32)] if spare else []
+            pay_ref[dest, plan.at_dt : plan.message, :] = jnp.concatenate(dts, axis=0).astype(BF16)
 
 
 def project(plan, consts, slide, w_in, w_bcd, tissue, dt_bias):
-    tile = plan.width // 2
-    picks = [consts[k] for k in ("lanei", "lanej")]
-    wt, t = w_bcd.T, tissue.T
+    chunks = 4
+    tile = plan.width // chunks
     depth = slide.shape[2]
+    args = [in_hbm(w_bcd.T), in_hbm(tissue.T), consts["lanei"], consts["lanej"]]
     count = 2 * plan.states + plan.heads
+    assert plan.width % chunks == 0 and tile % plan.group == 0 and tile % LANES == 0
+    outs = [
+        ((2 * LANES, plan.width), BF16),
+        ((plan.devices, plan.message, LANES), BF16),
+        ((count, 2 * LANES), F32),
+        ((plan.cells, depth), BF16),
+    ]
     return pl.pallas_call(
-        functools.partial(project_kernel, plan, tile),
-        grid=(plan.width // tile,),
-        in_specs=[
-            SMEM,
-            full(slide.shape),
-            pl.BlockSpec((depth, tile), lambda s: (0, s)),
-            full(wt.shape),
-            full(t.shape),
-        ]
-        + [full(x.shape) for x in picks],
-        out_specs=[
-            pl.BlockSpec((2 * LANES, tile), lambda s: (0, s)),
-            pl.BlockSpec((tile // plan.group, plan.message, LANES), lambda s: (s, 0, 0)),
-            full((count, 2 * LANES)),
-            full((plan.cells, depth)),
+        functools.partial(project_kernel, plan, chunks),
+        grid=(1,),
+        in_specs=[SMEM, HBM, HBM] + [full(x.shape) for x in args],
+        out_specs=[full(s) for s, _ in outs],
+        out_shape=[jax.ShapeDtypeStruct(s, d) for s, d in outs],
+        scratch_shapes=[
+            pltpu.VMEM(slide.shape, BF16),
+            pltpu.VMEM((chunks, depth, tile), BF16),
+            pltpu.VMEM((plan.cells, depth), F32),
+            pltpu.SemaphoreType.DMA,
+            pltpu.SemaphoreType.DMA((chunks,)),
         ],
-        out_shape=[
-            jax.ShapeDtypeStruct((2 * LANES, plan.width), BF16),
-            jax.ShapeDtypeStruct((plan.devices, plan.message, LANES), BF16),
-            jax.ShapeDtypeStruct((count, 2 * LANES), F32),
-            jax.ShapeDtypeStruct((plan.cells, depth), BF16),
-        ],
-        scratch_shapes=[pltpu.VMEM((plan.cells, depth), F32), pltpu.VMEM((plan.cells, LANES), F32)],
+        compiler_params=pltpu.CompilerParams(vmem_limit_bytes=24 * 2**20),
         name="project",
-    )(dt_bias, slide, w_in, wt, t, *picks)
-
-
-def own_kernel(
-    plan, rx_ref, ry_ref, skip_ref, v_ref, rows_ref, own1_ref, own2_ref, from1_ref, from2_ref,
-    mask_ref, out_ref, pair,
+    )(in_hbm(dt_bias), in_hbm(slide), in_hbm(w_in), *args)
+
+
+def home_kernel(
+    plan, rx_ref, ry_ref, skip_ref, w_hbm, v_ref, rows_ref, flat_ref, t_ref, gain_ref,
+    own1_ref, own2_ref, from1_ref, from2_ref, mask_ref, out_ref, gate_ref, gain_out, pair, w_ref, sem,
 ):
     states, cells, half = plan.states, plan.cells, plan.half
+    copy = pltpu.make_async_copy(w_hbm.at[:, plan.width :], w_ref, sem)
+    copy.start()
+    gain_out[...] = gain_ref[...]
     b = rows_ref[0:states, :].astype(BF16)
     c = rows_ref[states : 2 * states, :].astype(BF16)
     pairs = tn_dot(c, b)
@@ -252,21 +269,33 @@
             part = mm(weight.astype(BF16), v) + skip_ref[h] * vc
             total = part if total is None else jnp.where(lane < k * plan.head_width, total, part)
         out_ref[:, block * LANES : (block + 1) * LANES] = total.astype(BF16)
-
-
-def own_tile(plan, consts, v, rows, rate_x, rate_y, d_skip):
+    keep = cell_mask_of(plan, t_ref)
+    copy.wait()
+    tile = 2 * LANES
+    for block in range(plan.width // tile):
+        at = slice(block * tile, (block + 1) * tile)
+        z = mm(flat_ref[...], w_ref[:, at]).astype(BF16).astype(F32)
+        gate_ref[:, at] = (z * (1.0 / (1.0 + jnp.exp(-z))) * keep).astype(BF16)
+
+
+def home(plan, consts, v, rows, flat, w_in, tissue, gain, rate_x, rate_y, d_skip):
     maps = [consts[k] for k in ("own1", "own2", "from1", "from2", "ownmask")]
-    args = [v, rows] + maps
+    args = [v, rows, flat, in_hbm(tissue.T), in_hbm(gain)] + maps
+    outs = [((plan.cells, plan.width), BF16), ((plan.cells, plan.width), BF16), (gain.shape, F32)]
     return pl.pallas_call(
-        functools.partial(own_kernel, plan),
+        functools.partial(home_kernel, plan),
         grid=(1,),
-        in_specs=[SMEM, SMEM, SMEM] + [full(x.shape) for x in args],
-        out_specs=full((plan.cells, plan.width)),
-        out_shape=jax.ShapeDtypeStruct((plan.cells, plan.width), BF16),
-        scratch_shapes=[pltpu.VMEM((plan.cells, 2 * LANES), F32)],
+        in_specs=[SMEM, SMEM, SMEM, HBM] + [full(x.shape) for x in args],
+        out_specs=[full(s) for s, _ in outs],
+        out_shape=[jax.ShapeDtypeStruct(s, d) for s, d in outs],
+        scratch_shapes=[
+            pltpu.VMEM((plan.cells, 2 * LANES), F32),
+            pltpu.VMEM((w_in.shape[0], w_in.shape[1] - plan.width), BF16),
+            pltpu.SemaphoreType.DMA,
+        ],
         compiler_params=pltpu.CompilerParams(vmem_limit_bytes=24 * 2**20),
-        name="own",
-    )(rate_x, rate_y, d_skip, *args)
+        name="home",
+    )(in_hbm(rate_x), in_hbm(rate_y), in_hbm(d_skip), in_hbm(w_in), *args)
 
 
 def my_head(plan, axis, slot):
@@ -407,7 +436,7 @@
         scratch_shapes=[pltpu.VMEM(s, d) for s, d in scratch],
         compiler_params=pltpu.CompilerParams(vmem_limit_bytes=mib * 2**20),
         name=name,
-    )(*smem, *args)
+    )(*[in_hbm(x) for x in smem], *args)
 
 
 def scan_calls(plan, consts, row_axis, col_axis, pay, rate_x, rate_y):
@@ -472,7 +501,7 @@
     )[0]
 
 
-def finish_kernel(plan, y_ref, own_ref, z_ref, gain_ref, t_ref, w_ref, out_ref, full_ref):
+def finish_kernel(plan, y_ref, own_ref, gate_ref, gain_ref, w_ref, out_ref, full_ref):
     half, cells = plan.half, plan.cells
     slot, slots = plan.slot, plan.slots
     per = LANES // slot
@@ -490,29 +519,21 @@
             full_ref[lo:hi, block * LANES : (block + 1) * LANES] = joined[: hi - lo]
     y = full_ref[...] + own_ref[...].astype(F32)
     y = y.astype(BF16).astype(F32)
-    z = z_ref[...].astype(F32)
-    gated = y * (z * (1.0 / (1.0 + jnp.exp(-z))))
+    gated = y * gate_ref[...].astype(F32)
     scale = lax.rsqrt(jnp.mean(gated * gated, axis=-1, keepdims=True) + norm_eps)
     normed = (gated * scale * gain_ref[...]).astype(BF16)
-    full_ref[...] = mm(normed, w_ref[...]) * cell_mask_of(plan, t_ref)
+    full_ref[...] = mm(normed, w_ref[...])
     for i in range(plan.rows):
         out_ref[i] = full_ref[i * plan.col_pad : i * plan.col_pad + plan.cols, :].astype(BF16)
 
 
-def finish(plan, consts, y, own, z, gain, tissue, w_out):
-    args = (y, own, z, gain, tissue.T, w_out)
+def finish(plan, y, own, gate, gain, w_out):
+    args = (y, own, gate, gain, w_out)
     shape = (plan.rows, plan.cols, w_out.shape[1])
     assert w_out.shape[1] == plan.width
-    return pl.pallas_call(
-        functools.partial(finish_kernel, plan),
-        grid=(1,),
-        in_specs=[full(a.shape) for a in args],
-        out_specs=full(shape),
-        out_shape=jax.ShapeDtypeStruct(shape, BF16),
-        scratch_shapes=[pltpu.VMEM((plan.cells, plan.width), F32)],
-        compiler_params=pltpu.CompilerParams(vmem_limit_bytes=24 * 2**20),
-        name="finish",
-    )(*args)
+    return call(
+        functools.partial(finish_kernel, plan), "finish", [], args, [(shape, BF16)], [((plan.cells, plan.width), F32)]
+    )[0]
 
 
 def per_device(slide, tissue, w_in, w_bcd, dt_bias, rate_x, rate_y, d_skip, norm_gain, w_out):
@@ -525,11 +546,12 @@
     v, pay, table, x = project(plan, consts, slide, w_in, w_bcd, tissue, dt_bias)
     groups = plan.segments()
     pay = lax.all_to_all(pay, "col", 0, 0, tiled=True, axis_index_groups=groups)
-    own = own_tile(plan, consts, v, table, rate_x, rate_y, d_skip)
-    z = jnp.dot(x, w_in[:, width:], preferred_element_type=F32).astype(BF16)
+    gain = norm_gain.reshape(1, width)
+    own, gate, gain = home(plan, consts, v, table, x, w_in, tissue, gain, rate_x, rate_y, d_skip)
+    pay, own, gate, gain = lax.optimization_barrier((pay, own, gate, gain))
     y = scan_calls(plan, consts, "row", "col", pay, rate_x, rate_y)
     y = lax.all_to_all(y, "col", 0, 0, tiled=True, axis_index_groups=groups)
-    return finish(plan, consts, y, own, z, norm_gain.reshape(1, width), tissue, w_out)
+    return finish(plan, y, own, gate, gain, w_out)
 
 
 def solution(mesh):

time: 54.5 us -> 55 us (level)
  Pallas kernels: 16.6 us -> 22.1 us
  local copies, waits for them, and re-layouts: 5.37 us -> 0.77 us
  matrix products: 2.39 us -> 0 us
  waiting for transfers between devices: 1.99 us -> 4.1 us
  starting transfers between devices: 10.4 us -> 12 us
  blocking collectives: 16.9 us -> 15.5 us
    unnamed x52 -> x6, local copies, waits for them, and re-layouts: 5.37 us -> 0.77 us
    pallas_call x4 -> x5, Pallas kernels: 6.23 us -> 10 us  [call(): pl.pallas_call(kernel, grid=(1,), in_specs=[SMEM] * len(smem) + [full(x.s...]
    all_to_all x1, waiting for transfers between devices: 0.01 us -> 2.64 us  [per_device(): pay = lax.all_to_all(pay, 'col', 0, 0, tiled=True, axis_index_groups=groups)]
    dot_general x1 -> x0, matrix products: 2.39 us -> none  [per_device(): z = jnp.dot(x, w_in[:, width:], preferred_element_type=F32).astype(BF16)]
    pallas_call x3 -> x2, Pallas kernels: 10.4 us -> 12.1 us  [the longest x1 6.46 us: home(): pl.pallas_call(functools.partial(home_kernel, plan), grid=(1,), in_specs=...]
    all_to_all x1, starting transfers between devices: 4.63 us -> 6.22 us  [per_device(): pay = lax.all_to_all(pay, 'col', 0, 0, tiled=True, axis_index_groups=groups)]
    all_to_all x1, blocking collectives: 16.9 us -> 15.5 us  [per_device(): y = lax.all_to_all(y, 'col', 0, 0, tiled=True, axis_index_groups=groups)]
  transfers between devices with their start and end apart: 3 -> 3, of which waited for: 2 -> 3; matrix products, arithmetic and copies ran while one was open for 4% -> 0% of each run, Pallas kernels for 10% -> 16%
where the time goes in v4:
time: 55 us; the launch traced here: 54.6 us
  Pallas kernels  22.1 us (40%)
  blocking collectives  15.5 us (28%)
  starting transfers between devices  12 us (22%)
  waiting for transfers between devices  4.1 us (7%)
  local copies, waits for them, and re-layouts  0.77 us (1%)
    all_to_all x1, blocking collectives, per_device(): y = lax.all_to_all(y, 'col', 0, 0, tiled=True, axis_index_groups=groups)  15.5 us
    pallas_call x5, Pallas kernels, call(): pl.pallas_call(kernel, grid=(1,), in_specs=[SMEM] * len(smem) + [full(x.s...  10 us
    pallas_call x1, Pallas kernels, home(): pl.pallas_call(functools.partial(home_kernel, plan), grid=(1,), in_specs=...  6.46 us
    all_to_all x1, starting transfers between devices, per_device(): pay = lax.all_to_all(pay, 'col', 0, 0, tiled=True, axis_index_groups=groups)  6.22 us
    pallas_call x1, Pallas kernels, project(): pl.pallas_call(functools.partial(project_kernel, plan, chunks), grid=(1,)...  5.62 us
    ppermute x1, starting transfers between devices, scan_calls(): entry = lax.ppermute(last, col_axis, hops)  4.5 us
    all_to_all x1, waiting for transfers between devices, per_device(): pay = lax.all_to_all(pay, 'col', 0, 0, tiled=True, axis_index_groups=groups)  2.64 us
    ppermute x1, starting transfers between devices, scan_calls(): entry = lax.ppermute(tops, row_axis, chain)  1.31 us
  transfers between devices with their start and end apart: 3, of which 3 were waited for; matrix products, arithmetic and copies ran while one was open for 0% of the time, Pallas kernels for 16%

profile of v4, /device:TPU:0, one launch (start us, length us, event | category | flops | bytes accessed | tf_op | source)
XLA Modules:
  0.0 54.6 jit_solution(2806507299263239345)
XLA Ops:
  0.0 5.6 %project.1 = (bf16[256,1024]{1,0:T(8,128)(2,1)S(1)}, bf16[8,296,128]{2,1,0:T(8,128)(2,1)}, f32[48,256]{1,0:T(8,128)S(1)}, bf16[224,1024]{1,0:T(8,128)(2,1)S(1)}) custom-call(f32[16]{0:T(128)} %bias_ref.1, bf16[28,7,1024]{2,1,0:T(8,128)(2,1)} %x_hbm.1, bf16[1024,2048]{1,0:T(8,128)(2,1)} %w_hbm.3, bf16[48,1024]{1,0:T(8,128)(2,1)} %bitcast.3, s32[7,28]{1,0:T(8,128)} %bitcast.4, ...), custom_call_target="tpu_custom_call" | custom-call | tf_op jit(solution)/shard_map/project/pallas_call | solution.py:225
  5.6 6.2 %all-to-all-start = ((bf16[8,296,128]{2,1,0:T(8,128)(2,1)}), bf16[8,296,128]{2,1,0:T(8,128)(2,1)S(1)}, u32[]{:S(2)}, u32[]{:S(2)}) async-start(bf16[8,296,128]{2,1,0:T(8,128)(2,1)} %get-tuple-element.25), calls=%async_computation | async-start | bytes 1212416 | tf_op jit(solution)/shard_map/all_to_all | solution.py:548
  11.9 6.5 %home.1 = (bf16[224,1024]{1,0:T(8,128)(2,1)S(1)}, bf16[224,1024]{1,0:T(8,128)(2,1)S(1)}, f32[1,1024]{1,0:T(1,128)S(1)}) custom-call(f32[16]{0:T(128)} %rx_ref.5, f32[16]{0:T(128)} %ry_ref.3, f32[16]{0:T(128)} %skip_ref.1, bf16[1024,2048]{1,0:T(8,128)(2,1)} %w_hbm.3, bf16[256,1024]{1,0:T(8,128)(2,1)S(1)} %get-tuple-element.26.v_ref, ...), custom_call_target="tpu_custom_call" | custom-call | tf_op jit(solution)/shard_map/home/pallas_call | solution.py:285
  18.3 0.0 copy-start.1
  18.3 0.8 %copy-done.1 = bf16[224,1024]{1,0:T(8,128)(2,1)} copy-done((bf16[224,1024]{1,0:T(8,128)(2,1)}, bf16[224,1024]{1,0:T(8,128)(2,1)S(1)}, u32[]{:S(2)}) %copy-start.1) | copy-done | bytes 458776
  19.1 0.0 copy-start
  19.1 2.6 %all-to-all-done.pay_ref = bf16[8,296,128]{2,1,0:T(8,128)(2,1)S(1)} async-done(((bf16[8,296,128]{2,1,0:T(8,128)(2,1)}), bf16[8,296,128]{2,1,0:T(8,128)(2,1)S(1)}, u32[]{:S(2)}, u32[]{:S(2)}) %all-to-all-start) | async-done | bytes 606240 | tf_op jit(solution)/shard_map/all_to_all | solution.py:548
  21.7 0.0 copy-start.2
  21.7 2.6 %edges.1 = (bf16[16,64,512]{2,1,0:T(8,128)(2,1)S(1)}, f32[16,128]{1,0:T(8,128)S(1)}, bf16[2,64,512]{2,1,0:T(8,128)(2,1)S(1)}) custom-call(f32[16]{0:T(128)} %rx_ref.5, bf16[8,296,128]{2,1,0:T(8,128)(2,1)S(1)} %all-to-all-done.pay_ref, bf16[256,256]{1,0:T(8,128)(2,1)} %constant.38.clone.from1_ref, bf16[32,256]{1,0:T(8,128)(2,1)} %constant.40.clone.side1_ref, ...), custom_call_target="tpu_custom_call" | custom-call | tf_op jit(solution)/shard_map/edges/pallas_call | solution.py:430
  24.3 4.5 %collective-permute-start = (bf16[2,64,512]{2,1,0:T(8,128)(2,1)S(1)}, bf16[2,64,512]{2,1,0:T(8,128)(2,1)S(1)}, u32[]{:S(2)}, u32[]{:S(2)}) collective-permute-start(bf16[2,64,512]{2,1,0:T(8,128)(2,1)S(1)} %get-tuple-element.35), channel_id=1, source_target_pairs={{0,8},{1,9},{2,10},{3,11},{4,12},{5,13},{6,14},{7,15},{16,24},{17,... | collective-permute-start | bytes 393224 | tf_op jit(solution)/shard_map/ppermute | solution.py:455
  28.8 2.2 %maps.1 = (bf16[16,32,256]{2,1,0:T(8,128)(2,1)S(1)}, f32[16,256]{1,0:T(8,128)S(1)}, bf16[16,32,128]{2,1,0:T(8,128)(2,1)S(1)}, f32[16,64,128]{2,1,0:T(8,128)S(1)}) custom-call(f32[16]{0:T(128)} %rx_ref.5, f32[16]{0:T(128)} %ry_ref.3, bf16[8,296,128]{2,1,0:T(8,128)(2,1)S(1)} %all-to-all-done.pay_ref, bf16[256,256]{1,0:T(8,128)(2,1)} %constant.36.clone.to1_ref, ...), custom_call_target="tpu_custom_call" | custom-call | tf_op jit(solution)/shard_map/maps/pallas_call | solution.py:430
  31.0 0.3 collective-permute-done.entry_ref
  31.3 1.6 %join.1 = (bf16[16,64,512]{2,1,0:T(8,128)(2,1)S(1)}, bf16[16,64,128]{2,1,0:T(8,128)(2,1)S(1)}) custom-call(bf16[16,64,512]{2,1,0:T(8,128)(2,1)S(1)} %get-tuple-element.33.edge_ref, f32[16,128]{1,0:T(8,128)S(1)} %get-tuple-element.34.upto_ref, bf16[2,64,512]{2,1,0:T(8,128)(2,1)S(1)} %collective-permute-done.entry_ref, ...), custom_call_target="tpu_custom_call" | custom-call | tf_op jit(solution)/shard_map/join/pallas_call | solution.py:430
  32.9 1.3 %collective-permute-start.1 = (bf16[16,64,128]{2,1,0:T(8,128)(2,1)S(1)}, bf16[16,64,128]{2,1,0:T(8,128)(2,1)S(1)}, u32[]{:S(2)}, u32[]{:S(2)}) collective-permute-start(bf16[16,64,128]{2,1,0:T(8,128)(2,1)S(1)} %get-tuple-element.39), channel_id=1, source_target_pairs={{0,16},{1,17},{2,18},{3,19},{4,20},{5,21},{6,22},{7,23},{8,24},{9,... | collective-permute-start | bytes 786440 | tf_op jit(solution)/shard_map/ppermute | solution.py:488
  34.2 1.1 %collective-permute-done.1.top_ref = bf16[16,64,128]{2,1,0:T(8,128)(2,1)S(1)} collective-permute-done((bf16[16,64,128]{2,1,0:T(8,128)(2,1)S(1)}, bf16[16,64,128]{2,1,0:T(8,128)(2,1)S(1)}, u32[]{:S(2)}, u32[]{:S(2)}) %collective-permute-start.1) | collective-permute-done | bytes 262176 | tf_op jit(solution)/shard_map/ppermute | solution.py:488
  35.3 1.8 %cells.1 = bf16[8,224,128]{2,1,0:T(8,128)(2,1)S(1)} custom-call(bf16[8,296,128]{2,1,0:T(8,128)(2,1)S(1)} %all-to-all-done.pay_ref, bf16[16,64,512]{2,1,0:T(8,128)(2,1)S(1)} %get-tuple-element.38.edge_ref, bf16[16,64,128]{2,1,0:T(8,128)(2,1)S(1)} %collective-permute-done.1.top_ref, bf16[16,32,256]{2,1,0:T(8,128)(2,1)S(1)} %get-tuple-element.40.side_ref, ...), custom_call_target="tpu_custom_call" | custom-call | tf_op jit(solution)/shard_map/cells/pallas_call | solution.py:430
  37.1 15.5 %all_to_all.10.y_ref = bf16[8,224,128]{2,1,0:T(8,128)(2,1)S(1)} all-to-all(bf16[8,224,128]{2,1,0:T(8,128)(2,1)S(1)} %cells.1), channel_id=1, replica_groups={{0,1,2,3,4,5,6,7},{8,9,10,11,12,13,14,15},{16,17,18,19,20,21,22,23},{24..., dimensions={0} | all-to-all | bytes 917504 | tf_op jit(solution)/shard_map/all_to_all | solution.py:553
  52.6 0.0 copy-done
  52.6 0.0 copy-done.2
  52.6 1.9 %finish.1 = bf16[28,7,1024]{2,1,0:T(8,128)(2,1)} custom-call(bf16[8,224,128]{2,1,0:T(8,128)(2,1)S(1)} %all_to_all.10.y_ref, bf16[224,1024]{1,0:T(8,128)(2,1)S(1)} %get-tuple-element.42.own_ref, bf16[224,1024]{1,0:T(8,128)(2,1)S(1)} %copy-done.2, f32[1,1024]{1,0:T(1,128)S(1)} %get-tuple-element.44.gain_ref, bf16[1024,1024]{1,0:T(8,128)(2,1)S(1)} %copy-done), custom_call_target="tpu_custom_call" | custom-call | tf_op jit(solution)/shard_map/finish/pallas_call | solution.py:430
Async XLA Ops:
  5.6 16.1 %all-to-all-start = ((bf16[8,296,128]{2,1,0:T(8,128)(2,1)}), bf16[8,296,128]{2,1,0:T(8,128)(2,1)S(1)}, u32[]{:S(2)}, u32[]{:S(2)}) async-start(bf16[8,296,128]{2,1,0:T(8,128)(2,1)} %get-tuple-element.25), calls=%async_computation | async-start | bytes 1212416 | tf_op jit(solution)/shard_map/all_to_all | solution.py:548
  18.3 0.8 %copy-start.1 = (bf16[224,1024]{1,0:T(8,128)(2,1)}, bf16[224,1024]{1,0:T(8,128)(2,1)S(1)}, u32[]{:S(2)}) copy-start(bf16[224,1024]{1,0:T(8,128)(2,1)S(1)} %get-tuple-element.43.gate_ref) | copy-start | bytes 1376260
  19.1 33.5 %copy-start = (bf16[1024,1024]{1,0:T(8,128)(2,1)S(1)}, bf16[1024,1024]{1,0:T(8,128)(2,1)}, u32[]{:S(2)}) copy-start(bf16[1024,1024]{1,0:T(8,128)(2,1)} %w_ref.1) | copy-start | bytes 6291460
  21.7 30.9 %copy-start.2 = (bf16[224,1024]{1,0:T(8,128)(2,1)S(1)}, bf16[224,1024]{1,0:T(8,128)(2,1)}, u32[]{:S(2)}) copy-start(bf16[224,1024]{1,0:T(8,128)(2,1)} %copy-done.1) | copy-start | bytes 1376260
  24.3 7.0 %collective-permute-start = (bf16[2,64,512]{2,1,0:T(8,128)(2,1)S(1)}, bf16[2,64,512]{2,1,0:T(8,128)(2,1)S(1)}, u32[]{:S(2)}, u32[]{:S(2)}) collective-permute-start(bf16[2,64,512]{2,1,0:T(8,128)(2,1)S(1)} %get-tuple-element.35), channel_id=1, source_target_pairs={{0,8},{1,9},{2,10},{3,11},{4,12},{5,13},{6,14},{7,15},{16,24},{17,... | collective-permute-start | bytes 393224 | tf_op jit(solution)/shard_map/ppermute | solution.py:455
  32.9 2.4 %collective-permute-start.1 = (bf16[16,64,128]{2,1,0:T(8,128)(2,1)S(1)}, bf16[16,64,128]{2,1,0:T(8,128)(2,1)S(1)}, u32[]{:S(2)}, u32[]{:S(2)}) collective-permute-start(bf16[16,64,128]{2,1,0:T(8,128)(2,1)S(1)} %get-tuple-element.39), channel_id=1, source_target_pairs={{0,16},{1,17},{2,18},{3,19},{4,20},{5,21},{6,22},{7,23},{8,24},{9,... | collective-permute-start | bytes 786440 | tf_op jit(solution)/shard_map/ppermute | solution.py:488

commit v5 on v4

--- a/solution.py
+++ b/solution.py
@@ -50,8 +50,7 @@
         self.upper = -(-rows // 2)
         self.half = round_up(self.upper * self.col_pad, 8)
         self.cells = rows * self.col_pad
-        self.row_pad = 32
-        self.edge = states * self.row_pad
+        self.edge = rows * states
         self.top = states * self.col_pad
         self.bc = 2 * states
         self.at_bc = self.slots * self.half
@@ -59,8 +58,8 @@
         self.message = round_up(self.at_dt + 2 * self.slots, 8)
         assert self.head_width % self.slot == 0 and self.group % self.slot == 0
         assert LANES % self.head_width == 0 and self.half <= LANES
-        assert rows <= self.row_pad and self.cells - self.half <= self.half
-        assert states % 16 == 0 and self.edge % LANES == 0 and heads % 8 == 0
+        assert self.cells - self.half <= self.half
+        assert states % 16 == 0 and heads % 8 == 0
 
     def segments(self):
         return [list(range(p * self.devices, (p + 1) * self.devices)) for p in range(self.parts)]
@@ -78,10 +77,8 @@
         cell = np.arange(self.cells)
         ci, cj = cell // self.col_pad, cell % self.col_pad
         creal = cj < self.cols
-        le = np.arange(self.row_pad)
+        le = np.arange(round_up(self.rows, 8))
         lj = np.arange(self.col_pad)
-        n = np.arange(self.states)
-        edge = np.tile(le, LANES // self.row_pad)
         out = {}
         out["to1"] = (j[:, None] <= j[None]) & both
         out["to2"] = (j[:, None] == j[None]) & (i[:, None] <= i[None]) & both
@@ -93,11 +90,9 @@
         out["down1"] = (j[None] <= lj[:, None]) & real[None]
         out["down2"] = (j[None] == lj[:, None]) & real[None]
         out["downmask"] = (j[None] <= lj[:, None]) & (lj < self.cols)[:, None] & real[None]
-        out["keep"] = (i[:, None] == edge[None]) & real[:, None]
         out["pick"] = (
             (i == self.rows - 1)[:, None] & real[:, None] & (j[:, None] == np.tile(lj, self.states)[None])
         )
-        out["diag"] = np.repeat(n, self.row_pad)[:, None] == np.repeat(n, self.col_pad)[None]
         cboth = creal[:, None] & real[None]
         out["own1"] = (j[None] <= cj[:, None]) & cboth
         out["own2"] = (j[None] == cj[:, None]) & (i[None] <= ci[:, None]) & cboth
@@ -126,32 +121,38 @@
 
 
 def project_kernel(
-    plan, chunks, bias_ref, x_hbm, w_hbm, wt_ref, t_ref, lanei_ref, lanej_ref,
-    v_ref, pay_ref, rows_ref, flat_ref, x_ref, w_ref, wide, x_sem, w_sems,
+    plan, chunks, bias_hbm, x_hbm, w_hbm, wt_hbm, t_hbm, lanei_hbm, lanej_hbm,
+    v_ref, pay_hbm, rows_ref, flat_ref,
+    bias_ref, x_ref, w_ref, wt_ref, t_ref, lanei_ref, lanej_ref, pay_ref, wide, sems, w_sems, out_sems,
 ):
     group, states, cells, heads = plan.group, plan.states, plan.cells, plan.heads
     half, rest = plan.half, plan.cells - plan.half
     tile = plan.width // chunks
-    x_copy = pltpu.make_async_copy(x_hbm, x_ref, x_sem)
-    x_copy.start()
+    pairs = (
+        (x_hbm, x_ref), (t_hbm, t_ref), (wt_hbm, wt_ref), (lanei_hbm, lanei_ref), (lanej_hbm, lanej_ref),
+        (bias_hbm, bias_ref),
+    )
+    loads = [pltpu.make_async_copy(a, b, sems.at[k]) for k, (a, b) in enumerate(pairs)]
     copies = [
         pltpu.make_async_copy(w_hbm.at[:, k * tile : (k + 1) * tile], w_ref.at[k], w_sems.at[k])
         for k in range(chunks)
     ]
-    for copy in copies:
+    for copy in loads + copies:
         copy.start()
-    keep = cell_mask_of(plan, t_ref)
-    t = t_ref[...].astype(F32).astype(BF16)
-    m = jnp.sum(mm(t, lanei_ref[...]) * lanej_ref[...].astype(F32), axis=0, keepdims=True)
     wide[...] = jnp.zeros_like(wide)
     v_ref[half:LANES, :] = jnp.zeros((LANES - half, plan.width), BF16)
     v_ref[LANES + rest :, :] = jnp.zeros((LANES - rest, plan.width), BF16)
 
-    x_copy.wait()
+    loads[0].wait()
     for i in range(plan.rows):
         wide[i * plan.col_pad : i * plan.col_pad + plan.cols, :] = x_ref[i].astype(F32)
     x = wide[...].astype(BF16)
     flat_ref[...] = x
+    for copy in loads[1:]:
+        copy.wait()
+    keep = cell_mask_of(plan, t_ref)
+    t = t_ref[...].astype(F32).astype(BF16)
+    m = jnp.sum(mm(t, lanei_ref[...]) * lanej_ref[...].astype(F32), axis=0, keepdims=True)
     table = nt_dot(wt_ref[...], x)
     ext = jnp.concatenate([table, jnp.zeros((table.shape[0], 2 * LANES - cells), F32)], axis=1)
     lane = lax.broadcasted_iota(jnp.int32, (table.shape[0], LANES), 1)
@@ -175,14 +176,16 @@
     steps = rows_ref[2 * states :, :]
 
     lane = lax.broadcasted_iota(jnp.int32, (half, LANES), 1)
+    sent = []
     for chunk in range(chunks):
         copies[chunk].wait()
         v = mm(flat_ref[...], w_ref[chunk]).astype(BF16).astype(F32) * keep
         low = v.astype(BF16)
         v_ref[0:half, chunk * tile : (chunk + 1) * tile] = low[:half]
         v_ref[LANES : LANES + rest, chunk * tile : (chunk + 1) * tile] = low[half:]
-        for k in range(tile // group):
-            dest = chunk * (tile // group) + k
+        per = tile // group
+        for k in range(per):
+            dest = chunk * per + k
             dts = []
             for s in range(plan.slots):
                 offset = k * group + s * plan.slot
@@ -207,37 +210,46 @@
             spare = plan.message - plan.at_dt - len(dts)
             dts += [jnp.zeros((spare, LANES), F32)] if spare else []
             pay_ref[dest, plan.at_dt : plan.message, :] = jnp.concatenate(dts, axis=0).astype(BF16)
+        at = slice(chunk * per, (chunk + 1) * per)
+        sent.append(pltpu.make_async_copy(pay_ref.at[at], pay_hbm.at[at], out_sems.at[chunk]))
+        sent[-1].start()
+    for copy in sent:
+        copy.wait()
 
 
 def project(plan, consts, slide, w_in, w_bcd, tissue, dt_bias):
     chunks = 4
     tile = plan.width // chunks
     depth = slide.shape[2]
-    args = [in_hbm(w_bcd.T), in_hbm(tissue.T), consts["lanei"], consts["lanej"]]
+    args = [dt_bias, slide, w_in, w_bcd.T, tissue.T, consts["lanei"], consts["lanej"]]
     count = 2 * plan.states + plan.heads
     assert plan.width % chunks == 0 and tile % plan.group == 0 and tile % LANES == 0
-    outs = [
-        ((2 * LANES, plan.width), BF16),
-        ((plan.devices, plan.message, LANES), BF16),
-        ((count, 2 * LANES), F32),
-        ((plan.cells, depth), BF16),
-    ]
+    message = (plan.devices, plan.message, LANES)
+    outs = [((2 * LANES, plan.width), BF16), (message, BF16), ((count, 2 * LANES), F32), ((plan.cells, depth), BF16)]
+    specs = [full(s) for s, _ in outs]
+    specs[1] = HBM
     return pl.pallas_call(
         functools.partial(project_kernel, plan, chunks),
         grid=(1,),
-        in_specs=[SMEM, HBM, HBM] + [full(x.shape) for x in args],
-        out_specs=[full(s) for s, _ in outs],
+        in_specs=[HBM] * len(args),
+        out_specs=specs,
         out_shape=[jax.ShapeDtypeStruct(s, d) for s, d in outs],
         scratch_shapes=[
+            pltpu.SMEM(dt_bias.shape, F32),
             pltpu.VMEM(slide.shape, BF16),
             pltpu.VMEM((chunks, depth, tile), BF16),
+        ]
+        + [pltpu.VMEM(x.shape, x.dtype) for x in args[3:]]
+        + [
+            pltpu.VMEM(message, BF16),
             pltpu.VMEM((plan.cells, depth), F32),
-            pltpu.SemaphoreType.DMA,
+            pltpu.SemaphoreType.DMA((6,)),
+            pltpu.SemaphoreType.DMA((chunks,)),
             pltpu.SemaphoreType.DMA((chunks,)),
         ],
         compiler_params=pltpu.CompilerParams(vmem_limit_bytes=24 * 2**20),
         name="project",
-    )(in_hbm(dt_bias), in_hbm(slide), in_hbm(w_in), *args)
+    )(*[in_hbm(x) for x in args])
 
 
 def home_kernel(
@@ -279,13 +291,13 @@
 
 
 def home(plan, consts, v, rows, flat, w_in, tissue, gain, rate_x, rate_y, d_skip):
-    maps = [consts[k] for k in ("own1", "own2", "from1", "from2", "ownmask")]
-    args = [v, rows, flat, in_hbm(tissue.T), in_hbm(gain)] + maps
+    args = [in_hbm(w_in), v, rows, flat, in_hbm(tissue.T), in_hbm(gain)]
+    args += [consts[k] for k in ("own1", "own2", "from1", "from2", "ownmask")]
     outs = [((plan.cells, plan.width), BF16), ((plan.cells, plan.width), BF16), (gain.shape, F32)]
     return pl.pallas_call(
         functools.partial(home_kernel, plan),
         grid=(1,),
-        in_specs=[SMEM, SMEM, SMEM, HBM] + [full(x.shape) for x in args],
+        in_specs=[SMEM, SMEM, SMEM, HBM] + [full(x.shape) for x in args[1:]],
         out_specs=[full(s) for s, _ in outs],
         out_shape=[jax.ShapeDtypeStruct(s, d) for s, d in outs],
         scratch_shapes=[
@@ -295,7 +307,21 @@
         ],
         compiler_params=pltpu.CompilerParams(vmem_limit_bytes=24 * 2**20),
         name="home",
-    )(in_hbm(rate_x), in_hbm(rate_y), in_hbm(d_skip), in_hbm(w_in), *args)
+    )(in_hbm(rate_x), in_hbm(rate_y), in_hbm(d_skip), *args)
+
+
+def ones(mask):
+    return jnp.where(mask, 1.0, 0.0).astype(BF16)
+
+
+def places(plan, shape, axis):
+    at = lax.broadcasted_iota(jnp.int32, shape, axis)
+    late = at >= LANES
+    at = jnp.where(late, at - LANES, at)
+    i = lax.div(at, plan.col_pad)
+    j = at - i * plan.col_pad
+    real = (at < jnp.where(late, plan.cells - plan.half, plan.half)) & (j < plan.cols)
+    return jnp.where(late, i + plan.upper, i), j, real
 
 
 def my_head(plan, axis, slot):
@@ -313,10 +339,6 @@
         v = jnp.concatenate([v, jnp.zeros((LANES - plan.half, LANES), F32)], axis=0)
     v = v.T
     return jnp.concatenate([v[:HALF], v[HALF:]], axis=1).astype(BF16)
-
-
-def repeat_lanes(row, count):
-    return jnp.concatenate([row] * count, axis=1)
 
 
 def load_steps(plan, pay_ref, dts):
@@ -328,39 +350,46 @@
             dts[w : w + 1, LANES:] = rows[2 * s + 1 : 2 * s + 2]
 
 
-def slot_rates(plan, axis, ref, shape):
-    rate = jnp.full(shape, ref[my_head(plan, axis, 0)], F32)
-    at = lax.broadcasted_iota(jnp.int32, shape, 0)
+def slot_rates(plan, axis, rate_ref):
+    at = lax.broadcasted_iota(jnp.int32, (plan.work, 1), 0)
+    rate = jnp.full((plan.work, 1), rate_ref[my_head(plan, axis, 0)], F32)
     for s in range(1, plan.slots):
-        rate = jnp.where(at >= s * (shape[0] // plan.slots), ref[my_head(plan, axis, s)], rate)
+        rate = jnp.where(at >= s * plan.devices, rate_ref[my_head(plan, axis, s)], rate)
     return rate
 
 
-def edges_kernel(
-    plan, axis, rx_ref, pay_ref, from1_ref, side1_ref, keep_ref, edge_ref, upto_ref, last_ref,
-    dts, inner, kept,
-):
-    states, tiles = plan.states, plan.devices
+def edges_kernel(plan, axis, rx_hbm, pay_ref, edge_ref, upto_ref, last_ref, rx_ref, dts, inner, kept, sem):
+    states, tiles, wide = plan.states, plan.devices, 2 * LANES
+    copy = pltpu.make_async_copy(rx_hbm, rx_ref, sem)
+    copy.start()
     load_steps(plan, pay_ref, dts)
+    i, j, real = places(plan, (wide, wide), 0)
+    ti, tj, treal = places(plan, (wide, wide), 1)
+    from1 = ones((i == ti) & (j > tj) & real & treal)
+    edge_row = lax.div(lax.broadcasted_iota(jnp.int32, (wide, plan.edge), 1), states)
+    i, _, real = places(plan, (wide, plan.edge), 0)
+    keep = ones((i == edge_row) & real)
+    ti, _, treal = places(plan, (plan.rows, wide), 1)
+    rowsel = ones((ti == lax.broadcasted_iota(jnp.int32, (plan.rows, wide), 0)) & treal)
     dt = dts[...]
     low = dt.astype(BF16)
-    rate = slot_rates(plan, axis, rx_ref, (plan.work, 2 * LANES))
-    inner[...] = jnp.exp(-rate * mm(low, from1_ref[...])) * dt
-    kept[...] = jnp.exp(-rate[:, :LANES] * mm(low, keep_ref[...]))
-    rowsel = side1_ref[...]
-    width = plan.edge // LANES
+    inside, across = mm(low, from1), mm(low, keep)
+    copy.wait()
+    rate = slot_rates(plan, axis, rx_ref)
+    inner[...] = jnp.exp(-rate * inside) * dt
+    kept[...] = jnp.exp(-rate * across)
     for s in range(plan.slots):
         held = jnp.zeros((HALF, plan.edge), F32)
-        product = jnp.ones((1, LANES), F32)
+        product = jnp.ones((1, plan.edge), F32)
         for t in range(tiles):
             w = s * tiles + t
             b = wide_rows(pay_ref, t, plan.at_bc, states, plan.bc).astype(F32)
             bd = (b * inner[w : w + 1, :]).astype(BF16)
-            left = jnp.concatenate([rowsel * bd[n : n + 1] for n in range(states)], axis=0)
+            left = jnp.concatenate([bd * rowsel[i : i + 1] for i in range(plan.rows)], axis=0)
             edge_ref[w] = held.astype(BF16)
             upto_ref[w : w + 1, :] = product
             now = kept[w : w + 1, :]
-            held = held * repeat_lanes(now, width) + nt_dot(turned(plan, pay_ref, t, s), left)
+            held = held * now + nt_dot(turned(plan, pay_ref, t, s), left)
             product = product * now
         last_ref[s] = held.astype(BF16)
 
@@ -368,57 +397,64 @@
 def maps_kernel(
     plan, axis, rx_ref, ry_ref, pay_ref, to1_ref, to2_ref, from1_ref, from2_ref, side1_ref, side2_ref,
     sidemask_ref, down1_ref, down2_ref, downmask_ref, pick_ref,
-    side_ref, above_ref, bottom_ref, top_ref, dts, s1, s2, d1, d2, down,
+    side_ref, above_ref, bottom_ref, top_ref, dts, s1, s2, d1, d2,
 ):
-    states, tiles, rp, cp, work = plan.states, plan.devices, plan.row_pad, plan.col_pad, plan.work
+    states, tiles, cp, work = plan.states, plan.devices, plan.col_pad, plan.work
+    rp = side1_ref.shape[0]
     load_steps(plan, pay_ref, dts)
     low = dts[...].astype(BF16)
-    rate_y = slot_rates(plan, axis, ry_ref, (work, 2 * LANES))
-    above_ref[...] = jnp.exp(-rate_y * mm(low, to2_ref[...]))
+    above_ref[...] = jnp.exp(-slot_rates(plan, axis, ry_ref) * mm(low, to2_ref[...]))
     for w in range(work):
-        row = low[w : w + 1]
-        s1[w * rp : (w + 1) * rp, :] = side1_ref[...] * row
-        s2[w * rp : (w + 1) * rp, :] = side2_ref[...] * row
         rf = dts[w : w + 1, :]
+        s1[w * rp : (w + 1) * rp, :] = side1_ref[...].astype(F32) * rf
+        s2[w * rp : (w + 1) * rp, :] = side2_ref[...].astype(F32) * rf
         d1[w * cp : (w + 1) * cp, :] = down1_ref[...].astype(F32) * rf
         d2[w * cp : (w + 1) * cp, :] = down2_ref[...].astype(F32) * rf
     mask = sidemask_ref[...].astype(F32)
-    x, y = mm(s1[...], to1_ref[...]), mm(s2[...], to2_ref[...])
+    x, y = mm(s1[...].astype(BF16), to1_ref[...]), mm(s2[...].astype(BF16), to2_ref[...])
     for w in range(work):
         head = my_head(plan, axis, w // tiles)
+        rx, ry = rx_ref[head], ry_ref[head]
         at = slice(w * rp, (w + 1) * rp)
-        side_ref[w] = (jnp.exp(-(rx_ref[head] * x[at] + ry_ref[head] * y[at])) * mask).astype(BF16)
-        bottom_ref[w] = mm(side_ref[w], pick_ref[...]).astype(BF16)
+        side = (jnp.exp(-(rx * x[at] + ry * y[at])) * mask).astype(BF16)
+        side_ref[w] = side
+        bottom_ref[w] = mm(side, pick_ref[...]).astype(BF16)
     x, y = mm(d1[...].astype(BF16), from1_ref[...]), mm(d2[...].astype(BF16), from2_ref[...])
     mask = downmask_ref[...].astype(F32)
     for w in range(work):
-        head = my_head(plan, axis, w // tiles)
+        s, t = w // tiles, w % tiles
+        head = my_head(plan, axis, s)
+        rx, ry = rx_ref[head], ry_ref[head]
         at = slice(w * cp, (w + 1) * cp)
-        fall = jnp.exp(-(rx_ref[head] * x[at] + ry_ref[head] * y[at])) * mask * dts[w : w + 1, :]
-        b = wide_rows(pay_ref, w % tiles, plan.at_bc, states, plan.bc).astype(F32)
+        fall = jnp.exp(-(rx * x[at] + ry * y[at])) * mask * dts[w : w + 1, :]
+        b = wide_rows(pay_ref, t, plan.at_bc, states, plan.bc).astype(F32)
         falls = jnp.concatenate([fall * b[n : n + 1] for n in range(states)], axis=0).astype(BF16)
-        top_ref[w] = nt_dot(turned(plan, pay_ref, w % tiles, w // tiles), falls)
-
-
-def join_kernel(plan, edge_ref, upto_ref, entry_ref, bottom_ref, top_ref, diag_ref, whole_ref, out_ref):
-    width = plan.edge // LANES
+        top_ref[w] = nt_dot(turned(plan, pay_ref, t, s), falls)
+
+
+def join_kernel(plan, edge_ref, upto_ref, entry_ref, bottom_ref, top_ref, whole_ref, out_ref):
+    shape = (plan.states, plan.top)
+    n = lax.broadcasted_iota(jnp.int32, shape, 0)
+    diag = ones(n == lax.div(lax.broadcasted_iota(jnp.int32, shape, 1), plan.col_pad))
     for w in range(plan.work):
         entry = entry_ref[w // plan.devices].astype(F32)
-        whole = edge_ref[w].astype(F32) + entry * repeat_lanes(upto_ref[w : w + 1, :], width)
-        whole = whole.astype(BF16)
+        whole = (edge_ref[w].astype(F32) + entry * upto_ref[w : w + 1, :]).astype(BF16)
         whole_ref[w] = whole
-        passed = jnp.concatenate([bottom_ref[w]] * plan.states, axis=0) * diag_ref[...]
+        bottom = bottom_ref[w]
+        passed = jnp.concatenate([diag * bottom[i : i + 1] for i in range(plan.rows)], axis=0)
         out_ref[w] = (top_ref[w] + mm(whole, passed)).astype(BF16)
 
 
-def cells_kernel(plan, pay_ref, edge_ref, top_ref, side_ref, above_ref, colsel_ref, out_ref):
+def cells_kernel(plan, pay_ref, edge_ref, top_ref, side_ref, above_ref, out_ref):
     states, tiles = plan.states, plan.devices
-    colsel = colsel_ref[...].astype(F32)
+    shape = (plan.col_pad, 2 * LANES)
+    _, tj, treal = places(plan, shape, 1)
+    colsel = jnp.where((tj == lax.broadcasted_iota(jnp.int32, shape, 0)) & treal, 1.0, 0.0)
     for w in range(plan.work):
         t, s = w % tiles, w // tiles
         c = wide_rows(pay_ref, t, plan.at_bc + states, states, plan.bc)
         side = side_ref[w]
-        left = jnp.concatenate([side * c[n : n + 1] for n in range(states)], axis=0)
+        left = jnp.concatenate([c * side[i : i + 1] for i in range(plan.rows)], axis=0)
         ca = c.astype(F32) * above_ref[w : w + 1, :]
         down = jnp.concatenate([colsel * ca[n : n + 1] for n in range(states)], axis=0).astype(BF16)
         y = mm(edge_ref[w], left) + mm(top_ref[w], down)
@@ -426,29 +462,37 @@
         out_ref[t, s * plan.half : (s + 1) * plan.half, :] = y[: plan.half].astype(BF16)
 
 
-def call(kernel, name, smem, args, outs, scratch=(), mib=24):
+def call(kernel, name, args, outs, scratch=(), specs=()):
+    specs = list(specs) + [full(x.shape) for x in args[len(specs) :]]
     return pl.pallas_call(
         kernel,
         grid=(1,),
-        in_specs=[SMEM] * len(smem) + [full(x.shape) for x in args],
+        in_specs=specs,
         out_specs=[full(s) for s, _ in outs],
         out_shape=[jax.ShapeDtypeStruct(s, d) for s, d in outs],
-        scratch_shapes=[pltpu.VMEM(s, d) for s, d in scratch],
-        compiler_params=pltpu.CompilerParams(vmem_limit_bytes=mib * 2**20),
+        scratch_shapes=[x if not isinstance(x, tuple) else pltpu.VMEM(*x) for x in scratch],
+        compiler_params=pltpu.CompilerParams(vmem_limit_bytes=24 * 2**20),
         name=name,
-    )(*[in_hbm(x) for x in smem], *args)
+    )(*args)
 
 
 def scan_calls(plan, consts, row_axis, col_axis, pay, rate_x, rate_y):
-    work, rp, cp, wide = plan.work, plan.row_pad, plan.col_pad, 2 * LANES
-    names = ("from1", "side1", "keep")
+    work, cp, wide = plan.work, plan.col_pad, 2 * LANES
+    rp = consts["side1"].shape[0]
+    rate_x, rate_y = in_hbm(rate_x), in_hbm(rate_y)
     edges, upto, last = call(
         functools.partial(edges_kernel, plan, col_axis),
         "edges",
-        [rate_x],
-        [pay] + [consts[k] for k in names],
-        [((work, HALF, plan.edge), BF16), ((work, LANES), F32), ((plan.slots, HALF, plan.edge), BF16)],
-        [((work, wide), F32), ((work, wide), F32), ((work, LANES), F32)],
+        [rate_x, pay],
+        [((work, HALF, plan.edge), BF16), ((work, plan.edge), F32), ((plan.slots, HALF, plan.edge), BF16)],
+        [
+            pltpu.SMEM(rate_x.shape, F32),
+            ((work, wide), F32),
+            ((work, wide), F32),
+            ((work, plan.edge), F32),
+            pltpu.SemaphoreType.DMA,
+        ],
+        [HBM],
     )
     if plan.parts > 1:
         hops = [(k, k + plan.devices) for k in range(plan.devices)]
@@ -459,28 +503,20 @@
     side, above, bottom, tops = call(
         functools.partial(maps_kernel, plan, col_axis),
         "maps",
-        [rate_x, rate_y],
-        [pay] + [consts[k] for k in names],
+        [rate_x, rate_y, pay] + [consts[k] for k in names],
         [
             ((work, rp, wide), BF16),
             ((work, wide), F32),
             ((work, rp, LANES), BF16),
             ((work, HALF, plan.top), F32),
         ],
-        [
-            ((work, wide), F32),
-            ((work * rp, wide), BF16),
-            ((work * rp, wide), BF16),
-            ((work * cp, wide), F32),
-            ((work * cp, wide), F32),
-            ((work * cp, wide), F32),
-        ],
+        [((work, wide), F32)] + [((work * rp, wide), F32)] * 2 + [((work * cp, wide), F32)] * 2,
+        [SMEM, SMEM],
     )
     edges, tops = call(
         functools.partial(join_kernel, plan),
         "join",
-        [],
-        [edges, upto, entry, bottom, tops, consts["diag"]],
+        [edges, upto, entry, bottom, tops],
         [((work, HALF, plan.edge), BF16), ((work, HALF, plan.top), BF16)],
     )
     count = lax.axis_size(row_axis)
@@ -495,8 +531,7 @@
     return call(
         functools.partial(cells_kernel, plan),
         "cells",
-        [],
-        [pay, edges, entry, side, above, consts["down2"]],
+        [pay, edges, entry, side, above],
         [((plan.devices, plan.slots * plan.half, LANES), BF16)],
     )[0]
 
@@ -532,7 +567,7 @@
     shape = (plan.rows, plan.cols, w_out.shape[1])
     assert w_out.shape[1] == plan.width
     return call(
-        functools.partial(finish_kernel, plan), "finish", [], args, [(shape, BF16)], [((plan.cells, plan.width), F32)]
+        functools.partial(finish_kernel, plan), "finish", args, [(shape, BF16)], [((plan.cells, plan.width), F32)]
     )[0]
 
 

time: 55 us -> 51.4 us (0.935)
  Pallas kernels: 22.1 us -> 18.5 us
    pallas_call x5, Pallas kernels: 10 us -> 7.8 us  [call(): pl.pallas_call(kernel, grid=(1,), in_specs=specs, out_specs=[full(s) for...]
    pallas_call x1, Pallas kernels: 5.62 us -> 4.26 us  [project(): pl.pallas_call(functools.partial(project_kernel, plan, chunks), grid=(1,)...]
  transfers between devices with their start and end apart: 3 -> 3, of which waited for: 3 -> 3; matrix products, arithmetic and copies ran while one was open for 0% -> 0% of each run, Pallas kernels for 16% -> 17%
where the time goes in v5:
time: 51.4 us; the launch traced here: 51 us
  Pallas kernels  18.5 us (36%)
  blocking collectives  15.5 us (30%)
  starting transfers between devices  12 us (23%)
  waiting for transfers between devices  4.1 us (8%)
  local copies, waits for them, and re-layouts  0.77 us (1%)
    all_to_all x1, blocking collectives, per_device(): y = lax.all_to_all(y, 'col', 0, 0, tiled=True, axis_index_groups=groups)  15.5 us
    pallas_call x5, Pallas kernels, call(): pl.pallas_call(kernel, grid=(1,), in_specs=specs, out_specs=[full(s) for...  7.8 us
    pallas_call x1, Pallas kernels, home(): pl.pallas_call(functools.partial(home_kernel, plan), grid=(1,), in_specs=...  6.47 us
    all_to_all x1, starting transfers between devices, per_device(): pay = lax.all_to_all(pay, 'col', 0, 0, tiled=True, axis_index_groups=groups)  6.22 us
    ppermute x1, starting transfers between devices, scan_calls(): entry = lax.ppermute(last, col_axis, hops)  4.5 us
    pallas_call x1, Pallas kernels, project(): pl.pallas_call(functools.partial(project_kernel, plan, chunks), grid=(1,)...  4.26 us
    all_to_all x1, waiting for transfers between devices, per_device(): pay = lax.all_to_all(pay, 'col', 0, 0, tiled=True, axis_index_groups=groups)  2.64 us
    ppermute x1, starting transfers between devices, scan_calls(): entry = lax.ppermute(tops, row_axis, chain)  1.31 us
  transfers between devices with their start and end apart: 3, of which 3 were waited for; matrix products, arithmetic and copies ran while one was open for 0% of the time, Pallas kernels for 17%

profile of v5, /device:TPU:0, one launch (start us, length us, event | category | flops | bytes accessed | tf_op | source)
XLA Modules:
  0.0 51.0 jit_solution(3508631406512968699)
XLA Ops:
  0.0 4.3 %project.1 = (bf16[256,1024]{1,0:T(8,128)(2,1)S(1)}, bf16[8,296,128]{2,1,0:T(8,128)(2,1)}, f32[48,256]{1,0:T(8,128)S(1)}, bf16[224,1024]{1,0:T(8,128)(2,1)S(1)}) custom-call(f32[16]{0:T(128)} %bias_hbm.1, bf16[28,7,1024]{2,1,0:T(8,128)(2,1)} %x_hbm.1, bf16[1024,2048]{1,0:T(8,128)(2,1)} %w_hbm.3, bf16[48,1024]{1,0:T(8,128)(2,1)} %bitcast.3, s32[7,28]{1,0:T(8,128)} %bitcast.4, ...), custom_call_target="tpu_custom_call" | custom-call | tf_op jit(solution)/shard_map/project/pallas_call | solution.py:231
  4.3 6.2 %all-to-all-start = ((bf16[8,296,128]{2,1,0:T(8,128)(2,1)}), bf16[8,296,128]{2,1,0:T(8,128)(2,1)S(1)}, u32[]{:S(2)}, u32[]{:S(2)}) async-start(bf16[8,296,128]{2,1,0:T(8,128)(2,1)} %get-tuple-element.25), calls=%async_computation | async-start | bytes 1212416 | tf_op jit(solution)/shard_map/all_to_all | solution.py:583
  10.5 6.5 %home.1 = (bf16[224,1024]{1,0:T(8,128)(2,1)S(1)}, bf16[224,1024]{1,0:T(8,128)(2,1)S(1)}, f32[1,1024]{1,0:T(1,128)S(1)}) custom-call(f32[16]{0:T(128)} %rx_ref.3, f32[16]{0:T(128)} %ry_ref.3, f32[16]{0:T(128)} %skip_ref.1, bf16[1024,2048]{1,0:T(8,128)(2,1)} %w_hbm.3, bf16[256,1024]{1,0:T(8,128)(2,1)S(1)} %get-tuple-element.26.v_ref, ...), custom_call_target="tpu_custom_call" | custom-call | tf_op jit(solution)/shard_map/home/pallas_call | solution.py:297
  17.0 0.0 copy-start.1
  17.0 0.8 %copy-done.1 = bf16[224,1024]{1,0:T(8,128)(2,1)} copy-done((bf16[224,1024]{1,0:T(8,128)(2,1)}, bf16[224,1024]{1,0:T(8,128)(2,1)S(1)}, u32[]{:S(2)}) %copy-start.1) | copy-done | bytes 458776
  17.7 0.0 copy-start
  17.7 2.6 %all-to-all-done.pay_ref = bf16[8,296,128]{2,1,0:T(8,128)(2,1)S(1)} async-done(((bf16[8,296,128]{2,1,0:T(8,128)(2,1)}), bf16[8,296,128]{2,1,0:T(8,128)(2,1)S(1)}, u32[]{:S(2)}, u32[]{:S(2)}) %all-to-all-start) | async-done | bytes 606240 | tf_op jit(solution)/shard_map/all_to_all | solution.py:583
  20.4 0.0 copy-start.2
  20.4 2.0 %edges.1 = (bf16[16,64,448]{2,1,0:T(8,128)(2,1)S(1)}, f32[16,448]{1,0:T(8,128)S(1)}, bf16[2,64,448]{2,1,0:T(8,128)(2,1)S(1)}) custom-call(f32[16]{0:T(128)} %rx_ref.3, bf16[8,296,128]{2,1,0:T(8,128)(2,1)S(1)} %all-to-all-done.pay_ref), custom_call_target="tpu_custom_call" | custom-call | tf_op jit(solution)/shard_map/edges/pallas_call | solution.py:467
  22.4 4.5 %collective-permute-start = (bf16[2,64,448]{2,1,0:T(8,128)(2,1)S(1)}, bf16[2,64,448]{2,1,0:T(8,128)(2,1)S(1)}, u32[]{:S(2)}, u32[]{:S(2)}) collective-permute-start(bf16[2,64,448]{2,1,0:T(8,128)(2,1)S(1)} %get-tuple-element.35), channel_id=1, source_target_pairs={{0,8},{1,9},{2,10},{3,11},{4,12},{5,13},{6,14},{7,15},{16,24},{17,... | collective-permute-start | bytes 344072 | tf_op jit(solution)/shard_map/ppermute | solution.py:499
  26.9 2.2 %maps.1 = (bf16[16,32,256]{2,1,0:T(8,128)(2,1)S(1)}, f32[16,256]{1,0:T(8,128)S(1)}, bf16[16,32,128]{2,1,0:T(8,128)(2,1)S(1)}, f32[16,64,128]{2,1,0:T(8,128)S(1)}) custom-call(f32[16]{0:T(128)} %rx_ref.3, f32[16]{0:T(128)} %ry_ref.3, bf16[8,296,128]{2,1,0:T(8,128)(2,1)S(1)} %all-to-all-done.pay_ref, bf16[256,256]{1,0:T(8,128)(2,1)} %constant.32.clone.to1_ref, ...), custom_call_target="tpu_custom_call" | custom-call | tf_op jit(solution)/shard_map/maps/pallas_call | solution.py:467
  29.1 0.3 collective-permute-done.entry_ref
  29.4 0.6 %join.1 = (bf16[16,64,448]{2,1,0:T(8,128)(2,1)S(1)}, bf16[16,64,128]{2,1,0:T(8,128)(2,1)S(1)}) custom-call(bf16[16,64,448]{2,1,0:T(8,128)(2,1)S(1)} %get-tuple-element.33.edge_ref, f32[16,448]{1,0:T(8,128)S(1)} %get-tuple-element.34.upto_ref, bf16[2,64,448]{2,1,0:T(8,128)(2,1)S(1)} %collective-permute-done.entry_ref, ...), custom_call_target="tpu_custom_call" | custom-call | tf_op jit(solution)/shard_map/join/pallas_call | solution.py:467
  30.1 1.3 %collective-permute-start.1 = (bf16[16,64,128]{2,1,0:T(8,128)(2,1)S(1)}, bf16[16,64,128]{2,1,0:T(8,128)(2,1)S(1)}, u32[]{:S(2)}, u32[]{:S(2)}) collective-permute-start(bf16[16,64,128]{2,1,0:T(8,128)(2,1)S(1)} %get-tuple-element.39), channel_id=1, source_target_pairs={{0,16},{1,17},{2,18},{3,19},{4,20},{5,21},{6,22},{7,23},{8,24},{9,... | collective-permute-start | bytes 786440 | tf_op jit(solution)/shard_map/ppermute | solution.py:524
  31.4 1.1 %collective-permute-done.1.top_ref = bf16[16,64,128]{2,1,0:T(8,128)(2,1)S(1)} collective-permute-done((bf16[16,64,128]{2,1,0:T(8,128)(2,1)S(1)}, bf16[16,64,128]{2,1,0:T(8,128)(2,1)S(1)}, u32[]{:S(2)}, u32[]{:S(2)}) %collective-permute-start.1) | collective-permute-done | bytes 262176 | tf_op jit(solution)/shard_map/ppermute | solution.py:524
  32.5 1.1 %cells.1 = bf16[8,224,128]{2,1,0:T(8,128)(2,1)S(1)} custom-call(bf16[8,296,128]{2,1,0:T(8,128)(2,1)S(1)} %all-to-all-done.pay_ref, bf16[16,64,448]{2,1,0:T(8,128)(2,1)S(1)} %get-tuple-element.38.edge_ref, bf16[16,64,128]{2,1,0:T(8,128)(2,1)S(1)} %collective-permute-done.1.top_ref, bf16[16,32,256]{2,1,0:T(8,128)(2,1)S(1)} %get-tuple-element.40.side_ref, ...), custom_call_target="tpu_custom_call" | custom-call | tf_op jit(solution)/shard_map/cells/pallas_call | solution.py:467
  33.6 15.5 %all_to_all.10.y_ref = bf16[8,224,128]{2,1,0:T(8,128)(2,1)S(1)} all-to-all(bf16[8,224,128]{2,1,0:T(8,128)(2,1)S(1)} %cells.1), channel_id=1, replica_groups={{0,1,2,3,4,5,6,7},{8,9,10,11,12,13,14,15},{16,17,18,19,20,21,22,23},{24..., dimensions={0} | all-to-all | bytes 917504 | tf_op jit(solution)/shard_map/all_to_all | solution.py:588
  49.1 0.0 copy-done
  49.1 0.0 copy-done.2
  49.1 1.9 %finish.1 = bf16[28,7,1024]{2,1,0:T(8,128)(2,1)} custom-call(bf16[8,224,128]{2,1,0:T(8,128)(2,1)S(1)} %all_to_all.10.y_ref, bf16[224,1024]{1,0:T(8,128)(2,1)S(1)} %get-tuple-element.42.own_ref, bf16[224,1024]{1,0:T(8,128)(2,1)S(1)} %copy-done.2, f32[1,1024]{1,0:T(1,128)S(1)} %get-tuple-element.44.gain_ref, bf16[1024,1024]{1,0:T(8,128)(2,1)S(1)} %copy-done), custom_call_target="tpu_custom_call" | custom-call | tf_op jit(solution)/shard_map/finish/pallas_call | solution.py:467
Async XLA Ops:
  4.3 16.1 %all-to-all-start = ((bf16[8,296,128]{2,1,0:T(8,128)(2,1)}), bf16[8,296,128]{2,1,0:T(8,128)(2,1)S(1)}, u32[]{:S(2)}, u32[]{:S(2)}) async-start(bf16[8,296,128]{2,1,0:T(8,128)(2,1)} %get-tuple-element.25), calls=%async_computation | async-start | bytes 1212416 | tf_op jit(solution)/shard_map/all_to_all | solution.py:583
  17.0 0.8 %copy-start.1 = (bf16[224,1024]{1,0:T(8,128)(2,1)}, bf16[224,1024]{1,0:T(8,128)(2,1)S(1)}, u32[]{:S(2)}) copy-start(bf16[224,1024]{1,0:T(8,128)(2,1)S(1)} %get-tuple-element.43.gate_ref) | copy-start | bytes 1376260
  17.7 31.3 %copy-start = (bf16[1024,1024]{1,0:T(8,128)(2,1)S(1)}, bf16[1024,1024]{1,0:T(8,128)(2,1)}, u32[]{:S(2)}) copy-start(bf16[1024,1024]{1,0:T(8,128)(2,1)} %w_ref.1) | copy-start | bytes 6291460
  20.4 28.7 %copy-start.2 = (bf16[224,1024]{1,0:T(8,128)(2,1)S(1)}, bf16[224,1024]{1,0:T(8,128)(2,1)}, u32[]{:S(2)}) copy-start(bf16[224,1024]{1,0:T(8,128)(2,1)} %copy-done.1) | copy-start | bytes 1376260
  22.4 7.0 %collective-permute-start = (bf16[2,64,448]{2,1,0:T(8,128)(2,1)S(1)}, bf16[2,64,448]{2,1,0:T(8,128)(2,1)S(1)}, u32[]{:S(2)}, u32[]{:S(2)}) collective-permute-start(bf16[2,64,448]{2,1,0:T(8,128)(2,1)S(1)} %get-tuple-element.35), channel_id=1, source_target_pairs={{0,8},{1,9},{2,10},{3,11},{4,12},{5,13},{6,14},{7,15},{16,24},{17,... | collective-permute-start | bytes 344072 | tf_op jit(solution)/shard_map/ppermute | solution.py:499
  30.1 2.4 %collective-permute-start.1 = (bf16[16,64,128]{2,1,0:T(8,128)(2,1)S(1)}, bf16[16,64,128]{2,1,0:T(8,128)(2,1)S(1)}, u32[]{:S(2)}, u32[]{:S(2)}) collective-permute-start(bf16[16,64,128]{2,1,0:T(8,128)(2,1)S(1)} %get-tuple-element.39), channel_id=1, source_target_pairs={{0,16},{1,17},{2,18},{3,19},{4,20},{5,21},{6,22},{7,23},{8,24},{9,... | collective-permute-start | bytes 786440 | tf_op jit(solution)/shard_map/ppermute | solution.py:524

commit v6 on v5

--- a/solution.py
+++ b/solution.py
@@ -55,7 +55,12 @@
         self.bc = 2 * states
         self.at_bc = self.slots * self.half
         self.at_dt = self.at_bc + 2 * self.bc
-        self.message = round_up(self.at_dt + 2 * self.slots, 8)
+        self.at_rate = self.at_dt + 2 * self.slots
+        self.message = round_up(self.at_rate + 1, 8)
+        self.tail = self.edge % LANES
+        self.solid = self.edge // LANES
+        self.share = LANES // self.tail if self.tail else 1
+        self.packed = self.slots * self.solid + (-(-self.slots // self.share) if self.tail else 0)
         assert self.head_width % self.slot == 0 and self.group % self.slot == 0
         assert LANES % self.head_width == 0 and self.half <= LANES
         assert self.cells - self.half <= self.half
@@ -120,17 +125,33 @@
     return jnp.sum(jnp.where(lax.div(cell, plan.col_pad) == row, mm(pick, t), 0.0), axis=1, keepdims=True)
 
 
+def rate_row(heads_of, rx_ref, ry_ref):
+    at = lax.broadcasted_iota(jnp.int32, (1, LANES), 1)
+    rate = jnp.zeros((1, LANES), F32)
+    part = jnp.zeros((1, LANES), jnp.int32)
+    for s, head in enumerate(heads_of):
+        for k, ref in enumerate((rx_ref, ry_ref)):
+            first = 8 * s + 3 * k
+            here = (at >= first) & (at < first + 3)
+            rate = jnp.where(here, ref[head], rate)
+            part = jnp.where(here, at - first, part)
+    high = rate.astype(BF16).astype(F32)
+    middle = (rate - high).astype(BF16).astype(F32)
+    low = rate - high - middle
+    return jnp.where(part == 0, high, jnp.where(part == 1, middle, low))
+
+
 def project_kernel(
-    plan, chunks, bias_hbm, x_hbm, w_hbm, wt_hbm, t_hbm, lanei_hbm, lanej_hbm,
+    plan, chunks, bias_hbm, rx_hbm, ry_hbm, x_hbm, w_hbm, wt_hbm, t_hbm, lanei_hbm, lanej_hbm,
     v_ref, pay_hbm, rows_ref, flat_ref,
-    bias_ref, x_ref, w_ref, wt_ref, t_ref, lanei_ref, lanej_ref, pay_ref, wide, sems, w_sems, out_sems,
+    bias_ref, rx_ref, ry_ref, x_ref, w_ref, wt_ref, t_ref, lanei_ref, lanej_ref, pay_ref, wide, sems, w_sems, out_sems,
 ):
     group, states, cells, heads = plan.group, plan.states, plan.cells, plan.heads
     half, rest = plan.half, plan.cells - plan.half
     tile = plan.width // chunks
     pairs = (
         (x_hbm, x_ref), (t_hbm, t_ref), (wt_hbm, wt_ref), (lanei_hbm, lanei_ref), (lanej_hbm, lanej_ref),
-        (bias_hbm, bias_ref),
+        (bias_hbm, bias_ref), (rx_hbm, rx_ref), (ry_hbm, ry_ref),
     )
     loads = [pltpu.make_async_copy(a, b, sems.at[k]) for k, (a, b) in enumerate(pairs)]
     copies = [
@@ -186,7 +207,7 @@
         per = tile // group
         for k in range(per):
             dest = chunk * per + k
-            dts = []
+            dts, heads_of = [], []
             for s in range(plan.slots):
                 offset = k * group + s * plan.slot
                 base = offset // LANES * LANES
@@ -204,7 +225,9 @@
                     both = jnp.where(lane % HALF < plan.slot, both, 0.0)
                 pay_ref[dest, s * half : (s + 1) * half, :] = both.astype(BF16)
                 head = (chunk * tile + offset) // plan.head_width
+                heads_of.append(head)
                 dts += [steps[head : head + 1, :LANES], steps[head : head + 1, LANES:]]
+            dts.append(rate_row(heads_of, rx_ref, ry_ref))
             pay_ref[dest, plan.at_bc : plan.at_bc + plan.bc, :] = bc[:, :LANES]
             pay_ref[dest, plan.at_bc + plan.bc : plan.at_dt, :] = bc[:, LANES:]
             spare = plan.message - plan.at_dt - len(dts)
@@ -217,11 +240,11 @@
         copy.wait()
 
 
-def project(plan, consts, slide, w_in, w_bcd, tissue, dt_bias):
+def project(plan, consts, slide, w_in, w_bcd, tissue, dt_bias, rate_x, rate_y):
     chunks = 4
     tile = plan.width // chunks
     depth = slide.shape[2]
-    args = [dt_bias, slide, w_in, w_bcd.T, tissue.T, consts["lanei"], consts["lanej"]]
+    args = [dt_bias, rate_x, rate_y, slide, w_in, w_bcd.T, tissue.T, consts["lanei"], consts["lanej"]]
     count = 2 * plan.states + plan.heads
     assert plan.width % chunks == 0 and tile % plan.group == 0 and tile % LANES == 0
     message = (plan.devices, plan.message, LANES)
@@ -236,14 +259,16 @@
         out_shape=[jax.ShapeDtypeStruct(s, d) for s, d in outs],
         scratch_shapes=[
             pltpu.SMEM(dt_bias.shape, F32),
+            pltpu.SMEM(rate_x.shape, F32),
+            pltpu.SMEM(rate_y.shape, F32),
             pltpu.VMEM(slide.shape, BF16),
             pltpu.VMEM((chunks, depth, tile), BF16),
         ]
-        + [pltpu.VMEM(x.shape, x.dtype) for x in args[3:]]
+        + [pltpu.VMEM(x.shape, x.dtype) for x in args[5:]]
         + [
             pltpu.VMEM(message, BF16),
             pltpu.VMEM((plan.cells, depth), F32),
-            pltpu.SemaphoreType.DMA((6,)),
+            pltpu.SemaphoreType.DMA((8,)),
             pltpu.SemaphoreType.DMA((chunks,)),
             pltpu.SemaphoreType.DMA((chunks,)),
         ],
@@ -254,7 +279,7 @@
 
 def home_kernel(
     plan, rx_ref, ry_ref, skip_ref, w_hbm, v_ref, rows_ref, flat_ref, t_ref, gain_ref,
-    own1_ref, own2_ref, from1_ref, from2_ref, mask_ref, out_ref, gate_ref, gain_out, pair, w_ref, sem,
+    own1_ref, own2_ref, from1_ref, from2_ref, mask_ref, out_ref, gate_hbm, gain_out, pair, w_ref, gate_ref, sem, gate_sem,
 ):
     states, cells, half = plan.states, plan.cells, plan.half
     copy = pltpu.make_async_copy(w_hbm.at[:, plan.width :], w_ref, sem)
@@ -288,6 +313,9 @@
         at = slice(block * tile, (block + 1) * tile)
         z = mm(flat_ref[...], w_ref[:, at]).astype(BF16).astype(F32)
         gate_ref[:, at] = (z * (1.0 / (1.0 + jnp.exp(-z))) * keep).astype(BF16)
+    copy = pltpu.make_async_copy(gate_ref, gate_hbm, gate_sem)
+    copy.start()
+    copy.wait()
 
 
 def home(plan, consts, v, rows, flat, w_in, tissue, gain, rate_x, rate_y, d_skip):
@@ -298,11 +326,13 @@
         functools.partial(home_kernel, plan),
         grid=(1,),
         in_specs=[SMEM, SMEM, SMEM, HBM] + [full(x.shape) for x in args[1:]],
-        out_specs=[full(s) for s, _ in outs],
+        out_specs=[full(outs[0][0]), HBM, full(outs[2][0])],
         out_shape=[jax.ShapeDtypeStruct(s, d) for s, d in outs],
         scratch_shapes=[
             pltpu.VMEM((plan.cells, 2 * LANES), F32),
             pltpu.VMEM((w_in.shape[0], w_in.shape[1] - plan.width), BF16),
+            pltpu.VMEM((plan.cells, plan.width), BF16),
+            pltpu.SemaphoreType.DMA,
             pltpu.SemaphoreType.DMA,
         ],
         compiler_params=pltpu.CompilerParams(vmem_limit_bytes=24 * 2**20),
@@ -324,11 +354,6 @@
     return jnp.where(late, i + plan.upper, i), j, real
 
 
-def my_head(plan, axis, slot):
-    place = lax.rem(lax.axis_index(axis), plan.devices)
-    return (place * plan.group + slot * plan.slot) // plan.head_width
-
-
 def wide_rows(pay_ref, t, at, count, gap):
     return jnp.concatenate([pay_ref[t, at : at + count, :], pay_ref[t, at + gap : at + gap + count, :]], axis=1)
 
@@ -350,18 +375,43 @@
             dts[w : w + 1, LANES:] = rows[2 * s + 1 : 2 * s + 2]
 
 
-def slot_rates(plan, axis, rate_ref):
-    at = lax.broadcasted_iota(jnp.int32, (plan.work, 1), 0)
-    rate = jnp.full((plan.work, 1), rate_ref[my_head(plan, axis, 0)], F32)
-    for s in range(1, plan.slots):
-        rate = jnp.where(at >= s * plan.devices, rate_ref[my_head(plan, axis, s)], rate)
-    return rate
-
-
-def edges_kernel(plan, axis, rx_hbm, pay_ref, edge_ref, upto_ref, last_ref, rx_ref, dts, inner, kept, sem):
+def rates_of(plan, pay_ref, kind):
+    row = pay_ref[0, plan.at_dt : plan.message, :].astype(F32)[plan.at_rate - plan.at_dt : plan.at_rate - plan.at_dt + 1]
+    at = lax.broadcasted_iota(jnp.int32, (1, LANES), 1)
+    first = [8 * s + 3 * kind for s in range(plan.slots)]
+    return [jnp.sum(jnp.where((at >= f) & (at < f + 3), row, 0.0), axis=1, keepdims=True) for f in first]
+
+
+def slot_rates(plan, pay_ref, kind):
+    return jnp.concatenate(
+        [jnp.broadcast_to(r, (plan.devices, 1)) for r in rates_of(plan, pay_ref, kind)], axis=0
+    )
+
+
+def pack_edges(plan, out_ref, held):
+    for s in range(plan.slots):
+        for k in range(plan.solid):
+            out_ref[s * plan.solid + k] = held[s][:, k * LANES : (k + 1) * LANES].astype(BF16)
+    if plan.tail:
+        first = plan.slots * plan.solid
+        for k in range(plan.packed - first):
+            parts = [x[:, plan.solid * LANES :] for x in held[k * plan.share : (k + 1) * plan.share]]
+            spare = LANES - plan.tail * len(parts)
+            parts += [jnp.zeros((HALF, spare), F32)] if spare else []
+            out_ref[first + k] = jnp.concatenate(parts, axis=1).astype(BF16)
+
+
+def unpack_edges(plan, ref, s):
+    parts = [ref[s * plan.solid + k].astype(F32) for k in range(plan.solid)]
+    if plan.tail:
+        last = ref[plan.slots * plan.solid + s // plan.share].astype(F32)
+        at = s % plan.share * plan.tail
+        parts.append(last[:, at : at + plan.tail])
+    return jnp.concatenate(parts, axis=1)
+
+
+def edges_kernel(plan, pay_ref, edge_ref, upto_ref, last_ref, dts, inner, kept):
     states, tiles, wide = plan.states, plan.devices, 2 * LANES
-    copy = pltpu.make_async_copy(rx_hbm, rx_ref, sem)
-    copy.start()
     load_steps(plan, pay_ref, dts)
     i, j, real = places(plan, (wide, wide), 0)
     ti, tj, treal = places(plan, (wide, wide), 1)
@@ -373,11 +423,10 @@
     rowsel = ones((ti == lax.broadcasted_iota(jnp.int32, (plan.rows, wide), 0)) & treal)
     dt = dts[...]
     low = dt.astype(BF16)
-    inside, across = mm(low, from1), mm(low, keep)
-    copy.wait()
-    rate = slot_rates(plan, axis, rx_ref)
-    inner[...] = jnp.exp(-rate * inside) * dt
-    kept[...] = jnp.exp(-rate * across)
+    rate = slot_rates(plan, pay_ref, 0)
+    inner[...] = jnp.exp(-rate * mm(low, from1)) * dt
+    kept[...] = jnp.exp(-rate * mm(low, keep))
+    ends = []
     for s in range(plan.slots):
         held = jnp.zeros((HALF, plan.edge), F32)
         product = jnp.ones((1, plan.edge), F32)
@@ -391,19 +440,21 @@
             now = kept[w : w + 1, :]
             held = held * now + nt_dot(turned(plan, pay_ref, t, s), left)
             product = product * now
-        last_ref[s] = held.astype(BF16)
+        ends.append(held)
+    pack_edges(plan, last_ref, ends)
 
 
 def maps_kernel(
-    plan, axis, rx_ref, ry_ref, pay_ref, to1_ref, to2_ref, from1_ref, from2_ref, side1_ref, side2_ref,
+    plan, pay_ref, edge_ref, to1_ref, to2_ref, from1_ref, from2_ref, side1_ref, side2_ref,
     sidemask_ref, down1_ref, down2_ref, downmask_ref, pick_ref,
-    side_ref, above_ref, bottom_ref, top_ref, dts, s1, s2, d1, d2,
+    side_ref, above_ref, passed_ref, top_ref, dts, s1, s2, d1, d2,
 ):
     states, tiles, cp, work = plan.states, plan.devices, plan.col_pad, plan.work
     rp = side1_ref.shape[0]
     load_steps(plan, pay_ref, dts)
     low = dts[...].astype(BF16)
-    above_ref[...] = jnp.exp(-slot_rates(plan, axis, ry_ref) * mm(low, to2_ref[...]))
+    above_ref[...] = jnp.exp(-slot_rates(plan, pay_ref, 1) * mm(low, to2_ref[...]))
+    rates_x, rates_y = rates_of(plan, pay_ref, 0), rates_of(plan, pay_ref, 1)
     for w in range(work):
         rf = dts[w : w + 1, :]
         s1[w * rp : (w + 1) * rp, :] = side1_ref[...].astype(F32) * rf
@@ -412,63 +463,68 @@
         d2[w * cp : (w + 1) * cp, :] = down2_ref[...].astype(F32) * rf
     mask = sidemask_ref[...].astype(F32)
     x, y = mm(s1[...].astype(BF16), to1_ref[...]), mm(s2[...].astype(BF16), to2_ref[...])
+    shape = (states, plan.top)
+    n = lax.broadcasted_iota(jnp.int32, shape, 0)
+    diag = ones(n == lax.div(lax.broadcasted_iota(jnp.int32, shape, 1), cp))
     for w in range(work):
-        head = my_head(plan, axis, w // tiles)
-        rx, ry = rx_ref[head], ry_ref[head]
+        s = w // tiles
         at = slice(w * rp, (w + 1) * rp)
-        side = (jnp.exp(-(rx * x[at] + ry * y[at])) * mask).astype(BF16)
+        side = (jnp.exp(-(rates_x[s] * x[at] + rates_y[s] * y[at])) * mask).astype(BF16)
         side_ref[w] = side
-        bottom_ref[w] = mm(side, pick_ref[...]).astype(BF16)
+        bottom = mm(side, pick_ref[...]).astype(BF16)
+        passed_ref[w] = jnp.concatenate([diag * bottom[i : i + 1] for i in range(plan.rows)], axis=0)
     x, y = mm(d1[...].astype(BF16), from1_ref[...]), mm(d2[...].astype(BF16), from2_ref[...])
     mask = downmask_ref[...].astype(F32)
     for w in range(work):
         s, t = w // tiles, w % tiles
-        head = my_head(plan, axis, s)
-        rx, ry = rx_ref[head], ry_ref[head]
         at = slice(w * cp, (w + 1) * cp)
-        fall = jnp.exp(-(rx * x[at] + ry * y[at])) * mask * dts[w : w + 1, :]
+        fall = jnp.exp(-(rates_x[s] * x[at] + rates_y[s] * y[at])) * mask * dts[w : w + 1, :]
         b = wide_rows(pay_ref, t, plan.at_bc, states, plan.bc).astype(F32)
         falls = jnp.concatenate([fall * b[n : n + 1] for n in range(states)], axis=0).astype(BF16)
-        top_ref[w] = nt_dot(turned(plan, pay_ref, t, s), falls)
-
-
-def join_kernel(plan, edge_ref, upto_ref, entry_ref, bottom_ref, top_ref, whole_ref, out_ref):
-    shape = (plan.states, plan.top)
-    n = lax.broadcasted_iota(jnp.int32, shape, 0)
-    diag = ones(n == lax.div(lax.broadcasted_iota(jnp.int32, shape, 1), plan.col_pad))
-    for w in range(plan.work):
-        entry = entry_ref[w // plan.devices].astype(F32)
-        whole = (edge_ref[w].astype(F32) + entry * upto_ref[w : w + 1, :]).astype(BF16)
-        whole_ref[w] = whole
-        bottom = bottom_ref[w]
-        passed = jnp.concatenate([diag * bottom[i : i + 1] for i in range(plan.rows)], axis=0)
-        out_ref[w] = (top_ref[w] + mm(whole, passed)).astype(BF16)
-
-
-def cells_kernel(plan, pay_ref, edge_ref, top_ref, side_ref, above_ref, out_ref):
+        top_ref[w] = nt_dot(turned(plan, pay_ref, t, s), falls) + mm(edge_ref[w], passed_ref[w])
+
+
+def join_kernel(plan, upto_ref, entry_ref, passed_ref, top_ref, out_ref):
+    for s in range(plan.slots):
+        entry = unpack_edges(plan, entry_ref, s)
+        for t in range(plan.devices):
+            w = s * plan.devices + t
+            late = (entry * upto_ref[w : w + 1, :]).astype(BF16)
+            out_ref[w] = (top_ref[w] + mm(late, passed_ref[w])).astype(BF16)
+
+
+def sides_kernel(plan, pay_ref, edge_ref, upto_ref, entry_ref, side_ref, above_ref, y_ref, down_ref):
     states, tiles = plan.states, plan.devices
     shape = (plan.col_pad, 2 * LANES)
     _, tj, treal = places(plan, shape, 1)
     colsel = jnp.where((tj == lax.broadcasted_iota(jnp.int32, shape, 0)) & treal, 1.0, 0.0)
+    for s in range(plan.slots):
+        entry = unpack_edges(plan, entry_ref, s)
+        for t in range(tiles):
+            w = s * tiles + t
+            c = wide_rows(pay_ref, t, plan.at_bc + states, states, plan.bc)
+            side = side_ref[w]
+            left = jnp.concatenate([c * side[i : i + 1] for i in range(plan.rows)], axis=0)
+            whole = (edge_ref[w].astype(F32) + entry * upto_ref[w : w + 1, :]).astype(BF16)
+            y_ref[w] = mm(whole, left)
+            ca = c.astype(F32) * above_ref[w : w + 1, :]
+            down_ref[w] = jnp.concatenate([colsel * ca[n : n + 1] for n in range(states)], axis=0).astype(BF16)
+
+
+def cells_kernel(plan, y_ref, down_ref, top_ref, out_ref):
     for w in range(plan.work):
-        t, s = w % tiles, w // tiles
-        c = wide_rows(pay_ref, t, plan.at_bc + states, states, plan.bc)
-        side = side_ref[w]
-        left = jnp.concatenate([c * side[i : i + 1] for i in range(plan.rows)], axis=0)
-        ca = c.astype(F32) * above_ref[w : w + 1, :]
-        down = jnp.concatenate([colsel * ca[n : n + 1] for n in range(states)], axis=0).astype(BF16)
-        y = mm(edge_ref[w], left) + mm(top_ref[w], down)
+        t, s = w % plan.devices, w // plan.devices
+        y = y_ref[w] + mm(top_ref[w], down_ref[w])
         y = jnp.concatenate([y[:, :LANES], y[:, LANES:]], axis=0).T
         out_ref[t, s * plan.half : (s + 1) * plan.half, :] = y[: plan.half].astype(BF16)
 
 
-def call(kernel, name, args, outs, scratch=(), specs=()):
-    specs = list(specs) + [full(x.shape) for x in args[len(specs) :]]
+def call(kernel, name, args, outs, scratch=(), out_specs=None):
     return pl.pallas_call(
         kernel,
         grid=(1,),
-        in_specs=specs,
-        out_specs=[full(s) for s, _ in outs],
+        in_specs=[full(x.shape) for x in args],
+        out_specs=out_specs or [full(s) for s, _ in outs],
         out_shape=[jax.ShapeDtypeStruct(s, d) for s, d in outs],
         scratch_shapes=[x if not isinstance(x, tuple) else pltpu.VMEM(*x) for x in scratch],
         compiler_params=pltpu.CompilerParams(vmem_limit_bytes=24 * 2**20),
@@ -476,23 +532,15 @@
     )(*args)
 
 
-def scan_calls(plan, consts, row_axis, col_axis, pay, rate_x, rate_y):
+def scan_calls(plan, consts, row_axis, col_axis, pay):
     work, cp, wide = plan.work, plan.col_pad, 2 * LANES
     rp = consts["side1"].shape[0]
-    rate_x, rate_y = in_hbm(rate_x), in_hbm(rate_y)
     edges, upto, last = call(
-        functools.partial(edges_kernel, plan, col_axis),
+        functools.partial(edges_kernel, plan),
         "edges",
-        [rate_x, pay],
-        [((work, HALF, plan.edge), BF16), ((work, plan.edge), F32), ((plan.slots, HALF, plan.edge), BF16)],
-        [
-            pltpu.SMEM(rate_x.shape, F32),
-            ((work, wide), F32),
-            ((work, wide), F32),
-            ((work, plan.edge), F32),
-            pltpu.SemaphoreType.DMA,
-        ],
-        [HBM],
+        [pay],
+        [((work, HALF, plan.edge), BF16), ((work, plan.edge), F32), ((plan.packed, HALF, LANES), BF16)],
+        [((work, wide), F32), ((work, wide), F32), ((work, plan.edge), F32)],
     )
     if plan.parts > 1:
         hops = [(k, k + plan.devices) for k in range(plan.devices)]
@@ -500,25 +548,25 @@
     else:
         entry = jnp.zeros_like(last)
     names = ("to1", "to2", "from1", "from2", "side1", "side2", "sidemask", "down1", "down2", "downmask", "pick")
-    side, above, bottom, tops = call(
-        functools.partial(maps_kernel, plan, col_axis),
+    side, above, passed, tops = call(
+        functools.partial(maps_kernel, plan),
         "maps",
-        [rate_x, rate_y, pay] + [consts[k] for k in names],
+        [pay, edges] + [consts[k] for k in names],
         [
             ((work, rp, wide), BF16),
             ((work, wide), F32),
-            ((work, rp, LANES), BF16),
+            ((work, plan.edge, plan.top), BF16),
             ((work, HALF, plan.top), F32),
         ],
         [((work, wide), F32)] + [((work * rp, wide), F32)] * 2 + [((work * cp, wide), F32)] * 2,
-        [SMEM, SMEM],
     )
-    edges, tops = call(
+    edge_entry = entry
+    tops = call(
         functools.partial(join_kernel, plan),
         "join",
-        [edges, upto, entry, bottom, tops],
-        [((work, HALF, plan.edge), BF16), ((work, HALF, plan.top), BF16)],
-    )
+        [upto, entry, passed, tops],
+        [((work, HALF, plan.top), BF16)],
+    )[0]
     count = lax.axis_size(row_axis)
     chain = [(r, r + 1) for r in range(count - 1)]
     entry = lax.ppermute(tops, row_axis, chain)
@@ -528,21 +576,28 @@
             entry = lax.ppermute(
                 (tops.astype(F32) + keep * entry.astype(F32)).astype(BF16), row_axis, chain
             )
+    y, down = call(
+        functools.partial(sides_kernel, plan),
+        "sides",
+        [pay, edges, upto, edge_entry, side, above],
+        [((work, HALF, wide), F32), ((work, plan.top, wide), BF16)],
+    )
     return call(
         functools.partial(cells_kernel, plan),
         "cells",
-        [pay, edges, entry, side, above],
+        [y, down, entry],
         [((plan.devices, plan.slots * plan.half, LANES), BF16)],
     )[0]
 
 
-def finish_kernel(plan, y_ref, own_ref, gate_ref, gain_ref, w_ref, out_ref, full_ref):
+def finish_kernel(plan, y_ref, own_ref, gate_ref, gain_ref, w_ref, out_hbm, full_ref, out_ref, sems):
     half, cells = plan.half, plan.cells
     slot, slots = plan.slot, plan.slots
     per = LANES // slot
     lane = lax.broadcasted_iota(jnp.int32, (half, LANES), 1)
-    for block in range(plan.width // LANES):
-        for k, (lo, hi) in enumerate(((0, half), (half, cells))):
+    copies = []
+    for k, (lo, hi) in enumerate(((0, half), (half, cells))):
+        for block in range(plan.width // LANES):
             joined = None
             for d in range(per):
                 at = block * per + d
@@ -552,14 +607,19 @@
                     part = pltpu.roll(part, shift, 1)
                 joined = part if joined is None else jnp.where(lane < d * slot, joined, part)
             full_ref[lo:hi, block * LANES : (block + 1) * LANES] = joined[: hi - lo]
-    y = full_ref[...] + own_ref[...].astype(F32)
-    y = y.astype(BF16).astype(F32)
-    gated = y * gate_ref[...].astype(F32)
-    scale = lax.rsqrt(jnp.mean(gated * gated, axis=-1, keepdims=True) + norm_eps)
-    normed = (gated * scale * gain_ref[...]).astype(BF16)
-    full_ref[...] = mm(normed, w_ref[...])
-    for i in range(plan.rows):
-        out_ref[i] = full_ref[i * plan.col_pad : i * plan.col_pad + plan.cols, :].astype(BF16)
+        y = full_ref[lo:hi, :] + own_ref[lo:hi, :].astype(F32)
+        y = y.astype(BF16).astype(F32)
+        gated = y * gate_ref[lo:hi, :].astype(F32)
+        scale = lax.rsqrt(jnp.mean(gated * gated, axis=-1, keepdims=True) + norm_eps)
+        normed = (gated * scale * gain_ref[...]).astype(BF16)
+        full_ref[lo:hi, :] = mm(normed, w_ref[...])
+        first, last = lo // plan.col_pad, hi // plan.col_pad
+        for i in range(first, last):
+            out_ref[i] = full_ref[i * plan.col_pad : i * plan.col_pad + plan.cols, :].astype(BF16)
+        copies.append(pltpu.make_async_copy(out_ref.at[first:last], out_hbm.at[first:last], sems.at[k]))
+        copies[-1].start()
+    for copy in copies:
+        copy.wait()
 
 
 def finish(plan, y, own, gate, gain, w_out):
@@ -567,7 +627,12 @@
     shape = (plan.rows, plan.cols, w_out.shape[1])
     assert w_out.shape[1] == plan.width
     return call(
-        functools.partial(finish_kernel, plan), "finish", args, [(shape, BF16)], [((plan.cells, plan.width), F32)]
+        functools.partial(finish_kernel, plan),
+        "finish",
+        args,
+        [(shape, BF16)],
+        [((plan.cells, plan.width), F32), (shape, BF16), pltpu.SemaphoreType.DMA((2,))],
+        [HBM],
     )[0]
 
 
@@ -578,13 +643,13 @@
     states = (w_bcd.shape[1] - heads) // 2
     plan = Plan(rows, cols, states, heads, width, lax.axis_size("col"))
     consts = plan.constants()
-    v, pay, table, x = project(plan, consts, slide, w_in, w_bcd, tissue, dt_bias)
+    v, pay, table, x = project(plan, consts, slide, w_in, w_bcd, tissue, dt_bias, rate_x, rate_y)
     groups = plan.segments()
     pay = lax.all_to_all(pay, "col", 0, 0, tiled=True, axis_index_groups=groups)
     gain = norm_gain.reshape(1, width)
     own, gate, gain = home(plan, consts, v, table, x, w_in, tissue, gain, rate_x, rate_y, d_skip)
     pay, own, gate, gain = lax.optimization_barrier((pay, own, gate, gain))
-    y = scan_calls(plan, consts, "row", "col", pay, rate_x, rate_y)
+    y = scan_calls(plan, consts, "row", "col", pay)
     y = lax.all_to_all(y, "col", 0, 0, tiled=True, axis_index_groups=groups)
     return finish(plan, y, own, gate, gain, w_out)
 

time: 51.4 us -> 49.2 us (0.957)
  blocking collectives: 15.5 us -> 14.5 us
  waiting for transfers between devices: 4.1 us -> 3.18 us
  local copies, waits for them, and re-layouts: 0.77 us -> 0.01 us
    ppermute x1, waiting for transfers between devices: 1.13 us -> 0.1 us  [scan_calls(): entry = lax.ppermute(tops, row_axis, chain)]
    all_to_all x1, blocking collectives: 15.5 us -> 14.5 us  [per_device(): y = lax.all_to_all(y, 'col', 0, 0, tiled=True, axis_index_groups=groups)]
    unnamed x6 -> x2, local copies, waits for them, and re-layouts: 0.77 us -> 0.01 us
    pallas_call x5 -> x6, Pallas kernels: 7.8 us -> 8.01 us  [call(): pl.pallas_call(kernel, grid=(1,), in_specs=[full(x.shape) for x in args],...]
  transfers between devices with their start and end apart: 3 -> 3, of which waited for: 3 -> 2; matrix products, arithmetic and copies ran while one was open for 0% -> 0% of each run, Pallas kernels for 17% -> 22%
where the time goes in v6:
time: 49.2 us; the launch traced here: 48.8 us
  Pallas kernels  19 us (39%)
  blocking collectives  14.5 us (29%)
  starting transfers between devices  12 us (24%)
  waiting for transfers between devices  3.18 us (6%)
    all_to_all x1, blocking collectives, per_device(): y = lax.all_to_all(y, 'col', 0, 0, tiled=True, axis_index_groups=groups)  14.5 us
    pallas_call x6, Pallas kernels, call(): pl.pallas_call(kernel, grid=(1,), in_specs=[full(x.shape) for x in args],...  8.01 us
    pallas_call x1, Pallas kernels, home(): pl.pallas_call(functools.partial(home_kernel, plan), grid=(1,), in_specs=...  6.79 us
    all_to_all x1, starting transfers between devices, per_device(): pay = lax.all_to_all(pay, 'col', 0, 0, tiled=True, axis_index_groups=groups)  6.22 us
    ppermute x1, starting transfers between devices, scan_calls(): entry = lax.ppermute(last, col_axis, hops)  4.5 us
    pallas_call x1, Pallas kernels, project(): pl.pallas_call(functools.partial(project_kernel, plan, chunks), grid=(1,)...  4.24 us
    all_to_all x1, waiting for transfers between devices, per_device(): pay = lax.all_to_all(pay, 'col', 0, 0, tiled=True, axis_index_groups=groups)  3.08 us
    ppermute x1, starting transfers between devices, scan_calls(): entry = lax.ppermute(tops, row_axis, chain)  1.31 us
  transfers between devices with their start and end apart: 3, of which 2 were waited for; matrix products, arithmetic and copies ran while one was open for 0% of the time, Pallas kernels for 22%

profile of v6, /device:TPU:0, one launch (start us, length us, event | category | flops | bytes accessed | tf_op | source)
XLA Modules:
  0.0 48.8 jit_solution(2545701607828186490)
XLA Ops:
  0.0 4.2 %project.1 = (bf16[256,1024]{1,0:T(8,128)(2,1)S(1)}, bf16[8,296,128]{2,1,0:T(8,128)(2,1)}, f32[48,256]{1,0:T(8,128)S(1)}, bf16[224,1024]{1,0:T(8,128)(2,1)S(1)}) custom-call(f32[16]{0:T(128)} %bias_hbm.1, f32[16]{0:T(128)} %rx_ref.1, f32[16]{0:T(128)} %ry_ref.1, bf16[28,7,1024]{2,1,0:T(8,128)(2,1)} %x_hbm.1, bf16[1024,2048]{1,0:T(8,128)(2,1)} %w_hbm.3, ...), custom_call_target="tpu_custom_call" | custom-call | tf_op jit(solution)/shard_map/project/pallas_call | solution.py:254
  4.2 6.2 %all-to-all-start = ((bf16[8,296,128]{2,1,0:T(8,128)(2,1)}), bf16[8,296,128]{2,1,0:T(8,128)(2,1)S(1)}, u32[]{:S(2)}, u32[]{:S(2)}) async-start(bf16[8,296,128]{2,1,0:T(8,128)(2,1)} %get-tuple-element.25), calls=%async_computation | async-start | bytes 1212416 | tf_op jit(solution)/shard_map/all_to_all | solution.py:648
  10.5 6.8 %home.1 = (bf16[224,1024]{1,0:T(8,128)(2,1)S(1)}, bf16[224,1024]{1,0:T(8,128)(2,1)S(1)}, f32[1,1024]{1,0:T(1,128)S(1)}) custom-call(f32[16]{0:T(128)} %rx_ref.1, f32[16]{0:T(128)} %ry_ref.1, f32[16]{0:T(128)} %skip_ref.1, bf16[1024,2048]{1,0:T(8,128)(2,1)} %w_hbm.3, bf16[256,1024]{1,0:T(8,128)(2,1)S(1)} %get-tuple-element.26.v_ref, ...), custom_call_target="tpu_custom_call" | custom-call | tf_op jit(solution)/shard_map/home/pallas_call | solution.py:325
  17.3 3.1 %all-to-all-done.pay_ref = bf16[8,296,128]{2,1,0:T(8,128)(2,1)S(1)} async-done(((bf16[8,296,128]{2,1,0:T(8,128)(2,1)}), bf16[8,296,128]{2,1,0:T(8,128)(2,1)S(1)}, u32[]{:S(2)}, u32[]{:S(2)}) %all-to-all-start) | async-done | bytes 606240 | tf_op jit(solution)/shard_map/all_to_all | solution.py:648
  20.4 1.4 %edges.1 = (bf16[16,64,448]{2,1,0:T(8,128)(2,1)S(1)}, f32[16,448]{1,0:T(8,128)S(1)}, bf16[7,64,128]{2,1,0:T(8,128)(2,1)S(1)}) custom-call(bf16[8,296,128]{2,1,0:T(8,128)(2,1)S(1)} %all-to-all-done.pay_ref), custom_call_target="tpu_custom_call" | custom-call | tf_op jit(solution)/shard_map/edges/pallas_call | solution.py:523
  21.8 4.5 %collective-permute-start = (bf16[7,64,128]{2,1,0:T(8,128)(2,1)S(1)}, bf16[7,64,128]{2,1,0:T(8,128)(2,1)S(1)}, u32[]{:S(2)}, u32[]{:S(2)}) collective-permute-start(bf16[7,64,128]{2,1,0:T(8,128)(2,1)S(1)} %get-tuple-element.35), channel_id=1, source_target_pairs={{0,8},{1,9},{2,10},{3,11},{4,12},{5,13},{6,14},{7,15},{16,24},{17,... | collective-permute-start | bytes 344072 | tf_op jit(solution)/shard_map/ppermute | solution.py:547
  26.3 2.8 %maps.1 = (bf16[16,32,256]{2,1,0:T(8,128)(2,1)S(1)}, f32[16,256]{1,0:T(8,128)S(1)}, bf16[16,448,128]{2,1,0:T(8,128)(2,1)S(1)}, f32[16,64,128]{2,1,0:T(8,128)S(1)}) custom-call(bf16[8,296,128]{2,1,0:T(8,128)(2,1)S(1)} %all-to-all-done.pay_ref, bf16[16,64,448]{2,1,0:T(8,128)(2,1)S(1)} %get-tuple-element.33.edge_ref, bf16[256,256]{1,0:T(8,128)(2,1)} %constant.32.clone.to1_ref, ...), custom_call_target="tpu_custom_call" | custom-call | tf_op jit(solution)/shard_map/maps/pallas_call | solution.py:523
  29.1 0.0 collective-permute-done.entry_ref
  29.1 0.5 %join.1 = bf16[16,64,128]{2,1,0:T(8,128)(2,1)S(1)} custom-call(f32[16,448]{1,0:T(8,128)S(1)} %get-tuple-element.34.upto_ref, bf16[7,64,128]{2,1,0:T(8,128)(2,1)S(1)} %collective-permute-done.entry_ref, bf16[16,448,128]{2,1,0:T(8,128)(2,1)S(1)} %get-tuple-element.40.passed_ref, f32[16,64,128]{2,1,0:T(8,128)S(1)} %get-tuple-element.41.top_ref), custom_call_target="tpu_custom_call" | custom-call | tf_op jit(solution)/shard_map/join/pallas_call | solution.py:523
  29.6 1.3 %collective-permute-start.1 = (bf16[16,64,128]{2,1,0:T(8,128)(2,1)S(1)}, bf16[16,64,128]{2,1,0:T(8,128)(2,1)S(1)}, u32[]{:S(2)}, u32[]{:S(2)}) collective-permute-start(bf16[16,64,128]{2,1,0:T(8,128)(2,1)S(1)} %join.1), channel_id=1, source_target_pairs={{0,16},{1,17},{2,18},{3,19},{4,20},{5,21},{6,22},{7,23},{8,24},{9,... | collective-permute-start | bytes 786440 | tf_op jit(solution)/shard_map/ppermute | solution.py:572
  30.9 1.0 %sides.1 = (f32[16,64,256]{2,1,0:T(8,128)S(1)}, bf16[16,128,256]{2,1,0:T(8,128)(2,1)S(1)}) custom-call(bf16[8,296,128]{2,1,0:T(8,128)(2,1)S(1)} %all-to-all-done.pay_ref, bf16[16,64,448]{2,1,0:T(8,128)(2,1)S(1)} %get-tuple-element.33.edge_ref, f32[16,448]{1,0:T(8,128)S(1)} %get-tuple-element.34.upto_ref, ...), custom_call_target="tpu_custom_call" | custom-call | tf_op jit(solution)/shard_map/sides/pallas_call | solution.py:523
  31.9 0.0 copy-start
  31.9 0.1 collective-permute-done.1.top_ref
  32.0 0.4 cells.1
  32.4 14.5 %all_to_all.10.y_ref = bf16[8,224,128]{2,1,0:T(8,128)(2,1)S(1)} all-to-all(bf16[8,224,128]{2,1,0:T(8,128)(2,1)S(1)} %cells.1), channel_id=1, replica_groups={{0,1,2,3,4,5,6,7},{8,9,10,11,12,13,14,15},{16,17,18,19,20,21,22,23},{24..., dimensions={0} | all-to-all | bytes 917504 | tf_op jit(solution)/shard_map/all_to_all | solution.py:653
  46.9 0.0 copy-done
  46.9 1.9 %finish.1 = bf16[28,7,1024]{2,1,0:T(8,128)(2,1)} custom-call(bf16[8,224,128]{2,1,0:T(8,128)(2,1)S(1)} %all_to_all.10.y_ref, bf16[224,1024]{1,0:T(8,128)(2,1)S(1)} %get-tuple-element.42.own_ref, bf16[224,1024]{1,0:T(8,128)(2,1)S(1)} %get-tuple-element.43.gate_ref, f32[1,1024]{1,0:T(1,128)S(1)} %get-tuple-element.44.gain_ref, bf16[1024,1024]{1,0:T(8,128)(2,1)S(1)} %copy-done), custom_call_target="tpu_custom_call" | custom-call | tf_op jit(solution)/shard_map/finish/pallas_call | solution.py:523
Async XLA Ops:
  4.2 16.1 %all-to-all-start = ((bf16[8,296,128]{2,1,0:T(8,128)(2,1)}), bf16[8,296,128]{2,1,0:T(8,128)(2,1)S(1)}, u32[]{:S(2)}, u32[]{:S(2)}) async-start(bf16[8,296,128]{2,1,0:T(8,128)(2,1)} %get-tuple-element.25), calls=%async_computation | async-start | bytes 1212416 | tf_op jit(solution)/shard_map/all_to_all | solution.py:648
  21.8 7.3 %collective-permute-start = (bf16[7,64,128]{2,1,0:T(8,128)(2,1)S(1)}, bf16[7,64,128]{2,1,0:T(8,128)(2,1)S(1)}, u32[]{:S(2)}, u32[]{:S(2)}) collective-permute-start(bf16[7,64,128]{2,1,0:T(8,128)(2,1)S(1)} %get-tuple-element.35), channel_id=1, source_target_pairs={{0,8},{1,9},{2,10},{3,11},{4,12},{5,13},{6,14},{7,15},{16,24},{17,... | collective-permute-start | bytes 344072 | tf_op jit(solution)/shard_map/ppermute | solution.py:547
  29.6 2.4 %collective-permute-start.1 = (bf16[16,64,128]{2,1,0:T(8,128)(2,1)S(1)}, bf16[16,64,128]{2,1,0:T(8,128)(2,1)S(1)}, u32[]{:S(2)}, u32[]{:S(2)}) collective-permute-start(bf16[16,64,128]{2,1,0:T(8,128)(2,1)S(1)} %join.1), channel_id=1, source_target_pairs={{0,16},{1,17},{2,18},{3,19},{4,20},{5,21},{6,22},{7,23},{8,24},{9,... | collective-permute-start | bytes 786440 | tf_op jit(solution)/shard_map/ppermute | solution.py:572
  31.9 15.0 %copy-start = (bf16[1024,1024]{1,0:T(8,128)(2,1)S(1)}, bf16[1024,1024]{1,0:T(8,128)(2,1)}, u32[]{:S(2)}) copy-start(bf16[1024,1024]{1,0:T(8,128)(2,1)} %w_ref.1) | copy-start | bytes 6291460

commit v7 on v6

--- a/solution.py
+++ b/solution.py
@@ -410,9 +410,8 @@
     return jnp.concatenate(parts, axis=1)
 
 
-def edges_kernel(plan, pay_ref, edge_ref, upto_ref, last_ref, dts, inner, kept):
+def scan_edges(plan, pay_ref, dts, inner, kept, seen):
     states, tiles, wide = plan.states, plan.devices, 2 * LANES
-    load_steps(plan, pay_ref, dts)
     i, j, real = places(plan, (wide, wide), 0)
     ti, tj, treal = places(plan, (wide, wide), 1)
     from1 = ones((i == ti) & (j > tj) & real & treal)
@@ -432,26 +431,38 @@
         product = jnp.ones((1, plan.edge), F32)
         for t in range(tiles):
             w = s * tiles + t
+            seen(w, held, product)
             b = wide_rows(pay_ref, t, plan.at_bc, states, plan.bc).astype(F32)
             bd = (b * inner[w : w + 1, :]).astype(BF16)
             left = jnp.concatenate([bd * rowsel[i : i + 1] for i in range(plan.rows)], axis=0)
-            edge_ref[w] = held.astype(BF16)
-            upto_ref[w : w + 1, :] = product
             now = kept[w : w + 1, :]
             held = held * now + nt_dot(turned(plan, pay_ref, t, s), left)
             product = product * now
         ends.append(held)
-    pack_edges(plan, last_ref, ends)
+    return ends
+
+
+def last_kernel(plan, axis, pay_ref, last_ref, dts, inner, kept):
+    @pl.when(lax.axis_index(axis) < (plan.parts - 1) * plan.devices)
+    def _():
+        load_steps(plan, pay_ref, dts)
+        pack_edges(plan, last_ref, scan_edges(plan, pay_ref, dts, inner, kept, lambda w, held, product: None))
 
 
 def maps_kernel(
-    plan, pay_ref, edge_ref, to1_ref, to2_ref, from1_ref, from2_ref, side1_ref, side2_ref,
+    plan, pay_ref, to1_ref, to2_ref, from1_ref, from2_ref, side1_ref, side2_ref,
     sidemask_ref, down1_ref, down2_ref, downmask_ref, pick_ref,
-    side_ref, above_ref, passed_ref, top_ref, dts, s1, s2, d1, d2,
+    side_ref, above_ref, passed_ref, top_ref, edge_ref, upto_ref, dts, inner, kept, s1, s2, d1, d2,
 ):
     states, tiles, cp, work = plan.states, plan.devices, plan.col_pad, plan.work
     rp = side1_ref.shape[0]
     load_steps(plan, pay_ref, dts)
+
+    def seen(w, held, product):
+        edge_ref[w] = held.astype(BF16)
+        upto_ref[w : w + 1, :] = product
+
+    scan_edges(plan, pay_ref, dts, inner, kept, seen)
     low = dts[...].astype(BF16)
     above_ref[...] = jnp.exp(-slot_rates(plan, pay_ref, 1) * mm(low, to2_ref[...]))
     rates_x, rates_y = rates_of(plan, pay_ref, 0), rates_of(plan, pay_ref, 1)
@@ -535,30 +546,27 @@
 def scan_calls(plan, consts, row_axis, col_axis, pay):
     work, cp, wide = plan.work, plan.col_pad, 2 * LANES
     rp = consts["side1"].shape[0]
-    edges, upto, last = call(
-        functools.partial(edges_kernel, plan),
-        "edges",
-        [pay],
-        [((work, HALF, plan.edge), BF16), ((work, plan.edge), F32), ((plan.packed, HALF, LANES), BF16)],
-        [((work, wide), F32), ((work, wide), F32), ((work, plan.edge), F32)],
-    )
+    steps = [((work, wide), F32), ((work, wide), F32), ((work, plan.edge), F32)]
+    shape = (plan.packed, HALF, LANES)
     if plan.parts > 1:
-        hops = [(k, k + plan.devices) for k in range(plan.devices)]
-        entry = lax.ppermute(last, col_axis, hops)
+        last = call(functools.partial(last_kernel, plan, col_axis), "last", [pay], [(shape, BF16)], steps)[0]
+        entry = lax.ppermute(last, col_axis, [(k, k + plan.devices) for k in range(plan.devices)])
     else:
-        entry = jnp.zeros_like(last)
+        entry = jnp.zeros(shape, BF16)
     names = ("to1", "to2", "from1", "from2", "side1", "side2", "sidemask", "down1", "down2", "downmask", "pick")
-    side, above, passed, tops = call(
+    side, above, passed, tops, edges, upto = call(
         functools.partial(maps_kernel, plan),
         "maps",
-        [pay, edges] + [consts[k] for k in names],
+        [pay] + [consts[k] for k in names],
         [
             ((work, rp, wide), BF16),
             ((work, wide), F32),
             ((work, plan.edge, plan.top), BF16),
             ((work, HALF, plan.top), F32),
+            ((work, HALF, plan.edge), BF16),
+            ((work, plan.edge), F32),
         ],
-        [((work, wide), F32)] + [((work * rp, wide), F32)] * 2 + [((work * cp, wide), F32)] * 2,
+        steps + [((work * rp, wide), F32)] * 2 + [((work * cp, wide), F32)] * 2,
     )
     edge_entry = entry
     tops = call(

time: 49.2 us -> 47.8 us (0.972)
  starting transfers between devices: 12 us -> 10.6 us
  Pallas kernels: 19 us -> 20.1 us
  blocking collectives: 14.5 us -> 13.4 us
    ppermute x1, starting transfers between devices: 4.5 us -> 3.07 us  [scan_calls(): lax.ppermute(last, col_axis, [(k, k + plan.devices) for k in range(plan.d...]
    pallas_call x6, Pallas kernels: 8.01 us -> 9.11 us  [call(): pl.pallas_call(kernel, grid=(1,), in_specs=[full(x.shape) for x in args],...]
    all_to_all x1, blocking collectives: 14.5 us -> 13.4 us  [per_device(): y = lax.all_to_all(y, 'col', 0, 0, tiled=True, axis_index_groups=groups)]
  transfers between devices with their start and end apart: 3 -> 3, of which waited for: 2 -> 2; matrix products, arithmetic and copies ran while one was open for 0% -> 0% of each run, Pallas kernels for 22% -> 25%
where the time goes in v7:
time: 47.8 us; the launch traced here: 47.4 us
  Pallas kernels  20.1 us (42%)
  blocking collectives  13.4 us (28%)
  starting transfers between devices  10.6 us (22%)
  waiting for transfers between devices  3.18 us (7%)
    all_to_all x1, blocking collectives, per_device(): y = lax.all_to_all(y, 'col', 0, 0, tiled=True, axis_index_groups=groups)  13.4 us
    pallas_call x6, Pallas kernels, call(): pl.pallas_call(kernel, grid=(1,), in_specs=[full(x.shape) for x in args],...  9.11 us
    pallas_call x1, Pallas kernels, home(): pl.pallas_call(functools.partial(home_kernel, plan), grid=(1,), in_specs=...  6.8 us
    all_to_all x1, starting transfers between devices, per_device(): pay = lax.all_to_all(pay, 'col', 0, 0, tiled=True, axis_index_groups=groups)  6.22 us
    pallas_call x1, Pallas kernels, project(): pl.pallas_call(functools.partial(project_kernel, plan, chunks), grid=(1,)...  4.23 us
    all_to_all x1, waiting for transfers between devices, per_device(): pay = lax.all_to_all(pay, 'col', 0, 0, tiled=True, axis_index_groups=groups)  3.08 us
    ppermute x1, starting transfers between devices, scan_calls(): lax.ppermute(last, col_axis, [(k, k + plan.devices) for k in range(plan.d...  3.07 us
    ppermute x1, starting transfers between devices, scan_calls(): entry = lax.ppermute(tops, row_axis, chain)  1.31 us
  transfers between devices with their start and end apart: 3, of which 2 were waited for; matrix products, arithmetic and copies ran while one was open for 0% of the time, Pallas kernels for 25%

profile of v7, /device:TPU:0, one launch (start us, length us, event | category | flops | bytes accessed | tf_op | source)
XLA Modules:
  0.0 47.4 jit_solution(7990667480554031332)
XLA Ops:
  0.0 4.2 %project.1 = (bf16[256,1024]{1,0:T(8,128)(2,1)S(1)}, bf16[8,296,128]{2,1,0:T(8,128)(2,1)}, f32[48,256]{1,0:T(8,128)S(1)}, bf16[224,1024]{1,0:T(8,128)(2,1)S(1)}) custom-call(f32[16]{0:T(128)} %bias_hbm.1, f32[16]{0:T(128)} %rx_ref.1, f32[16]{0:T(128)} %ry_ref.1, bf16[28,7,1024]{2,1,0:T(8,128)(2,1)} %x_hbm.1, bf16[1024,2048]{1,0:T(8,128)(2,1)} %w_hbm.3, ...), custom_call_target="tpu_custom_call" | custom-call | tf_op jit(solution)/shard_map/project/pallas_call | solution.py:254
  4.2 6.2 %all-to-all-start = ((bf16[8,296,128]{2,1,0:T(8,128)(2,1)}), bf16[8,296,128]{2,1,0:T(8,128)(2,1)S(1)}, u32[]{:S(2)}, u32[]{:S(2)}) async-start(bf16[8,296,128]{2,1,0:T(8,128)(2,1)} %get-tuple-element.24), calls=%async_computation | async-start | bytes 1212416 | tf_op jit(solution)/shard_map/all_to_all | solution.py:656
  10.5 6.8 %home.1 = (bf16[224,1024]{1,0:T(8,128)(2,1)S(1)}, bf16[224,1024]{1,0:T(8,128)(2,1)S(1)}, f32[1,1024]{1,0:T(1,128)S(1)}) custom-call(f32[16]{0:T(128)} %rx_ref.1, f32[16]{0:T(128)} %ry_ref.1, f32[16]{0:T(128)} %skip_ref.1, bf16[1024,2048]{1,0:T(8,128)(2,1)} %w_hbm.3, bf16[256,1024]{1,0:T(8,128)(2,1)S(1)} %get-tuple-element.25.v_ref, ...), custom_call_target="tpu_custom_call" | custom-call | tf_op jit(solution)/shard_map/home/pallas_call | solution.py:325
  17.3 3.1 %all-to-all-done.pay_ref = bf16[8,296,128]{2,1,0:T(8,128)(2,1)S(1)} async-done(((bf16[8,296,128]{2,1,0:T(8,128)(2,1)}), bf16[8,296,128]{2,1,0:T(8,128)(2,1)S(1)}, u32[]{:S(2)}, u32[]{:S(2)}) %all-to-all-start) | async-done | bytes 606240 | tf_op jit(solution)/shard_map/all_to_all | solution.py:656
  20.3 1.4 %last.1 = bf16[7,64,128]{2,1,0:T(8,128)(2,1)S(1)} custom-call(bf16[8,296,128]{2,1,0:T(8,128)(2,1)S(1)} %all-to-all-done.pay_ref), custom_call_target="tpu_custom_call" | custom-call | tf_op jit(solution)/shard_map/last/pallas_call | solution.py:534
  21.8 3.1 %collective-permute-start = (bf16[7,64,128]{2,1,0:T(8,128)(2,1)S(1)}, bf16[7,64,128]{2,1,0:T(8,128)(2,1)S(1)}, u32[]{:S(2)}, u32[]{:S(2)}) collective-permute-start(bf16[7,64,128]{2,1,0:T(8,128)(2,1)S(1)} %last.1), channel_id=1, source_target_pairs={{0,8},{1,9},{2,10},{3,11},{4,12},{5,13},{6,14},{7,15},{16,24},{17,... | collective-permute-start | bytes 344072 | tf_op jit(solution)/shard_map/ppermute | solution.py:553
  24.8 3.9 %maps.1 = (bf16[16,32,256]{2,1,0:T(8,128)(2,1)S(1)}, f32[16,256]{1,0:T(8,128)S(1)}, bf16[16,448,128]{2,1,0:T(8,128)(2,1)S(1)}, f32[16,64,128]{2,1,0:T(8,128)S(1)...) custom-call(bf16[8,296,128]{2,1,0:T(8,128)(2,1)S(1)} %all-to-all-done.pay_ref, ...), custom_call_target="tpu_custom_call" | custom-call | tf_op jit(solution)/shard_map/maps/pallas_call | solution.py:534
  28.7 0.0 collective-permute-done.entry_ref
  28.7 0.5 %join.1 = bf16[16,64,128]{2,1,0:T(8,128)(2,1)S(1)} custom-call(f32[16,448]{1,0:T(8,128)S(1)} %get-tuple-element.33.upto_ref, bf16[7,64,128]{2,1,0:T(8,128)(2,1)S(1)} %collective-permute-done.entry_ref, bf16[16,448,128]{2,1,0:T(8,128)(2,1)S(1)} %get-tuple-element.38.passed_ref, f32[16,64,128]{2,1,0:T(8,128)S(1)} %get-tuple-element.39.top_ref), custom_call_target="tpu_custom_call" | custom-call | tf_op jit(solution)/shard_map/join/pallas_call | solution.py:534
  29.2 1.3 %collective-permute-start.1 = (bf16[16,64,128]{2,1,0:T(8,128)(2,1)S(1)}, bf16[16,64,128]{2,1,0:T(8,128)(2,1)S(1)}, u32[]{:S(2)}, u32[]{:S(2)}) collective-permute-start(bf16[16,64,128]{2,1,0:T(8,128)(2,1)S(1)} %join.1), channel_id=1, source_target_pairs={{0,16},{1,17},{2,18},{3,19},{4,20},{5,21},{6,22},{7,23},{8,24},{9,... | collective-permute-start | bytes 786440 | tf_op jit(solution)/shard_map/ppermute | solution.py:580
  30.5 1.0 %sides.1 = (f32[16,64,256]{2,1,0:T(8,128)S(1)}, bf16[16,128,256]{2,1,0:T(8,128)(2,1)S(1)}) custom-call(bf16[8,296,128]{2,1,0:T(8,128)(2,1)S(1)} %all-to-all-done.pay_ref, bf16[16,64,448]{2,1,0:T(8,128)(2,1)S(1)} %get-tuple-element.32.edge_ref, f32[16,448]{1,0:T(8,128)S(1)} %get-tuple-element.33.upto_ref, ...), custom_call_target="tpu_custom_call" | custom-call | tf_op jit(solution)/shard_map/sides/pallas_call | solution.py:534
  31.6 0.0 copy-start
  31.6 0.1 collective-permute-done.1.top_ref
  31.7 0.4 cells.1
  32.0 13.4 %all_to_all.10.y_ref = bf16[8,224,128]{2,1,0:T(8,128)(2,1)S(1)} all-to-all(bf16[8,224,128]{2,1,0:T(8,128)(2,1)S(1)} %cells.1), channel_id=1, replica_groups={{0,1,2,3,4,5,6,7},{8,9,10,11,12,13,14,15},{16,17,18,19,20,21,22,23},{24..., dimensions={0} | all-to-all | bytes 917504 | tf_op jit(solution)/shard_map/all_to_all | solution.py:661
  45.5 0.0 copy-done
  45.5 1.9 %finish.1 = bf16[28,7,1024]{2,1,0:T(8,128)(2,1)} custom-call(bf16[8,224,128]{2,1,0:T(8,128)(2,1)S(1)} %all_to_all.10.y_ref, bf16[224,1024]{1,0:T(8,128)(2,1)S(1)} %get-tuple-element.40.own_ref, bf16[224,1024]{1,0:T(8,128)(2,1)S(1)} %get-tuple-element.41.gate_ref, f32[1,1024]{1,0:T(1,128)S(1)} %get-tuple-element.42.gain_ref, bf16[1024,1024]{1,0:T(8,128)(2,1)S(1)} %copy-done), custom_call_target="tpu_custom_call" | custom-call | tf_op jit(solution)/shard_map/finish/pallas_call | solution.py:534
Async XLA Ops:
  4.2 16.1 %all-to-all-start = ((bf16[8,296,128]{2,1,0:T(8,128)(2,1)}), bf16[8,296,128]{2,1,0:T(8,128)(2,1)S(1)}, u32[]{:S(2)}, u32[]{:S(2)}) async-start(bf16[8,296,128]{2,1,0:T(8,128)(2,1)} %get-tuple-element.24), calls=%async_computation | async-start | bytes 1212416 | tf_op jit(solution)/shard_map/all_to_all | solution.py:656
  21.8 7.0 %collective-permute-start = (bf16[7,64,128]{2,1,0:T(8,128)(2,1)S(1)}, bf16[7,64,128]{2,1,0:T(8,128)(2,1)S(1)}, u32[]{:S(2)}, u32[]{:S(2)}) collective-permute-start(bf16[7,64,128]{2,1,0:T(8,128)(2,1)S(1)} %last.1), channel_id=1, source_target_pairs={{0,8},{1,9},{2,10},{3,11},{4,12},{5,13},{6,14},{7,15},{16,24},{17,... | collective-permute-start | bytes 344072 | tf_op jit(solution)/shard_map/ppermute | solution.py:553
  29.2 2.4 %collective-permute-start.1 = (bf16[16,64,128]{2,1,0:T(8,128)(2,1)S(1)}, bf16[16,64,128]{2,1,0:T(8,128)(2,1)S(1)}, u32[]{:S(2)}, u32[]{:S(2)}) collective-permute-start(bf16[16,64,128]{2,1,0:T(8,128)(2,1)S(1)} %join.1), channel_id=1, source_target_pairs={{0,16},{1,17},{2,18},{3,19},{4,20},{5,21},{6,22},{7,23},{8,24},{9,... | collective-permute-start | bytes 786440 | tf_op jit(solution)/shard_map/ppermute | solution.py:580
  31.6 13.9 %copy-start = (bf16[1024,1024]{1,0:T(8,128)(2,1)S(1)}, bf16[1024,1024]{1,0:T(8,128)(2,1)}, u32[]{:S(2)}) copy-start(bf16[1024,1024]{1,0:T(8,128)(2,1)} %w_ref.1) | copy-start | bytes 6291460

commit v8 on v7

--- a/solution.py
+++ b/solution.py
@@ -241,7 +241,7 @@
 
 
 def project(plan, consts, slide, w_in, w_bcd, tissue, dt_bias, rate_x, rate_y):
-    chunks = 4
+    chunks = 2
     tile = plan.width // chunks
     depth = slide.shape[2]
     args = [dt_bias, rate_x, rate_y, slide, w_in, w_bcd.T, tissue.T, consts["lanei"], consts["lanej"]]
@@ -442,11 +442,39 @@
     return ends
 
 
-def last_kernel(plan, axis, pay_ref, last_ref, dts, inner, kept):
+def last_kernel(plan, axis, pay_ref, last_ref, dts, inner):
     @pl.when(lax.axis_index(axis) < (plan.parts - 1) * plan.devices)
     def _():
+        states, tiles, wide = plan.states, plan.devices, 2 * LANES
         load_steps(plan, pay_ref, dts)
-        pack_edges(plan, last_ref, scan_edges(plan, pay_ref, dts, inner, kept, lambda w, held, product: None))
+        i, j, real = places(plan, (wide, wide), 0)
+        ti, tj, treal = places(plan, (wide, wide), 1)
+        same = (i == ti) & real & treal
+        ti, _, treal = places(plan, (plan.rows, wide), 1)
+        rowsel = ones((ti == lax.broadcasted_iota(jnp.int32, (plan.rows, wide), 0)) & treal)
+        low = dts[...].astype(BF16)
+        rest, whole = mm(low, ones(same & (j > tj))), mm(low, ones(same))
+        left = []
+        for s in range(plan.slots):
+            after = jnp.zeros((1, wide), F32)
+            rows = []
+            for t in reversed(range(tiles)):
+                rows.append(after)
+                after = after + whole[s * tiles + t : s * tiles + t + 1]
+            left += rows[::-1]
+        inner[...] = jnp.exp(-slot_rates(plan, pay_ref, 0) * (rest + jnp.concatenate(left, axis=0))) * dts[...]
+        ends = []
+        for s in range(plan.slots):
+            held = None
+            for t in range(tiles):
+                w = s * tiles + t
+                b = wide_rows(pay_ref, t, plan.at_bc, states, plan.bc).astype(F32)
+                bd = (b * inner[w : w + 1, :]).astype(BF16)
+                left = jnp.concatenate([bd * rowsel[i : i + 1] for i in range(plan.rows)], axis=0)
+                part = nt_dot(turned(plan, pay_ref, t, s), left)
+                held = part if held is None else held + part
+            ends.append(held)
+        pack_edges(plan, last_ref, ends)
 
 
 def maps_kernel(
@@ -549,7 +577,7 @@
     steps = [((work, wide), F32), ((work, wide), F32), ((work, plan.edge), F32)]
     shape = (plan.packed, HALF, LANES)
     if plan.parts > 1:
-        last = call(functools.partial(last_kernel, plan, col_axis), "last", [pay], [(shape, BF16)], steps)[0]
+        last = call(functools.partial(last_kernel, plan, col_axis), "last", [pay], [(shape, BF16)], steps[:2])[0]
         entry = lax.ppermute(last, col_axis, [(k, k + plan.devices) for k in range(plan.devices)])
     else:
         entry = jnp.zeros(shape, BF16)
@@ -603,9 +631,8 @@
     slot, slots = plan.slot, plan.slots
     per = LANES // slot
     lane = lax.broadcasted_iota(jnp.int32, (half, LANES), 1)
-    copies = []
-    for k, (lo, hi) in enumerate(((0, half), (half, cells))):
-        for block in range(plan.width // LANES):
+    for block in range(plan.width // LANES):
+        for k, (lo, hi) in enumerate(((0, half), (half, cells))):
             joined = None
             for d in range(per):
                 at = block * per + d
@@ -614,17 +641,21 @@
                 if shift:
                     part = pltpu.roll(part, shift, 1)
                 joined = part if joined is None else jnp.where(lane < d * slot, joined, part)
-            full_ref[lo:hi, block * LANES : (block + 1) * LANES] = joined[: hi - lo]
-        y = full_ref[lo:hi, :] + own_ref[lo:hi, :].astype(F32)
-        y = y.astype(BF16).astype(F32)
-        gated = y * gate_ref[lo:hi, :].astype(F32)
-        scale = lax.rsqrt(jnp.mean(gated * gated, axis=-1, keepdims=True) + norm_eps)
-        normed = (gated * scale * gain_ref[...]).astype(BF16)
-        full_ref[lo:hi, :] = mm(normed, w_ref[...])
-        first, last = lo // plan.col_pad, hi // plan.col_pad
-        for i in range(first, last):
-            out_ref[i] = full_ref[i * plan.col_pad : i * plan.col_pad + plan.cols, :].astype(BF16)
-        copies.append(pltpu.make_async_copy(out_ref.at[first:last], out_hbm.at[first:last], sems.at[k]))
+            at = slice(block * LANES, (block + 1) * LANES)
+            y = joined[: hi - lo] + own_ref[lo:hi, at].astype(F32)
+            full_ref[lo:hi, at] = y.astype(BF16).astype(F32) * gate_ref[lo:hi, at].astype(F32)
+    gated = full_ref[...]
+    scale = lax.rsqrt(jnp.mean(gated * gated, axis=-1, keepdims=True) + norm_eps)
+    normed = (gated * scale * gain_ref[...]).astype(BF16)
+    copies = []
+    chunks = sems.shape[0]
+    tile = w_ref.shape[1] // chunks
+    for k in range(chunks):
+        at = slice(k * tile, (k + 1) * tile)
+        out = mm(normed, w_ref[:, at])
+        for i in range(plan.rows):
+            out_ref[i, :, at] = out[i * plan.col_pad : i * plan.col_pad + plan.cols].astype(BF16)
+        copies.append(pltpu.make_async_copy(out_ref.at[:, :, at], out_hbm.at[:, :, at], sems.at[k]))
         copies[-1].start()
     for copy in copies:
         copy.wait()
@@ -639,7 +670,7 @@
         "finish",
         args,
         [(shape, BF16)],
-        [((plan.cells, plan.width), F32), (shape, BF16), pltpu.SemaphoreType.DMA((2,))],
+        [((plan.cells, plan.width), F32), (shape, BF16), pltpu.SemaphoreType.DMA((4,))],
         [HBM],
     )[0]
 

time: 47.8 us -> 46.8 us (0.979)
  Pallas kernels: 20.1 us -> 19.2 us
    pallas_call x1, Pallas kernels: 4.23 us -> 3.37 us  [project(): pl.pallas_call(functools.partial(project_kernel, plan, chunks), grid=(1,)...]
where the time goes in v8:
time: 46.8 us; the launch traced here: 46.4 us
  Pallas kernels  19.2 us (41%)
  blocking collectives  13.4 us (29%)
  starting transfers between devices  10.6 us (23%)
  waiting for transfers between devices  3.18 us (7%)
    all_to_all x1, blocking collectives, per_device(): y = lax.all_to_all(y, 'col', 0, 0, tiled=True, axis_index_groups=groups)  13.4 us
    pallas_call x6, Pallas kernels, call(): pl.pallas_call(kernel, grid=(1,), in_specs=[full(x.shape) for x in args],...  9.03 us
    pallas_call x1, Pallas kernels, home(): pl.pallas_call(functools.partial(home_kernel, plan), grid=(1,), in_specs=...  6.8 us
    all_to_all x1, starting transfers between devices, per_device(): pay = lax.all_to_all(pay, 'col', 0, 0, tiled=True, axis_index_groups=groups)  6.22 us
    pallas_call x1, Pallas kernels, project(): pl.pallas_call(functools.partial(project_kernel, plan, chunks), grid=(1,)...  3.37 us
    all_to_all x1, waiting for transfers between devices, per_device(): pay = lax.all_to_all(pay, 'col', 0, 0, tiled=True, axis_index_groups=groups)  3.08 us
    ppermute x1, starting transfers between devices, scan_calls(): lax.ppermute(last, col_axis, [(k, k + plan.devices) for k in range(plan.d...  3.04 us
    ppermute x1, starting transfers between devices, scan_calls(): entry = lax.ppermute(tops, row_axis, chain)  1.31 us
  transfers between devices with their start and end apart: 3, of which 2 were waited for; matrix products, arithmetic and copies ran while one was open for 0% of the time, Pallas kernels for 25%

profile of v8, /device:TPU:0, one launch (start us, length us, event | category | flops | bytes accessed | tf_op | source)
XLA Modules:
  0.0 46.4 jit_solution(10216714869937485637)
XLA Ops:
  0.0 3.4 %project.1 = (bf16[256,1024]{1,0:T(8,128)(2,1)S(1)}, bf16[8,296,128]{2,1,0:T(8,128)(2,1)}, f32[48,256]{1,0:T(8,128)S(1)}, bf16[224,1024]{1,0:T(8,128)(2,1)S(1)}) custom-call(f32[16]{0:T(128)} %bias_hbm.1, f32[16]{0:T(128)} %rx_ref.1, f32[16]{0:T(128)} %ry_ref.1, bf16[28,7,1024]{2,1,0:T(8,128)(2,1)} %x_hbm.1, bf16[1024,2048]{1,0:T(8,128)(2,1)} %w_hbm.3, ...), custom_call_target="tpu_custom_call" | custom-call | tf_op jit(solution)/shard_map/project/pallas_call | solution.py:254
  3.4 6.2 %all-to-all-start = ((bf16[8,296,128]{2,1,0:T(8,128)(2,1)}), bf16[8,296,128]{2,1,0:T(8,128)(2,1)S(1)}, u32[]{:S(2)}, u32[]{:S(2)}) async-start(bf16[8,296,128]{2,1,0:T(8,128)(2,1)} %get-tuple-element.24), calls=%async_computation | async-start | bytes 1212416 | tf_op jit(solution)/shard_map/all_to_all | solution.py:687
  9.6 6.8 %home.1 = (bf16[224,1024]{1,0:T(8,128)(2,1)S(1)}, bf16[224,1024]{1,0:T(8,128)(2,1)S(1)}, f32[1,1024]{1,0:T(1,128)S(1)}) custom-call(f32[16]{0:T(128)} %rx_ref.1, f32[16]{0:T(128)} %ry_ref.1, f32[16]{0:T(128)} %skip_ref.1, bf16[1024,2048]{1,0:T(8,128)(2,1)} %w_hbm.3, bf16[256,1024]{1,0:T(8,128)(2,1)S(1)} %get-tuple-element.25.v_ref, ...), custom_call_target="tpu_custom_call" | custom-call | tf_op jit(solution)/shard_map/home/pallas_call | solution.py:325
  16.4 3.1 %all-to-all-done.pay_ref = bf16[8,296,128]{2,1,0:T(8,128)(2,1)S(1)} async-done(((bf16[8,296,128]{2,1,0:T(8,128)(2,1)}), bf16[8,296,128]{2,1,0:T(8,128)(2,1)S(1)}, u32[]{:S(2)}, u32[]{:S(2)}) %all-to-all-start) | async-done | bytes 606240 | tf_op jit(solution)/shard_map/all_to_all | solution.py:687
  19.5 1.4 %last.1 = bf16[7,64,128]{2,1,0:T(8,128)(2,1)S(1)} custom-call(bf16[8,296,128]{2,1,0:T(8,128)(2,1)S(1)} %all-to-all-done.pay_ref), custom_call_target="tpu_custom_call" | custom-call | tf_op jit(solution)/shard_map/last/pallas_call | solution.py:562
  20.9 3.0 %collective-permute-start = (bf16[7,64,128]{2,1,0:T(8,128)(2,1)S(1)}, bf16[7,64,128]{2,1,0:T(8,128)(2,1)S(1)}, u32[]{:S(2)}, u32[]{:S(2)}) collective-permute-start(bf16[7,64,128]{2,1,0:T(8,128)(2,1)S(1)} %last.1), channel_id=1, source_target_pairs={{0,8},{1,9},{2,10},{3,11},{4,12},{5,13},{6,14},{7,15},{16,24},{17,... | collective-permute-start | bytes 344072 | tf_op jit(solution)/shard_map/ppermute | solution.py:581
  24.0 3.9 %maps.1 = (bf16[16,32,256]{2,1,0:T(8,128)(2,1)S(1)}, f32[16,256]{1,0:T(8,128)S(1)}, bf16[16,448,128]{2,1,0:T(8,128)(2,1)S(1)}, f32[16,64,128]{2,1,0:T(8,128)S(1)...) custom-call(bf16[8,296,128]{2,1,0:T(8,128)(2,1)S(1)} %all-to-all-done.pay_ref, ...), custom_call_target="tpu_custom_call" | custom-call | tf_op jit(solution)/shard_map/maps/pallas_call | solution.py:562
  27.9 0.0 collective-permute-done.entry_ref
  27.9 0.5 %join.1 = bf16[16,64,128]{2,1,0:T(8,128)(2,1)S(1)} custom-call(f32[16,448]{1,0:T(8,128)S(1)} %get-tuple-element.33.upto_ref, bf16[7,64,128]{2,1,0:T(8,128)(2,1)S(1)} %collective-permute-done.entry_ref, bf16[16,448,128]{2,1,0:T(8,128)(2,1)S(1)} %get-tuple-element.38.passed_ref, f32[16,64,128]{2,1,0:T(8,128)S(1)} %get-tuple-element.39.top_ref), custom_call_target="tpu_custom_call" | custom-call | tf_op jit(solution)/shard_map/join/pallas_call | solution.py:562
  28.4 1.3 %collective-permute-start.1 = (bf16[16,64,128]{2,1,0:T(8,128)(2,1)S(1)}, bf16[16,64,128]{2,1,0:T(8,128)(2,1)S(1)}, u32[]{:S(2)}, u32[]{:S(2)}) collective-permute-start(bf16[16,64,128]{2,1,0:T(8,128)(2,1)S(1)} %join.1), channel_id=1, source_target_pairs={{0,16},{1,17},{2,18},{3,19},{4,20},{5,21},{6,22},{7,23},{8,24},{9,... | collective-permute-start | bytes 786440 | tf_op jit(solution)/shard_map/ppermute | solution.py:608
  29.7 1.0 %sides.1 = (f32[16,64,256]{2,1,0:T(8,128)S(1)}, bf16[16,128,256]{2,1,0:T(8,128)(2,1)S(1)}) custom-call(bf16[8,296,128]{2,1,0:T(8,128)(2,1)S(1)} %all-to-all-done.pay_ref, bf16[16,64,448]{2,1,0:T(8,128)(2,1)S(1)} %get-tuple-element.32.edge_ref, f32[16,448]{1,0:T(8,128)S(1)} %get-tuple-element.33.upto_ref, ...), custom_call_target="tpu_custom_call" | custom-call | tf_op jit(solution)/shard_map/sides/pallas_call | solution.py:562
  30.7 0.0 copy-start
  30.7 0.1 collective-permute-done.1.top_ref
  30.8 0.4 cells.1
  31.2 13.4 %all_to_all.10.y_ref = bf16[8,224,128]{2,1,0:T(8,128)(2,1)S(1)} all-to-all(bf16[8,224,128]{2,1,0:T(8,128)(2,1)S(1)} %cells.1), channel_id=1, replica_groups={{0,1,2,3,4,5,6,7},{8,9,10,11,12,13,14,15},{16,17,18,19,20,21,22,23},{24..., dimensions={0} | all-to-all | bytes 917504 | tf_op jit(solution)/shard_map/all_to_all | solution.py:692
  44.6 0.0 copy-done
  44.6 1.8 %finish.1 = bf16[28,7,1024]{2,1,0:T(8,128)(2,1)} custom-call(bf16[8,224,128]{2,1,0:T(8,128)(2,1)S(1)} %all_to_all.10.y_ref, bf16[224,1024]{1,0:T(8,128)(2,1)S(1)} %get-tuple-element.40.own_ref, bf16[224,1024]{1,0:T(8,128)(2,1)S(1)} %get-tuple-element.41.gate_ref, f32[1,1024]{1,0:T(1,128)S(1)} %get-tuple-element.42.gain_ref, bf16[1024,1024]{1,0:T(8,128)(2,1)S(1)} %copy-done), custom_call_target="tpu_custom_call" | custom-call | tf_op jit(solution)/shard_map/finish/pallas_call | solution.py:562
Async XLA Ops:
  3.4 16.1 %all-to-all-start = ((bf16[8,296,128]{2,1,0:T(8,128)(2,1)}), bf16[8,296,128]{2,1,0:T(8,128)(2,1)S(1)}, u32[]{:S(2)}, u32[]{:S(2)}) async-start(bf16[8,296,128]{2,1,0:T(8,128)(2,1)} %get-tuple-element.24), calls=%async_computation | async-start | bytes 1212416 | tf_op jit(solution)/shard_map/all_to_all | solution.py:687
  20.9 6.9 %collective-permute-start = (bf16[7,64,128]{2,1,0:T(8,128)(2,1)S(1)}, bf16[7,64,128]{2,1,0:T(8,128)(2,1)S(1)}, u32[]{:S(2)}, u32[]{:S(2)}) collective-permute-start(bf16[7,64,128]{2,1,0:T(8,128)(2,1)S(1)} %last.1), channel_id=1, source_target_pairs={{0,8},{1,9},{2,10},{3,11},{4,12},{5,13},{6,14},{7,15},{16,24},{17,... | collective-permute-start | bytes 344072 | tf_op jit(solution)/shard_map/ppermute | solution.py:581
  28.4 2.4 %collective-permute-start.1 = (bf16[16,64,128]{2,1,0:T(8,128)(2,1)S(1)}, bf16[16,64,128]{2,1,0:T(8,128)(2,1)S(1)}, u32[]{:S(2)}, u32[]{:S(2)}) collective-permute-start(bf16[16,64,128]{2,1,0:T(8,128)(2,1)S(1)} %join.1), channel_id=1, source_target_pairs={{0,16},{1,17},{2,18},{3,19},{4,20},{5,21},{6,22},{7,23},{8,24},{9,... | collective-permute-start | bytes 786440 | tf_op jit(solution)/shard_map/ppermute | solution.py:608
  30.7 13.9 %copy-start = (bf16[1024,1024]{1,0:T(8,128)(2,1)S(1)}, bf16[1024,1024]{1,0:T(8,128)(2,1)}, u32[]{:S(2)}) copy-start(bf16[1024,1024]{1,0:T(8,128)(2,1)} %w_ref.1) | copy-start | bytes 6291460

commit v9 on v8

--- a/solution.py
+++ b/solution.py
@@ -47,13 +47,14 @@
         self.work = self.slots * self.devices
         self.head_width = width // heads
         self.col_pad = round_up(cols, 8)
-        self.upper = -(-rows // 2)
-        self.half = round_up(self.upper * self.col_pad, 8)
-        self.cells = rows * self.col_pad
+        self.count = rows * cols
+        self.half = self.count // 2 // 8 * 8
+        self.cells = round_up(self.count, 8)
+        self.stride = max(self.half, self.cells - self.half)
         self.edge = rows * states
         self.top = states * self.col_pad
         self.bc = 2 * states
-        self.at_bc = self.slots * self.half
+        self.at_bc = self.slots * self.stride
         self.at_dt = self.at_bc + 2 * self.bc
         self.at_rate = self.at_dt + 2 * self.slots
         self.message = round_up(self.at_rate + 1, 8)
@@ -62,8 +63,7 @@
         self.share = LANES // self.tail if self.tail else 1
         self.packed = self.slots * self.solid + (-(-self.slots // self.share) if self.tail else 0)
         assert self.head_width % self.slot == 0 and self.group % self.slot == 0
-        assert LANES % self.head_width == 0 and self.half <= LANES
-        assert self.cells - self.half <= self.half
+        assert LANES % self.head_width == 0 and self.stride <= LANES
         assert states % 16 == 0 and heads % 8 == 0
 
     def segments(self):
@@ -72,16 +72,15 @@
     def lanes(self):
         at = np.arange(2 * LANES)
         cell = np.where(at < LANES, at, at - LANES + self.half)
-        live = np.where(at < LANES, at < self.half, cell < self.cells)
-        i, j = cell // self.col_pad, cell % self.col_pad
-        return i, j, live & (j < self.cols)
+        live = np.where(at < LANES, at < self.half, cell < self.count)
+        return cell // self.cols, cell % self.cols, live
 
     def constants(self):
         i, j, real = self.lanes()
         both = real[:, None] & real[None]
         cell = np.arange(self.cells)
-        ci, cj = cell // self.col_pad, cell % self.col_pad
-        creal = cj < self.cols
+        ci, cj = cell // self.cols, cell % self.cols
+        creal = cell < self.count
         le = np.arange(round_up(self.rows, 8))
         lj = np.arange(self.col_pad)
         out = {}
@@ -115,14 +114,20 @@
 SMEM = pl.BlockSpec(memory_space=pltpu.SMEM)
 
 
+def split_cell(plan, cell):
+    i = lax.shift_right_logical(cell * (-(-65536 // plan.cols)), 16)
+    return i, cell - i * plan.cols
+
+
 def cell_mask_of(plan, t_ref):
     t = t_ref[...].astype(F32).astype(BF16)
-    cell = lax.broadcasted_iota(jnp.int32, (plan.cells, plan.cols), 0)
-    col = lax.broadcasted_iota(jnp.int32, (plan.cells, plan.cols), 1)
-    pick = (lax.rem(cell, plan.col_pad) == col).astype(F32).astype(BF16)
-    cell = lax.broadcasted_iota(jnp.int32, (plan.cells, plan.rows), 0)
-    row = lax.broadcasted_iota(jnp.int32, (plan.cells, plan.rows), 1)
-    return jnp.sum(jnp.where(lax.div(cell, plan.col_pad) == row, mm(pick, t), 0.0), axis=1, keepdims=True)
+    shape = (plan.cells, plan.cols)
+    _, j = split_cell(plan, lax.broadcasted_iota(jnp.int32, shape, 0))
+    pick = ones(j == lax.broadcasted_iota(jnp.int32, shape, 1))
+    shape = (plan.cells, plan.rows)
+    i, _ = split_cell(plan, lax.broadcasted_iota(jnp.int32, shape, 0))
+    here = i == lax.broadcasted_iota(jnp.int32, shape, 1)
+    return jnp.sum(jnp.where(here, mm(pick, t), 0.0), axis=1, keepdims=True)
 
 
 def rate_row(heads_of, rx_ref, ry_ref):
@@ -166,7 +171,7 @@
 
     loads[0].wait()
     for i in range(plan.rows):
-        wide[i * plan.col_pad : i * plan.col_pad + plan.cols, :] = x_ref[i].astype(F32)
+        wide[i * plan.cols : (i + 1) * plan.cols, :] = x_ref[i].astype(F32)
     x = wide[...].astype(BF16)
     flat_ref[...] = x
     for copy in loads[1:]:
@@ -185,7 +190,7 @@
         )
     else:
         moved = hi
-    table = jnp.concatenate([jnp.where(lane < half, lo, 0.0), jnp.where(lane < rest, moved, 0.0)], axis=1)
+    table = jnp.concatenate([jnp.where(lane < half, lo, 0.0), jnp.where(lane < plan.count - half, moved, 0.0)], axis=1)
     z = table[2 * states :]
     at = lax.broadcasted_iota(jnp.int32, z.shape, 0)
     for h in range(heads):
@@ -196,7 +201,7 @@
     bc = table[: 2 * states]
     steps = rows_ref[2 * states :, :]
 
-    lane = lax.broadcasted_iota(jnp.int32, (half, LANES), 1)
+    lane = lax.broadcasted_iota(jnp.int32, (plan.stride, LANES), 1)
     sent = []
     for chunk in range(chunks):
         copies[chunk].wait()
@@ -214,8 +219,10 @@
                 at = offset % LANES
                 first = v[:half, base : base + LANES]
                 last = v[half:, base : base + LANES]
-                if rest < half:
-                    last = jnp.concatenate([last, jnp.zeros((half - rest, LANES), F32)], axis=0)
+                if half < plan.stride:
+                    first = jnp.concatenate([first, jnp.zeros((plan.stride - half, LANES), F32)], axis=0)
+                if rest < plan.stride:
+                    last = jnp.concatenate([last, jnp.zeros((plan.stride - rest, LANES), F32)], axis=0)
                 if at:
                     first = pltpu.roll(first, LANES - at, 1)
                 if at != HALF:
@@ -223,7 +230,7 @@
                 both = jnp.where(lane < HALF, first, last)
                 if plan.slot < HALF:
                     both = jnp.where(lane % HALF < plan.slot, both, 0.0)
-                pay_ref[dest, s * half : (s + 1) * half, :] = both.astype(BF16)
+                pay_ref[dest, s * plan.stride : (s + 1) * plan.stride, :] = both.astype(BF16)
                 head = (chunk * tile + offset) // plan.head_width
                 heads_of.append(head)
                 dts += [steps[head : head + 1, :LANES], steps[head : head + 1, LANES:]]
@@ -347,11 +354,9 @@
 def places(plan, shape, axis):
     at = lax.broadcasted_iota(jnp.int32, shape, axis)
     late = at >= LANES
-    at = jnp.where(late, at - LANES, at)
-    i = lax.div(at, plan.col_pad)
-    j = at - i * plan.col_pad
-    real = (at < jnp.where(late, plan.cells - plan.half, plan.half)) & (j < plan.cols)
-    return jnp.where(late, i + plan.upper, i), j, real
+    cell = jnp.where(late, at - (LANES - plan.half), at)
+    i, j = split_cell(plan, cell)
+    return i, j, cell < jnp.where(late, plan.count, plan.half)
 
 
 def wide_rows(pay_ref, t, at, count, gap):
@@ -359,9 +364,9 @@
 
 
 def turned(plan, pay_ref, t, s):
-    v = pay_ref[t, s * plan.half : (s + 1) * plan.half, :].astype(F32)
-    if plan.half < LANES:
-        v = jnp.concatenate([v, jnp.zeros((LANES - plan.half, LANES), F32)], axis=0)
+    v = pay_ref[t, s * plan.stride : (s + 1) * plan.stride, :].astype(F32)
+    if plan.stride < LANES:
+        v = jnp.concatenate([v, jnp.zeros((LANES - plan.stride, LANES), F32)], axis=0)
     v = v.T
     return jnp.concatenate([v[:HALF], v[HALF:]], axis=1).astype(BF16)
 
@@ -555,7 +560,7 @@
         t, s = w % plan.devices, w // plan.devices
         y = y_ref[w] + mm(top_ref[w], down_ref[w])
         y = jnp.concatenate([y[:, :LANES], y[:, LANES:]], axis=0).T
-        out_ref[t, s * plan.half : (s + 1) * plan.half, :] = y[: plan.half].astype(BF16)
+        out_ref[t, s * plan.stride : (s + 1) * plan.stride, :] = y[: plan.stride].astype(BF16)
 
 
 def call(kernel, name, args, outs, scratch=(), out_specs=None):
@@ -622,21 +627,21 @@
         functools.partial(cells_kernel, plan),
         "cells",
         [y, down, entry],
-        [((plan.devices, plan.slots * plan.half, LANES), BF16)],
+        [((plan.devices, plan.slots * plan.stride, LANES), BF16)],
     )[0]
 
 
 def finish_kernel(plan, y_ref, own_ref, gate_ref, gain_ref, w_ref, out_hbm, full_ref, out_ref, sems):
-    half, cells = plan.half, plan.cells
+    half, cells, stride = plan.half, plan.cells, plan.stride
     slot, slots = plan.slot, plan.slots
     per = LANES // slot
-    lane = lax.broadcasted_iota(jnp.int32, (half, LANES), 1)
+    lane = lax.broadcasted_iota(jnp.int32, (stride, LANES), 1)
     for block in range(plan.width // LANES):
         for k, (lo, hi) in enumerate(((0, half), (half, cells))):
             joined = None
             for d in range(per):
                 at = block * per + d
-                part = y_ref[at // slots, at % slots * half : (at % slots + 1) * half, :].astype(F32)
+                part = y_ref[at // slots, at % slots * stride : (at % slots + 1) * stride, :].astype(F32)
                 shift = (d * slot - k * HALF) % LANES
                 if shift:
                     part = pltpu.roll(part, shift, 1)
@@ -654,7 +659,7 @@
         at = slice(k * tile, (k + 1) * tile)
         out = mm(normed, w_ref[:, at])
         for i in range(plan.rows):
-            out_ref[i, :, at] = out[i * plan.col_pad : i * plan.col_pad + plan.cols].astype(BF16)
+            out_ref[i, :, at] = out[i * plan.cols : (i + 1) * plan.cols].astype(BF16)
         copies.append(pltpu.make_async_copy(out_ref.at[:, :, at], out_hbm.at[:, :, at], sems.at[k]))
         copies[-1].start()
     for copy in copies:

time: 46.8 us -> 46 us (0.983)
  transfers between devices with their start and end apart: 3 -> 3, of which waited for: 2 -> 2; matrix products, arithmetic and copies ran while one was open for 0% -> 0% of each run, Pallas kernels for 25% -> 26%
where the time goes in v9:
time: 46 us; the launch traced here: 45.7 us
  Pallas kernels  19.2 us (42%)
  blocking collectives  13 us (28%)
  starting transfers between devices  10.6 us (23%)
  waiting for transfers between devices  2.81 us (6%)
    all_to_all x1, blocking collectives, per_device(): y = lax.all_to_all(y, 'col', 0, 0, tiled=True, axis_index_groups=groups)  13 us
    pallas_call x6, Pallas kernels, call(): pl.pallas_call(kernel, grid=(1,), in_specs=[full(x.shape) for x in args],...  9 us
    pallas_call x1, Pallas kernels, home(): pl.pallas_call(functools.partial(home_kernel, plan), grid=(1,), in_specs=...  6.85 us
    all_to_all x1, starting transfers between devices, per_device(): pay = lax.all_to_all(pay, 'col', 0, 0, tiled=True, axis_index_groups=groups)  6.22 us
    pallas_call x1, Pallas kernels, project(): pl.pallas_call(functools.partial(project_kernel, plan, chunks), grid=(1,)...  3.35 us
    ppermute x1, starting transfers between devices, scan_calls(): lax.ppermute(last, col_axis, [(k, k + plan.devices) for k in range(plan.d...  3.04 us
    all_to_all x1, waiting for transfers between devices, per_device(): pay = lax.all_to_all(pay, 'col', 0, 0, tiled=True, axis_index_groups=groups)  2.71 us
    ppermute x1, starting transfers between devices, scan_calls(): entry = lax.ppermute(tops, row_axis, chain)  1.31 us
  transfers between devices with their start and end apart: 3, of which 2 were waited for; matrix products, arithmetic and copies ran while one was open for 0% of the time, Pallas kernels for 26%

profile of v9, /device:TPU:0, one launch (start us, length us, event | category | flops | bytes accessed | tf_op | source)
XLA Modules:
  0.0 45.7 jit_solution(15540153369524019460)
XLA Ops:
  0.0 3.3 %project.1 = (bf16[256,1024]{1,0:T(8,128)(2,1)S(1)}, bf16[8,280,128]{2,1,0:T(8,128)(2,1)}, f32[48,256]{1,0:T(8,128)S(1)}, bf16[200,1024]{1,0:T(8,128)(2,1)S(1)}) custom-call(f32[16]{0:T(128)} %bias_hbm.1, f32[16]{0:T(128)} %rx_ref.1, f32[16]{0:T(128)} %ry_ref.1, bf16[28,7,1024]{2,1,0:T(8,128)(2,1)} %x_hbm.1, bf16[1024,2048]{1,0:T(8,128)(2,1)} %w_hbm.3, ...), custom_call_target="tpu_custom_call" | custom-call | tf_op jit(solution)/shard_map/project/pallas_call | solution.py:261
  3.4 6.2 %all-to-all-start = ((bf16[8,280,128]{2,1,0:T(8,128)(2,1)}), bf16[8,280,128]{2,1,0:T(8,128)(2,1)S(1)}, u32[]{:S(2)}, u32[]{:S(2)}) async-start(bf16[8,280,128]{2,1,0:T(8,128)(2,1)} %get-tuple-element.24), calls=%async_computation | async-start | bytes 1146880 | tf_op jit(solution)/shard_map/all_to_all | solution.py:692
  9.6 6.9 %home.1 = (bf16[200,1024]{1,0:T(8,128)(2,1)S(1)}, bf16[200,1024]{1,0:T(8,128)(2,1)S(1)}, f32[1,1024]{1,0:T(1,128)S(1)}) custom-call(f32[16]{0:T(128)} %rx_ref.1, f32[16]{0:T(128)} %ry_ref.1, f32[16]{0:T(128)} %skip_ref.1, bf16[1024,2048]{1,0:T(8,128)(2,1)} %w_hbm.3, bf16[256,1024]{1,0:T(8,128)(2,1)S(1)} %get-tuple-element.25.v_ref, ...), custom_call_target="tpu_custom_call" | custom-call | tf_op jit(solution)/shard_map/home/pallas_call | solution.py:332
  16.4 2.7 %all-to-all-done.pay_ref = bf16[8,280,128]{2,1,0:T(8,128)(2,1)S(1)} async-done(((bf16[8,280,128]{2,1,0:T(8,128)(2,1)}), bf16[8,280,128]{2,1,0:T(8,128)(2,1)S(1)}, u32[]{:S(2)}, u32[]{:S(2)}) %all-to-all-start) | async-done | bytes 573472 | tf_op jit(solution)/shard_map/all_to_all | solution.py:692
  19.2 1.4 %last.1 = bf16[7,64,128]{2,1,0:T(8,128)(2,1)S(1)} custom-call(bf16[8,280,128]{2,1,0:T(8,128)(2,1)S(1)} %all-to-all-done.pay_ref), custom_call_target="tpu_custom_call" | custom-call | tf_op jit(solution)/shard_map/last/pallas_call | solution.py:567
  20.6 3.0 %collective-permute-start = (bf16[7,64,128]{2,1,0:T(8,128)(2,1)S(1)}, bf16[7,64,128]{2,1,0:T(8,128)(2,1)S(1)}, u32[]{:S(2)}, u32[]{:S(2)}) collective-permute-start(bf16[7,64,128]{2,1,0:T(8,128)(2,1)S(1)} %last.1), channel_id=1, source_target_pairs={{0,8},{1,9},{2,10},{3,11},{4,12},{5,13},{6,14},{7,15},{16,24},{17,... | collective-permute-start | bytes 344072 | tf_op jit(solution)/shard_map/ppermute | solution.py:586
  23.7 3.9 %maps.1 = (bf16[16,32,256]{2,1,0:T(8,128)(2,1)S(1)}, f32[16,256]{1,0:T(8,128)S(1)}, bf16[16,448,128]{2,1,0:T(8,128)(2,1)S(1)}, f32[16,64,128]{2,1,0:T(8,128)S(1)...) custom-call(bf16[8,280,128]{2,1,0:T(8,128)(2,1)S(1)} %all-to-all-done.pay_ref, ...), custom_call_target="tpu_custom_call" | custom-call | tf_op jit(solution)/shard_map/maps/pallas_call | solution.py:567
  27.6 0.0 collective-permute-done.entry_ref
  27.6 0.5 %join.1 = bf16[16,64,128]{2,1,0:T(8,128)(2,1)S(1)} custom-call(f32[16,448]{1,0:T(8,128)S(1)} %get-tuple-element.33.upto_ref, bf16[7,64,128]{2,1,0:T(8,128)(2,1)S(1)} %collective-permute-done.entry_ref, bf16[16,448,128]{2,1,0:T(8,128)(2,1)S(1)} %get-tuple-element.38.passed_ref, f32[16,64,128]{2,1,0:T(8,128)S(1)} %get-tuple-element.39.top_ref), custom_call_target="tpu_custom_call" | custom-call | tf_op jit(solution)/shard_map/join/pallas_call | solution.py:567
  28.1 1.3 %collective-permute-start.1 = (bf16[16,64,128]{2,1,0:T(8,128)(2,1)S(1)}, bf16[16,64,128]{2,1,0:T(8,128)(2,1)S(1)}, u32[]{:S(2)}, u32[]{:S(2)}) collective-permute-start(bf16[16,64,128]{2,1,0:T(8,128)(2,1)S(1)} %join.1), channel_id=1, source_target_pairs={{0,16},{1,17},{2,18},{3,19},{4,20},{5,21},{6,22},{7,23},{8,24},{9,... | collective-permute-start | bytes 786440 | tf_op jit(solution)/shard_map/ppermute | solution.py:613
  29.4 1.0 %sides.1 = (f32[16,64,256]{2,1,0:T(8,128)S(1)}, bf16[16,128,256]{2,1,0:T(8,128)(2,1)S(1)}) custom-call(bf16[8,280,128]{2,1,0:T(8,128)(2,1)S(1)} %all-to-all-done.pay_ref, bf16[16,64,448]{2,1,0:T(8,128)(2,1)S(1)} %get-tuple-element.32.edge_ref, f32[16,448]{1,0:T(8,128)S(1)} %get-tuple-element.33.upto_ref, ...), custom_call_target="tpu_custom_call" | custom-call | tf_op jit(solution)/shard_map/sides/pallas_call | solution.py:567
  30.4 0.0 copy-start
  30.4 0.1 collective-permute-done.1.top_ref
  30.5 0.4 cells.1
  30.9 13.0 %all_to_all.10.y_ref = bf16[8,208,128]{2,1,0:T(8,128)(2,1)S(1)} all-to-all(bf16[8,208,128]{2,1,0:T(8,128)(2,1)S(1)} %cells.1), channel_id=1, replica_groups={{0,1,2,3,4,5,6,7},{8,9,10,11,12,13,14,15},{16,17,18,19,20,21,22,23},{24..., dimensions={0} | all-to-all | bytes 851968 | tf_op jit(solution)/shard_map/all_to_all | solution.py:697
  43.9 0.0 copy-done
  43.9 1.8 %finish.1 = bf16[28,7,1024]{2,1,0:T(8,128)(2,1)} custom-call(bf16[8,208,128]{2,1,0:T(8,128)(2,1)S(1)} %all_to_all.10.y_ref, bf16[200,1024]{1,0:T(8,128)(2,1)S(1)} %get-tuple-element.40.own_ref, bf16[200,1024]{1,0:T(8,128)(2,1)S(1)} %get-tuple-element.41.gate_ref, f32[1,1024]{1,0:T(1,128)S(1)} %get-tuple-element.42.gain_ref, bf16[1024,1024]{1,0:T(8,128)(2,1)S(1)} %copy-done), custom_call_target="tpu_custom_call" | custom-call | tf_op jit(solution)/shard_map/finish/pallas_call | solution.py:567
Async XLA Ops:
  3.4 15.8 %all-to-all-start = ((bf16[8,280,128]{2,1,0:T(8,128)(2,1)}), bf16[8,280,128]{2,1,0:T(8,128)(2,1)S(1)}, u32[]{:S(2)}, u32[]{:S(2)}) async-start(bf16[8,280,128]{2,1,0:T(8,128)(2,1)} %get-tuple-element.24), calls=%async_computation | async-start | bytes 1146880 | tf_op jit(solution)/shard_map/all_to_all | solution.py:692
  20.6 7.0 %collective-permute-start = (bf16[7,64,128]{2,1,0:T(8,128)(2,1)S(1)}, bf16[7,64,128]{2,1,0:T(8,128)(2,1)S(1)}, u32[]{:S(2)}, u32[]{:S(2)}) collective-permute-start(bf16[7,64,128]{2,1,0:T(8,128)(2,1)S(1)} %last.1), channel_id=1, source_target_pairs={{0,8},{1,9},{2,10},{3,11},{4,12},{5,13},{6,14},{7,15},{16,24},{17,... | collective-permute-start | bytes 344072 | tf_op jit(solution)/shard_map/ppermute | solution.py:586
  28.1 2.4 %collective-permute-start.1 = (bf16[16,64,128]{2,1,0:T(8,128)(2,1)S(1)}, bf16[16,64,128]{2,1,0:T(8,128)(2,1)S(1)}, u32[]{:S(2)}, u32[]{:S(2)}) collective-permute-start(bf16[16,64,128]{2,1,0:T(8,128)(2,1)S(1)} %join.1), channel_id=1, source_target_pairs={{0,16},{1,17},{2,18},{3,19},{4,20},{5,21},{6,22},{7,23},{8,24},{9,... | collective-permute-start | bytes 786440 | tf_op jit(solution)/shard_map/ppermute | solution.py:613
  30.4 13.5 %copy-start = (bf16[1024,1024]{1,0:T(8,128)(2,1)S(1)}, bf16[1024,1024]{1,0:T(8,128)(2,1)}, u32[]{:S(2)}) copy-start(bf16[1024,1024]{1,0:T(8,128)(2,1)} %w_ref.1) | copy-start | bytes 6291460

commit v10 on v9

--- a/solution.py
+++ b/solution.py
@@ -482,20 +482,25 @@
         pack_edges(plan, last_ref, ends)
 
 
+def scan_kernel(plan, pay_ref, last_ref, edge_ref, upto_ref, again_ref, dts, inner, kept):
+    again_ref[...] = last_ref[...]
+    load_steps(plan, pay_ref, dts)
+
+    def seen(w, held, product):
+        edge_ref[w] = held.astype(BF16)
+        upto_ref[w : w + 1, :] = product
+
+    scan_edges(plan, pay_ref, dts, inner, kept, seen)
+
+
 def maps_kernel(
-    plan, pay_ref, to1_ref, to2_ref, from1_ref, from2_ref, side1_ref, side2_ref,
+    plan, pay_ref, edge_ref, to1_ref, to2_ref, from1_ref, from2_ref, side1_ref, side2_ref,
     sidemask_ref, down1_ref, down2_ref, downmask_ref, pick_ref,
-    side_ref, above_ref, passed_ref, top_ref, edge_ref, upto_ref, dts, inner, kept, s1, s2, d1, d2,
+    side_ref, above_ref, passed_ref, top_ref, dts, s1, s2, d1, d2,
 ):
     states, tiles, cp, work = plan.states, plan.devices, plan.col_pad, plan.work
     rp = side1_ref.shape[0]
     load_steps(plan, pay_ref, dts)
-
-    def seen(w, held, product):
-        edge_ref[w] = held.astype(BF16)
-        upto_ref[w : w + 1, :] = product
-
-    scan_edges(plan, pay_ref, dts, inner, kept, seen)
     low = dts[...].astype(BF16)
     above_ref[...] = jnp.exp(-slot_rates(plan, pay_ref, 1) * mm(low, to2_ref[...]))
     rates_x, rates_y = rates_of(plan, pay_ref, 0), rates_of(plan, pay_ref, 1)
@@ -537,13 +542,13 @@
             out_ref[w] = (top_ref[w] + mm(late, passed_ref[w])).astype(BF16)
 
 
-def sides_kernel(plan, pay_ref, edge_ref, upto_ref, entry_ref, side_ref, above_ref, y_ref, down_ref):
+def sides_kernel(plan, pay_ref, edge_ref, upto_ref, first_ref, second_ref, side_ref, above_ref, y_ref, down_ref):
     states, tiles = plan.states, plan.devices
     shape = (plan.col_pad, 2 * LANES)
     _, tj, treal = places(plan, shape, 1)
     colsel = jnp.where((tj == lax.broadcasted_iota(jnp.int32, shape, 0)) & treal, 1.0, 0.0)
     for s in range(plan.slots):
-        entry = unpack_edges(plan, entry_ref, s)
+        entry = unpack_edges(plan, first_ref, s) + unpack_edges(plan, second_ref, s)
         for t in range(tiles):
             w = s * tiles + t
             c = wide_rows(pay_ref, t, plan.at_bc + states, states, plan.bc)
@@ -563,7 +568,7 @@
         out_ref[t, s * plan.stride : (s + 1) * plan.stride, :] = y[: plan.stride].astype(BF16)
 
 
-def call(kernel, name, args, outs, scratch=(), out_specs=None):
+def call(kernel, args, outs, scratch=(), out_specs=None):
     return pl.pallas_call(
         kernel,
         grid=(1,),
@@ -572,7 +577,6 @@
         out_shape=[jax.ShapeDtypeStruct(s, d) for s, d in outs],
         scratch_shapes=[x if not isinstance(x, tuple) else pltpu.VMEM(*x) for x in scratch],
         compiler_params=pltpu.CompilerParams(vmem_limit_bytes=24 * 2**20),
-        name=name,
     )(*args)
 
 
@@ -581,34 +585,40 @@
     rp = consts["side1"].shape[0]
     steps = [((work, wide), F32), ((work, wide), F32), ((work, plan.edge), F32)]
     shape = (plan.packed, HALF, LANES)
+    count, across = lax.axis_size(row_axis), plan.parts * plan.devices
+    axes = (row_axis, col_axis)
+    hops = [[(r * across + k, r * across + k + plan.devices) for k in range(plan.devices)] for r in range(count)]
+    early, late = hops[:-1], hops[-1:]
+    if count > 2:
+        early, late = hops, []
     if plan.parts > 1:
-        last = call(functools.partial(last_kernel, plan, col_axis), "last", [pay], [(shape, BF16)], steps[:2])[0]
-        entry = lax.ppermute(last, col_axis, [(k, k + plan.devices) for k in range(plan.devices)])
+        last = call(functools.partial(last_kernel, plan, col_axis), [pay], [(shape, BF16)], steps[:2])[0]
+        first = lax.ppermute(last, axes, sum(early, []))
     else:
-        entry = jnp.zeros(shape, BF16)
+        last = first = jnp.zeros(shape, BF16)
+    edges, upto, again = call(
+        functools.partial(scan_kernel, plan),
+        [pay, last],
+        [((work, HALF, plan.edge), BF16), ((work, plan.edge), F32), (shape, BF16)],
+        steps,
+    )
+    if plan.parts > 1 and late:
+        second = lax.ppermute(again, axes, sum(late, []))
+    else:
+        second = jnp.zeros(shape, BF16)
     names = ("to1", "to2", "from1", "from2", "side1", "side2", "sidemask", "down1", "down2", "downmask", "pick")
-    side, above, passed, tops, edges, upto = call(
+    side, above, passed, tops = call(
         functools.partial(maps_kernel, plan),
-        "maps",
-        [pay] + [consts[k] for k in names],
+        [pay, edges] + [consts[k] for k in names],
         [
             ((work, rp, wide), BF16),
             ((work, wide), F32),
             ((work, plan.edge, plan.top), BF16),
             ((work, HALF, plan.top), F32),
-            ((work, HALF, plan.edge), BF16),
-            ((work, plan.edge), F32),
         ],
-        steps + [((work * rp, wide), F32)] * 2 + [((work * cp, wide), F32)] * 2,
+        [((work, wide), F32)] + [((work * rp, wide), F32)] * 2 + [((work * cp, wide), F32)] * 2,
     )
-    edge_entry = entry
-    tops = call(
-        functools.partial(join_kernel, plan),
-        "join",
-        [upto, entry, passed, tops],
-        [((work, HALF, plan.top), BF16)],
-    )[0]
-    count = lax.axis_size(row_axis)
+    tops = call(functools.partial(join_kernel, plan), [upto, first, passed, tops], [((work, HALF, plan.top), BF16)])[0]
     chain = [(r, r + 1) for r in range(count - 1)]
     entry = lax.ppermute(tops, row_axis, chain)
     if count > 2:
@@ -619,13 +629,11 @@
             )
     y, down = call(
         functools.partial(sides_kernel, plan),
-        "sides",
-        [pay, edges, upto, edge_entry, side, above],
+        [pay, edges, upto, first, second, side, above],
         [((work, HALF, wide), F32), ((work, plan.top, wide), BF16)],
     )
     return call(
         functools.partial(cells_kernel, plan),
-        "cells",
         [y, down, entry],
         [((plan.devices, plan.slots * plan.stride, LANES), BF16)],
     )[0]
@@ -672,7 +680,6 @@
     assert w_out.shape[1] == plan.width
     return call(
         functools.partial(finish_kernel, plan),
-        "finish",
         args,
         [(shape, BF16)],
         [((plan.cells, plan.width), F32), (shape, BF16), pltpu.SemaphoreType.DMA((4,))],
@@ -681,7 +688,7 @@
 
 
 def per_device(slide, tissue, w_in, w_bcd, dt_bias, rate_x, rate_y, d_skip, norm_gain, w_out):
-    rows, cols, model_width = slide.shape
+    rows, cols, _ = slide.shape
     width = w_out.shape[0]
     heads = dt_bias.shape[0]
     states = (w_bcd.shape[1] - heads) // 2

time: 46 us -> 45.6 us (level)
  the two profiles are of different devices: /device:TPU:0 before, /device:TPU:1 now
where the time goes in v10:
time: 45.6 us; the launch traced here: 45.2 us
  Pallas kernels  19.3 us (42%)
  blocking collectives  12.5 us (27%)
  starting transfers between devices  10 us (22%)
  waiting for transfers between devices  3.24 us (7%)
    all_to_all x1, blocking collectives, per_device(): y = lax.all_to_all(y, 'col', 0, 0, tiled=True, axis_index_groups=groups)  12.5 us
    pallas_call x7, Pallas kernels, call(): pl.pallas_call(kernel, grid=(1,), in_specs=[full(x.shape) for x in args],...  9.12 us
    pallas_call x1, Pallas kernels, home(): pl.pallas_call(functools.partial(home_kernel, plan), grid=(1,), in_specs=...  6.85 us
    all_to_all x1, starting transfers between devices, per_device(): pay = lax.all_to_all(pay, 'col', 0, 0, tiled=True, axis_index_groups=groups)  5.28 us
    pallas_call x1, Pallas kernels, project(): pl.pallas_call(functools.partial(project_kernel, plan, chunks), grid=(1,)...  3.35 us
    ppermute x1, starting transfers between devices, scan_calls(): second = lax.ppermute(again, axes, sum(late, []))  2.77 us
    ppermute x1, waiting for transfers between devices, scan_calls(): second = lax.ppermute(again, axes, sum(late, []))  1.77 us
    all_to_all x1, waiting for transfers between devices, per_device(): pay = lax.all_to_all(pay, 'col', 0, 0, tiled=True, axis_index_groups=groups)  1.32 us
  transfers between devices with their start and end apart: 4, of which 3 were waited for; matrix products, arithmetic and copies ran while one was open for 0% of the time, Pallas kernels for 26%

profile of v10, /device:TPU:1, one launch (start us, length us, event | category | flops | bytes accessed | tf_op | source)
XLA Modules:
  0.0 45.2 jit_solution(12914555831429831567)
XLA Ops:
  0.0 3.4 %project.1 = (bf16[256,1024]{1,0:T(8,128)(2,1)S(1)}, bf16[8,280,128]{2,1,0:T(8,128)(2,1)}, f32[48,256]{1,0:T(8,128)S(1)}, bf16[200,1024]{1,0:T(8,128)(2,1)S(1)}) custom-call(f32[16]{0:T(128)} %bias_hbm.1, f32[16]{0:T(128)} %rx_ref.1, f32[16]{0:T(128)} %ry_ref.1, bf16[28,7,1024]{2,1,0:T(8,128)(2,1)} %x_hbm.1, bf16[1024,2048]{1,0:T(8,128)(2,1)} %w_hbm.3, ...), custom_call_target="tpu_custom_call" | custom-call | tf_op jit(solution)/shard_map/project/pallas_call | solution.py:261
  3.4 5.3 %all-to-all-start = ((bf16[8,280,128]{2,1,0:T(8,128)(2,1)}), bf16[8,280,128]{2,1,0:T(8,128)(2,1)S(1)}, u32[]{:S(2)}, u32[]{:S(2)}) async-start(bf16[8,280,128]{2,1,0:T(8,128)(2,1)} %get-tuple-element.25), calls=%async_computation | async-start | bytes 1146880 | tf_op jit(solution)/shard_map/all_to_all | solution.py:699
  8.6 6.9 %home.1 = (bf16[200,1024]{1,0:T(8,128)(2,1)S(1)}, bf16[200,1024]{1,0:T(8,128)(2,1)S(1)}, f32[1,1024]{1,0:T(1,128)S(1)}) custom-call(f32[16]{0:T(128)} %rx_ref.1, f32[16]{0:T(128)} %ry_ref.1, f32[16]{0:T(128)} %skip_ref.1, bf16[1024,2048]{1,0:T(8,128)(2,1)} %w_hbm.3, bf16[256,1024]{1,0:T(8,128)(2,1)S(1)} %get-tuple-element.26.v_ref, ...), custom_call_target="tpu_custom_call" | custom-call | tf_op jit(solution)/shard_map/home/pallas_call | solution.py:332
  15.5 1.3 %all-to-all-done.pay_ref = bf16[8,280,128]{2,1,0:T(8,128)(2,1)S(1)} async-done(((bf16[8,280,128]{2,1,0:T(8,128)(2,1)}), bf16[8,280,128]{2,1,0:T(8,128)(2,1)S(1)}, u32[]{:S(2)}, u32[]{:S(2)}) %all-to-all-start) | async-done | bytes 573472 | tf_op jit(solution)/shard_map/all_to_all | solution.py:699
  16.8 1.4 %shard_map.244.last_ref = bf16[7,64,128]{2,1,0:T(8,128)(2,1)S(1)} custom-call(bf16[8,280,128]{2,1,0:T(8,128)(2,1)S(1)} %all-to-all-done.pay_ref), custom_call_target="tpu_custom_call" | custom-call | tf_op jit(solution)/shard_map/pallas_call | solution.py:572
  18.3 0.7 %collective-permute-start = (bf16[7,64,128]{2,1,0:T(8,128)(2,1)S(1)}, bf16[7,64,128]{2,1,0:T(8,128)(2,1)S(1)}, u32[]{:S(2)}, u32[]{:S(2)}) collective-permute-start(bf16[7,64,128]{2,1,0:T(8,128)(2,1)S(1)} %shard_map.244.last_ref), channel_id=1, source_target_pairs={{0,8},{1,9},{2,10},{3,11},{4,12},{5,13},{6,14},{7,15}} | collective-permute-start | bytes 344072 | tf_op jit(solution)/shard_map/ppermute | solution.py:596
  18.9 1.3 %shard_map.245 = (bf16[16,64,448]{2,1,0:T(8,128)(2,1)S(1)}, f32[16,448]{1,0:T(8,128)S(1)}, bf16[7,64,128]{2,1,0:T(8,128)(2,1)S(1)}) custom-call(bf16[8,280,128]{2,1,0:T(8,128)(2,1)S(1)} %all-to-all-done.pay_ref, bf16[7,64,128]{2,1,0:T(8,128)(2,1)S(1)} %shard_map.244.last_ref), custom_call_target="tpu_custom_call" | custom-call | tf_op jit(solution)/shard_map/pallas_call | solution.py:572
  20.2 2.8 %shard_map.246 = (bf16[16,32,256]{2,1,0:T(8,128)(2,1)S(1)}, f32[16,256]{1,0:T(8,128)S(1)}, bf16[16,448,128]{2,1,0:T(8,128)(2,1)S(1)}, f32[16,64,128]{2,1,0:T(8,128)S(1)}) custom-call(bf16[8,280,128]{2,1,0:T(8,128)(2,1)S(1)} %all-to-all-done.pay_ref, bf16[16,64,448]{2,1,0:T(8,128)(2,1)S(1)} %get-tuple-element.33.edge_ref, ...), custom_call_target="tpu_custom_call" | custom-call | tf_op jit(solution)/shard_map/pallas_call | solution.py:572
  23.0 0.0 collective-permute-done.first_ref.entry_ref
  23.0 0.5 %shard_map.248 = bf16[16,64,128]{2,1,0:T(8,128)(2,1)S(1)} custom-call(f32[16,448]{1,0:T(8,128)S(1)} %get-tuple-element.34.upto_ref, bf16[7,64,128]{2,1,0:T(8,128)(2,1)S(1)} %collective-permute-done.first_ref.entry_ref, bf16[16,448,128]{2,1,0:T(8,128)(2,1)S(1)} %get-tuple-element.40.passed_ref, f32[16,64,128]{2,1,0:T(8,128)S(1)} %get-tuple-element.41.top_ref), custom_call_target="tpu_custom_call" | custom-call | tf_op jit(solution)/shard_map/pallas_call | solution.py:572
  23.5 1.3 %collective-permute-start.2 = (bf16[16,64,128]{2,1,0:T(8,128)(2,1)S(1)}, bf16[16,64,128]{2,1,0:T(8,128)(2,1)S(1)}, u32[]{:S(2)}, u32[]{:S(2)}) collective-permute-start(bf16[16,64,128]{2,1,0:T(8,128)(2,1)S(1)} %shard_map.248), channel_id=1, source_target_pairs={{0,16},{1,17},{2,18},{3,19},{4,20},{5,21},{6,22},{7,23},{8,24},{9,... | collective-permute-start | bytes 786440 | tf_op jit(solution)/shard_map/ppermute | solution.py:623
  24.8 2.8 %collective-permute-start.1 = (bf16[7,64,128]{2,1,0:T(8,128)(2,1)S(1)}, bf16[7,64,128]{2,1,0:T(8,128)(2,1)S(1)}, u32[]{:S(2)}, u32[]{:S(2)}) collective-permute-start(bf16[7,64,128]{2,1,0:T(8,128)(2,1)S(1)} %get-tuple-element.35), channel_id=1, source_target_pairs={{16,24},{17,25},{18,26},{19,27},{20,28},{21,29},{22,30},{23,31}} | collective-permute-start | bytes 344072 | tf_op jit(solution)/shard_map/ppermute | solution.py:606
  27.6 1.8 %collective-permute-done.1.second_ref = bf16[7,64,128]{2,1,0:T(8,128)(2,1)S(1)} collective-permute-done((bf16[7,64,128]{2,1,0:T(8,128)(2,1)S(1)}, bf16[7,64,128]{2,1,0:T(8,128)(2,1)S(1)}, u32[]{:S(2)}, u32[]{:S(2)}) %collective-permute-start.1) | collective-permute-done | bytes 114720 | tf_op jit(solution)/shard_map/ppermute | solution.py:606
  29.3 1.0 %shard_map.247 = (f32[16,64,256]{2,1,0:T(8,128)S(1)}, bf16[16,128,256]{2,1,0:T(8,128)(2,1)S(1)}) custom-call(bf16[8,280,128]{2,1,0:T(8,128)(2,1)S(1)} %all-to-all-done.pay_ref, bf16[16,64,448]{2,1,0:T(8,128)(2,1)S(1)} %get-tuple-element.33.edge_ref, f32[16,448]{1,0:T(8,128)S(1)} %get-tuple-element.34.upto_ref, ...), custom_call_target="tpu_custom_call" | custom-call | tf_op jit(solution)/shard_map/pallas_call | solution.py:572
  30.4 0.0 copy-start
  30.4 0.1 collective-permute-done.2.top_ref
  30.5 0.4 shard_map.249
  30.9 12.5 %all_to_all.10.y_ref = bf16[8,208,128]{2,1,0:T(8,128)(2,1)S(1)} all-to-all(bf16[8,208,128]{2,1,0:T(8,128)(2,1)S(1)} %shard_map.249), channel_id=1, replica_groups={{0,1,2,3,4,5,6,7},{8,9,10,11,12,13,14,15},{16,17,18,19,20,21,22,23},{24..., dimensions={0} | all-to-all | bytes 851968 | tf_op jit(solution)/shard_map/all_to_all | solution.py:704
  43.4 0.0 copy-done
  43.4 1.8 %shard_map.250 = bf16[28,7,1024]{2,1,0:T(8,128)(2,1)} custom-call(bf16[8,208,128]{2,1,0:T(8,128)(2,1)S(1)} %all_to_all.10.y_ref, bf16[200,1024]{1,0:T(8,128)(2,1)S(1)} %get-tuple-element.42.own_ref, bf16[200,1024]{1,0:T(8,128)(2,1)S(1)} %get-tuple-element.43.gate_ref, f32[1,1024]{1,0:T(1,128)S(1)} %get-tuple-element.44.gain_ref, bf16[1024,1024]{1,0:T(8,128)(2,1)S(1)} %copy-done), custom_call_target="tpu_custom_call" | custom-call | tf_op jit(solution)/shard_map/pallas_call | solution.py:572
Async XLA Ops:
  3.4 13.5 %all-to-all-start = ((bf16[8,280,128]{2,1,0:T(8,128)(2,1)}), bf16[8,280,128]{2,1,0:T(8,128)(2,1)S(1)}, u32[]{:S(2)}, u32[]{:S(2)}) async-start(bf16[8,280,128]{2,1,0:T(8,128)(2,1)} %get-tuple-element.25), calls=%async_computation | async-start | bytes 1146880 | tf_op jit(solution)/shard_map/all_to_all | solution.py:699
  18.3 4.7 %collective-permute-start = (bf16[7,64,128]{2,1,0:T(8,128)(2,1)S(1)}, bf16[7,64,128]{2,1,0:T(8,128)(2,1)S(1)}, u32[]{:S(2)}, u32[]{:S(2)}) collective-permute-start(bf16[7,64,128]{2,1,0:T(8,128)(2,1)S(1)} %shard_map.244.last_ref), channel_id=1, source_target_pairs={{0,8},{1,9},{2,10},{3,11},{4,12},{5,13},{6,14},{7,15}} | collective-permute-start | bytes 344072 | tf_op jit(solution)/shard_map/ppermute | solution.py:596
  23.5 7.0 %collective-permute-start.2 = (bf16[16,64,128]{2,1,0:T(8,128)(2,1)S(1)}, bf16[16,64,128]{2,1,0:T(8,128)(2,1)S(1)}, u32[]{:S(2)}, u32[]{:S(2)}) collective-permute-start(bf16[16,64,128]{2,1,0:T(8,128)(2,1)S(1)} %shard_map.248), channel_id=1, source_target_pairs={{0,16},{1,17},{2,18},{3,19},{4,20},{5,21},{6,22},{7,23},{8,24},{9,... | collective-permute-start | bytes 786440 | tf_op jit(solution)/shard_map/ppermute | solution.py:623
  24.8 4.6 %collective-permute-start.1 = (bf16[7,64,128]{2,1,0:T(8,128)(2,1)S(1)}, bf16[7,64,128]{2,1,0:T(8,128)(2,1)S(1)}, u32[]{:S(2)}, u32[]{:S(2)}) collective-permute-start(bf16[7,64,128]{2,1,0:T(8,128)(2,1)S(1)} %get-tuple-element.35), channel_id=1, source_target_pairs={{16,24},{17,25},{18,26},{19,27},{20,28},{21,29},{22,30},{23,31}} | collective-permute-start | bytes 344072 | tf_op jit(solution)/shard_map/ppermute | solution.py:606
  30.4 13.1 %copy-start = (bf16[1024,1024]{1,0:T(8,128)(2,1)S(1)}, bf16[1024,1024]{1,0:T(8,128)(2,1)}, u32[]{:S(2)}) copy-start(bf16[1024,1024]{1,0:T(8,128)(2,1)} %w_ref.1) | copy-start | bytes 6291460

commit v11 on v9

--- a/solution.py
+++ b/solution.py
@@ -50,11 +50,10 @@
         self.count = rows * cols
         self.half = self.count // 2 // 8 * 8
         self.cells = round_up(self.count, 8)
-        self.stride = max(self.half, self.cells - self.half)
         self.edge = rows * states
         self.top = states * self.col_pad
         self.bc = 2 * states
-        self.at_bc = self.slots * self.stride
+        self.at_bc = self.cells
         self.at_dt = self.at_bc + 2 * self.bc
         self.at_rate = self.at_dt + 2 * self.slots
         self.message = round_up(self.at_rate + 1, 8)
@@ -63,7 +62,8 @@
         self.share = LANES // self.tail if self.tail else 1
         self.packed = self.slots * self.solid + (-(-self.slots // self.share) if self.tail else 0)
         assert self.head_width % self.slot == 0 and self.group % self.slot == 0
-        assert LANES % self.head_width == 0 and self.stride <= LANES
+        assert LANES % self.head_width == 0 and LANES % self.group == 0
+        assert self.cells - self.half <= LANES
         assert states % 16 == 0 and heads % 8 == 0
 
     def segments(self):
@@ -201,7 +201,7 @@
     bc = table[: 2 * states]
     steps = rows_ref[2 * states :, :]
 
-    lane = lax.broadcasted_iota(jnp.int32, (plan.stride, LANES), 1)
+    lane = lax.broadcasted_iota(jnp.int32, (cells, LANES), 1)
     sent = []
     for chunk in range(chunks):
         copies[chunk].wait()
@@ -212,26 +212,16 @@
         per = tile // group
         for k in range(per):
             dest = chunk * per + k
+            base, at = k * group // LANES * LANES, k * group % LANES
+            mine = v[:, base : base + LANES]
+            if at:
+                mine = pltpu.roll(mine, LANES - at, 1)
+            if group < LANES:
+                mine = jnp.where(lane < group, mine, 0.0)
+            pay_ref[dest, 0:cells, :] = mine.astype(BF16)
             dts, heads_of = [], []
             for s in range(plan.slots):
-                offset = k * group + s * plan.slot
-                base = offset // LANES * LANES
-                at = offset % LANES
-                first = v[:half, base : base + LANES]
-                last = v[half:, base : base + LANES]
-                if half < plan.stride:
-                    first = jnp.concatenate([first, jnp.zeros((plan.stride - half, LANES), F32)], axis=0)
-                if rest < plan.stride:
-                    last = jnp.concatenate([last, jnp.zeros((plan.stride - rest, LANES), F32)], axis=0)
-                if at:
-                    first = pltpu.roll(first, LANES - at, 1)
-                if at != HALF:
-                    last = pltpu.roll(last, (HALF - at) % LANES, 1)
-                both = jnp.where(lane < HALF, first, last)
-                if plan.slot < HALF:
-                    both = jnp.where(lane % HALF < plan.slot, both, 0.0)
-                pay_ref[dest, s * plan.stride : (s + 1) * plan.stride, :] = both.astype(BF16)
-                head = (chunk * tile + offset) // plan.head_width
+                head = (chunk * tile + k * group + s * plan.slot) // plan.head_width
                 heads_of.append(head)
                 dts += [steps[head : head + 1, :LANES], steps[head : head + 1, LANES:]]
             dts.append(rate_row(heads_of, rx_ref, ry_ref))
@@ -363,12 +353,17 @@
     return jnp.concatenate([pay_ref[t, at : at + count, :], pay_ref[t, at + gap : at + gap + count, :]], axis=1)
 
 
-def turned(plan, pay_ref, t, s):
-    v = pay_ref[t, s * plan.stride : (s + 1) * plan.stride, :].astype(F32)
-    if plan.stride < LANES:
-        v = jnp.concatenate([v, jnp.zeros((LANES - plan.stride, LANES), F32)], axis=0)
-    v = v.T
-    return jnp.concatenate([v[:HALF], v[HALF:]], axis=1).astype(BF16)
+def turn_all(plan, pay_ref, turned):
+    for t in range(plan.devices):
+        sides = []
+        for lo, hi in ((0, plan.half), (plan.half, plan.cells)):
+            v = pay_ref[t, lo:hi, :].astype(F32)
+            if hi - lo < LANES:
+                v = jnp.concatenate([v, jnp.zeros((LANES - hi + lo, LANES), F32)], axis=0)
+            sides.append(v.T)
+        v = jnp.concatenate(sides, axis=1).astype(BF16)
+        for s in range(plan.slots):
+            turned[s * plan.devices + t] = v[s * HALF : (s + 1) * HALF]
 
 
 def load_steps(plan, pay_ref, dts):
@@ -415,7 +410,7 @@
     return jnp.concatenate(parts, axis=1)
 
 
-def scan_edges(plan, pay_ref, dts, inner, kept, seen):
+def scan_edges(plan, pay_ref, turned, dts, inner, kept, seen):
     states, tiles, wide = plan.states, plan.devices, 2 * LANES
     i, j, real = places(plan, (wide, wide), 0)
     ti, tj, treal = places(plan, (wide, wide), 1)
@@ -441,16 +436,17 @@
             bd = (b * inner[w : w + 1, :]).astype(BF16)
             left = jnp.concatenate([bd * rowsel[i : i + 1] for i in range(plan.rows)], axis=0)
             now = kept[w : w + 1, :]
-            held = held * now + nt_dot(turned(plan, pay_ref, t, s), left)
+            held = held * now + nt_dot(turned[w], left)
             product = product * now
         ends.append(held)
     return ends
 
 
-def last_kernel(plan, axis, pay_ref, last_ref, dts, inner):
+def last_kernel(plan, axis, pay_ref, last_ref, turned, dts, inner):
     @pl.when(lax.axis_index(axis) < (plan.parts - 1) * plan.devices)
     def _():
         states, tiles, wide = plan.states, plan.devices, 2 * LANES
+        turn_all(plan, pay_ref, turned)
         load_steps(plan, pay_ref, dts)
         i, j, real = places(plan, (wide, wide), 0)
         ti, tj, treal = places(plan, (wide, wide), 1)
@@ -476,7 +472,7 @@
                 b = wide_rows(pay_ref, t, plan.at_bc, states, plan.bc).astype(F32)
                 bd = (b * inner[w : w + 1, :]).astype(BF16)
                 left = jnp.concatenate([bd * rowsel[i : i + 1] for i in range(plan.rows)], axis=0)
-                part = nt_dot(turned(plan, pay_ref, t, s), left)
+                part = nt_dot(turned[w], left)
                 held = part if held is None else held + part
             ends.append(held)
         pack_edges(plan, last_ref, ends)
@@ -485,17 +481,18 @@
 def maps_kernel(
     plan, pay_ref, to1_ref, to2_ref, from1_ref, from2_ref, side1_ref, side2_ref,
     sidemask_ref, down1_ref, down2_ref, downmask_ref, pick_ref,
-    side_ref, above_ref, passed_ref, top_ref, edge_ref, upto_ref, dts, inner, kept, s1, s2, d1, d2,
+    side_ref, above_ref, passed_ref, top_ref, edge_ref, upto_ref, turned, dts, inner, kept, s1, s2, d1, d2,
 ):
     states, tiles, cp, work = plan.states, plan.devices, plan.col_pad, plan.work
     rp = side1_ref.shape[0]
+    turn_all(plan, pay_ref, turned)
     load_steps(plan, pay_ref, dts)
 
     def seen(w, held, product):
         edge_ref[w] = held.astype(BF16)
         upto_ref[w : w + 1, :] = product
 
-    scan_edges(plan, pay_ref, dts, inner, kept, seen)
+    scan_edges(plan, pay_ref, turned, dts, inner, kept, seen)
     low = dts[...].astype(BF16)
     above_ref[...] = jnp.exp(-slot_rates(plan, pay_ref, 1) * mm(low, to2_ref[...]))
     rates_x, rates_y = rates_of(plan, pay_ref, 0), rates_of(plan, pay_ref, 1)
@@ -525,7 +522,7 @@
         fall = jnp.exp(-(rates_x[s] * x[at] + rates_y[s] * y[at])) * mask * dts[w : w + 1, :]
         b = wide_rows(pay_ref, t, plan.at_bc, states, plan.bc).astype(F32)
         falls = jnp.concatenate([fall * b[n : n + 1] for n in range(states)], axis=0).astype(BF16)
-        top_ref[w] = nt_dot(turned(plan, pay_ref, t, s), falls) + mm(edge_ref[w], passed_ref[w])
+        top_ref[w] = nt_dot(turned[w], falls) + mm(edge_ref[w], passed_ref[w])
 
 
 def join_kernel(plan, upto_ref, entry_ref, passed_ref, top_ref, out_ref):
@@ -556,11 +553,14 @@
 
 
 def cells_kernel(plan, y_ref, down_ref, top_ref, out_ref):
-    for w in range(plan.work):
-        t, s = w % plan.devices, w // plan.devices
-        y = y_ref[w] + mm(top_ref[w], down_ref[w])
-        y = jnp.concatenate([y[:, :LANES], y[:, LANES:]], axis=0).T
-        out_ref[t, s * plan.stride : (s + 1) * plan.stride, :] = y[: plan.stride].astype(BF16)
+    tiles = plan.devices
+    for t in range(tiles):
+        ys = [y_ref[w] + mm(top_ref[w], down_ref[w]) for w in range(t, plan.work, tiles)]
+        if plan.slots == 1:
+            ys.append(jnp.zeros_like(ys[0]))
+        y = jnp.concatenate(ys, axis=0)
+        for k, (lo, hi) in enumerate(((0, plan.half), (plan.half, plan.cells))):
+            out_ref[t, lo:hi, :] = y[:, k * LANES : (k + 1) * LANES].T[: hi - lo].astype(BF16)
 
 
 def call(kernel, name, args, outs, scratch=(), out_specs=None):
@@ -579,10 +579,10 @@
 def scan_calls(plan, consts, row_axis, col_axis, pay):
     work, cp, wide = plan.work, plan.col_pad, 2 * LANES
     rp = consts["side1"].shape[0]
-    steps = [((work, wide), F32), ((work, wide), F32), ((work, plan.edge), F32)]
+    steps = [((work, HALF, wide), BF16), ((work, wide), F32), ((work, wide), F32), ((work, plan.edge), F32)]
     shape = (plan.packed, HALF, LANES)
     if plan.parts > 1:
-        last = call(functools.partial(last_kernel, plan, col_axis), "last", [pay], [(shape, BF16)], steps[:2])[0]
+        last = call(functools.partial(last_kernel, plan, col_axis), "last", [pay], [(shape, BF16)], steps[:3])[0]
         entry = lax.ppermute(last, col_axis, [(k, k + plan.devices) for k in range(plan.devices)])
     else:
         entry = jnp.zeros(shape, BF16)
@@ -627,28 +627,24 @@
         functools.partial(cells_kernel, plan),
         "cells",
         [y, down, entry],
-        [((plan.devices, plan.slots * plan.stride, LANES), BF16)],
+        [((plan.devices, plan.cells, LANES), BF16)],
     )[0]
 
 
 def finish_kernel(plan, y_ref, own_ref, gate_ref, gain_ref, w_ref, out_hbm, full_ref, out_ref, sems):
-    half, cells, stride = plan.half, plan.cells, plan.stride
-    slot, slots = plan.slot, plan.slots
-    per = LANES // slot
-    lane = lax.broadcasted_iota(jnp.int32, (stride, LANES), 1)
+    group = plan.group
+    per = LANES // group
+    lane = lax.broadcasted_iota(jnp.int32, (plan.cells, LANES), 1)
     for block in range(plan.width // LANES):
-        for k, (lo, hi) in enumerate(((0, half), (half, cells))):
-            joined = None
-            for d in range(per):
-                at = block * per + d
-                part = y_ref[at // slots, at % slots * stride : (at % slots + 1) * stride, :].astype(F32)
-                shift = (d * slot - k * HALF) % LANES
-                if shift:
-                    part = pltpu.roll(part, shift, 1)
-                joined = part if joined is None else jnp.where(lane < d * slot, joined, part)
-            at = slice(block * LANES, (block + 1) * LANES)
-            y = joined[: hi - lo] + own_ref[lo:hi, at].astype(F32)
-            full_ref[lo:hi, at] = y.astype(BF16).astype(F32) * gate_ref[lo:hi, at].astype(F32)
+        joined = None
+        for d in range(per):
+            part = y_ref[block * per + d].astype(F32)
+            if d:
+                part = pltpu.roll(part, d * group, 1)
+            joined = part if joined is None else jnp.where(lane < d * group, joined, part)
+        at = slice(block * LANES, (block + 1) * LANES)
+        y = joined + own_ref[:, at].astype(F32)
+        full_ref[:, at] = y.astype(BF16).astype(F32) * gate_ref[:, at].astype(F32)
     gated = full_ref[...]
     scale = lax.rsqrt(jnp.mean(gated * gated, axis=-1, keepdims=True) + norm_eps)
     normed = (gated * scale * gain_ref[...]).astype(BF16)

time: 46 us -> 45.4 us (0.987)
  no operation moved by 1% of the time
where the time goes in v11:
time: 45.4 us; the launch traced here: 45 us
  Pallas kernels  18.9 us (42%)
  blocking collectives  12.8 us (28%)
  starting transfers between devices  10.6 us (23%)
  waiting for transfers between devices  2.66 us (6%)
    all_to_all x1, blocking collectives, per_device(): y = lax.all_to_all(y, 'col', 0, 0, tiled=True, axis_index_groups=groups)  12.8 us
    pallas_call x6, Pallas kernels, call(): pl.pallas_call(kernel, grid=(1,), in_specs=[full(x.shape) for x in args],...  8.82 us
    pallas_call x1, Pallas kernels, home(): pl.pallas_call(functools.partial(home_kernel, plan), grid=(1,), in_specs=...  6.85 us
    all_to_all x1, starting transfers between devices, per_device(): pay = lax.all_to_all(pay, 'col', 0, 0, tiled=True, axis_index_groups=groups)  6.22 us
    pallas_call x1, Pallas kernels, project(): pl.pallas_call(functools.partial(project_kernel, plan, chunks), grid=(1,)...  3.2 us
    ppermute x1, starting transfers between devices, scan_calls(): lax.ppermute(last, col_axis, [(k, k + plan.devices) for k in range(plan.d...  3.04 us
    all_to_all x1, waiting for transfers between devices, per_device(): pay = lax.all_to_all(pay, 'col', 0, 0, tiled=True, axis_index_groups=groups)  2.56 us
    ppermute x1, starting transfers between devices, scan_calls(): entry = lax.ppermute(tops, row_axis, chain)  1.31 us
  transfers between devices with their start and end apart: 3, of which 2 were waited for; matrix products, arithmetic and copies ran while one was open for 0% of the time, Pallas kernels for 26%

profile of v11, /device:TPU:0, one launch (start us, length us, event | category | flops | bytes accessed | tf_op | source)
XLA Modules:
  0.0 45.0 jit_solution(3365632128268875816)
XLA Ops:
  0.0 3.2 %project.1 = (bf16[256,1024]{1,0:T(8,128)(2,1)S(1)}, bf16[8,272,128]{2,1,0:T(8,128)(2,1)}, f32[48,256]{1,0:T(8,128)S(1)}, bf16[200,1024]{1,0:T(8,128)(2,1)S(1)}) custom-call(f32[16]{0:T(128)} %bias_hbm.1, f32[16]{0:T(128)} %rx_ref.1, f32[16]{0:T(128)} %ry_ref.1, bf16[28,7,1024]{2,1,0:T(8,128)(2,1)} %x_hbm.1, bf16[1024,2048]{1,0:T(8,128)(2,1)} %w_hbm.3, ...), custom_call_target="tpu_custom_call" | custom-call | tf_op jit(solution)/shard_map/project/pallas_call | solution.py:251
  3.2 6.2 %all-to-all-start = ((bf16[8,272,128]{2,1,0:T(8,128)(2,1)}), bf16[8,272,128]{2,1,0:T(8,128)(2,1)S(1)}, u32[]{:S(2)}, u32[]{:S(2)}) async-start(bf16[8,272,128]{2,1,0:T(8,128)(2,1)} %get-tuple-element.24), calls=%async_computation | async-start | bytes 1114112 | tf_op jit(solution)/shard_map/all_to_all | solution.py:688
  9.4 6.9 %home.1 = (bf16[200,1024]{1,0:T(8,128)(2,1)S(1)}, bf16[200,1024]{1,0:T(8,128)(2,1)S(1)}, f32[1,1024]{1,0:T(1,128)S(1)}) custom-call(f32[16]{0:T(128)} %rx_ref.1, f32[16]{0:T(128)} %ry_ref.1, f32[16]{0:T(128)} %skip_ref.1, bf16[1024,2048]{1,0:T(8,128)(2,1)} %w_hbm.3, bf16[256,1024]{1,0:T(8,128)(2,1)S(1)} %get-tuple-element.25.v_ref, ...), custom_call_target="tpu_custom_call" | custom-call | tf_op jit(solution)/shard_map/home/pallas_call | solution.py:322
  16.3 2.6 %all-to-all-done.pay_ref = bf16[8,272,128]{2,1,0:T(8,128)(2,1)S(1)} async-done(((bf16[8,272,128]{2,1,0:T(8,128)(2,1)}), bf16[8,272,128]{2,1,0:T(8,128)(2,1)S(1)}, u32[]{:S(2)}, u32[]{:S(2)}) %all-to-all-start) | async-done | bytes 557088 | tf_op jit(solution)/shard_map/all_to_all | solution.py:688
  18.8 1.5 %last.1 = bf16[7,64,128]{2,1,0:T(8,128)(2,1)S(1)} custom-call(bf16[8,272,128]{2,1,0:T(8,128)(2,1)S(1)} %all-to-all-done.pay_ref), custom_call_target="tpu_custom_call" | custom-call | tf_op jit(solution)/shard_map/last/pallas_call | solution.py:567
  20.3 3.0 %collective-permute-start = (bf16[7,64,128]{2,1,0:T(8,128)(2,1)S(1)}, bf16[7,64,128]{2,1,0:T(8,128)(2,1)S(1)}, u32[]{:S(2)}, u32[]{:S(2)}) collective-permute-start(bf16[7,64,128]{2,1,0:T(8,128)(2,1)S(1)} %last.1), channel_id=1, source_target_pairs={{0,8},{1,9},{2,10},{3,11},{4,12},{5,13},{6,14},{7,15},{16,24},{17,... | collective-permute-start | bytes 344072 | tf_op jit(solution)/shard_map/ppermute | solution.py:586
  23.3 3.9 %maps.1 = (bf16[16,32,256]{2,1,0:T(8,128)(2,1)S(1)}, f32[16,256]{1,0:T(8,128)S(1)}, bf16[16,448,128]{2,1,0:T(8,128)(2,1)S(1)}, f32[16,64,128]{2,1,0:T(8,128)S(1)...) custom-call(bf16[8,272,128]{2,1,0:T(8,128)(2,1)S(1)} %all-to-all-done.pay_ref, ...), custom_call_target="tpu_custom_call" | custom-call | tf_op jit(solution)/shard_map/maps/pallas_call | solution.py:567
  27.2 0.0 collective-permute-done.entry_ref
  27.2 0.5 %join.1 = bf16[16,64,128]{2,1,0:T(8,128)(2,1)S(1)} custom-call(f32[16,448]{1,0:T(8,128)S(1)} %get-tuple-element.33.upto_ref, bf16[7,64,128]{2,1,0:T(8,128)(2,1)S(1)} %collective-permute-done.entry_ref, bf16[16,448,128]{2,1,0:T(8,128)(2,1)S(1)} %get-tuple-element.38.passed_ref, f32[16,64,128]{2,1,0:T(8,128)S(1)} %get-tuple-element.39.top_ref), custom_call_target="tpu_custom_call" | custom-call | tf_op jit(solution)/shard_map/join/pallas_call | solution.py:567
  27.7 1.3 %collective-permute-start.1 = (bf16[16,64,128]{2,1,0:T(8,128)(2,1)S(1)}, bf16[16,64,128]{2,1,0:T(8,128)(2,1)S(1)}, u32[]{:S(2)}, u32[]{:S(2)}) collective-permute-start(bf16[16,64,128]{2,1,0:T(8,128)(2,1)S(1)} %join.1), channel_id=1, source_target_pairs={{0,16},{1,17},{2,18},{3,19},{4,20},{5,21},{6,22},{7,23},{8,24},{9,... | collective-permute-start | bytes 786440 | tf_op jit(solution)/shard_map/ppermute | solution.py:613
  29.1 1.0 %sides.1 = (f32[16,64,256]{2,1,0:T(8,128)S(1)}, bf16[16,128,256]{2,1,0:T(8,128)(2,1)S(1)}) custom-call(bf16[8,272,128]{2,1,0:T(8,128)(2,1)S(1)} %all-to-all-done.pay_ref, bf16[16,64,448]{2,1,0:T(8,128)(2,1)S(1)} %get-tuple-element.32.edge_ref, f32[16,448]{1,0:T(8,128)S(1)} %get-tuple-element.33.upto_ref, ...), custom_call_target="tpu_custom_call" | custom-call | tf_op jit(solution)/shard_map/sides/pallas_call | solution.py:567
  30.1 0.0 copy-start
  30.1 0.1 collective-permute-done.1.top_ref
  30.2 0.4 cells.1
  30.6 12.8 %all_to_all.10.y_ref = bf16[8,200,128]{2,1,0:T(8,128)(2,1)S(1)} all-to-all(bf16[8,200,128]{2,1,0:T(8,128)(2,1)S(1)} %cells.1), channel_id=1, replica_groups={{0,1,2,3,4,5,6,7},{8,9,10,11,12,13,14,15},{16,17,18,19,20,21,22,23},{24..., dimensions={0} | all-to-all | bytes 819200 | tf_op jit(solution)/shard_map/all_to_all | solution.py:693
  43.4 0.0 copy-done
  43.4 1.6 %finish.1 = bf16[28,7,1024]{2,1,0:T(8,128)(2,1)} custom-call(bf16[8,200,128]{2,1,0:T(8,128)(2,1)S(1)} %all_to_all.10.y_ref, bf16[200,1024]{1,0:T(8,128)(2,1)S(1)} %get-tuple-element.40.own_ref, bf16[200,1024]{1,0:T(8,128)(2,1)S(1)} %get-tuple-element.41.gate_ref, f32[1,1024]{1,0:T(1,128)S(1)} %get-tuple-element.42.gain_ref, bf16[1024,1024]{1,0:T(8,128)(2,1)S(1)} %copy-done), custom_call_target="tpu_custom_call" | custom-call | tf_op jit(solution)/shard_map/finish/pallas_call | solution.py:567
Async XLA Ops:
  3.2 15.6 %all-to-all-start = ((bf16[8,272,128]{2,1,0:T(8,128)(2,1)}), bf16[8,272,128]{2,1,0:T(8,128)(2,1)S(1)}, u32[]{:S(2)}, u32[]{:S(2)}) async-start(bf16[8,272,128]{2,1,0:T(8,128)(2,1)} %get-tuple-element.24), calls=%async_computation | async-start | bytes 1114112 | tf_op jit(solution)/shard_map/all_to_all | solution.py:688
  20.3 6.9 %collective-permute-start = (bf16[7,64,128]{2,1,0:T(8,128)(2,1)S(1)}, bf16[7,64,128]{2,1,0:T(8,128)(2,1)S(1)}, u32[]{:S(2)}, u32[]{:S(2)}) collective-permute-start(bf16[7,64,128]{2,1,0:T(8,128)(2,1)S(1)} %last.1), channel_id=1, source_target_pairs={{0,8},{1,9},{2,10},{3,11},{4,12},{5,13},{6,14},{7,15},{16,24},{17,... | collective-permute-start | bytes 344072 | tf_op jit(solution)/shard_map/ppermute | solution.py:586
  27.7 2.4 %collective-permute-start.1 = (bf16[16,64,128]{2,1,0:T(8,128)(2,1)S(1)}, bf16[16,64,128]{2,1,0:T(8,128)(2,1)S(1)}, u32[]{:S(2)}, u32[]{:S(2)}) collective-permute-start(bf16[16,64,128]{2,1,0:T(8,128)(2,1)S(1)} %join.1), channel_id=1, source_target_pairs={{0,16},{1,17},{2,18},{3,19},{4,20},{5,21},{6,22},{7,23},{8,24},{9,... | collective-permute-start | bytes 786440 | tf_op jit(solution)/shard_map/ppermute | solution.py:613
  30.1 13.3 %copy-start = (bf16[1024,1024]{1,0:T(8,128)(2,1)S(1)}, bf16[1024,1024]{1,0:T(8,128)(2,1)}, u32[]{:S(2)}) copy-start(bf16[1024,1024]{1,0:T(8,128)(2,1)} %w_ref.1) | copy-start | bytes 6291460

commit v12 on v11

--- a/solution.py
+++ b/solution.py
@@ -478,11 +478,20 @@
         pack_edges(plan, last_ref, ends)
 
 
-def maps_kernel(
-    plan, pay_ref, to1_ref, to2_ref, from1_ref, from2_ref, side1_ref, side2_ref,
-    sidemask_ref, down1_ref, down2_ref, downmask_ref, pick_ref,
-    side_ref, above_ref, passed_ref, top_ref, edge_ref, upto_ref, turned, dts, inner, kept, s1, s2, d1, d2,
-):
+map_names = ("to1", "to2", "from1", "from2", "side1", "side2", "sidemask", "down1", "down2", "downmask", "pick")
+
+
+def maps_kernel(plan, pay_ref, *refs):
+    count = len(map_names)
+    maps, refs = refs[:count], refs[count:]
+    passed_ref, top_ref, upto_ref, y_ref, left_ref, down_ref = refs[:6]
+    turned, dts, inner, kept, s1, s2, d1, d2, edge_ref, side_ref, above_ref = refs[6:17]
+    held, sems = refs[17 : 17 + count], refs[17 + count]
+    copies = [pltpu.make_async_copy(a, b, sems.at[k]) for k, (a, b) in enumerate(zip(maps, held))]
+    for copy in copies:
+        copy.start()
+    to1_ref, to2_ref, from1_ref, from2_ref, side1_ref, side2_ref = held[:6]
+    sidemask_ref, down1_ref, down2_ref, downmask_ref, pick_ref = held[6:]
     states, tiles, cp, work = plan.states, plan.devices, plan.col_pad, plan.work
     rp = side1_ref.shape[0]
     turn_all(plan, pay_ref, turned)
@@ -493,6 +502,8 @@
         upto_ref[w : w + 1, :] = product
 
     scan_edges(plan, pay_ref, turned, dts, inner, kept, seen)
+    for copy in copies:
+        copy.wait()
     low = dts[...].astype(BF16)
     above_ref[...] = jnp.exp(-slot_rates(plan, pay_ref, 1) * mm(low, to2_ref[...]))
     rates_x, rates_y = rates_of(plan, pay_ref, 0), rates_of(plan, pay_ref, 1)
@@ -523,33 +534,30 @@
         b = wide_rows(pay_ref, t, plan.at_bc, states, plan.bc).astype(F32)
         falls = jnp.concatenate([fall * b[n : n + 1] for n in range(states)], axis=0).astype(BF16)
         top_ref[w] = nt_dot(turned[w], falls) + mm(edge_ref[w], passed_ref[w])
-
-
-def join_kernel(plan, upto_ref, entry_ref, passed_ref, top_ref, out_ref):
+    colsel = down2_ref[...].astype(F32)
+    for w in range(work):
+        c = wide_rows(pay_ref, w % tiles, plan.at_bc + states, states, plan.bc)
+        side = side_ref[w]
+        left = jnp.concatenate([c * side[i : i + 1] for i in range(plan.rows)], axis=0)
+        left_ref[w] = left
+        y_ref[w] = mm(edge_ref[w], left)
+        ca = c.astype(F32) * above_ref[w : w + 1, :]
+        down_ref[w] = jnp.concatenate([colsel * ca[n : n + 1] for n in range(states)], axis=0).astype(BF16)
+
+
+def join_kernel(plan, upto_ref, entry_ref, passed_ref, top_ref, out_ref, late_ref):
     for s in range(plan.slots):
         entry = unpack_edges(plan, entry_ref, s)
         for t in range(plan.devices):
             w = s * plan.devices + t
             late = (entry * upto_ref[w : w + 1, :]).astype(BF16)
+            late_ref[w] = late
             out_ref[w] = (top_ref[w] + mm(late, passed_ref[w])).astype(BF16)
 
 
-def sides_kernel(plan, pay_ref, edge_ref, upto_ref, entry_ref, side_ref, above_ref, y_ref, down_ref):
-    states, tiles = plan.states, plan.devices
-    shape = (plan.col_pad, 2 * LANES)
-    _, tj, treal = places(plan, shape, 1)
-    colsel = jnp.where((tj == lax.broadcasted_iota(jnp.int32, shape, 0)) & treal, 1.0, 0.0)
-    for s in range(plan.slots):
-        entry = unpack_edges(plan, entry_ref, s)
-        for t in range(tiles):
-            w = s * tiles + t
-            c = wide_rows(pay_ref, t, plan.at_bc + states, states, plan.bc)
-            side = side_ref[w]
-            left = jnp.concatenate([c * side[i : i + 1] for i in range(plan.rows)], axis=0)
-            whole = (edge_ref[w].astype(F32) + entry * upto_ref[w : w + 1, :]).astype(BF16)
-            y_ref[w] = mm(whole, left)
-            ca = c.astype(F32) * above_ref[w : w + 1, :]
-            down_ref[w] = jnp.concatenate([colsel * ca[n : n + 1] for n in range(states)], axis=0).astype(BF16)
+def sides_kernel(plan, y_ref, left_ref, late_ref, out_ref):
+    for w in range(plan.work):
+        out_ref[w] = y_ref[w] + mm(late_ref[w], left_ref[w])
 
 
 def cells_kernel(plan, y_ref, down_ref, top_ref, out_ref):
@@ -563,11 +571,11 @@
             out_ref[t, lo:hi, :] = y[:, k * LANES : (k + 1) * LANES].T[: hi - lo].astype(BF16)
 
 
-def call(kernel, name, args, outs, scratch=(), out_specs=None):
+def call(kernel, name, args, outs, scratch=(), out_specs=None, in_specs=None):
     return pl.pallas_call(
         kernel,
         grid=(1,),
-        in_specs=[full(x.shape) for x in args],
+        in_specs=in_specs or [full(x.shape) for x in args],
         out_specs=out_specs or [full(s) for s, _ in outs],
         out_shape=[jax.ShapeDtypeStruct(s, d) for s, d in outs],
         scratch_shapes=[x if not isinstance(x, tuple) else pltpu.VMEM(*x) for x in scratch],
@@ -576,7 +584,7 @@
     )(*args)
 
 
-def scan_calls(plan, consts, row_axis, col_axis, pay):
+def scan_calls(plan, consts, row_axis, col_axis, pay, rate_y):
     work, cp, wide = plan.work, plan.col_pad, 2 * LANES
     rp = consts["side1"].shape[0]
     steps = [((work, HALF, wide), BF16), ((work, wide), F32), ((work, wide), F32), ((work, plan.edge), F32)]
@@ -586,43 +594,52 @@
         entry = lax.ppermute(last, col_axis, [(k, k + plan.devices) for k in range(plan.devices)])
     else:
         entry = jnp.zeros(shape, BF16)
-    names = ("to1", "to2", "from1", "from2", "side1", "side2", "sidemask", "down1", "down2", "downmask", "pick")
-    side, above, passed, tops, edges, upto = call(
+    maps = [consts[k] for k in map_names]
+    passed, tops, upto, y, left, down = call(
         functools.partial(maps_kernel, plan),
         "maps",
-        [pay] + [consts[k] for k in names],
+        [pay] + maps,
         [
-            ((work, rp, wide), BF16),
-            ((work, wide), F32),
             ((work, plan.edge, plan.top), BF16),
             ((work, HALF, plan.top), F32),
-            ((work, HALF, plan.edge), BF16),
             ((work, plan.edge), F32),
+            ((work, HALF, wide), F32),
+            ((work, plan.edge, wide), BF16),
+            ((work, plan.top, wide), BF16),
         ],
-        steps + [((work * rp, wide), F32)] * 2 + [((work * cp, wide), F32)] * 2,
+        steps
+        + [((work * rp, wide), F32)] * 2
+        + [((work * cp, wide), F32)] * 2
+        + [((work, HALF, plan.edge), BF16), ((work, rp, wide), BF16), ((work, wide), F32)]
+        + [(x.shape, BF16) for x in maps]
+        + [pltpu.SemaphoreType.DMA((len(maps),))],
+        in_specs=[full(pay.shape)] + [HBM] * len(maps),
     )
-    edge_entry = entry
-    tops = call(
+    tops, late = call(
         functools.partial(join_kernel, plan),
         "join",
         [upto, entry, passed, tops],
-        [((work, HALF, plan.top), BF16)],
-    )[0]
+        [((work, HALF, plan.top), BF16), ((work, HALF, plan.edge), BF16)],
+    )
     count = lax.axis_size(row_axis)
     chain = [(r, r + 1) for r in range(count - 1)]
     entry = lax.ppermute(tops, row_axis, chain)
     if count > 2:
-        keep = jnp.dot(above.astype(BF16), consts["pick"], preferred_element_type=F32)[:, None, :]
+        place = lax.rem(lax.axis_index(col_axis), plan.devices) * plan.group
+        spread = jnp.tile(consts["down2"].T, (1, plan.states))
+        keep = []
+        for s in range(plan.slots):
+            dt = pay[:, plan.at_dt + 2 * s : plan.at_dt + 2 * s + 2].reshape(plan.devices, wide)
+            rate = rate_y[(place + s * plan.slot) // plan.head_width]
+            keep.append(jnp.exp(-rate * jnp.dot(dt, spread, preferred_element_type=F32)))
+        keep = jnp.concatenate(keep, axis=0)[:, None, :]
         for _ in range(count - 2):
             entry = lax.ppermute(
                 (tops.astype(F32) + keep * entry.astype(F32)).astype(BF16), row_axis, chain
             )
-    y, down = call(
-        functools.partial(sides_kernel, plan),
-        "sides",
-        [pay, edges, upto, edge_entry, side, above],
-        [((work, HALF, wide), F32), ((work, plan.top, wide), BF16)],
-    )
+    y = call(
+        functools.partial(sides_kernel, plan), "sides", [y, left, late], [((work, HALF, wide), F32)]
+    )[0]
     return call(
         functools.partial(cells_kernel, plan),
         "cells",
@@ -689,7 +706,7 @@
     gain = norm_gain.reshape(1, width)
     own, gate, gain = home(plan, consts, v, table, x, w_in, tissue, gain, rate_x, rate_y, d_skip)
     pay, own, gate, gain = lax.optimization_barrier((pay, own, gate, gain))
-    y = scan_calls(plan, consts, "row", "col", pay)
+    y = scan_calls(plan, consts, "row", "col", pay, rate_y)
     y = lax.all_to_all(y, "col", 0, 0, tiled=True, axis_index_groups=groups)
     return finish(plan, y, own, gate, gain, w_out)
 

time: 45.4 us -> 45.4 us (level)
  no operation moved by 1% of the time
where the time goes in v12:
time: 45.4 us; the launch traced here: 45 us
  Pallas kernels  19 us (42%)
  blocking collectives  12.4 us (27%)
  starting transfers between devices  10.6 us (23%)
  waiting for transfers between devices  2.93 us (6%)
    all_to_all x1, blocking collectives, per_device(): y = lax.all_to_all(y, 'col', 0, 0, tiled=True, axis_index_groups=groups)  12.4 us
    pallas_call x6, Pallas kernels, call(): pl.pallas_call(kernel, grid=(1,), in_specs=in_specs or [full(x.shape) for...  8.98 us
    pallas_call x1, Pallas kernels, home(): pl.pallas_call(functools.partial(home_kernel, plan), grid=(1,), in_specs=...  6.85 us
    all_to_all x1, starting transfers between devices, per_device(): pay = lax.all_to_all(pay, 'col', 0, 0, tiled=True, axis_index_groups=groups)  6.22 us
    pallas_call x1, Pallas kernels, project(): pl.pallas_call(functools.partial(project_kernel, plan, chunks), grid=(1,)...  3.2 us
    ppermute x1, starting transfers between devices, scan_calls(): lax.ppermute(last, col_axis, [(k, k + plan.devices) for k in range(plan.d...  3.04 us
    all_to_all x1, waiting for transfers between devices, per_device(): pay = lax.all_to_all(pay, 'col', 0, 0, tiled=True, axis_index_groups=groups)  2.56 us
    ppermute x1, starting transfers between devices, scan_calls(): entry = lax.ppermute(tops, row_axis, chain)  1.31 us
  transfers between devices with their start and end apart: 3, of which 2 were waited for; matrix products, arithmetic and copies ran while one was open for 0% of the time, Pallas kernels for 26%

profile of v12, /device:TPU:0, one launch (start us, length us, event | category | flops | bytes accessed | tf_op | source)
XLA Modules:
  0.0 45.0 jit_solution(7965303770391065702)
XLA Ops:
  0.0 3.2 %project.1 = (bf16[256,1024]{1,0:T(8,128)(2,1)S(1)}, bf16[8,272,128]{2,1,0:T(8,128)(2,1)}, f32[48,256]{1,0:T(8,128)S(1)}, bf16[200,1024]{1,0:T(8,128)(2,1)S(1)}) custom-call(f32[16]{0:T(128)} %bias_hbm.1, f32[16]{0:T(128)} %rx_ref.1, f32[16]{0:T(128)} %ry_ref.1, bf16[28,7,1024]{2,1,0:T(8,128)(2,1)} %x_hbm.1, bf16[1024,2048]{1,0:T(8,128)(2,1)} %w_hbm.3, ...), custom_call_target="tpu_custom_call" | custom-call | tf_op jit(solution)/shard_map/project/pallas_call | solution.py:251
  3.2 6.2 %all-to-all-start = ((bf16[8,272,128]{2,1,0:T(8,128)(2,1)}), bf16[8,272,128]{2,1,0:T(8,128)(2,1)S(1)}, u32[]{:S(2)}, u32[]{:S(2)}) async-start(bf16[8,272,128]{2,1,0:T(8,128)(2,1)} %get-tuple-element.24), calls=%async_computation | async-start | bytes 1114112 | tf_op jit(solution)/shard_map/all_to_all | solution.py:705
  9.4 6.9 %home.1 = (bf16[200,1024]{1,0:T(8,128)(2,1)S(1)}, bf16[200,1024]{1,0:T(8,128)(2,1)S(1)}, f32[1,1024]{1,0:T(1,128)S(1)}) custom-call(f32[16]{0:T(128)} %rx_ref.1, f32[16]{0:T(128)} %ry_ref.1, f32[16]{0:T(128)} %skip_ref.1, bf16[1024,2048]{1,0:T(8,128)(2,1)} %w_hbm.3, bf16[256,1024]{1,0:T(8,128)(2,1)S(1)} %get-tuple-element.25.v_ref, ...), custom_call_target="tpu_custom_call" | custom-call | tf_op jit(solution)/shard_map/home/pallas_call | solution.py:322
  16.3 2.6 %all-to-all-done.pay_ref = bf16[8,272,128]{2,1,0:T(8,128)(2,1)S(1)} async-done(((bf16[8,272,128]{2,1,0:T(8,128)(2,1)}), bf16[8,272,128]{2,1,0:T(8,128)(2,1)S(1)}, u32[]{:S(2)}, u32[]{:S(2)}) %all-to-all-start) | async-done | bytes 557088 | tf_op jit(solution)/shard_map/all_to_all | solution.py:705
  18.8 1.5 %last.1 = bf16[7,64,128]{2,1,0:T(8,128)(2,1)S(1)} custom-call(bf16[8,272,128]{2,1,0:T(8,128)(2,1)S(1)} %all-to-all-done.pay_ref), custom_call_target="tpu_custom_call" | custom-call | tf_op jit(solution)/shard_map/last/pallas_call | solution.py:575
  20.3 3.0 %collective-permute-start = (bf16[7,64,128]{2,1,0:T(8,128)(2,1)S(1)}, bf16[7,64,128]{2,1,0:T(8,128)(2,1)S(1)}, u32[]{:S(2)}, u32[]{:S(2)}) collective-permute-start(bf16[7,64,128]{2,1,0:T(8,128)(2,1)S(1)} %last.1), channel_id=1, source_target_pairs={{0,8},{1,9},{2,10},{3,11},{4,12},{5,13},{6,14},{7,15},{16,24},{17,... | collective-permute-start | bytes 344072 | tf_op jit(solution)/shard_map/ppermute | solution.py:594
  23.3 4.3 %maps.1 = (bf16[16,448,128]{2,1,0:T(8,128)(2,1)S(1)}, f32[16,64,128]{2,1,0:T(8,128)S(1)}, f32[16,448]{1,0:T(8,128)S(1)}, f32[16,64,256]{2,1,0:T(8,128)S(1)}, bf1...) custom-call(bf16[8,272,128]{2,1,0:T(8,128)(2,1)S(1)} %all-to-all-done.pay_ref, ...), custom_call_target="tpu_custom_call" | custom-call | tf_op jit(solution)/shard_map/maps/pallas_call | solution.py:575
  27.7 0.0 collective-permute-done.entry_ref
  27.7 0.5 %join.1 = (bf16[16,64,128]{2,1,0:T(8,128)(2,1)S(1)}, bf16[16,64,448]{2,1,0:T(8,128)(2,1)S(1)}) custom-call(f32[16,448]{1,0:T(8,128)S(1)} %get-tuple-element.34.upto_ref, bf16[7,64,128]{2,1,0:T(8,128)(2,1)S(1)} %collective-permute-done.entry_ref, bf16[16,448,128]{2,1,0:T(8,128)(2,1)S(1)} %get-tuple-element.35.passed_ref, ...), custom_call_target="tpu_custom_call" | custom-call | tf_op jit(solution)/shard_map/join/pallas_call | solution.py:575
  28.2 1.3 %collective-permute-start.1 = (bf16[16,64,128]{2,1,0:T(8,128)(2,1)S(1)}, bf16[16,64,128]{2,1,0:T(8,128)(2,1)S(1)}, u32[]{:S(2)}, u32[]{:S(2)}) collective-permute-start(bf16[16,64,128]{2,1,0:T(8,128)(2,1)S(1)} %get-tuple-element.39), channel_id=1, source_target_pairs={{0,16},{1,17},{2,18},{3,19},{4,20},{5,21},{6,22},{7,23},{8,24},{9,... | collective-permute-start | bytes 786440 | tf_op jit(solution)/shard_map/ppermute | solution.py:626
  29.5 0.0 copy-start
  29.5 0.7 %sides.1.y_ref = f32[16,64,256]{2,1,0:T(8,128)S(1)} custom-call(f32[16,64,256]{2,1,0:T(8,128)S(1)} %get-tuple-element.32.y_ref, bf16[16,448,256]{2,1,0:T(8,128)(2,1)S(1)} %get-tuple-element.33.left_ref, bf16[16,64,448]{2,1,0:T(8,128)(2,1)S(1)} %get-tuple-element.37.late_ref), custom_call_target="tpu_custom_call" | custom-call | tf_op jit(solution)/shard_map/sides/pallas_call | solution.py:575
  30.3 0.4 collective-permute-done.1.top_ref
  30.6 0.4 cells.1
  31.0 12.4 %all_to_all.10.y_ref = bf16[8,200,128]{2,1,0:T(8,128)(2,1)S(1)} all-to-all(bf16[8,200,128]{2,1,0:T(8,128)(2,1)S(1)} %cells.1), channel_id=1, replica_groups={{0,1,2,3,4,5,6,7},{8,9,10,11,12,13,14,15},{16,17,18,19,20,21,22,23},{24..., dimensions={0} | all-to-all | bytes 819200 | tf_op jit(solution)/shard_map/all_to_all | solution.py:710
  43.4 0.0 copy-done
  43.4 1.6 %finish.1 = bf16[28,7,1024]{2,1,0:T(8,128)(2,1)} custom-call(bf16[8,200,128]{2,1,0:T(8,128)(2,1)S(1)} %all_to_all.10.y_ref, bf16[200,1024]{1,0:T(8,128)(2,1)S(1)} %get-tuple-element.40.own_ref, bf16[200,1024]{1,0:T(8,128)(2,1)S(1)} %get-tuple-element.41.gate_ref, f32[1,1024]{1,0:T(1,128)S(1)} %get-tuple-element.42.gain_ref, bf16[1024,1024]{1,0:T(8,128)(2,1)S(1)} %copy-done), custom_call_target="tpu_custom_call" | custom-call | tf_op jit(solution)/shard_map/finish/pallas_call | solution.py:575
Async XLA Ops:
  3.2 15.6 %all-to-all-start = ((bf16[8,272,128]{2,1,0:T(8,128)(2,1)}), bf16[8,272,128]{2,1,0:T(8,128)(2,1)S(1)}, u32[]{:S(2)}, u32[]{:S(2)}) async-start(bf16[8,272,128]{2,1,0:T(8,128)(2,1)} %get-tuple-element.24), calls=%async_computation | async-start | bytes 1114112 | tf_op jit(solution)/shard_map/all_to_all | solution.py:705
  20.3 7.4 %collective-permute-start = (bf16[7,64,128]{2,1,0:T(8,128)(2,1)S(1)}, bf16[7,64,128]{2,1,0:T(8,128)(2,1)S(1)}, u32[]{:S(2)}, u32[]{:S(2)}) collective-permute-start(bf16[7,64,128]{2,1,0:T(8,128)(2,1)S(1)} %last.1), channel_id=1, source_target_pairs={{0,8},{1,9},{2,10},{3,11},{4,12},{5,13},{6,14},{7,15},{16,24},{17,... | collective-permute-start | bytes 344072 | tf_op jit(solution)/shard_map/ppermute | solution.py:594
  28.2 2.4 %collective-permute-start.1 = (bf16[16,64,128]{2,1,0:T(8,128)(2,1)S(1)}, bf16[16,64,128]{2,1,0:T(8,128)(2,1)S(1)}, u32[]{:S(2)}, u32[]{:S(2)}) collective-permute-start(bf16[16,64,128]{2,1,0:T(8,128)(2,1)S(1)} %get-tuple-element.39), channel_id=1, source_target_pairs={{0,16},{1,17},{2,18},{3,19},{4,20},{5,21},{6,22},{7,23},{8,24},{9,... | collective-permute-start | bytes 786440 | tf_op jit(solution)/shard_map/ppermute | solution.py:626
  29.5 13.9 %copy-start = (bf16[1024,1024]{1,0:T(8,128)(2,1)S(1)}, bf16[1024,1024]{1,0:T(8,128)(2,1)}, u32[]{:S(2)}) copy-start(bf16[1024,1024]{1,0:T(8,128)(2,1)} %w_ref.1) | copy-start | bytes 6291460

commit v13 on v11

--- a/solution.py
+++ b/solution.py
@@ -230,9 +230,8 @@
             spare = plan.message - plan.at_dt - len(dts)
             dts += [jnp.zeros((spare, LANES), F32)] if spare else []
             pay_ref[dest, plan.at_dt : plan.message, :] = jnp.concatenate(dts, axis=0).astype(BF16)
-        at = slice(chunk * per, (chunk + 1) * per)
-        sent.append(pltpu.make_async_copy(pay_ref.at[at], pay_hbm.at[at], out_sems.at[chunk]))
-        sent[-1].start()
+            sent.append(pltpu.make_async_copy(pay_ref.at[dest], pay_hbm.at[dest], out_sems.at[dest]))
+            sent[-1].start()
     for copy in sent:
         copy.wait()
 
@@ -267,25 +266,30 @@
             pltpu.VMEM((plan.cells, depth), F32),
             pltpu.SemaphoreType.DMA((8,)),
             pltpu.SemaphoreType.DMA((chunks,)),
-            pltpu.SemaphoreType.DMA((chunks,)),
+            pltpu.SemaphoreType.DMA((plan.devices,)),
         ],
         compiler_params=pltpu.CompilerParams(vmem_limit_bytes=24 * 2**20),
         name="project",
     )(*[in_hbm(x) for x in args])
 
 
-def home_kernel(
-    plan, rx_ref, ry_ref, skip_ref, w_hbm, v_ref, rows_ref, flat_ref, t_ref, gain_ref,
-    own1_ref, own2_ref, from1_ref, from2_ref, mask_ref, out_ref, gate_hbm, gain_out, pair, w_ref, gate_ref, sem, gate_sem,
-):
+def home_kernel(plan, v_ref, rows_ref, flat_ref, w_hbm, *refs):
+    sources, refs = refs[:9], refs[9:]
+    gain_hbm, out_ref, gate_hbm, gain_out, pair, w_ref, gate_ref = refs[:7]
+    held, (sem, gain_sem, sems, gate_sems) = refs[7:16], refs[16:]
     states, cells, half = plan.states, plan.cells, plan.half
+    reads = [pltpu.make_async_copy(a, b, sems.at[k]) for k, (a, b) in enumerate(zip(sources, held))]
+    reads.append(pltpu.make_async_copy(gain_hbm, gain_out, gain_sem))
     copy = pltpu.make_async_copy(w_hbm.at[:, plan.width :], w_ref, sem)
-    copy.start()
-    gain_out[...] = gain_ref[...]
+    for each in reads + [copy]:
+        each.start()
+    rx_ref, ry_ref, skip_ref, t_ref, own1_ref, own2_ref, from1_ref, from2_ref, mask_ref = held
     b = rows_ref[0:states, :].astype(BF16)
     c = rows_ref[states : 2 * states, :].astype(BF16)
     pairs = tn_dot(c, b)
     pairs = jnp.concatenate([pairs[:half], pairs[LANES : LANES + cells - half]], axis=0)
+    for each in reads:
+        each.wait()
     pair[...] = pairs * mask_ref[...].astype(F32)
     lane = lax.broadcasted_iota(jnp.int32, (cells, LANES), 1)
     per = LANES // plan.head_width
@@ -305,36 +309,44 @@
         out_ref[:, block * LANES : (block + 1) * LANES] = total.astype(BF16)
     keep = cell_mask_of(plan, t_ref)
     copy.wait()
-    tile = 2 * LANES
+    tile = plan.width // gate_sems.shape[0]
+    sent = []
     for block in range(plan.width // tile):
         at = slice(block * tile, (block + 1) * tile)
         z = mm(flat_ref[...], w_ref[:, at]).astype(BF16).astype(F32)
         gate_ref[:, at] = (z * (1.0 / (1.0 + jnp.exp(-z))) * keep).astype(BF16)
-    copy = pltpu.make_async_copy(gate_ref, gate_hbm, gate_sem)
-    copy.start()
-    copy.wait()
+        sent.append(pltpu.make_async_copy(gate_ref.at[:, at], gate_hbm.at[:, at], gate_sems.at[block]))
+        sent[-1].start()
+    for each in sent:
+        each.wait()
 
 
 def home(plan, consts, v, rows, flat, w_in, tissue, gain, rate_x, rate_y, d_skip):
-    args = [in_hbm(w_in), v, rows, flat, in_hbm(tissue.T), in_hbm(gain)]
-    args += [consts[k] for k in ("own1", "own2", "from1", "from2", "ownmask")]
+    sources = [rate_x, rate_y, d_skip, tissue.T] + [consts[k] for k in ("own1", "own2", "from1", "from2", "ownmask")]
+    fixed = [in_hbm(x) for x in [w_in] + sources + [gain]]
     outs = [((plan.cells, plan.width), BF16), ((plan.cells, plan.width), BF16), (gain.shape, F32)]
     return pl.pallas_call(
         functools.partial(home_kernel, plan),
         grid=(1,),
-        in_specs=[SMEM, SMEM, SMEM, HBM] + [full(x.shape) for x in args[1:]],
+        in_specs=[full(x.shape) for x in (v, rows, flat)] + [HBM] * len(fixed),
         out_specs=[full(outs[0][0]), HBM, full(outs[2][0])],
         out_shape=[jax.ShapeDtypeStruct(s, d) for s, d in outs],
         scratch_shapes=[
             pltpu.VMEM((plan.cells, 2 * LANES), F32),
             pltpu.VMEM((w_in.shape[0], w_in.shape[1] - plan.width), BF16),
             pltpu.VMEM((plan.cells, plan.width), BF16),
+        ]
+        + [pltpu.SMEM(x.shape, F32) for x in sources[:3]]
+        + [pltpu.VMEM(x.shape, x.dtype) for x in sources[3:]]
+        + [
             pltpu.SemaphoreType.DMA,
             pltpu.SemaphoreType.DMA,
+            pltpu.SemaphoreType.DMA((len(sources),)),
+            pltpu.SemaphoreType.DMA((4,)),
         ],
         compiler_params=pltpu.CompilerParams(vmem_limit_bytes=24 * 2**20),
         name="home",
-    )(in_hbm(rate_x), in_hbm(rate_y), in_hbm(d_skip), *args)
+    )(v, rows, flat, *fixed)
 
 
 def ones(mask):

time: 45.4 us -> 45.4 us (level)
  waiting for transfers between devices: 2.66 us -> 3.46 us
  Pallas kernels: 18.9 us -> 18.1 us
    pallas_call x1, Pallas kernels: 6.85 us -> 6.05 us  [home(): pl.pallas_call(functools.partial(home_kernel, plan), grid=(1,), in_specs=...]
    all_to_all x1, waiting for transfers between devices: 2.56 us -> 3.36 us  [per_device(): pay = lax.all_to_all(pay, 'col', 0, 0, tiled=True, axis_index_groups=groups)]
  transfers between devices with their start and end apart: 3 -> 3, of which waited for: 2 -> 2; matrix products, arithmetic and copies ran while one was open for 0% -> 0% of each run, Pallas kernels for 26% -> 24%
where the time goes in v13:
time: 45.4 us; the launch traced here: 45.1 us
  Pallas kernels  18.1 us (40%)
  blocking collectives  12.8 us (28%)
  starting transfers between devices  10.6 us (23%)
  waiting for transfers between devices  3.46 us (8%)
    all_to_all x1, blocking collectives, per_device(): y = lax.all_to_all(y, 'col', 0, 0, tiled=True, axis_index_groups=groups)  12.8 us
    pallas_call x6, Pallas kernels, call(): pl.pallas_call(kernel, grid=(1,), in_specs=[full(x.shape) for x in args],...  8.82 us
    all_to_all x1, starting transfers between devices, per_device(): pay = lax.all_to_all(pay, 'col', 0, 0, tiled=True, axis_index_groups=groups)  6.22 us
    pallas_call x1, Pallas kernels, home(): pl.pallas_call(functools.partial(home_kernel, plan), grid=(1,), in_specs=...  6.05 us
    all_to_all x1, waiting for transfers between devices, per_device(): pay = lax.all_to_all(pay, 'col', 0, 0, tiled=True, axis_index_groups=groups)  3.36 us
    pallas_call x1, Pallas kernels, project(): pl.pallas_call(functools.partial(project_kernel, plan, chunks), grid=(1,)...  3.26 us
    ppermute x1, starting transfers between devices, scan_calls(): lax.ppermute(last, col_axis, [(k, k + plan.devices) for k in range(plan.d...  3.04 us
    ppermute x1, starting transfers between devices, scan_calls(): entry = lax.ppermute(tops, row_axis, chain)  1.31 us
  transfers between devices with their start and end apart: 3, of which 2 were waited for; matrix products, arithmetic and copies ran while one was open for 0% of the time, Pallas kernels for 24%

profile of v13, /device:TPU:0, one launch (start us, length us, event | category | flops | bytes accessed | tf_op | source)
XLA Modules:
  0.0 45.1 jit_solution(7880611802693301488)
XLA Ops:
  0.0 3.3 %project.1 = (bf16[256,1024]{1,0:T(8,128)(2,1)S(1)}, bf16[8,272,128]{2,1,0:T(8,128)(2,1)}, f32[48,256]{1,0:T(8,128)S(1)}, bf16[200,1024]{1,0:T(8,128)(2,1)S(1)}) custom-call(f32[16]{0:T(128)} %bias_hbm.1, f32[16]{0:T(128)} %refs_0_.1, f32[16]{0:T(128)} %refs_1_.1, bf16[28,7,1024]{2,1,0:T(8,128)(2,1)} %x_hbm.1, bf16[1024,2048]{1,0:T(8,128)(2,1)} %w_hbm.3, ...), custom_call_target="tpu_custom_call" | custom-call | tf_op jit(solution)/shard_map/project/pallas_call | solution.py:250
  3.3 6.2 %all-to-all-start = ((bf16[8,272,128]{2,1,0:T(8,128)(2,1)}), bf16[8,272,128]{2,1,0:T(8,128)(2,1)S(1)}, u32[]{:S(2)}, u32[]{:S(2)}) async-start(bf16[8,272,128]{2,1,0:T(8,128)(2,1)} %get-tuple-element.24), calls=%async_computation | async-start | bytes 1114112 | tf_op jit(solution)/shard_map/all_to_all | solution.py:700
  9.5 6.1 %home.1 = (bf16[200,1024]{1,0:T(8,128)(2,1)S(1)}, bf16[200,1024]{1,0:T(8,128)(2,1)S(1)}, f32[1,1024]{1,0:T(1,128)S(1)}) custom-call(bf16[256,1024]{1,0:T(8,128)(2,1)S(1)} %get-tuple-element.25.v_ref, f32[48,256]{1,0:T(8,128)S(1)} %get-tuple-element.26.rows_ref, bf16[200,1024]{1,0:T(8,128)(2,1)S(1)} %get-tuple-element.27.flat_ref, bf16[1024,2048]{1,0:T(8,128)(2,1)} %w_hbm.3, ...), custom_call_target="tpu_custom_call" | custom-call | tf_op jit(solution)/shard_map/home/pallas_call | solution.py:328
  15.6 3.4 %all-to-all-done.pay_ref = bf16[8,272,128]{2,1,0:T(8,128)(2,1)S(1)} async-done(((bf16[8,272,128]{2,1,0:T(8,128)(2,1)}), bf16[8,272,128]{2,1,0:T(8,128)(2,1)S(1)}, u32[]{:S(2)}, u32[]{:S(2)}) %all-to-all-start) | async-done | bytes 557088 | tf_op jit(solution)/shard_map/all_to_all | solution.py:700
  18.9 1.5 %last.1 = bf16[7,64,128]{2,1,0:T(8,128)(2,1)S(1)} custom-call(bf16[8,272,128]{2,1,0:T(8,128)(2,1)S(1)} %all-to-all-done.pay_ref), custom_call_target="tpu_custom_call" | custom-call | tf_op jit(solution)/shard_map/last/pallas_call | solution.py:579
  20.4 3.0 %collective-permute-start = (bf16[7,64,128]{2,1,0:T(8,128)(2,1)S(1)}, bf16[7,64,128]{2,1,0:T(8,128)(2,1)S(1)}, u32[]{:S(2)}, u32[]{:S(2)}) collective-permute-start(bf16[7,64,128]{2,1,0:T(8,128)(2,1)S(1)} %last.1), channel_id=1, source_target_pairs={{0,8},{1,9},{2,10},{3,11},{4,12},{5,13},{6,14},{7,15},{16,24},{17,... | collective-permute-start | bytes 344072 | tf_op jit(solution)/shard_map/ppermute | solution.py:598
  23.4 3.9 %maps.1 = (bf16[16,32,256]{2,1,0:T(8,128)(2,1)S(1)}, f32[16,256]{1,0:T(8,128)S(1)}, bf16[16,448,128]{2,1,0:T(8,128)(2,1)S(1)}, f32[16,64,128]{2,1,0:T(8,128)S(1)...) custom-call(bf16[8,272,128]{2,1,0:T(8,128)(2,1)S(1)} %all-to-all-done.pay_ref, ...), custom_call_target="tpu_custom_call" | custom-call | tf_op jit(solution)/shard_map/maps/pallas_call | solution.py:579
  27.3 0.0 collective-permute-done.entry_ref
  27.3 0.5 %join.1 = bf16[16,64,128]{2,1,0:T(8,128)(2,1)S(1)} custom-call(f32[16,448]{1,0:T(8,128)S(1)} %get-tuple-element.33.upto_ref, bf16[7,64,128]{2,1,0:T(8,128)(2,1)S(1)} %collective-permute-done.entry_ref, bf16[16,448,128]{2,1,0:T(8,128)(2,1)S(1)} %get-tuple-element.38.passed_ref, f32[16,64,128]{2,1,0:T(8,128)S(1)} %get-tuple-element.39.top_ref), custom_call_target="tpu_custom_call" | custom-call | tf_op jit(solution)/shard_map/join/pallas_call | solution.py:579
  27.8 1.3 %collective-permute-start.1 = (bf16[16,64,128]{2,1,0:T(8,128)(2,1)S(1)}, bf16[16,64,128]{2,1,0:T(8,128)(2,1)S(1)}, u32[]{:S(2)}, u32[]{:S(2)}) collective-permute-start(bf16[16,64,128]{2,1,0:T(8,128)(2,1)S(1)} %join.1), channel_id=1, source_target_pairs={{0,16},{1,17},{2,18},{3,19},{4,20},{5,21},{6,22},{7,23},{8,24},{9,... | collective-permute-start | bytes 786440 | tf_op jit(solution)/shard_map/ppermute | solution.py:625
  29.1 1.0 %sides.1 = (f32[16,64,256]{2,1,0:T(8,128)S(1)}, bf16[16,128,256]{2,1,0:T(8,128)(2,1)S(1)}) custom-call(bf16[8,272,128]{2,1,0:T(8,128)(2,1)S(1)} %all-to-all-done.pay_ref, bf16[16,64,448]{2,1,0:T(8,128)(2,1)S(1)} %get-tuple-element.32.edge_ref, f32[16,448]{1,0:T(8,128)S(1)} %get-tuple-element.33.upto_ref, ...), custom_call_target="tpu_custom_call" | custom-call | tf_op jit(solution)/shard_map/sides/pallas_call | solution.py:579
  30.1 0.0 copy-start
  30.2 0.1 collective-permute-done.1.top_ref
  30.3 0.4 cells.1
  30.6 12.8 %all_to_all.10.y_ref = bf16[8,200,128]{2,1,0:T(8,128)(2,1)S(1)} all-to-all(bf16[8,200,128]{2,1,0:T(8,128)(2,1)S(1)} %cells.1), channel_id=1, replica_groups={{0,1,2,3,4,5,6,7},{8,9,10,11,12,13,14,15},{16,17,18,19,20,21,22,23},{24..., dimensions={0} | all-to-all | bytes 819200 | tf_op jit(solution)/shard_map/all_to_all | solution.py:705
  43.4 0.0 copy-done
  43.5 1.6 %finish.1 = bf16[28,7,1024]{2,1,0:T(8,128)(2,1)} custom-call(bf16[8,200,128]{2,1,0:T(8,128)(2,1)S(1)} %all_to_all.10.y_ref, bf16[200,1024]{1,0:T(8,128)(2,1)S(1)} %get-tuple-element.40.own_ref, bf16[200,1024]{1,0:T(8,128)(2,1)S(1)} %get-tuple-element.41.gate_ref, f32[1,1024]{1,0:T(1,128)S(1)} %get-tuple-element.42.gain_ref, bf16[1024,1024]{1,0:T(8,128)(2,1)S(1)} %copy-done), custom_call_target="tpu_custom_call" | custom-call | tf_op jit(solution)/shard_map/finish/pallas_call | solution.py:579
Async XLA Ops:
  3.3 15.6 %all-to-all-start = ((bf16[8,272,128]{2,1,0:T(8,128)(2,1)}), bf16[8,272,128]{2,1,0:T(8,128)(2,1)S(1)}, u32[]{:S(2)}, u32[]{:S(2)}) async-start(bf16[8,272,128]{2,1,0:T(8,128)(2,1)} %get-tuple-element.24), calls=%async_computation | async-start | bytes 1114112 | tf_op jit(solution)/shard_map/all_to_all | solution.py:700
  20.4 6.9 %collective-permute-start = (bf16[7,64,128]{2,1,0:T(8,128)(2,1)S(1)}, bf16[7,64,128]{2,1,0:T(8,128)(2,1)S(1)}, u32[]{:S(2)}, u32[]{:S(2)}) collective-permute-start(bf16[7,64,128]{2,1,0:T(8,128)(2,1)S(1)} %last.1), channel_id=1, source_target_pairs={{0,8},{1,9},{2,10},{3,11},{4,12},{5,13},{6,14},{7,15},{16,24},{17,... | collective-permute-start | bytes 344072 | tf_op jit(solution)/shard_map/ppermute | solution.py:598
  27.8 2.4 %collective-permute-start.1 = (bf16[16,64,128]{2,1,0:T(8,128)(2,1)S(1)}, bf16[16,64,128]{2,1,0:T(8,128)(2,1)S(1)}, u32[]{:S(2)}, u32[]{:S(2)}) collective-permute-start(bf16[16,64,128]{2,1,0:T(8,128)(2,1)S(1)} %join.1), channel_id=1, source_target_pairs={{0,16},{1,17},{2,18},{3,19},{4,20},{5,21},{6,22},{7,23},{8,24},{9,... | collective-permute-start | bytes 786440 | tf_op jit(solution)/shard_map/ppermute | solution.py:625
  30.1 13.3 %copy-start = (bf16[1024,1024]{1,0:T(8,128)(2,1)S(1)}, bf16[1024,1024]{1,0:T(8,128)(2,1)}, u32[]{:S(2)}) copy-start(bf16[1024,1024]{1,0:T(8,128)(2,1)} %w_ref.1) | copy-start | bytes 6291460

commit v14 on v13

--- a/solution.py
+++ b/solution.py
@@ -53,8 +53,11 @@
         self.edge = rows * states
         self.top = states * self.col_pad
         self.bc = 2 * states
+        self.spare = LANES - self.half
+        self.tail_cells = self.count - self.half - HALF - self.spare
         self.at_bc = self.cells
-        self.at_dt = self.at_bc + 2 * self.bc
+        self.at_dt = self.at_bc + self.bc + states
+        assert HALF <= self.half and 0 < self.tail_cells <= self.cells - self.count and self.bc <= HALF
         self.at_rate = self.at_dt + 2 * self.slots
         self.message = round_up(self.at_rate + 1, 8)
         self.tail = self.edge % LANES
@@ -198,7 +201,15 @@
     soft = m * (jnp.maximum(z, 0.0) + jnp.log1p(jnp.exp(-jnp.abs(z))))
     table = jnp.concatenate([table[: 2 * states], soft], axis=0).astype(BF16)
     rows_ref[...] = table.astype(F32)
-    bc = table[: 2 * states]
+    bc = rows_ref[: 2 * states, :]
+    lane = lax.broadcasted_iota(jnp.int32, (2 * states, LANES), 1)
+    early = jnp.where(lane < half, bc[:, :LANES], pltpu.roll(bc[:, LANES:], half - HALF, 1)).astype(BF16)
+    lane = lax.broadcasted_iota(jnp.int32, (states, LANES), 1)
+    late = jnp.where(lane < HALF, bc[:states, LANES:], pltpu.roll(bc[states:, LANES:], HALF, 1)).astype(BF16)
+    ends = nt_dot(x[cells - 8 :], wt_ref[0 : 2 * states, :])
+    ends = jnp.concatenate([ends, jnp.zeros((8, LANES - 2 * states), F32)], axis=1)
+    ends = pltpu.roll(ends, plan.tail_cells, 0)
+    pad_row = lax.broadcasted_iota(jnp.int32, (8, LANES), 0) >= plan.count - (cells - 8)
     steps = rows_ref[2 * states :, :]
 
     lane = lax.broadcasted_iota(jnp.int32, (cells, LANES), 1)
@@ -218,15 +229,16 @@
                 mine = pltpu.roll(mine, LANES - at, 1)
             if group < LANES:
                 mine = jnp.where(lane < group, mine, 0.0)
-            pay_ref[dest, 0:cells, :] = mine.astype(BF16)
+            pay_ref[dest, 0 : cells - 8, :] = mine[: cells - 8].astype(BF16)
+            pay_ref[dest, cells - 8 : cells, :] = jnp.where(pad_row, ends, mine[cells - 8 :]).astype(BF16)
             dts, heads_of = [], []
             for s in range(plan.slots):
                 head = (chunk * tile + k * group + s * plan.slot) // plan.head_width
                 heads_of.append(head)
                 dts += [steps[head : head + 1, :LANES], steps[head : head + 1, LANES:]]
             dts.append(rate_row(heads_of, rx_ref, ry_ref))
-            pay_ref[dest, plan.at_bc : plan.at_bc + plan.bc, :] = bc[:, :LANES]
-            pay_ref[dest, plan.at_bc + plan.bc : plan.at_dt, :] = bc[:, LANES:]
+            pay_ref[dest, plan.at_bc : plan.at_bc + plan.bc, :] = early
+            pay_ref[dest, plan.at_bc + plan.bc : plan.at_dt, :] = late
             spare = plan.message - plan.at_dt - len(dts)
             dts += [jnp.zeros((spare, LANES), F32)] if spare else []
             pay_ref[dest, plan.at_dt : plan.message, :] = jnp.concatenate(dts, axis=0).astype(BF16)
@@ -361,8 +373,18 @@
     return i, j, cell < jnp.where(late, plan.count, plan.half)
 
 
-def wide_rows(pay_ref, t, at, count, gap):
-    return jnp.concatenate([pay_ref[t, at : at + count, :], pay_ref[t, at + gap : at + gap + count, :]], axis=1)
+def map_rows(plan, pay_ref, turned, t, k):
+    n = plan.states
+    first = pay_ref[t, plan.at_bc + k * n : plan.at_bc + (k + 1) * n, :].astype(F32)
+    second = pay_ref[t, plan.at_bc + plan.bc : plan.at_dt, :].astype(F32)
+    if k:
+        second = pltpu.roll(second, HALF, 1)
+    ends = turned[t][k * n : (k + 1) * n, LANES:].astype(F32)
+    lane = lax.broadcasted_iota(jnp.int32, (n, LANES), 1)
+    moved = pltpu.roll(first, LANES + HALF - plan.half, 1)
+    ends = pltpu.roll(ends, LANES - plan.tail_cells, 1)
+    second = jnp.where(lane < HALF, second, jnp.where(lane < HALF + plan.spare, moved, ends))
+    return jnp.concatenate([first, second], axis=1)
 
 
 def turn_all(plan, pay_ref, turned):
@@ -444,7 +466,7 @@
         for t in range(tiles):
             w = s * tiles + t
             seen(w, held, product)
-            b = wide_rows(pay_ref, t, plan.at_bc, states, plan.bc).astype(F32)
+            b = map_rows(plan, pay_ref, turned, t, 0)
             bd = (b * inner[w : w + 1, :]).astype(BF16)
             left = jnp.concatenate([bd * rowsel[i : i + 1] for i in range(plan.rows)], axis=0)
             now = kept[w : w + 1, :]
@@ -481,7 +503,7 @@
             held = None
             for t in range(tiles):
                 w = s * tiles + t
-                b = wide_rows(pay_ref, t, plan.at_bc, states, plan.bc).astype(F32)
+                b = map_rows(plan, pay_ref, turned, t, 0)
                 bd = (b * inner[w : w + 1, :]).astype(BF16)
                 left = jnp.concatenate([bd * rowsel[i : i + 1] for i in range(plan.rows)], axis=0)
                 part = nt_dot(turned[w], left)
@@ -493,12 +515,14 @@
 def maps_kernel(
     plan, pay_ref, to1_ref, to2_ref, from1_ref, from2_ref, side1_ref, side2_ref,
     sidemask_ref, down1_ref, down2_ref, downmask_ref, pick_ref,
-    side_ref, above_ref, passed_ref, top_ref, edge_ref, upto_ref, turned, dts, inner, kept, s1, s2, d1, d2,
+    side_ref, above_ref, passed_ref, top_ref, edge_ref, upto_ref, c_ref, turned, dts, inner, kept, s1, s2, d1, d2,
 ):
     states, tiles, cp, work = plan.states, plan.devices, plan.col_pad, plan.work
     rp = side1_ref.shape[0]
     turn_all(plan, pay_ref, turned)
     load_steps(plan, pay_ref, dts)
+    for t in range(tiles):
+        c_ref[t] = map_rows(plan, pay_ref, turned, t, 1).astype(BF16)
 
     def seen(w, held, product):
         edge_ref[w] = held.astype(BF16)
@@ -532,7 +556,7 @@
         s, t = w // tiles, w % tiles
         at = slice(w * cp, (w + 1) * cp)
         fall = jnp.exp(-(rates_x[s] * x[at] + rates_y[s] * y[at])) * mask * dts[w : w + 1, :]
-        b = wide_rows(pay_ref, t, plan.at_bc, states, plan.bc).astype(F32)
+        b = map_rows(plan, pay_ref, turned, t, 0)
         falls = jnp.concatenate([fall * b[n : n + 1] for n in range(states)], axis=0).astype(BF16)
         top_ref[w] = nt_dot(turned[w], falls) + mm(edge_ref[w], passed_ref[w])
 
@@ -546,7 +570,7 @@
             out_ref[w] = (top_ref[w] + mm(late, passed_ref[w])).astype(BF16)
 
 
-def sides_kernel(plan, pay_ref, edge_ref, upto_ref, entry_ref, side_ref, above_ref, y_ref, down_ref):
+def sides_kernel(plan, c_ref, edge_ref, upto_ref, entry_ref, side_ref, above_ref, y_ref, down_ref):
     states, tiles = plan.states, plan.devices
     shape = (plan.col_pad, 2 * LANES)
     _, tj, treal = places(plan, shape, 1)
@@ -555,7 +579,7 @@
         entry = unpack_edges(plan, entry_ref, s)
         for t in range(tiles):
             w = s * tiles + t
-            c = wide_rows(pay_ref, t, plan.at_bc + states, states, plan.bc)
+            c = c_ref[t]
             side = side_ref[w]
             left = jnp.concatenate([c * side[i : i + 1] for i in range(plan.rows)], axis=0)
             whole = (edge_ref[w].astype(F32) + entry * upto_ref[w : w + 1, :]).astype(BF16)
@@ -599,7 +623,7 @@
     else:
         entry = jnp.zeros(shape, BF16)
     names = ("to1", "to2", "from1", "from2", "side1", "side2", "sidemask", "down1", "down2", "downmask", "pick")
-    side, above, passed, tops, edges, upto = call(
+    side, above, passed, tops, edges, upto, c = call(
         functools.partial(maps_kernel, plan),
         "maps",
         [pay] + [consts[k] for k in names],
@@ -610,6 +634,7 @@
             ((work, HALF, plan.top), F32),
             ((work, HALF, plan.edge), BF16),
             ((work, plan.edge), F32),
+            ((plan.devices, plan.states, wide), BF16),
         ],
         steps + [((work * rp, wide), F32)] * 2 + [((work * cp, wide), F32)] * 2,
     )
@@ -632,7 +657,7 @@
     y, down = call(
         functools.partial(sides_kernel, plan),
         "sides",
-        [pay, edges, upto, edge_entry, side, above],
+        [c, edges, upto, edge_entry, side, above],
         [((work, HALF, wide), F32), ((work, plan.top, wide), BF16)],
     )
     return call(

time: 45.4 us -> 45.1 us (level)
  Pallas kernels: 18.1 us -> 18.7 us
  transfers between devices with their start and end apart: 3 -> 3, of which waited for: 2 -> 1; matrix products, arithmetic and copies ran while one was open for 0% -> 0% of each run, Pallas kernels for 24% -> 25%
where the time goes in v14:
time: 45.1 us; the launch traced here: 44.7 us
  Pallas kernels  18.7 us (41%)
  blocking collectives  12.6 us (28%)
  starting transfers between devices  10.4 us (23%)
  waiting for transfers between devices  3.06 us (7%)
    all_to_all x1, blocking collectives, per_device(): y = lax.all_to_all(y, 'col', 0, 0, tiled=True, axis_index_groups=groups)  12.6 us
    pallas_call x6, Pallas kernels, call(): pl.pallas_call(kernel, grid=(1,), in_specs=[full(x.shape) for x in args],...  9.25 us
    all_to_all x1, starting transfers between devices, per_device(): pay = lax.all_to_all(pay, 'col', 0, 0, tiled=True, axis_index_groups=groups)  6.23 us
    pallas_call x1, Pallas kernels, home(): pl.pallas_call(functools.partial(home_kernel, plan), grid=(1,), in_specs=...  6.05 us
    pallas_call x1, Pallas kernels, project(): pl.pallas_call(functools.partial(project_kernel, plan, chunks), grid=(1,)...  3.36 us
    all_to_all x1, waiting for transfers between devices, per_device(): pay = lax.all_to_all(pay, 'col', 0, 0, tiled=True, axis_index_groups=groups)  3.05 us
    ppermute x1, starting transfers between devices, scan_calls(): lax.ppermute(last, col_axis, [(k, k + plan.devices) for k in range(plan.d...  2.85 us
    ppermute x1, starting transfers between devices, scan_calls(): entry = lax.ppermute(tops, row_axis, chain)  1.31 us
  transfers between devices with their start and end apart: 3, of which 1 were waited for; matrix products, arithmetic and copies ran while one was open for 0% of the time, Pallas kernels for 25%

profile of v14, /device:TPU:0, one launch (start us, length us, event | category | flops | bytes accessed | tf_op | source)
XLA Modules:
  0.0 44.7 jit_solution(18084849839841686657)
XLA Ops:
  0.0 3.4 %project.1 = (bf16[256,1024]{1,0:T(8,128)(2,1)S(1)}, bf16[8,256,128]{2,1,0:T(8,128)(2,1)}, f32[48,256]{1,0:T(8,128)S(1)}, bf16[200,1024]{1,0:T(8,128)(2,1)S(1)}) custom-call(f32[16]{0:T(128)} %bias_hbm.1, f32[16]{0:T(128)} %refs_0_.1, f32[16]{0:T(128)} %refs_1_.1, bf16[28,7,1024]{2,1,0:T(8,128)(2,1)} %x_hbm.1, bf16[1024,2048]{1,0:T(8,128)(2,1)} %w_hbm.3, ...), custom_call_target="tpu_custom_call" | custom-call | tf_op jit(solution)/shard_map/project/pallas_call | solution.py:262
  3.4 6.2 %all-to-all-start = ((bf16[8,256,128]{2,1,0:T(8,128)(2,1)}), bf16[8,256,128]{2,1,0:T(8,128)(2,1)S(1)}, u32[]{:S(2)}, u32[]{:S(2)}) async-start(bf16[8,256,128]{2,1,0:T(8,128)(2,1)} %get-tuple-element.25), calls=%async_computation | async-start | bytes 1048576 | tf_op jit(solution)/shard_map/all_to_all | solution.py:725
  9.6 6.1 %home.1 = (bf16[200,1024]{1,0:T(8,128)(2,1)S(1)}, bf16[200,1024]{1,0:T(8,128)(2,1)S(1)}, f32[1,1024]{1,0:T(1,128)S(1)}) custom-call(bf16[256,1024]{1,0:T(8,128)(2,1)S(1)} %get-tuple-element.26.v_ref, f32[48,256]{1,0:T(8,128)S(1)} %get-tuple-element.27.rows_ref, bf16[200,1024]{1,0:T(8,128)(2,1)S(1)} %get-tuple-element.28.flat_ref, bf16[1024,2048]{1,0:T(8,128)(2,1)} %w_hbm.3, ...), custom_call_target="tpu_custom_call" | custom-call | tf_op jit(solution)/shard_map/home/pallas_call | solution.py:340
  15.7 3.1 %all-to-all-done.pay_ref = bf16[8,256,128]{2,1,0:T(8,128)(2,1)S(1)} async-done(((bf16[8,256,128]{2,1,0:T(8,128)(2,1)}), bf16[8,256,128]{2,1,0:T(8,128)(2,1)S(1)}, u32[]{:S(2)}, u32[]{:S(2)}) %all-to-all-start) | async-done | bytes 524320 | tf_op jit(solution)/shard_map/all_to_all | solution.py:725
  18.7 1.6 %last.1 = bf16[7,64,128]{2,1,0:T(8,128)(2,1)S(1)} custom-call(bf16[8,256,128]{2,1,0:T(8,128)(2,1)S(1)} %all-to-all-done.pay_ref), custom_call_target="tpu_custom_call" | custom-call | tf_op jit(solution)/shard_map/last/pallas_call | solution.py:603
  20.3 2.8 %collective-permute-start = (bf16[7,64,128]{2,1,0:T(8,128)(2,1)S(1)}, bf16[7,64,128]{2,1,0:T(8,128)(2,1)S(1)}, u32[]{:S(2)}, u32[]{:S(2)}) collective-permute-start(bf16[7,64,128]{2,1,0:T(8,128)(2,1)S(1)} %last.1), channel_id=1, source_target_pairs={{0,8},{1,9},{2,10},{3,11},{4,12},{5,13},{6,14},{7,15},{16,24},{17,... | collective-permute-start | bytes 344072 | tf_op jit(solution)/shard_map/ppermute | solution.py:622
  23.2 4.0 %maps.1 = (bf16[16,32,256]{2,1,0:T(8,128)(2,1)S(1)}, f32[16,256]{1,0:T(8,128)S(1)}, bf16[16,448,128]{2,1,0:T(8,128)(2,1)S(1)}, f32[16,64,128]{2,1,0:T(8,128)S(1)...) custom-call(bf16[8,256,128]{2,1,0:T(8,128)(2,1)S(1)} %all-to-all-done.pay_ref, ...), custom_call_target="tpu_custom_call" | custom-call | tf_op jit(solution)/shard_map/maps/pallas_call | solution.py:603
  27.2 0.0 collective-permute-done.entry_ref
  27.3 0.5 %join.1 = bf16[16,64,128]{2,1,0:T(8,128)(2,1)S(1)} custom-call(f32[16,448]{1,0:T(8,128)S(1)} %get-tuple-element.35.upto_ref, bf16[7,64,128]{2,1,0:T(8,128)(2,1)S(1)} %collective-permute-done.entry_ref, bf16[16,448,128]{2,1,0:T(8,128)(2,1)S(1)} %get-tuple-element.40.passed_ref, f32[16,64,128]{2,1,0:T(8,128)S(1)} %get-tuple-element.41.top_ref), custom_call_target="tpu_custom_call" | custom-call | tf_op jit(solution)/shard_map/join/pallas_call | solution.py:603
  27.8 1.3 %collective-permute-start.1 = (bf16[16,64,128]{2,1,0:T(8,128)(2,1)S(1)}, bf16[16,64,128]{2,1,0:T(8,128)(2,1)S(1)}, u32[]{:S(2)}, u32[]{:S(2)}) collective-permute-start(bf16[16,64,128]{2,1,0:T(8,128)(2,1)S(1)} %join.1), channel_id=1, source_target_pairs={{0,16},{1,17},{2,18},{3,19},{4,20},{5,21},{6,22},{7,23},{8,24},{9,... | collective-permute-start | bytes 786440 | tf_op jit(solution)/shard_map/ppermute | solution.py:650
  29.1 1.1 %sides.1 = (f32[16,64,256]{2,1,0:T(8,128)S(1)}, bf16[16,128,256]{2,1,0:T(8,128)(2,1)S(1)}) custom-call(bf16[8,16,256]{2,1,0:T(8,128)(2,1)S(1)} %get-tuple-element.33.c_ref, bf16[16,64,448]{2,1,0:T(8,128)(2,1)S(1)} %get-tuple-element.34.edge_ref, f32[16,448]{1,0:T(8,128)S(1)} %get-tuple-element.35.upto_ref, ...), custom_call_target="tpu_custom_call" | custom-call | tf_op jit(solution)/shard_map/sides/pallas_call | solution.py:603
  30.2 0.0 copy-start
  30.2 0.0 collective-permute-done.1.top_ref
  30.2 0.4 cells.1
  30.6 12.6 %all_to_all.10.y_ref = bf16[8,200,128]{2,1,0:T(8,128)(2,1)S(1)} all-to-all(bf16[8,200,128]{2,1,0:T(8,128)(2,1)S(1)} %cells.1), channel_id=1, replica_groups={{0,1,2,3,4,5,6,7},{8,9,10,11,12,13,14,15},{16,17,18,19,20,21,22,23},{24..., dimensions={0} | all-to-all | bytes 819200 | tf_op jit(solution)/shard_map/all_to_all | solution.py:730
  43.1 0.0 copy-done
  43.1 1.6 %finish.1 = bf16[28,7,1024]{2,1,0:T(8,128)(2,1)} custom-call(bf16[8,200,128]{2,1,0:T(8,128)(2,1)S(1)} %all_to_all.10.y_ref, bf16[200,1024]{1,0:T(8,128)(2,1)S(1)} %get-tuple-element.42.own_ref, bf16[200,1024]{1,0:T(8,128)(2,1)S(1)} %get-tuple-element.43.gate_ref, f32[1,1024]{1,0:T(1,128)S(1)} %get-tuple-element.44.gain_ref, bf16[1024,1024]{1,0:T(8,128)(2,1)S(1)} %copy-done), custom_call_target="tpu_custom_call" | custom-call | tf_op jit(solution)/shard_map/finish/pallas_call | solution.py:603
Async XLA Ops:
  3.4 15.3 %all-to-all-start = ((bf16[8,256,128]{2,1,0:T(8,128)(2,1)}), bf16[8,256,128]{2,1,0:T(8,128)(2,1)S(1)}, u32[]{:S(2)}, u32[]{:S(2)}) async-start(bf16[8,256,128]{2,1,0:T(8,128)(2,1)} %get-tuple-element.25), calls=%async_computation | async-start | bytes 1048576 | tf_op jit(solution)/shard_map/all_to_all | solution.py:725
  20.3 6.9 %collective-permute-start = (bf16[7,64,128]{2,1,0:T(8,128)(2,1)S(1)}, bf16[7,64,128]{2,1,0:T(8,128)(2,1)S(1)}, u32[]{:S(2)}, u32[]{:S(2)}) collective-permute-start(bf16[7,64,128]{2,1,0:T(8,128)(2,1)S(1)} %last.1), channel_id=1, source_target_pairs={{0,8},{1,9},{2,10},{3,11},{4,12},{5,13},{6,14},{7,15},{16,24},{17,... | collective-permute-start | bytes 344072 | tf_op jit(solution)/shard_map/ppermute | solution.py:622
  27.8 2.4 %collective-permute-start.1 = (bf16[16,64,128]{2,1,0:T(8,128)(2,1)S(1)}, bf16[16,64,128]{2,1,0:T(8,128)(2,1)S(1)}, u32[]{:S(2)}, u32[]{:S(2)}) collective-permute-start(bf16[16,64,128]{2,1,0:T(8,128)(2,1)S(1)} %join.1), channel_id=1, source_target_pairs={{0,16},{1,17},{2,18},{3,19},{4,20},{5,21},{6,22},{7,23},{8,24},{9,... | collective-permute-start | bytes 786440 | tf_op jit(solution)/shard_map/ppermute | solution.py:650
  30.2 13.0 %copy-start = (bf16[1024,1024]{1,0:T(8,128)(2,1)S(1)}, bf16[1024,1024]{1,0:T(8,128)(2,1)}, u32[]{:S(2)}) copy-start(bf16[1024,1024]{1,0:T(8,128)(2,1)} %w_ref.1) | copy-start | bytes 6291460

commit v15 on v14

--- a/solution.py
+++ b/solution.py
@@ -206,7 +206,8 @@
     early = jnp.where(lane < half, bc[:, :LANES], pltpu.roll(bc[:, LANES:], half - HALF, 1)).astype(BF16)
     lane = lax.broadcasted_iota(jnp.int32, (states, LANES), 1)
     late = jnp.where(lane < HALF, bc[:states, LANES:], pltpu.roll(bc[states:, LANES:], HALF, 1)).astype(BF16)
-    ends = nt_dot(x[cells - 8 :], wt_ref[0 : 2 * states, :])
+    first_end = HALF + plan.spare
+    ends = bc[:, LANES:].T[first_end : first_end + 8]
     ends = jnp.concatenate([ends, jnp.zeros((8, LANES - 2 * states), F32)], axis=1)
     ends = pltpu.roll(ends, plan.tail_cells, 0)
     pad_row = lax.broadcasted_iota(jnp.int32, (8, LANES), 0) >= plan.count - (cells - 8)
@@ -379,7 +380,7 @@
     second = pay_ref[t, plan.at_bc + plan.bc : plan.at_dt, :].astype(F32)
     if k:
         second = pltpu.roll(second, HALF, 1)
-    ends = turned[t][k * n : (k + 1) * n, LANES:].astype(F32)
+    ends = turned[k * n : (k + 1) * n, LANES:].astype(F32)
     lane = lax.broadcasted_iota(jnp.int32, (n, LANES), 1)
     moved = pltpu.roll(first, LANES + HALF - plan.half, 1)
     ends = pltpu.roll(ends, LANES - plan.tail_cells, 1)
@@ -387,7 +388,7 @@
     return jnp.concatenate([first, second], axis=1)
 
 
-def turn_all(plan, pay_ref, turned):
+def turn_all(plan, pay_ref, turned, b_ref):
     for t in range(plan.devices):
         sides = []
         for lo, hi in ((0, plan.half), (plan.half, plan.cells)):
@@ -398,6 +399,7 @@
         v = jnp.concatenate(sides, axis=1).astype(BF16)
         for s in range(plan.slots):
             turned[s * plan.devices + t] = v[s * HALF : (s + 1) * HALF]
+        b_ref[t] = map_rows(plan, pay_ref, v, t, 0)
 
 
 def load_steps(plan, pay_ref, dts):
@@ -444,7 +446,7 @@
     return jnp.concatenate(parts, axis=1)
 
 
-def scan_edges(plan, pay_ref, turned, dts, inner, kept, seen):
+def scan_edges(plan, pay_ref, turned, b_ref, dts, inner, kept, seen):
     states, tiles, wide = plan.states, plan.devices, 2 * LANES
     i, j, real = places(plan, (wide, wide), 0)
     ti, tj, treal = places(plan, (wide, wide), 1)
@@ -466,7 +468,7 @@
         for t in range(tiles):
             w = s * tiles + t
             seen(w, held, product)
-            b = map_rows(plan, pay_ref, turned, t, 0)
+            b = b_ref[t]
             bd = (b * inner[w : w + 1, :]).astype(BF16)
             left = jnp.concatenate([bd * rowsel[i : i + 1] for i in range(plan.rows)], axis=0)
             now = kept[w : w + 1, :]
@@ -476,11 +478,11 @@
     return ends
 
 
-def last_kernel(plan, axis, pay_ref, last_ref, turned, dts, inner):
+def last_kernel(plan, axis, pay_ref, last_ref, turned, b_ref, dts, inner):
     @pl.when(lax.axis_index(axis) < (plan.parts - 1) * plan.devices)
     def _():
         states, tiles, wide = plan.states, plan.devices, 2 * LANES
-        turn_all(plan, pay_ref, turned)
+        turn_all(plan, pay_ref, turned, b_ref)
         load_steps(plan, pay_ref, dts)
         i, j, real = places(plan, (wide, wide), 0)
         ti, tj, treal = places(plan, (wide, wide), 1)
@@ -503,7 +505,7 @@
             held = None
             for t in range(tiles):
                 w = s * tiles + t
-                b = map_rows(plan, pay_ref, turned, t, 0)
+                b = b_ref[t]
                 bd = (b * inner[w : w + 1, :]).astype(BF16)
                 left = jnp.concatenate([bd * rowsel[i : i + 1] for i in range(plan.rows)], axis=0)
                 part = nt_dot(turned[w], left)
@@ -515,20 +517,20 @@
 def maps_kernel(
     plan, pay_ref, to1_ref, to2_ref, from1_ref, from2_ref, side1_ref, side2_ref,
     sidemask_ref, down1_ref, down2_ref, downmask_ref, pick_ref,
-    side_ref, above_ref, passed_ref, top_ref, edge_ref, upto_ref, c_ref, turned, dts, inner, kept, s1, s2, d1, d2,
+    side_ref, above_ref, passed_ref, top_ref, edge_ref, upto_ref, c_ref, turned, b_ref, dts, inner, kept, s1, s2, d1, d2,
 ):
     states, tiles, cp, work = plan.states, plan.devices, plan.col_pad, plan.work
     rp = side1_ref.shape[0]
-    turn_all(plan, pay_ref, turned)
+    turn_all(plan, pay_ref, turned, b_ref)
     load_steps(plan, pay_ref, dts)
     for t in range(tiles):
-        c_ref[t] = map_rows(plan, pay_ref, turned, t, 1).astype(BF16)
+        c_ref[t] = map_rows(plan, pay_ref, turned[t], t, 1).astype(BF16)
 
     def seen(w, held, product):
         edge_ref[w] = held.astype(BF16)
         upto_ref[w : w + 1, :] = product
 
-    scan_edges(plan, pay_ref, turned, dts, inner, kept, seen)
+    scan_edges(plan, pay_ref, turned, b_ref, dts, inner, kept, seen)
     low = dts[...].astype(BF16)
     above_ref[...] = jnp.exp(-slot_rates(plan, pay_ref, 1) * mm(low, to2_ref[...]))
     rates_x, rates_y = rates_of(plan, pay_ref, 0), rates_of(plan, pay_ref, 1)
@@ -556,7 +558,7 @@
         s, t = w // tiles, w % tiles
         at = slice(w * cp, (w + 1) * cp)
         fall = jnp.exp(-(rates_x[s] * x[at] + rates_y[s] * y[at])) * mask * dts[w : w + 1, :]
-        b = map_rows(plan, pay_ref, turned, t, 0)
+        b = b_ref[t]
         falls = jnp.concatenate([fall * b[n : n + 1] for n in range(states)], axis=0).astype(BF16)
         top_ref[w] = nt_dot(turned[w], falls) + mm(edge_ref[w], passed_ref[w])
 
@@ -615,10 +617,10 @@
 def scan_calls(plan, consts, row_axis, col_axis, pay):
     work, cp, wide = plan.work, plan.col_pad, 2 * LANES
     rp = consts["side1"].shape[0]
-    steps = [((work, HALF, wide), BF16), ((work, wide), F32), ((work, wide), F32), ((work, plan.edge), F32)]
+    steps = [((work, HALF, wide), BF16), ((plan.devices, plan.states, wide), F32), ((work, wide), F32), ((work, wide), F32), ((work, plan.edge), F32)]
     shape = (plan.packed, HALF, LANES)
     if plan.parts > 1:
-        last = call(functools.partial(last_kernel, plan, col_axis), "last", [pay], [(shape, BF16)], steps[:3])[0]
+        last = call(functools.partial(last_kernel, plan, col_axis), "last", [pay], [(shape, BF16)], steps[:4])[0]
         entry = lax.ppermute(last, col_axis, [(k, k + plan.devices) for k in range(plan.devices)])
     else:
         entry = jnp.zeros(shape, BF16)

time: 45.1 us -> 45.1 us (level)
  no operation moved by 1% of the time
where the time goes in v15:
time: 45.1 us; the launch traced here: 44.7 us
  Pallas kernels  18.5 us (41%)
  blocking collectives  12.6 us (28%)
  starting transfers between devices  10.5 us (23%)
  waiting for transfers between devices  3.06 us (7%)
    all_to_all x1, blocking collectives, per_device(): y = lax.all_to_all(y, 'col', 0, 0, tiled=True, axis_index_groups=groups)  12.6 us
    pallas_call x6, Pallas kernels, call(): pl.pallas_call(kernel, grid=(1,), in_specs=[full(x.shape) for x in args],...  9.09 us
    all_to_all x1, starting transfers between devices, per_device(): pay = lax.all_to_all(pay, 'col', 0, 0, tiled=True, axis_index_groups=groups)  6.21 us
    pallas_call x1, Pallas kernels, home(): pl.pallas_call(functools.partial(home_kernel, plan), grid=(1,), in_specs=...  6.05 us
    pallas_call x1, Pallas kernels, project(): pl.pallas_call(functools.partial(project_kernel, plan, chunks), grid=(1,)...  3.34 us
    all_to_all x1, waiting for transfers between devices, per_device(): pay = lax.all_to_all(pay, 'col', 0, 0, tiled=True, axis_index_groups=groups)  3.06 us
    ppermute x1, starting transfers between devices, scan_calls(): lax.ppermute(last, col_axis, [(k, k + plan.devices) for k in range(plan.d...  2.97 us
    ppermute x1, starting transfers between devices, scan_calls(): entry = lax.ppermute(tops, row_axis, chain)  1.31 us
  transfers between devices with their start and end apart: 3, of which 1 were waited for; matrix products, arithmetic and copies ran while one was open for 0% of the time, Pallas kernels for 25%

profile of v15, /device:TPU:0, one launch (start us, length us, event | category | flops | bytes accessed | tf_op | source)
XLA Modules:
  0.0 44.7 jit_solution(9337499602575378540)
XLA Ops:
  0.0 3.3 %project.1 = (bf16[256,1024]{1,0:T(8,128)(2,1)S(1)}, bf16[8,256,128]{2,1,0:T(8,128)(2,1)}, f32[48,256]{1,0:T(8,128)S(1)}, bf16[200,1024]{1,0:T(8,128)(2,1)S(1)}) custom-call(f32[16]{0:T(128)} %bias_hbm.1, f32[16]{0:T(128)} %refs_0_.1, f32[16]{0:T(128)} %refs_1_.1, bf16[28,7,1024]{2,1,0:T(8,128)(2,1)} %x_hbm.1, bf16[1024,2048]{1,0:T(8,128)(2,1)} %w_hbm.3, ...), custom_call_target="tpu_custom_call" | custom-call | tf_op jit(solution)/shard_map/project/pallas_call | solution.py:263
  3.4 6.2 %all-to-all-start = ((bf16[8,256,128]{2,1,0:T(8,128)(2,1)}), bf16[8,256,128]{2,1,0:T(8,128)(2,1)S(1)}, u32[]{:S(2)}, u32[]{:S(2)}) async-start(bf16[8,256,128]{2,1,0:T(8,128)(2,1)} %get-tuple-element.25), calls=%async_computation | async-start | bytes 1048576 | tf_op jit(solution)/shard_map/all_to_all | solution.py:727
  9.6 6.1 %home.1 = (bf16[200,1024]{1,0:T(8,128)(2,1)S(1)}, bf16[200,1024]{1,0:T(8,128)(2,1)S(1)}, f32[1,1024]{1,0:T(1,128)S(1)}) custom-call(bf16[256,1024]{1,0:T(8,128)(2,1)S(1)} %get-tuple-element.26.v_ref, f32[48,256]{1,0:T(8,128)S(1)} %get-tuple-element.27.rows_ref, bf16[200,1024]{1,0:T(8,128)(2,1)S(1)} %get-tuple-element.28.flat_ref, bf16[1024,2048]{1,0:T(8,128)(2,1)} %w_hbm.3, ...), custom_call_target="tpu_custom_call" | custom-call | tf_op jit(solution)/shard_map/home/pallas_call | solution.py:341
  15.6 3.1 %all-to-all-done.pay_ref = bf16[8,256,128]{2,1,0:T(8,128)(2,1)S(1)} async-done(((bf16[8,256,128]{2,1,0:T(8,128)(2,1)}), bf16[8,256,128]{2,1,0:T(8,128)(2,1)S(1)}, u32[]{:S(2)}, u32[]{:S(2)}) %all-to-all-start) | async-done | bytes 524320 | tf_op jit(solution)/shard_map/all_to_all | solution.py:727
  18.7 1.5 %last.1 = bf16[7,64,128]{2,1,0:T(8,128)(2,1)S(1)} custom-call(bf16[8,256,128]{2,1,0:T(8,128)(2,1)S(1)} %all-to-all-done.pay_ref), custom_call_target="tpu_custom_call" | custom-call | tf_op jit(solution)/shard_map/last/pallas_call | solution.py:605
  20.2 3.0 %collective-permute-start = (bf16[7,64,128]{2,1,0:T(8,128)(2,1)S(1)}, bf16[7,64,128]{2,1,0:T(8,128)(2,1)S(1)}, u32[]{:S(2)}, u32[]{:S(2)}) collective-permute-start(bf16[7,64,128]{2,1,0:T(8,128)(2,1)S(1)} %last.1), channel_id=1, source_target_pairs={{0,8},{1,9},{2,10},{3,11},{4,12},{5,13},{6,14},{7,15},{16,24},{17,... | collective-permute-start | bytes 344072 | tf_op jit(solution)/shard_map/ppermute | solution.py:624
  23.2 4.0 %maps.1 = (bf16[16,32,256]{2,1,0:T(8,128)(2,1)S(1)}, f32[16,256]{1,0:T(8,128)S(1)}, bf16[16,448,128]{2,1,0:T(8,128)(2,1)S(1)}, f32[16,64,128]{2,1,0:T(8,128)S(1)...) custom-call(bf16[8,256,128]{2,1,0:T(8,128)(2,1)S(1)} %all-to-all-done.pay_ref, ...), custom_call_target="tpu_custom_call" | custom-call | tf_op jit(solution)/shard_map/maps/pallas_call | solution.py:605
  27.2 0.0 collective-permute-done.entry_ref
  27.2 0.5 %join.1 = bf16[16,64,128]{2,1,0:T(8,128)(2,1)S(1)} custom-call(f32[16,448]{1,0:T(8,128)S(1)} %get-tuple-element.35.upto_ref, bf16[7,64,128]{2,1,0:T(8,128)(2,1)S(1)} %collective-permute-done.entry_ref, bf16[16,448,128]{2,1,0:T(8,128)(2,1)S(1)} %get-tuple-element.40.passed_ref, f32[16,64,128]{2,1,0:T(8,128)S(1)} %get-tuple-element.41.top_ref), custom_call_target="tpu_custom_call" | custom-call | tf_op jit(solution)/shard_map/join/pallas_call | solution.py:605
  27.7 1.3 %collective-permute-start.1 = (bf16[16,64,128]{2,1,0:T(8,128)(2,1)S(1)}, bf16[16,64,128]{2,1,0:T(8,128)(2,1)S(1)}, u32[]{:S(2)}, u32[]{:S(2)}) collective-permute-start(bf16[16,64,128]{2,1,0:T(8,128)(2,1)S(1)} %join.1), channel_id=1, source_target_pairs={{0,16},{1,17},{2,18},{3,19},{4,20},{5,21},{6,22},{7,23},{8,24},{9,... | collective-permute-start | bytes 786440 | tf_op jit(solution)/shard_map/ppermute | solution.py:652
  29.0 1.1 %sides.1 = (f32[16,64,256]{2,1,0:T(8,128)S(1)}, bf16[16,128,256]{2,1,0:T(8,128)(2,1)S(1)}) custom-call(bf16[8,16,256]{2,1,0:T(8,128)(2,1)S(1)} %get-tuple-element.33.c_ref, bf16[16,64,448]{2,1,0:T(8,128)(2,1)S(1)} %get-tuple-element.34.edge_ref, f32[16,448]{1,0:T(8,128)S(1)} %get-tuple-element.35.upto_ref, ...), custom_call_target="tpu_custom_call" | custom-call | tf_op jit(solution)/shard_map/sides/pallas_call | solution.py:605
  30.1 0.0 copy-start
  30.1 0.0 collective-permute-done.1.top_ref
  30.1 0.4 cells.1
  30.5 12.6 %all_to_all.10.y_ref = bf16[8,200,128]{2,1,0:T(8,128)(2,1)S(1)} all-to-all(bf16[8,200,128]{2,1,0:T(8,128)(2,1)S(1)} %cells.1), channel_id=1, replica_groups={{0,1,2,3,4,5,6,7},{8,9,10,11,12,13,14,15},{16,17,18,19,20,21,22,23},{24..., dimensions={0} | all-to-all | bytes 819200 | tf_op jit(solution)/shard_map/all_to_all | solution.py:732
  43.1 0.0 copy-done
  43.1 1.6 %finish.1 = bf16[28,7,1024]{2,1,0:T(8,128)(2,1)} custom-call(bf16[8,200,128]{2,1,0:T(8,128)(2,1)S(1)} %all_to_all.10.y_ref, bf16[200,1024]{1,0:T(8,128)(2,1)S(1)} %get-tuple-element.42.own_ref, bf16[200,1024]{1,0:T(8,128)(2,1)S(1)} %get-tuple-element.43.gate_ref, f32[1,1024]{1,0:T(1,128)S(1)} %get-tuple-element.44.gain_ref, bf16[1024,1024]{1,0:T(8,128)(2,1)S(1)} %copy-done), custom_call_target="tpu_custom_call" | custom-call | tf_op jit(solution)/shard_map/finish/pallas_call | solution.py:605
Async XLA Ops:
  3.4 15.3 %all-to-all-start = ((bf16[8,256,128]{2,1,0:T(8,128)(2,1)}), bf16[8,256,128]{2,1,0:T(8,128)(2,1)S(1)}, u32[]{:S(2)}, u32[]{:S(2)}) async-start(bf16[8,256,128]{2,1,0:T(8,128)(2,1)} %get-tuple-element.25), calls=%async_computation | async-start | bytes 1048576 | tf_op jit(solution)/shard_map/all_to_all | solution.py:727
  20.2 7.0 %collective-permute-start = (bf16[7,64,128]{2,1,0:T(8,128)(2,1)S(1)}, bf16[7,64,128]{2,1,0:T(8,128)(2,1)S(1)}, u32[]{:S(2)}, u32[]{:S(2)}) collective-permute-start(bf16[7,64,128]{2,1,0:T(8,128)(2,1)S(1)} %last.1), channel_id=1, source_target_pairs={{0,8},{1,9},{2,10},{3,11},{4,12},{5,13},{6,14},{7,15},{16,24},{17,... | collective-permute-start | bytes 344072 | tf_op jit(solution)/shard_map/ppermute | solution.py:624
  27.7 2.4 %collective-permute-start.1 = (bf16[16,64,128]{2,1,0:T(8,128)(2,1)S(1)}, bf16[16,64,128]{2,1,0:T(8,128)(2,1)S(1)}, u32[]{:S(2)}, u32[]{:S(2)}) collective-permute-start(bf16[16,64,128]{2,1,0:T(8,128)(2,1)S(1)} %join.1), channel_id=1, source_target_pairs={{0,16},{1,17},{2,18},{3,19},{4,20},{5,21},{6,22},{7,23},{8,24},{9,... | collective-permute-start | bytes 786440 | tf_op jit(solution)/shard_map/ppermute | solution.py:652
  30.1 13.0 %copy-start = (bf16[1024,1024]{1,0:T(8,128)(2,1)S(1)}, bf16[1024,1024]{1,0:T(8,128)(2,1)}, u32[]{:S(2)}) copy-start(bf16[1024,1024]{1,0:T(8,128)(2,1)} %w_ref.1) | copy-start | bytes 6291460

commit v16 on v15

--- a/solution.py
+++ b/solution.py
@@ -563,13 +563,15 @@
         top_ref[w] = nt_dot(turned[w], falls) + mm(edge_ref[w], passed_ref[w])
 
 
-def join_kernel(plan, upto_ref, entry_ref, passed_ref, top_ref, out_ref):
-    for s in range(plan.slots):
-        entry = unpack_edges(plan, entry_ref, s)
-        for t in range(plan.devices):
-            w = s * plan.devices + t
-            late = (entry * upto_ref[w : w + 1, :]).astype(BF16)
-            out_ref[w] = (top_ref[w] + mm(late, passed_ref[w])).astype(BF16)
+def join_kernel(plan, axis, upto_ref, entry_ref, passed_ref, top_ref, out_ref):
+    @pl.when(lax.axis_index(axis) < lax.axis_size(axis) - 1)
+    def _():
+        for s in range(plan.slots):
+            entry = unpack_edges(plan, entry_ref, s)
+            for t in range(plan.devices):
+                w = s * plan.devices + t
+                late = (entry * upto_ref[w : w + 1, :]).astype(BF16)
+                out_ref[w] = (top_ref[w] + mm(late, passed_ref[w])).astype(BF16)
 
 
 def sides_kernel(plan, c_ref, edge_ref, upto_ref, entry_ref, side_ref, above_ref, y_ref, down_ref):
@@ -642,7 +644,7 @@
     )
     edge_entry = entry
     tops = call(
-        functools.partial(join_kernel, plan),
+        functools.partial(join_kernel, plan, row_axis),
         "join",
         [upto, entry, passed, tops],
         [((work, HALF, plan.top), BF16)],

time: 45.1 us -> 44.6 us (0.989)
  blocking collectives: 12.6 us -> 12.1 us
    all_to_all x1, blocking collectives: 12.6 us -> 12.1 us  [per_device(): y = lax.all_to_all(y, 'col', 0, 0, tiled=True, axis_index_groups=groups)]
where the time goes in v16:
time: 44.6 us; the launch traced here: 44.2 us
  Pallas kernels  18.5 us (41%)
  blocking collectives  12.1 us (27%)
  starting transfers between devices  10.5 us (24%)
  waiting for transfers between devices  3.06 us (7%)
    all_to_all x1, blocking collectives, per_device(): y = lax.all_to_all(y, 'col', 0, 0, tiled=True, axis_index_groups=groups)  12.1 us
    pallas_call x6, Pallas kernels, call(): pl.pallas_call(kernel, grid=(1,), in_specs=[full(x.shape) for x in args],...  9.1 us
    all_to_all x1, starting transfers between devices, per_device(): pay = lax.all_to_all(pay, 'col', 0, 0, tiled=True, axis_index_groups=groups)  6.21 us
    pallas_call x1, Pallas kernels, home(): pl.pallas_call(functools.partial(home_kernel, plan), grid=(1,), in_specs=...  6.05 us
    pallas_call x1, Pallas kernels, project(): pl.pallas_call(functools.partial(project_kernel, plan, chunks), grid=(1,)...  3.34 us
    all_to_all x1, waiting for transfers between devices, per_device(): pay = lax.all_to_all(pay, 'col', 0, 0, tiled=True, axis_index_groups=groups)  3.06 us
    ppermute x1, starting transfers between devices, scan_calls(): lax.ppermute(last, col_axis, [(k, k + plan.devices) for k in range(plan.d...  2.97 us
    ppermute x1, starting transfers between devices, scan_calls(): entry = lax.ppermute(tops, row_axis, chain)  1.31 us
  transfers between devices with their start and end apart: 3, of which 1 were waited for; matrix products, arithmetic and copies ran while one was open for 0% of the time, Pallas kernels for 25%

profile of v16, /device:TPU:0, one launch (start us, length us, event | category | flops | bytes accessed | tf_op | source)
XLA Modules:
  0.0 44.2 jit_solution(6299207713358128051)
XLA Ops:
  0.0 3.3 %project.1 = (bf16[256,1024]{1,0:T(8,128)(2,1)S(1)}, bf16[8,256,128]{2,1,0:T(8,128)(2,1)}, f32[48,256]{1,0:T(8,128)S(1)}, bf16[200,1024]{1,0:T(8,128)(2,1)S(1)}) custom-call(f32[16]{0:T(128)} %bias_hbm.1, f32[16]{0:T(128)} %refs_0_.1, f32[16]{0:T(128)} %refs_1_.1, bf16[28,7,1024]{2,1,0:T(8,128)(2,1)} %x_hbm.1, bf16[1024,2048]{1,0:T(8,128)(2,1)} %w_hbm.3, ...), custom_call_target="tpu_custom_call" | custom-call | tf_op jit(solution)/shard_map/project/pallas_call | solution.py:263
  3.4 6.2 %all-to-all-start = ((bf16[8,256,128]{2,1,0:T(8,128)(2,1)}), bf16[8,256,128]{2,1,0:T(8,128)(2,1)S(1)}, u32[]{:S(2)}, u32[]{:S(2)}) async-start(bf16[8,256,128]{2,1,0:T(8,128)(2,1)} %get-tuple-element.25), calls=%async_computation | async-start | bytes 1048576 | tf_op jit(solution)/shard_map/all_to_all | solution.py:729
  9.6 6.1 %home.1 = (bf16[200,1024]{1,0:T(8,128)(2,1)S(1)}, bf16[200,1024]{1,0:T(8,128)(2,1)S(1)}, f32[1,1024]{1,0:T(1,128)S(1)}) custom-call(bf16[256,1024]{1,0:T(8,128)(2,1)S(1)} %get-tuple-element.26.v_ref, f32[48,256]{1,0:T(8,128)S(1)} %get-tuple-element.27.rows_ref, bf16[200,1024]{1,0:T(8,128)(2,1)S(1)} %get-tuple-element.28.flat_ref, bf16[1024,2048]{1,0:T(8,128)(2,1)} %w_hbm.3, ...), custom_call_target="tpu_custom_call" | custom-call | tf_op jit(solution)/shard_map/home/pallas_call | solution.py:341
  15.6 3.1 %all-to-all-done.pay_ref = bf16[8,256,128]{2,1,0:T(8,128)(2,1)S(1)} async-done(((bf16[8,256,128]{2,1,0:T(8,128)(2,1)}), bf16[8,256,128]{2,1,0:T(8,128)(2,1)S(1)}, u32[]{:S(2)}, u32[]{:S(2)}) %all-to-all-start) | async-done | bytes 524320 | tf_op jit(solution)/shard_map/all_to_all | solution.py:729
  18.7 1.5 %last.1 = bf16[7,64,128]{2,1,0:T(8,128)(2,1)S(1)} custom-call(bf16[8,256,128]{2,1,0:T(8,128)(2,1)S(1)} %all-to-all-done.pay_ref), custom_call_target="tpu_custom_call" | custom-call | tf_op jit(solution)/shard_map/last/pallas_call | solution.py:607
  20.2 3.0 %collective-permute-start = (bf16[7,64,128]{2,1,0:T(8,128)(2,1)S(1)}, bf16[7,64,128]{2,1,0:T(8,128)(2,1)S(1)}, u32[]{:S(2)}, u32[]{:S(2)}) collective-permute-start(bf16[7,64,128]{2,1,0:T(8,128)(2,1)S(1)} %last.1), channel_id=1, source_target_pairs={{0,8},{1,9},{2,10},{3,11},{4,12},{5,13},{6,14},{7,15},{16,24},{17,... | collective-permute-start | bytes 344072 | tf_op jit(solution)/shard_map/ppermute | solution.py:626
  23.2 4.0 %maps.1 = (bf16[16,32,256]{2,1,0:T(8,128)(2,1)S(1)}, f32[16,256]{1,0:T(8,128)S(1)}, bf16[16,448,128]{2,1,0:T(8,128)(2,1)S(1)}, f32[16,64,128]{2,1,0:T(8,128)S(1)...) custom-call(bf16[8,256,128]{2,1,0:T(8,128)(2,1)S(1)} %all-to-all-done.pay_ref, ...), custom_call_target="tpu_custom_call" | custom-call | tf_op jit(solution)/shard_map/maps/pallas_call | solution.py:607
  27.2 0.0 collective-permute-done.entry_ref
  27.2 0.5 %join.1 = bf16[16,64,128]{2,1,0:T(8,128)(2,1)S(1)} custom-call(f32[16,448]{1,0:T(8,128)S(1)} %get-tuple-element.35.upto_ref, bf16[7,64,128]{2,1,0:T(8,128)(2,1)S(1)} %collective-permute-done.entry_ref, bf16[16,448,128]{2,1,0:T(8,128)(2,1)S(1)} %get-tuple-element.40.passed_ref, f32[16,64,128]{2,1,0:T(8,128)S(1)} %get-tuple-element.41.top_ref), custom_call_target="tpu_custom_call" | custom-call | tf_op jit(solution)/shard_map/join/pallas_call | solution.py:607
  27.7 1.3 %collective-permute-start.1 = (bf16[16,64,128]{2,1,0:T(8,128)(2,1)S(1)}, bf16[16,64,128]{2,1,0:T(8,128)(2,1)S(1)}, u32[]{:S(2)}, u32[]{:S(2)}) collective-permute-start(bf16[16,64,128]{2,1,0:T(8,128)(2,1)S(1)} %join.1), channel_id=1, source_target_pairs={{0,16},{1,17},{2,18},{3,19},{4,20},{5,21},{6,22},{7,23},{8,24},{9,... | collective-permute-start | bytes 786440 | tf_op jit(solution)/shard_map/ppermute | solution.py:654
  29.0 1.1 %sides.1 = (f32[16,64,256]{2,1,0:T(8,128)S(1)}, bf16[16,128,256]{2,1,0:T(8,128)(2,1)S(1)}) custom-call(bf16[8,16,256]{2,1,0:T(8,128)(2,1)S(1)} %get-tuple-element.33.c_ref, bf16[16,64,448]{2,1,0:T(8,128)(2,1)S(1)} %get-tuple-element.34.edge_ref, f32[16,448]{1,0:T(8,128)S(1)} %get-tuple-element.35.upto_ref, ...), custom_call_target="tpu_custom_call" | custom-call | tf_op jit(solution)/shard_map/sides/pallas_call | solution.py:607
  30.1 0.0 copy-start
  30.1 0.0 collective-permute-done.1.top_ref
  30.1 0.4 cells.1
  30.5 12.1 %all_to_all.10.y_ref = bf16[8,200,128]{2,1,0:T(8,128)(2,1)S(1)} all-to-all(bf16[8,200,128]{2,1,0:T(8,128)(2,1)S(1)} %cells.1), channel_id=1, replica_groups={{0,1,2,3,4,5,6,7},{8,9,10,11,12,13,14,15},{16,17,18,19,20,21,22,23},{24..., dimensions={0} | all-to-all | bytes 819200 | tf_op jit(solution)/shard_map/all_to_all | solution.py:734
  42.6 0.0 copy-done
  42.6 1.6 %finish.1 = bf16[28,7,1024]{2,1,0:T(8,128)(2,1)} custom-call(bf16[8,200,128]{2,1,0:T(8,128)(2,1)S(1)} %all_to_all.10.y_ref, bf16[200,1024]{1,0:T(8,128)(2,1)S(1)} %get-tuple-element.42.own_ref, bf16[200,1024]{1,0:T(8,128)(2,1)S(1)} %get-tuple-element.43.gate_ref, f32[1,1024]{1,0:T(1,128)S(1)} %get-tuple-element.44.gain_ref, bf16[1024,1024]{1,0:T(8,128)(2,1)S(1)} %copy-done), custom_call_target="tpu_custom_call" | custom-call | tf_op jit(solution)/shard_map/finish/pallas_call | solution.py:607
Async XLA Ops:
  3.4 15.3 %all-to-all-start = ((bf16[8,256,128]{2,1,0:T(8,128)(2,1)}), bf16[8,256,128]{2,1,0:T(8,128)(2,1)S(1)}, u32[]{:S(2)}, u32[]{:S(2)}) async-start(bf16[8,256,128]{2,1,0:T(8,128)(2,1)} %get-tuple-element.25), calls=%async_computation | async-start | bytes 1048576 | tf_op jit(solution)/shard_map/all_to_all | solution.py:729
  20.2 7.0 %collective-permute-start = (bf16[7,64,128]{2,1,0:T(8,128)(2,1)S(1)}, bf16[7,64,128]{2,1,0:T(8,128)(2,1)S(1)}, u32[]{:S(2)}, u32[]{:S(2)}) collective-permute-start(bf16[7,64,128]{2,1,0:T(8,128)(2,1)S(1)} %last.1), channel_id=1, source_target_pairs={{0,8},{1,9},{2,10},{3,11},{4,12},{5,13},{6,14},{7,15},{16,24},{17,... | collective-permute-start | bytes 344072 | tf_op jit(solution)/shard_map/ppermute | solution.py:626
  27.7 2.4 %collective-permute-start.1 = (bf16[16,64,128]{2,1,0:T(8,128)(2,1)S(1)}, bf16[16,64,128]{2,1,0:T(8,128)(2,1)S(1)}, u32[]{:S(2)}, u32[]{:S(2)}) collective-permute-start(bf16[16,64,128]{2,1,0:T(8,128)(2,1)S(1)} %join.1), channel_id=1, source_target_pairs={{0,16},{1,17},{2,18},{3,19},{4,20},{5,21},{6,22},{7,23},{8,24},{9,... | collective-permute-start | bytes 786440 | tf_op jit(solution)/shard_map/ppermute | solution.py:654
  30.1 12.5 %copy-start = (bf16[1024,1024]{1,0:T(8,128)(2,1)S(1)}, bf16[1024,1024]{1,0:T(8,128)(2,1)}, u32[]{:S(2)}) copy-start(bf16[1024,1024]{1,0:T(8,128)(2,1)} %w_ref.1) | copy-start | bytes 6291460

commit v17 on v16

--- a/solution.py
+++ b/solution.py
@@ -563,8 +563,15 @@
         top_ref[w] = nt_dot(turned[w], falls) + mm(edge_ref[w], passed_ref[w])
 
 
-def join_kernel(plan, axis, upto_ref, entry_ref, passed_ref, top_ref, out_ref):
-    @pl.when(lax.axis_index(axis) < lax.axis_size(axis) - 1)
+def join_kernel(plan, row_axis, col_axis, upto_ref, entry_ref, passed_ref, top_ref, out_ref):
+    sends = lax.axis_index(row_axis) < lax.axis_size(row_axis) - 1
+    first = lax.axis_index(col_axis) < plan.devices
+
+    @pl.when(sends & first)
+    def _():
+        out_ref[...] = top_ref[...].astype(BF16)
+
+    @pl.when(sends & jnp.logical_not(first))
     def _():
         for s in range(plan.slots):
             entry = unpack_edges(plan, entry_ref, s)
@@ -644,7 +651,7 @@
     )
     edge_entry = entry
     tops = call(
-        functools.partial(join_kernel, plan, row_axis),
+        functools.partial(join_kernel, plan, row_axis, col_axis),
         "join",
         [upto, entry, passed, tops],
         [((work, HALF, plan.top), BF16)],

time: 44.6 us -> 44.6 us (level)
  Pallas kernels: 18.5 us -> 18 us
  blocking collectives: 12.1 us -> 12.6 us
    all_to_all x1, blocking collectives: 12.1 us -> 12.6 us  [per_device(): y = lax.all_to_all(y, 'col', 0, 0, tiled=True, axis_index_groups=groups)]
    pallas_call x6, Pallas kernels: 9.1 us -> 8.64 us  [call(): pl.pallas_call(kernel, grid=(1,), in_specs=[full(x.shape) for x in args],...]
where the time goes in v17:
time: 44.6 us; the launch traced here: 44.2 us
  Pallas kernels  18 us (40%)
  blocking collectives  12.6 us (28%)
  starting transfers between devices  10.5 us (24%)
  waiting for transfers between devices  3.06 us (7%)
    all_to_all x1, blocking collectives, per_device(): y = lax.all_to_all(y, 'col', 0, 0, tiled=True, axis_index_groups=groups)  12.6 us
    pallas_call x6, Pallas kernels, call(): pl.pallas_call(kernel, grid=(1,), in_specs=[full(x.shape) for x in args],...  8.64 us
    all_to_all x1, starting transfers between devices, per_device(): pay = lax.all_to_all(pay, 'col', 0, 0, tiled=True, axis_index_groups=groups)  6.21 us
    pallas_call x1, Pallas kernels, home(): pl.pallas_call(functools.partial(home_kernel, plan), grid=(1,), in_specs=...  6.05 us
    pallas_call x1, Pallas kernels, project(): pl.pallas_call(functools.partial(project_kernel, plan, chunks), grid=(1,)...  3.34 us
    all_to_all x1, waiting for transfers between devices, per_device(): pay = lax.all_to_all(pay, 'col', 0, 0, tiled=True, axis_index_groups=groups)  3.06 us
    ppermute x1, starting transfers between devices, scan_calls(): lax.ppermute(last, col_axis, [(k, k + plan.devices) for k in range(plan.d...  2.97 us
    ppermute x1, starting transfers between devices, scan_calls(): entry = lax.ppermute(tops, row_axis, chain)  1.31 us
  transfers between devices with their start and end apart: 3, of which 1 were waited for; matrix products, arithmetic and copies ran while one was open for 0% of the time, Pallas kernels for 25%

profile of v17, /device:TPU:0, one launch (start us, length us, event | category | flops | bytes accessed | tf_op | source)
XLA Modules:
  0.0 44.2 jit_solution(17651504531525007987)
XLA Ops:
  0.0 3.3 %project.1 = (bf16[256,1024]{1,0:T(8,128)(2,1)S(1)}, bf16[8,256,128]{2,1,0:T(8,128)(2,1)}, f32[48,256]{1,0:T(8,128)S(1)}, bf16[200,1024]{1,0:T(8,128)(2,1)S(1)}) custom-call(f32[16]{0:T(128)} %bias_hbm.1, f32[16]{0:T(128)} %refs_0_.1, f32[16]{0:T(128)} %refs_1_.1, bf16[28,7,1024]{2,1,0:T(8,128)(2,1)} %x_hbm.1, bf16[1024,2048]{1,0:T(8,128)(2,1)} %w_hbm.3, ...), custom_call_target="tpu_custom_call" | custom-call | tf_op jit(solution)/shard_map/project/pallas_call | solution.py:263
  3.4 6.2 %all-to-all-start = ((bf16[8,256,128]{2,1,0:T(8,128)(2,1)}), bf16[8,256,128]{2,1,0:T(8,128)(2,1)S(1)}, u32[]{:S(2)}, u32[]{:S(2)}) async-start(bf16[8,256,128]{2,1,0:T(8,128)(2,1)} %get-tuple-element.25), calls=%async_computation | async-start | bytes 1048576 | tf_op jit(solution)/shard_map/all_to_all | solution.py:736
  9.6 6.1 %home.1 = (bf16[200,1024]{1,0:T(8,128)(2,1)S(1)}, bf16[200,1024]{1,0:T(8,128)(2,1)S(1)}, f32[1,1024]{1,0:T(1,128)S(1)}) custom-call(bf16[256,1024]{1,0:T(8,128)(2,1)S(1)} %get-tuple-element.26.v_ref, f32[48,256]{1,0:T(8,128)S(1)} %get-tuple-element.27.rows_ref, bf16[200,1024]{1,0:T(8,128)(2,1)S(1)} %get-tuple-element.28.flat_ref, bf16[1024,2048]{1,0:T(8,128)(2,1)} %w_hbm.3, ...), custom_call_target="tpu_custom_call" | custom-call | tf_op jit(solution)/shard_map/home/pallas_call | solution.py:341
  15.6 3.1 %all-to-all-done.pay_ref = bf16[8,256,128]{2,1,0:T(8,128)(2,1)S(1)} async-done(((bf16[8,256,128]{2,1,0:T(8,128)(2,1)}), bf16[8,256,128]{2,1,0:T(8,128)(2,1)S(1)}, u32[]{:S(2)}, u32[]{:S(2)}) %all-to-all-start) | async-done | bytes 524320 | tf_op jit(solution)/shard_map/all_to_all | solution.py:736
  18.7 1.5 %last.1 = bf16[7,64,128]{2,1,0:T(8,128)(2,1)S(1)} custom-call(bf16[8,256,128]{2,1,0:T(8,128)(2,1)S(1)} %all-to-all-done.pay_ref), custom_call_target="tpu_custom_call" | custom-call | tf_op jit(solution)/shard_map/last/pallas_call | solution.py:614
  20.2 3.0 %collective-permute-start = (bf16[7,64,128]{2,1,0:T(8,128)(2,1)S(1)}, bf16[7,64,128]{2,1,0:T(8,128)(2,1)S(1)}, u32[]{:S(2)}, u32[]{:S(2)}) collective-permute-start(bf16[7,64,128]{2,1,0:T(8,128)(2,1)S(1)} %last.1), channel_id=1, source_target_pairs={{0,8},{1,9},{2,10},{3,11},{4,12},{5,13},{6,14},{7,15},{16,24},{17,... | collective-permute-start | bytes 344072 | tf_op jit(solution)/shard_map/ppermute | solution.py:633
  23.2 4.0 %maps.1 = (bf16[16,32,256]{2,1,0:T(8,128)(2,1)S(1)}, f32[16,256]{1,0:T(8,128)S(1)}, bf16[16,448,128]{2,1,0:T(8,128)(2,1)S(1)}, f32[16,64,128]{2,1,0:T(8,128)S(1)...) custom-call(bf16[8,256,128]{2,1,0:T(8,128)(2,1)S(1)} %all-to-all-done.pay_ref, ...), custom_call_target="tpu_custom_call" | custom-call | tf_op jit(solution)/shard_map/maps/pallas_call | solution.py:614
  27.2 0.0 collective-permute-done.entry_ref
  27.2 1.3 %collective-permute-start.1 = (bf16[16,64,128]{2,1,0:T(8,128)(2,1)S(1)}, bf16[16,64,128]{2,1,0:T(8,128)(2,1)S(1)}, u32[]{:S(2)}, u32[]{:S(2)}) collective-permute-start(bf16[16,64,128]{2,1,0:T(8,128)(2,1)S(1)} %join.1), channel_id=1, source_target_pairs={{0,16},{1,17},{2,18},{3,19},{4,20},{5,21},{6,22},{7,23},{8,24},{9,... | collective-permute-start | bytes 786440 | tf_op jit(solution)/shard_map/ppermute | solution.py:661
  28.6 1.1 %sides.1 = (f32[16,64,256]{2,1,0:T(8,128)S(1)}, bf16[16,128,256]{2,1,0:T(8,128)(2,1)S(1)}) custom-call(bf16[8,16,256]{2,1,0:T(8,128)(2,1)S(1)} %get-tuple-element.33.c_ref, bf16[16,64,448]{2,1,0:T(8,128)(2,1)S(1)} %get-tuple-element.34.edge_ref, f32[16,448]{1,0:T(8,128)S(1)} %get-tuple-element.35.upto_ref, ...), custom_call_target="tpu_custom_call" | custom-call | tf_op jit(solution)/shard_map/sides/pallas_call | solution.py:614
  29.7 0.0 copy-start
  29.7 0.0 collective-permute-done.1.top_ref
  29.7 0.4 cells.1
  30.1 12.6 %all_to_all.10.y_ref = bf16[8,200,128]{2,1,0:T(8,128)(2,1)S(1)} all-to-all(bf16[8,200,128]{2,1,0:T(8,128)(2,1)S(1)} %cells.1), channel_id=1, replica_groups={{0,1,2,3,4,5,6,7},{8,9,10,11,12,13,14,15},{16,17,18,19,20,21,22,23},{24..., dimensions={0} | all-to-all | bytes 819200 | tf_op jit(solution)/shard_map/all_to_all | solution.py:741
  42.6 0.0 copy-done
  42.6 1.6 %finish.1 = bf16[28,7,1024]{2,1,0:T(8,128)(2,1)} custom-call(bf16[8,200,128]{2,1,0:T(8,128)(2,1)S(1)} %all_to_all.10.y_ref, bf16[200,1024]{1,0:T(8,128)(2,1)S(1)} %get-tuple-element.42.own_ref, bf16[200,1024]{1,0:T(8,128)(2,1)S(1)} %get-tuple-element.43.gate_ref, f32[1,1024]{1,0:T(1,128)S(1)} %get-tuple-element.44.gain_ref, bf16[1024,1024]{1,0:T(8,128)(2,1)S(1)} %copy-done), custom_call_target="tpu_custom_call" | custom-call | tf_op jit(solution)/shard_map/finish/pallas_call | solution.py:614
  (1 shorter events, 0.0 us)
Async XLA Ops:
  3.4 15.3 %all-to-all-start = ((bf16[8,256,128]{2,1,0:T(8,128)(2,1)}), bf16[8,256,128]{2,1,0:T(8,128)(2,1)S(1)}, u32[]{:S(2)}, u32[]{:S(2)}) async-start(bf16[8,256,128]{2,1,0:T(8,128)(2,1)} %get-tuple-element.25), calls=%async_computation | async-start | bytes 1048576 | tf_op jit(solution)/shard_map/all_to_all | solution.py:736
  20.2 7.0 %collective-permute-start = (bf16[7,64,128]{2,1,0:T(8,128)(2,1)S(1)}, bf16[7,64,128]{2,1,0:T(8,128)(2,1)S(1)}, u32[]{:S(2)}, u32[]{:S(2)}) collective-permute-start(bf16[7,64,128]{2,1,0:T(8,128)(2,1)S(1)} %last.1), channel_id=1, source_target_pairs={{0,8},{1,9},{2,10},{3,11},{4,12},{5,13},{6,14},{7,15},{16,24},{17,... | collective-permute-start | bytes 344072 | tf_op jit(solution)/shard_map/ppermute | solution.py:633
  27.2 2.4 %collective-permute-start.1 = (bf16[16,64,128]{2,1,0:T(8,128)(2,1)S(1)}, bf16[16,64,128]{2,1,0:T(8,128)(2,1)S(1)}, u32[]{:S(2)}, u32[]{:S(2)}) collective-permute-start(bf16[16,64,128]{2,1,0:T(8,128)(2,1)S(1)} %join.1), channel_id=1, source_target_pairs={{0,16},{1,17},{2,18},{3,19},{4,20},{5,21},{6,22},{7,23},{8,24},{9,... | collective-permute-start | bytes 786440 | tf_op jit(solution)/shard_map/ppermute | solution.py:661
  29.7 13.0 %copy-start = (bf16[1024,1024]{1,0:T(8,128)(2,1)S(1)}, bf16[1024,1024]{1,0:T(8,128)(2,1)}, u32[]{:S(2)}) copy-start(bf16[1024,1024]{1,0:T(8,128)(2,1)} %w_ref.1) | copy-start | bytes 6291460

commit v18 on v17

--- a/solution.py
+++ b/solution.py
@@ -581,22 +581,39 @@
                 out_ref[w] = (top_ref[w] + mm(late, passed_ref[w])).astype(BF16)
 
 
-def sides_kernel(plan, c_ref, edge_ref, upto_ref, entry_ref, side_ref, above_ref, y_ref, down_ref):
+def sides_kernel(plan, axis, c_ref, edge_ref, upto_ref, entry_ref, side_ref, above_ref, y_ref, down_ref):
     states, tiles = plan.states, plan.devices
     shape = (plan.col_pad, 2 * LANES)
     _, tj, treal = places(plan, shape, 1)
     colsel = jnp.where((tj == lax.broadcasted_iota(jnp.int32, shape, 0)) & treal, 1.0, 0.0)
-    for s in range(plan.slots):
-        entry = unpack_edges(plan, entry_ref, s)
-        for t in range(tiles):
-            w = s * tiles + t
-            c = c_ref[t]
-            side = side_ref[w]
-            left = jnp.concatenate([c * side[i : i + 1] for i in range(plan.rows)], axis=0)
-            whole = (edge_ref[w].astype(F32) + entry * upto_ref[w : w + 1, :]).astype(BF16)
-            y_ref[w] = mm(whole, left)
-            ca = c.astype(F32) * above_ref[w : w + 1, :]
-            down_ref[w] = jnp.concatenate([colsel * ca[n : n + 1] for n in range(states)], axis=0).astype(BF16)
+    first = lax.axis_index(axis) < plan.devices
+
+    @pl.when(first)
+    def _():
+        for s in range(plan.slots):
+            for t in range(tiles):
+                w = s * tiles + t
+                c = c_ref[t]
+                side = side_ref[w]
+                left = jnp.concatenate([c * side[i : i + 1] for i in range(plan.rows)], axis=0)
+                whole = edge_ref[w]
+                y_ref[w] = mm(whole, left)
+                ca = c.astype(F32) * above_ref[w : w + 1, :]
+                down_ref[w] = jnp.concatenate([colsel * ca[n : n + 1] for n in range(states)], axis=0).astype(BF16)
+
+    @pl.when(jnp.logical_not(first))
+    def _():
+        for s in range(plan.slots):
+            entry = unpack_edges(plan, entry_ref, s)
+            for t in range(tiles):
+                w = s * tiles + t
+                c = c_ref[t]
+                side = side_ref[w]
+                left = jnp.concatenate([c * side[i : i + 1] for i in range(plan.rows)], axis=0)
+                whole = (edge_ref[w].astype(F32) + entry * upto_ref[w : w + 1, :]).astype(BF16)
+                y_ref[w] = mm(whole, left)
+                ca = c.astype(F32) * above_ref[w : w + 1, :]
+                down_ref[w] = jnp.concatenate([colsel * ca[n : n + 1] for n in range(states)], axis=0).astype(BF16)
 
 
 def cells_kernel(plan, y_ref, down_ref, top_ref, out_ref):
@@ -666,7 +683,7 @@
                 (tops.astype(F32) + keep * entry.astype(F32)).astype(BF16), row_axis, chain
             )
     y, down = call(
-        functools.partial(sides_kernel, plan),
+        functools.partial(sides_kernel, plan, col_axis),
         "sides",
         [c, edges, upto, edge_entry, side, above],
         [((work, HALF, wide), F32), ((work, plan.top, wide), BF16)],

time: 44.6 us -> 44.6 us (level)
  transfers between devices with their start and end apart: 3 -> 3, of which waited for: 1 -> 2; matrix products, arithmetic and copies ran while one was open for 0% -> 0% of each run, Pallas kernels for 25% -> 25%
where the time goes in v18:
time: 44.6 us; the launch traced here: 44.2 us
  Pallas kernels  17.9 us (40%)
  blocking collectives  12.6 us (28%)
  starting transfers between devices  10.5 us (24%)
  waiting for transfers between devices  3.19 us (7%)
    all_to_all x1, blocking collectives, per_device(): y = lax.all_to_all(y, 'col', 0, 0, tiled=True, axis_index_groups=groups)  12.6 us
    pallas_call x6, Pallas kernels, call(): pl.pallas_call(kernel, grid=(1,), in_specs=[full(x.shape) for x in args],...  8.51 us
    all_to_all x1, starting transfers between devices, per_device(): pay = lax.all_to_all(pay, 'col', 0, 0, tiled=True, axis_index_groups=groups)  6.21 us
    pallas_call x1, Pallas kernels, home(): pl.pallas_call(functools.partial(home_kernel, plan), grid=(1,), in_specs=...  6.05 us
    pallas_call x1, Pallas kernels, project(): pl.pallas_call(functools.partial(project_kernel, plan, chunks), grid=(1,)...  3.34 us
    all_to_all x1, waiting for transfers between devices, per_device(): pay = lax.all_to_all(pay, 'col', 0, 0, tiled=True, axis_index_groups=groups)  3.06 us
    ppermute x1, starting transfers between devices, scan_calls(): lax.ppermute(last, col_axis, [(k, k + plan.devices) for k in range(plan.d...  2.97 us
    ppermute x1, starting transfers between devices, scan_calls(): entry = lax.ppermute(tops, row_axis, chain)  1.31 us
  transfers between devices with their start and end apart: 3, of which 2 were waited for; matrix products, arithmetic and copies ran while one was open for 0% of the time, Pallas kernels for 25%

profile of v18, /device:TPU:0, one launch (start us, length us, event | category | flops | bytes accessed | tf_op | source)
XLA Modules:
  0.0 44.2 jit_solution(1191111748784678905)
XLA Ops:
  0.0 3.3 %project.1 = (bf16[256,1024]{1,0:T(8,128)(2,1)S(1)}, bf16[8,256,128]{2,1,0:T(8,128)(2,1)}, f32[48,256]{1,0:T(8,128)S(1)}, bf16[200,1024]{1,0:T(8,128)(2,1)S(1)}) custom-call(f32[16]{0:T(128)} %bias_hbm.1, f32[16]{0:T(128)} %refs_0_.1, f32[16]{0:T(128)} %refs_1_.1, bf16[28,7,1024]{2,1,0:T(8,128)(2,1)} %x_hbm.1, bf16[1024,2048]{1,0:T(8,128)(2,1)} %w_hbm.3, ...), custom_call_target="tpu_custom_call" | custom-call | tf_op jit(solution)/shard_map/project/pallas_call | solution.py:263
  3.4 6.2 %all-to-all-start = ((bf16[8,256,128]{2,1,0:T(8,128)(2,1)}), bf16[8,256,128]{2,1,0:T(8,128)(2,1)S(1)}, u32[]{:S(2)}, u32[]{:S(2)}) async-start(bf16[8,256,128]{2,1,0:T(8,128)(2,1)} %get-tuple-element.25), calls=%async_computation | async-start | bytes 1048576 | tf_op jit(solution)/shard_map/all_to_all | solution.py:753
  9.6 6.1 %home.1 = (bf16[200,1024]{1,0:T(8,128)(2,1)S(1)}, bf16[200,1024]{1,0:T(8,128)(2,1)S(1)}, f32[1,1024]{1,0:T(1,128)S(1)}) custom-call(bf16[256,1024]{1,0:T(8,128)(2,1)S(1)} %get-tuple-element.26.v_ref, f32[48,256]{1,0:T(8,128)S(1)} %get-tuple-element.27.rows_ref, bf16[200,1024]{1,0:T(8,128)(2,1)S(1)} %get-tuple-element.28.flat_ref, bf16[1024,2048]{1,0:T(8,128)(2,1)} %w_hbm.3, ...), custom_call_target="tpu_custom_call" | custom-call | tf_op jit(solution)/shard_map/home/pallas_call | solution.py:341
  15.6 3.1 %all-to-all-done.pay_ref = bf16[8,256,128]{2,1,0:T(8,128)(2,1)S(1)} async-done(((bf16[8,256,128]{2,1,0:T(8,128)(2,1)}), bf16[8,256,128]{2,1,0:T(8,128)(2,1)S(1)}, u32[]{:S(2)}, u32[]{:S(2)}) %all-to-all-start) | async-done | bytes 524320 | tf_op jit(solution)/shard_map/all_to_all | solution.py:753
  18.7 1.5 %last.1 = bf16[7,64,128]{2,1,0:T(8,128)(2,1)S(1)} custom-call(bf16[8,256,128]{2,1,0:T(8,128)(2,1)S(1)} %all-to-all-done.pay_ref), custom_call_target="tpu_custom_call" | custom-call | tf_op jit(solution)/shard_map/last/pallas_call | solution.py:631
  20.2 3.0 %collective-permute-start = (bf16[7,64,128]{2,1,0:T(8,128)(2,1)S(1)}, bf16[7,64,128]{2,1,0:T(8,128)(2,1)S(1)}, u32[]{:S(2)}, u32[]{:S(2)}) collective-permute-start(bf16[7,64,128]{2,1,0:T(8,128)(2,1)S(1)} %last.1), channel_id=1, source_target_pairs={{0,8},{1,9},{2,10},{3,11},{4,12},{5,13},{6,14},{7,15},{16,24},{17,... | collective-permute-start | bytes 344072 | tf_op jit(solution)/shard_map/ppermute | solution.py:650
  23.2 4.0 %maps.1 = (bf16[16,32,256]{2,1,0:T(8,128)(2,1)S(1)}, f32[16,256]{1,0:T(8,128)S(1)}, bf16[16,448,128]{2,1,0:T(8,128)(2,1)S(1)}, f32[16,64,128]{2,1,0:T(8,128)S(1)...) custom-call(bf16[8,256,128]{2,1,0:T(8,128)(2,1)S(1)} %all-to-all-done.pay_ref, ...), custom_call_target="tpu_custom_call" | custom-call | tf_op jit(solution)/shard_map/maps/pallas_call | solution.py:631
  27.2 0.0 collective-permute-done.entry_ref
  27.2 1.3 %collective-permute-start.1 = (bf16[16,64,128]{2,1,0:T(8,128)(2,1)S(1)}, bf16[16,64,128]{2,1,0:T(8,128)(2,1)S(1)}, u32[]{:S(2)}, u32[]{:S(2)}) collective-permute-start(bf16[16,64,128]{2,1,0:T(8,128)(2,1)S(1)} %join.1), channel_id=1, source_target_pairs={{0,16},{1,17},{2,18},{3,19},{4,20},{5,21},{6,22},{7,23},{8,24},{9,... | collective-permute-start | bytes 786440 | tf_op jit(solution)/shard_map/ppermute | solution.py:678
  28.6 1.0 %sides.1 = (f32[16,64,256]{2,1,0:T(8,128)S(1)}, bf16[16,128,256]{2,1,0:T(8,128)(2,1)S(1)}) custom-call(bf16[8,16,256]{2,1,0:T(8,128)(2,1)S(1)} %get-tuple-element.33.c_ref, bf16[16,64,448]{2,1,0:T(8,128)(2,1)S(1)} %get-tuple-element.34.edge_ref, f32[16,448]{1,0:T(8,128)S(1)} %get-tuple-element.35.upto_ref, ...), custom_call_target="tpu_custom_call" | custom-call | tf_op jit(solution)/shard_map/sides/pallas_call | solution.py:631
  29.5 0.0 copy-start
  29.5 0.1 collective-permute-done.1.top_ref
  29.7 0.4 cells.1
  30.1 12.6 %all_to_all.10.y_ref = bf16[8,200,128]{2,1,0:T(8,128)(2,1)S(1)} all-to-all(bf16[8,200,128]{2,1,0:T(8,128)(2,1)S(1)} %cells.1), channel_id=1, replica_groups={{0,1,2,3,4,5,6,7},{8,9,10,11,12,13,14,15},{16,17,18,19,20,21,22,23},{24..., dimensions={0} | all-to-all | bytes 819200 | tf_op jit(solution)/shard_map/all_to_all | solution.py:758
  42.6 0.0 copy-done
  42.6 1.6 %finish.1 = bf16[28,7,1024]{2,1,0:T(8,128)(2,1)} custom-call(bf16[8,200,128]{2,1,0:T(8,128)(2,1)S(1)} %all_to_all.10.y_ref, bf16[200,1024]{1,0:T(8,128)(2,1)S(1)} %get-tuple-element.42.own_ref, bf16[200,1024]{1,0:T(8,128)(2,1)S(1)} %get-tuple-element.43.gate_ref, f32[1,1024]{1,0:T(1,128)S(1)} %get-tuple-element.44.gain_ref, bf16[1024,1024]{1,0:T(8,128)(2,1)S(1)} %copy-done), custom_call_target="tpu_custom_call" | custom-call | tf_op jit(solution)/shard_map/finish/pallas_call | solution.py:631
  (1 shorter events, 0.0 us)
Async XLA Ops:
  3.4 15.3 %all-to-all-start = ((bf16[8,256,128]{2,1,0:T(8,128)(2,1)}), bf16[8,256,128]{2,1,0:T(8,128)(2,1)S(1)}, u32[]{:S(2)}, u32[]{:S(2)}) async-start(bf16[8,256,128]{2,1,0:T(8,128)(2,1)} %get-tuple-element.25), calls=%async_computation | async-start | bytes 1048576 | tf_op jit(solution)/shard_map/all_to_all | solution.py:753
  20.2 7.0 %collective-permute-start = (bf16[7,64,128]{2,1,0:T(8,128)(2,1)S(1)}, bf16[7,64,128]{2,1,0:T(8,128)(2,1)S(1)}, u32[]{:S(2)}, u32[]{:S(2)}) collective-permute-start(bf16[7,64,128]{2,1,0:T(8,128)(2,1)S(1)} %last.1), channel_id=1, source_target_pairs={{0,8},{1,9},{2,10},{3,11},{4,12},{5,13},{6,14},{7,15},{16,24},{17,... | collective-permute-start | bytes 344072 | tf_op jit(solution)/shard_map/ppermute | solution.py:650
  27.2 2.4 %collective-permute-start.1 = (bf16[16,64,128]{2,1,0:T(8,128)(2,1)S(1)}, bf16[16,64,128]{2,1,0:T(8,128)(2,1)S(1)}, u32[]{:S(2)}, u32[]{:S(2)}) collective-permute-start(bf16[16,64,128]{2,1,0:T(8,128)(2,1)S(1)} %join.1), channel_id=1, source_target_pairs={{0,16},{1,17},{2,18},{3,19},{4,20},{5,21},{6,22},{7,23},{8,24},{9,... | collective-permute-start | bytes 786440 | tf_op jit(solution)/shard_map/ppermute | solution.py:678
  29.5 13.1 %copy-start = (bf16[1024,1024]{1,0:T(8,128)(2,1)S(1)}, bf16[1024,1024]{1,0:T(8,128)(2,1)}, u32[]{:S(2)}) copy-start(bf16[1024,1024]{1,0:T(8,128)(2,1)} %w_ref.1) | copy-start | bytes 6291460
